TPU v7x, 32 devices: a whole 2x2x4 slice. The times are simulated.
32 devices in a mesh: ctx: 8 (over z, x), head: 4 (over y, core).
Axes of the slice: x: 2, y: 2, z: 4, core: 2. Of those that a mesh axis runs over, the one named last changes fastest.
Arguments:
- queries: bfloat16 [8192, 4096], P('ctx', 'head'), may hold values from -24 to 24
- keys: bfloat16 [8192, 4096], P('ctx', 'head'), may hold values from -4 to 4
- values: bfloat16 [8192, 4096], P('ctx', 'head'), may hold values from -6 to 6
- cluster_of: int32 [32, 8192], P('head', 'ctx'), may hold values from 0 to 255, as said below
- slot_of: int32 [32, 8192], P('head', 'ctx'), may hold values from 0 to 7
- centroids: float32 [32, 256, 128], P('head', 'ctx'), may hold values from -6 to 6
- out_weight: bfloat16 [4096, 4096], P('head'), may hold values from -0.125 to 0.125
Outputs:
- projected: bfloat16 [8192, 4096], P('ctx', 'head')
- new_centroids: float32 [32, 256, 128], P('head', 'ctx')
Inputs may be any that keep to these rules, and one draw needn't show every extreme that they name: `cluster_of`: within the tokens of one index of ctx and one head, no two tokens share both cluster and slot, and in every such block some cluster holds all 8 slots; a cluster of a head may hold no token at all.
All inputs are finite; a program needn't handle non-finite values.
Results may differ from a plain program's by a relative error of at most 0.0085.
Values may be sent and summed in bfloat16 or wider, within the bound.
No kernel may reach another device: no remote copies, remote signals or barrier semaphores. Data moves between devices by JAX's collectives and lax.ppermute only.
A program may use at most 128 MiB of HBM per device.

v0:
```python
import math

import jax
import jax.numpy as jnp
from jax import lax
from jax.sharding import PartitionSpec as P

CLUSTERS = 256
SLOTS = 8


mix_rate = 0.5
neg_fill = -1e30


def attend(q_rows, k_rows, v_rows, positions):
    scale = 1.0 / math.sqrt(q_rows.shape[-1])
    scores = jnp.einsum("gqd,gkd->gqk", q_rows, k_rows, preferred_element_type=jnp.float32) * scale
    allowed = (positions[:, None, :] >= 0) & (positions[:, None, :] <= positions[:, :, None])
    scores = jnp.where(allowed, scores, neg_fill)
    top = jnp.max(scores, axis=2, keepdims=True)
    weights = jnp.where(allowed, jnp.exp(scores - top), 0.0).astype(jnp.bfloat16)
    total = jnp.sum(weights.astype(jnp.float32), axis=2, keepdims=True)
    mixed = jnp.einsum("gqk,gkd->gqd", weights, v_rows, preferred_element_type=jnp.float32)
    return (mixed / jnp.where(total > 0.0, total, 1.0)).astype(jnp.bfloat16)


def to_clusters(rows, cl_dev):
    senders, width, items = (rows.shape[0], rows.shape[1], rows.shape[2])
    slots = width // cl_dev
    shaped = rows.reshape((senders, cl_dev, slots, items) + rows.shape[3:])
    if rows.ndim == 4:
        order = (3, 1, 0, 2, 4)
    else:
        order = (3, 1, 0, 2)
    return jnp.transpose(shaped, order).reshape((items * cl_dev, senders * slots) + rows.shape[3:])


def from_clusters(mixed, senders, cl_dev, items):
    slots = mixed.shape[1] // senders
    shaped = mixed.reshape(items, cl_dev, senders, slots, mixed.shape[2])
    return jnp.transpose(shaped, (2, 1, 3, 0, 4)).reshape(
        senders, cl_dev * slots, items, mixed.shape[2]
    )


def owner_work(incoming, cl_dev):
    q_in, k_in, v_in, p_in = incoming
    senders, items = (q_in.shape[0], q_in.shape[2])
    q_rows = to_clusters(q_in, cl_dev)
    k_rows = to_clusters(k_in, cl_dev)
    v_rows = to_clusters(v_in, cl_dev)
    p_rows = to_clusters(p_in, cl_dev)
    mixed = attend(q_rows, k_rows, v_rows, p_rows)
    back = from_clusters(mixed, senders, cl_dev, items)
    return back


def body(queries, keys, values, cluster_of, slot_of, centroids, out_weight):
    ranks = lax.axis_size("ctx")
    rank_here = lax.axis_index("ctx")
    tok_rows = queries.shape[0]
    head_rows = cluster_of.shape[0]
    head_size = queries.shape[1] // head_rows
    cl_dev = CLUSTERS // ranks
    width = CLUSTERS * SLOTS
    target = jnp.transpose(cluster_of * SLOTS + slot_of)
    head_ids = jnp.broadcast_to(jnp.arange(head_rows, dtype=jnp.int32)[None, :], target.shape)

    def place(rows):
        shaped = rows.reshape(tok_rows, head_rows, head_size)
        filled = (
            jnp.zeros((width, head_rows, head_size), rows.dtype).at[target, head_ids].set(shaped)
        )
        return filled.reshape(ranks, width // ranks, head_rows, head_size)

    token_pos = rank_here * tok_rows + jnp.arange(tok_rows, dtype=jnp.int32)
    pos_slots = (
        jnp.full((width, head_rows), -1, jnp.int32)
        .at[target, head_ids]
        .set(jnp.broadcast_to(token_pos[:, None], target.shape))
    )
    pos_slots = pos_slots.reshape(ranks, width // ranks, head_rows)
    incoming = (
        lax.all_to_all(place(queries), "ctx", split_axis=0, concat_axis=0, tiled=True),
        lax.all_to_all(place(keys), "ctx", split_axis=0, concat_axis=0, tiled=True),
        lax.all_to_all(place(values), "ctx", split_axis=0, concat_axis=0, tiled=True),
        lax.all_to_all(pos_slots, "ctx", split_axis=0, concat_axis=0, tiled=True),
    )
    worked = owner_work(incoming, cl_dev)
    returned = lax.all_to_all(worked, "ctx", split_axis=0, concat_axis=0, tiled=True)
    rows_back = returned.reshape(width, head_rows, head_size)
    attended = rows_back[target, head_ids].reshape(tok_rows, head_rows * head_size)
    member = (
        cluster_of[:, :, None] == jnp.arange(CLUSTERS, dtype=jnp.int32)[None, None, :]
    ).astype(jnp.bfloat16)
    q_three = queries.reshape(tok_rows, head_rows, head_size)
    k_three = keys.reshape(tok_rows, head_rows, head_size)
    local_sums = jnp.einsum("htc,thd->hcd", member, q_three, preferred_element_type=jnp.float32)
    local_sums = local_sums + jnp.einsum(
        "htc,thd->hcd", member, k_three, preferred_element_type=jnp.float32
    )
    local_counts = jnp.sum(member, axis=1, dtype=jnp.float32)
    totals, counts = (
        lax.psum_scatter(
            local_sums.astype(jnp.bfloat16), "ctx", scatter_dimension=1, tiled=True
        ).astype(jnp.float32),
        lax.psum_scatter(
            local_counts.astype(jnp.bfloat16), "ctx", scatter_dimension=1, tiled=True
        ).astype(jnp.float32),
    )
    means = totals / (2.0 * jnp.maximum(counts, 1.0))[:, :, None]
    new_centroids = mix_rate * centroids + (1.0 - mix_rate) * means
    summed = lax.psum_scatter(
        lax.dot_general(
            out_weight, attended, (((0,), (1,)), ((), ())), preferred_element_type=jnp.float32
        ),
        "head",
        scatter_dimension=0,
        tiled=True,
    )
    projected = jnp.transpose(summed).astype(jnp.bfloat16)
    return (projected, new_centroids)


def solution(mesh):
    in_specs = (
        P("ctx", "head"),
        P("ctx", "head"),
        P("ctx", "head"),
        P("head", "ctx"),
        P("head", "ctx"),
        P("head", "ctx", None),
        P("head", None),
    )
    out_specs = (P("ctx", "head"), P("head", "ctx", None))
    return jax.shard_map(body, mesh=mesh, in_specs=in_specs, out_specs=out_specs, check_vma=False)
```

profile of v0, /device:TPU:0, one launch (start us, length us, event | category | flops | bytes accessed | tf_op | source)
XLA Modules:
  0.0 731.0 jit_solution(1626910484176494951)
XLA Ops:
  10.6 30.5 %scatter_custom_fusion = s32[16384]{0:T(1024)S(1)} fusion(s32[8192]{0:T(1024)S(1)} %reshape.135, s32[8192]{0:T(1024)S(1)} %reshape.137, s32[]{:T(128)} %constant.15.clone.1), kind=kCustom, calls=%fused_computation.47 | custom fusion | bytes 65540
  41.7 7.3 all-to-all-start
  51.7 23.9 %scatter_custom_fusion.2 = bf16[16384,128]{1,0:T(8,128)(2,1)} fusion(s32[8192]{0:T(1024)S(1)} %reshape.141, bf16[8192,128]{1,0:T(8,128)(2,1)} %reshape.149, bf16[]{:T(256)} %constant.7.clone.1), kind=kCustom, calls=%fused_computation.31 | custom fusion | bytes 4194816
  75.6 6.1 all-to-all-start.2
  84.1 23.9 %scatter_custom_fusion.1 = bf16[16384,128]{1,0:T(8,128)(2,1)} fusion(s32[8192]{0:T(1024)S(1)} %reshape.141, bf16[8192,128]{1,0:T(8,128)(2,1)} %reshape.143, bf16[]{:T(256)} %constant.7.clone.1), kind=kCustom, calls=%fused_computation.33 | custom fusion | bytes 4194816
  108.0 66.5 %all-to-all-done.2 = bf16[8,256,8,128]{3,2,1,0:T(8,128)(2,1)} async-done(((bf16[8,256,8,128]{3,2,1,0:T(8,128)(2,1)}), bf16[8,256,8,128]{3,2,1,0:T(8,128)(2,1)}, u32[]{:S(2)}, u32[]{:S(2)}) %all-to-all-start.2) | async-done | bytes 4194336 | tf_op jit(solution)/shard_map/all_to_all | solution.py:86
  174.5 4.9 all-to-all-start.1
  181.7 23.9 %scatter_custom_fusion.3 = bf16[16384,128]{1,0:T(8,128)(2,1)} fusion(s32[8192]{0:T(1024)S(1)} %reshape.141, bf16[8192,128]{1,0:T(8,128)(2,1)} %reshape.155, bf16[]{:T(256)} %constant.7.clone.1), kind=kCustom, calls=%fused_computation.29 | custom fusion | bytes 4194816
  205.6 66.2 %all-to-all-done.1 = bf16[8,256,8,128]{3,2,1,0:T(8,128)(2,1)} async-done(((bf16[8,256,8,128]{3,2,1,0:T(8,128)(2,1)}), bf16[8,256,8,128]{3,2,1,0:T(8,128)(2,1)}, u32[]{:S(2)}, u32[]{:S(2)}) %all-to-all-start.1) | async-done | bytes 4194336 | tf_op jit(solution)/shard_map/all_to_all | solution.py:85
  271.8 4.5 all-to-all-start.3
  277.7 5.3 copy.31
  283.0 5.3 copy.30
  288.3 12.5 %convert_reduce_fusion = (f32[256,64]{1,0:T(8,128)S(1)}, bf16[256,64,64]{1,2,0:T(8,128)(2,1)}) fusion(s32[256,64]{1,0:T(8,128)S(1)} %copy.27, pred[256,64]{1,0:T(8,128)(4,1)S(1)} %copy.26, bf16[256,64,128]{2,1,0:T(8,128)(2,1)} %bitcast.76, bf16[256,64,128]{2,1,0:T(8,128)(2,1)} %bitcast.75), kind=kOutput, calls=%fused_computation.12 | convolution fusion | flops 279969856 | bytes 10633216 | tf_op jit(solution)/shard_map/sub | solution.py:22
  300.9 67.9 %all-to-all-done.3 = bf16[8,256,8,128]{3,2,1,0:T(8,128)(2,1)} async-done(((bf16[8,256,8,128]{3,2,1,0:T(8,128)(2,1)}), bf16[8,256,8,128]{3,2,1,0:T(8,128)(2,1)}, u32[]{:S(2)}, u32[]{:S(2)}) %all-to-all-start.3) | async-done | bytes 4194336 | tf_op jit(solution)/shard_map/all_to_all | solution.py:87
  368.8 3.5 copy.32
  372.3 4.3 divide_convert_fusion
  376.6 6.8 copy.34
  383.4 4.7 all-to-all-start.4
  391.7 2.5 fusion.26
  394.8 86.8 %all-to-all-done.4 = bf16[8,256,8,128]{3,2,1,0:T(8,128)(2,1)} async-done(((bf16[8,256,8,128]{3,2,1,0:T(8,128)(2,1)}), bf16[8,256,8,128]{3,2,1,0:T(8,128)(2,1)}, u32[]{:S(2)}, u32[]{:S(2)}) %all-to-all-start.4) | async-done | bytes 4194336 | tf_op jit(solution)/shard_map/all_to_all | solution.py:91
  481.5 95.3 %gather_fusion = bf16[8192,128]{1,0:T(8,128)(2,1)S(1)} fusion(bf16[2048,8,128]{2,1,0:T(8,128)(2,1)} %bitcast.20, s32[8192]{0:T(1024)S(1)} %reshape.129), kind=kCustom, calls=%fused_computation | custom fusion | bytes 4259840 | tf_op jit(solution)/shard_map/gather | solution.py:93
  579.1 16.0 %convolution_bitcast_fusion = f32[4096,1024]{0,1:T(8,128)} fusion(bf16[1024,1024]{1,0:T(8,128)(2,1)} %reshape.109, bf16[1024,4096]{1,0:T(8,128)(2,1)} %param.13), kind=kOutput, calls=%fused_computation.6 | convolution fusion | flops 8589934592 | bytes 27262976 | tf_op jit(solution)/shard_map/dot_general | solution.py:115
  597.6 123.1 %reduce-scatter.6.cloned.1.call-done = f32[1024,1024]{0,1:T(8,128)} async-done(((f32[4096,1024]{0,1:T(8,128)}), f32[1024,1024]{0,1:T(8,128)}) %reduce-scatter.6.cloned.1.call-update) | async-done | bytes 4194320 | tf_op jit(solution)/shard_map/reduce_scatter | solution.py:114
  720.6 3.8 convert_bitcast_fusion
  (57 shorter events, 21.5 us)
Async XLA Ops:
  7.2 42.3 %copy-start.1 = (bf16[1024,1024]{1,0:T(8,128)(2,1)S(1)}, bf16[1024,1024]{1,0:T(8,128)(2,1)}, u32[]{:S(2)}) copy-start(bf16[1024,1024]{1,0:T(8,128)(2,1)} %param.8) | copy-start | bytes 6291460
  41.7 33.9 %all-to-all-start = ((s32[8,256,8]{1,2,0:T(8,128)}), s32[8,256,8]{1,2,0:T(8,128)S(1)}, u32[]{:S(2)}, u32[]{:S(2)}) async-start(s32[8,256,8]{1,2,0:T(8,128)} %bitcast.3), calls=%async_computation | async-start | bytes 131072 | tf_op jit(solution)/shard_map/all_to_all | solution.py:88
  75.6 6.1 copy-start.3
  75.6 98.9 %all-to-all-start.2 = ((bf16[8,256,8,128]{3,2,1,0:T(8,128)(2,1)}), bf16[8,256,8,128]{3,2,1,0:T(8,128)(2,1)}, u32[]{:S(2)}, u32[]{:S(2)}) async-start(bf16[8,256,8,128]{3,2,1,0:T(8,128)(2,1)} %bitcast.73), calls=%async_computation.2 | async-start | bytes 8388608 | tf_op jit(solution)/shard_map/all_to_all | solution.py:86
  174.5 4.9 copy-start
  174.5 97.3 %all-to-all-start.1 = ((bf16[8,256,8,128]{3,2,1,0:T(8,128)(2,1)}), bf16[8,256,8,128]{3,2,1,0:T(8,128)(2,1)}, u32[]{:S(2)}, u32[]{:S(2)}) async-start(bf16[8,256,8,128]{3,2,1,0:T(8,128)(2,1)} %bitcast.72), calls=%async_computation.1 | async-start | bytes 8388608 | tf_op jit(solution)/shard_map/all_to_all | solution.py:85
  271.8 96.9 %all-to-all-start.3 = ((bf16[8,256,8,128]{3,2,1,0:T(8,128)(2,1)}), bf16[8,256,8,128]{3,2,1,0:T(8,128)(2,1)}, u32[]{:S(2)}, u32[]{:S(2)}) async-start(bf16[8,256,8,128]{3,2,1,0:T(8,128)(2,1)} %bitcast.71), calls=%async_computation.3 | async-start | bytes 8388608 | tf_op jit(solution)/shard_map/all_to_all | solution.py:87
  368.8 3.5 copy-start.7
  383.4 4.7 copy-start.5
  383.4 6.7 copy-start.2
  383.4 98.1 %all-to-all-start.4 = ((bf16[8,256,8,128]{3,2,1,0:T(8,128)(2,1)}), bf16[8,256,8,128]{3,2,1,0:T(8,128)(2,1)}, u32[]{:S(2)}, u32[]{:S(2)}) async-start(bf16[8,256,8,128]{3,2,1,0:T(8,128)(2,1)} %bitcast.70), calls=%async_computation.4 | async-start | bytes 8388608 | tf_op jit(solution)/shard_map/all_to_all | solution.py:91
  388.1 207.0 %reduce-scatter.10.cloned.1.call-start = ((), (), s32[]{:S(2)}) async-start(), calls=%async_computation.10 | async-start | bytes 73728
  389.8 206.1 %reduce-scatter.8.cloned.1.call-start = ((), (), s32[]{:S(2)}) async-start(), calls=%async_computation.9 | async-start | bytes 589824 | tf_op jit(solution)/shard_map/reduce_scatter | solution.py:105
  390.1 1.6 copy-start.4
  394.2 326.4 %reduce-scatter.6.cloned.1.call-start = ((), (), s32[]{:S(2)}) async-start(), calls=%async_computation.8 | async-start | bytes 20971520 | tf_op jit(solution)/shard_map/reduce_scatter | solution.py:114
  595.0 0.9 copy-start.6
Sparse Core Ops, SparseCore 0:
  392.9 102.7 reduce-scatter.9
  499.0 61.3 reduce-scatter.7
  595.2 125.3 reduce-scatter.5
where the time goes:
time: 733 us; the launch traced here: 731 us
  waiting for transfers between devices  411 us (56%)
  local copies, waits for them, and re-layouts  233 us (32%)
  matrix products  36.8 us (5%)
  starting transfers between devices  27.8 us (4%)
  between operations  14 us (2%)
  other arithmetic  8.88 us (1%)
    reduce_scatter x1, waiting for transfers between devices, body(): lax.psum_scatter(lax.dot_general(out_weight, attended, (((0,), (1,)), (()...  123 us
    unnamed x27, local copies, waits for them, and re-layouts  105 us
    gather x1, local copies, waits for them, and re-layouts, body(): rows_back[target, head_ids].reshape(tok_rows, head_rows * head_size)  95.3 us
    all_to_all x1, waiting for transfers between devices, body(): lax.all_to_all(worked, 'ctx', split_axis=0, concat_axis=0, tiled=True)  86.8 us
    all_to_all x1, waiting for transfers between devices, body(): lax.all_to_all(place(values), 'ctx', split_axis=0, concat_axis=0, tiled=T...  67.9 us
    all_to_all x1, waiting for transfers between devices, body(): lax.all_to_all(place(keys), 'ctx', split_axis=0, concat_axis=0, tiled=True)  66.5 us
    all_to_all x1, waiting for transfers between devices, body(): lax.all_to_all(place(queries), 'ctx', split_axis=0, concat_axis=0, tiled=...  66.2 us
    dot_general x1, matrix products, body(): lax.dot_general(out_weight, attended, (((0,), (1,)), ((), ())), preferred...  16 us
  transfers between devices with their start and end apart: 8, of which 5 were waited for; matrix products, arithmetic and copies ran while one was open for 31% of the time, Pallas kernels for 0%

commit v1 on v0

--- a/solution.py
+++ b/solution.py
@@ -3,6 +3,8 @@
 import jax
 import jax.numpy as jnp
 from jax import lax
+from jax.experimental import pallas as pl
+from jax.experimental.pallas import tpu as pltpu
 from jax.sharding import PartitionSpec as P
 
 CLUSTERS = 256
@@ -123,6 +125,312 @@
     return (projected, new_centroids)
 
 
+BF16 = jnp.bfloat16
+F32 = jnp.float32
+GROUP = 4
+
+
+def params(limit):
+    return pltpu.CompilerParams(
+        dimension_semantics=("arbitrary",), vmem_limit_bytes=limit * 1024 * 1024
+    )
+
+
+def pick_rows(first, count, target):
+    rows = first + lax.broadcasted_iota(jnp.int32, (count, target.shape[1]), 0)
+    return (rows == target).astype(BF16)
+
+
+def place_pair_kernel(target_ref, q_ref, k_ref, q_out, k_out, p_out, right):
+    tokens = q_ref.shape[1]
+    slots = q_out.shape[0] * SLOTS
+    step = 512
+    right[:, :128] = q_ref[0]
+    right[:, 128:256] = k_ref[0]
+    token = lax.broadcasted_iota(jnp.int32, (tokens, 128), 0)
+    lane = lax.broadcasted_iota(jnp.int32, (tokens, 128), 1)
+    high, low = (token // 32) * 32, token % 32 + 1
+    right[:, 256:] = jnp.where(lane < 64, high, low).astype(F32).astype(BF16)
+    base = (pl.program_id(0) * tokens).astype(F32)
+    target = target_ref[0]
+
+    def move(i, carry):
+        picked = pick_rows(i * step, step, target)
+        out = jnp.dot(picked, right[...], preferred_element_type=F32)
+        where = pl.ds(i * (step // SLOTS), step // SLOTS)
+        q_out[where] = out[:, :128].reshape(step // SLOTS, SLOTS, 128).astype(BF16)
+        k_out[where] = out[:, 128:256].reshape(step // SLOTS, SLOTS, 128).astype(BF16)
+        at = out[:, 256:]
+        at = at + pltpu.roll(at, 64, 1)
+        at = jnp.where(at > 0.0, at + base, 0.0)
+        p_out[where] = at.reshape(step // SLOTS, SLOTS, 128)
+        return carry
+
+    lax.fori_loop(0, slots // step, move, 0)
+
+
+def place_pair(target, pair, tokens):
+    ranks = pair.shape[0]
+    spec_out = pl.BlockSpec((CLUSTERS, SLOTS, 128), lambda j: (0, j, 0))
+    shape = (CLUSTERS, ranks * SLOTS, 128)
+    return pl.pallas_call(
+        place_pair_kernel,
+        grid=(ranks,),
+        in_specs=[
+            pl.BlockSpec((1, 1, tokens), lambda j: (j, 0, 0)),
+            pl.BlockSpec((1, tokens, 128), lambda j: (j, 0, 0)),
+            pl.BlockSpec((1, tokens, 128), lambda j: (j, 1, 0)),
+        ],
+        out_specs=[spec_out, spec_out, spec_out],
+        out_shape=[
+            jax.ShapeDtypeStruct(shape, BF16),
+            jax.ShapeDtypeStruct(shape, BF16),
+            jax.ShapeDtypeStruct(shape, F32),
+        ],
+        scratch_shapes=[pltpu.VMEM((tokens, 384), BF16)],
+        compiler_params=params(40),
+        cost_estimate=pl.CostEstimate(
+            flops=2 * ranks * CLUSTERS * SLOTS * tokens * 512,
+            bytes_accessed=16 * 1024 * 1024,
+            transcendentals=0,
+        ),
+    )(target, pair, pair)
+
+
+def place_one_kernel(target_ref, v_ref, v_out):
+    slots = v_out.shape[0] * SLOTS
+    step = 512
+    target = target_ref[0]
+
+    def move(i, carry):
+        picked = pick_rows(i * step, step, target)
+        out = jnp.dot(picked, v_ref[0], preferred_element_type=F32)
+        where = pl.ds(i * (step // SLOTS), step // SLOTS)
+        v_out[where] = out.reshape(step // SLOTS, SLOTS, 128).astype(BF16)
+        return carry
+
+    lax.fori_loop(0, slots // step, move, 0)
+
+
+def place_one(target, rows, tokens):
+    ranks = rows.shape[0]
+    return pl.pallas_call(
+        place_one_kernel,
+        grid=(ranks,),
+        in_specs=[
+            pl.BlockSpec((1, 1, tokens), lambda j: (j, 0, 0)),
+            pl.BlockSpec((1, tokens, 128), lambda j: (j, 0, 0)),
+        ],
+        out_specs=pl.BlockSpec((CLUSTERS, SLOTS, 128), lambda j: (0, j, 0)),
+        out_shape=jax.ShapeDtypeStruct((CLUSTERS, ranks * SLOTS, 128), BF16),
+        compiler_params=params(40),
+        cost_estimate=pl.CostEstimate(
+            flops=2 * ranks * CLUSTERS * SLOTS * tokens * 256,
+            bytes_accessed=6 * 1024 * 1024,
+            transcendentals=0,
+        ),
+    )(target, rows)
+
+
+def weigh_kernel(q_ref, k_ref, p_ref, w_out, mean_out):
+    rows = q_ref.shape[1]
+    cap = rows // GROUP
+    scale = 1.0 / math.sqrt(q_ref.shape[2])
+    for n in range(q_ref.shape[0]):
+        q, k, at = q_ref[n], k_ref[n], p_ref[n]
+        scores = lax.dot_general(q, k, (((1,), (1,)), ((), ())), preferred_element_type=F32) * scale
+        own = jnp.tile(at, (1, rows // 128))
+        other = jnp.broadcast_to(jnp.transpose(at)[0:1, :], (rows, rows))
+        same = (
+            lax.broadcasted_iota(jnp.int32, (rows, rows), 0) // cap
+            == lax.broadcasted_iota(jnp.int32, (rows, rows), 1) // cap
+        )
+        allowed = same & (other > 0.0) & (other <= own)
+        scores = jnp.where(allowed, scores, neg_fill)
+        top = jnp.max(scores, axis=1, keepdims=True)
+        w_out[n] = jnp.where(allowed, jnp.exp(scores - top), 0.0).astype(BF16)
+        both = q.astype(F32) + k.astype(F32)
+        sums = jnp.sum(both.reshape(GROUP, cap, 128), axis=1)
+        counts = jnp.sum((at > 0.0).astype(F32).reshape(GROUP, cap, 128), axis=1)
+        mean_out[n] = sums / (2.0 * jnp.maximum(counts, 1.0))
+
+
+def weigh(q_rows, k_rows, at):
+    groups, rows = q_rows.shape[0], q_rows.shape[1]
+    step = 4
+    spec = pl.BlockSpec((step, rows, 128), lambda i: (i, 0, 0))
+    return pl.pallas_call(
+        weigh_kernel,
+        grid=(groups // step,),
+        in_specs=[spec, spec, spec],
+        out_specs=[
+            pl.BlockSpec((step, rows, rows), lambda i: (i, 0, 0)),
+            pl.BlockSpec((step, GROUP, 128), lambda i: (i, 0, 0)),
+        ],
+        out_shape=[
+            jax.ShapeDtypeStruct((groups, rows, rows), BF16),
+            jax.ShapeDtypeStruct((groups, GROUP, 128), F32),
+        ],
+        compiler_params=params(40),
+        cost_estimate=pl.CostEstimate(
+            flops=2 * groups * rows * rows * 256,
+            bytes_accessed=24 * 1024 * 1024,
+            transcendentals=groups * rows * rows,
+        ),
+    )(q_rows, k_rows, at)
+
+
+def mix_kernel(w_ref, v_ref, o_out):
+    rows = v_ref.shape[1]
+    ones = jnp.ones((rows, 128), BF16)
+    for n in range(v_ref.shape[0]):
+        right = jnp.concatenate([v_ref[n], ones], axis=1)
+        out = jnp.dot(w_ref[n], right, preferred_element_type=F32)
+        total = out[:, 128:]
+        o_out[n] = (out[:, :128] / jnp.where(total > 0.0, total, 1.0)).astype(BF16)
+
+
+def mix(weights, v_rows):
+    groups, rows = v_rows.shape[0], v_rows.shape[1]
+    step = 8
+    return pl.pallas_call(
+        mix_kernel,
+        grid=(groups // step,),
+        in_specs=[
+            pl.BlockSpec((step, rows, rows), lambda i: (i, 0, 0)),
+            pl.BlockSpec((step, rows, 128), lambda i: (i, 0, 0)),
+        ],
+        out_specs=pl.BlockSpec((step, rows, 128), lambda i: (i, 0, 0)),
+        out_shape=jax.ShapeDtypeStruct((groups, rows, 128), BF16),
+        compiler_params=params(40),
+        cost_estimate=pl.CostEstimate(
+            flops=2 * groups * rows * rows * 256,
+            bytes_accessed=16 * 1024 * 1024,
+            transcendentals=0,
+        ),
+    )(weights, v_rows)
+
+
+def unplace_kernel(target_ref, o_ref, mean_ref, out_ref, right):
+    tokens = target_ref.shape[1]
+    slots = o_ref.shape[0] * SLOTS
+    step = 256
+    right[...] = o_ref[...].astype(F32).reshape(slots, 128).astype(BF16)
+
+    def move(i, carry):
+        target = target_ref[0, pl.ds(i * step, step), :]
+        columns = lax.broadcasted_iota(jnp.int32, (step, slots), 1)
+        picked = (columns == target).astype(BF16)
+        out = jnp.dot(picked, right[...], preferred_element_type=F32)
+        out_ref[0, pl.ds(i * step, step), :] = out.astype(BF16)
+        return carry
+
+    lax.fori_loop(0, tokens // step, move, 0)
+    means = mean_ref[0]
+    high = means.astype(BF16)
+    count = means.shape[0]
+    out_ref[0, tokens : tokens + count, :] = high
+    out_ref[0, tokens + count :, :] = (means - high.astype(F32)).astype(BF16)
+
+
+def unplace(target, mixed, means):
+    ranks, tokens = target.shape[0], target.shape[1]
+    extra = 2 * means.shape[1]
+    return pl.pallas_call(
+        unplace_kernel,
+        grid=(ranks,),
+        in_specs=[
+            pl.BlockSpec((1, tokens, 1), lambda j: (j, 0, 0)),
+            pl.BlockSpec((CLUSTERS, SLOTS, 128), lambda j: (0, j, 0)),
+            pl.BlockSpec((1, means.shape[1], 128), lambda j: (j, 0, 0)),
+        ],
+        out_specs=pl.BlockSpec((1, tokens + extra, 128), lambda j: (j, 0, 0)),
+        out_shape=jax.ShapeDtypeStruct((ranks, tokens + extra, 128), BF16),
+        scratch_shapes=[pltpu.VMEM((CLUSTERS * SLOTS, 128), BF16)],
+        compiler_params=params(40),
+        cost_estimate=pl.CostEstimate(
+            flops=2 * ranks * CLUSTERS * SLOTS * tokens * 256,
+            bytes_accessed=6 * 1024 * 1024,
+            transcendentals=0,
+        ),
+    )(target, mixed, means)
+
+
+def head_body(queries, keys, values, cluster_of, slot_of, centroids, out_weight):
+    ranks = lax.axis_size("ctx")
+    me = lax.axis_index("ctx")
+    mine = lax.axis_index("head")
+    tokens = queries.shape[0]
+    cl_dev = CLUSTERS // ranks
+    cap = ranks * SLOTS
+
+    def swap_y(x):
+        return lax.ppermute(x, "head", [(0, 2), (1, 3), (2, 0), (3, 1)])
+
+    def swap_core(x):
+        return lax.ppermute(x, "head", [(0, 1), (1, 0), (2, 3), (3, 2)])
+
+    def by_head(x):
+        return jnp.transpose(x.reshape(tokens, ranks, 128), (1, 0, 2))
+
+    marks = [x.astype(BF16).reshape(ranks, tokens // 128, 128) for x in (cluster_of, slot_of)]
+    pair = jnp.concatenate([by_head(queries), by_head(keys)] + marks, axis=1)
+    pair = lax.all_to_all(pair, "ctx", split_axis=0, concat_axis=0, tiled=True)
+    rows_v = lax.all_to_all(by_head(values), "ctx", split_axis=0, concat_axis=0, tiled=True)
+
+    lanes = tuple(range(ranks))
+    own_w = jnp.concatenate(
+        [lax.dynamic_slice_in_dim(out_weight, (me ^ d) * 128, 128, 0) for d in lanes], axis=0
+    )
+    cols = out_weight.shape[1] // 4
+    half = 2 * cols
+    y, core = mine // 2, mine % 2
+    keep = lax.dynamic_slice_in_dim(own_w, y * half, half, 1)
+    across = swap_y(lax.dynamic_slice_in_dim(own_w, (1 - y) * half, half, 1))
+    w_parts = [lax.dynamic_slice_in_dim(w, core * cols, cols, 1) for w in (keep, across)]
+    w_parts += [
+        swap_core(lax.dynamic_slice_in_dim(w, (1 - core) * cols, cols, 1)) for w in (keep, across)
+    ]
+
+    marks = pair[:, 2 * tokens :, :].astype(jnp.int32)
+    target = marks[:, : tokens // 128, :] * SLOTS + marks[:, tokens // 128 :, :]
+    target_row = target.reshape(ranks, 1, tokens)
+    target_col = target.reshape(ranks, tokens, 1)
+    q_rows, k_rows, at = place_pair(target_row, pair, tokens)
+
+    def grouped(x):
+        return x.reshape(CLUSTERS // GROUP, GROUP * cap, 128)
+
+    weights, means = weigh(grouped(q_rows), grouped(k_rows), grouped(at))
+    v_rows = place_one(target_row, rows_v, tokens)
+    mixed = mix(weights, grouped(v_rows)).reshape(CLUSTERS, cap, 128)
+    back = unplace(target_col, mixed, means.reshape(ranks, cl_dev, 128))
+
+    got = {0: lax.dynamic_index_in_dim(back, me, 0, False)}
+    for d in (1, 2, 3, 4, 5, 6, 7):
+        block = lax.dynamic_index_in_dim(back, me ^ d, 0, False)
+        got[d] = lax.ppermute(block, "ctx", [(i, i ^ d) for i in range(ranks)])
+
+    total = 0.0
+    for some in ((0, 1, 2, 3), (4, 5), (6, 7)):
+        part = jnp.concatenate([got[d][:tokens] for d in some], axis=1)
+        there = swap_y(part)
+        parts = [part, there, swap_core(part), swap_core(there)]
+        left = jnp.concatenate(parts, axis=1)
+        first = some[0] * 128
+        right = jnp.concatenate([w[first : first + 128 * len(some)] for w in w_parts], axis=0)
+        total = total + jnp.dot(left, right, preferred_element_type=F32)
+    projected = total.astype(BF16)
+
+    sent = jnp.stack([got[d][tokens:] for d in lanes]).astype(F32)
+    sent = sent[:, :cl_dev] + sent[:, cl_dev:]
+    sent = jnp.concatenate(
+        [lax.dynamic_slice_in_dim(sent, me ^ d, 1, 0) for d in lanes], axis=0
+    )
+    new_centroids = mix_rate * centroids + (1.0 - mix_rate) * sent
+    return (projected, new_centroids)
+
+
 def solution(mesh):
     in_specs = (
         P("ctx", "head"),
@@ -134,4 +442,12 @@
         P("head", None),
     )
     out_specs = (P("ctx", "head"), P("head", "ctx", None))
-    return jax.shard_map(body, mesh=mesh, in_specs=in_specs, out_specs=out_specs, check_vma=False)
+    ranks, heads_here = mesh.shape["ctx"], 32 // mesh.shape["head"]
+    whole_heads = ranks == heads_here and ranks & (ranks - 1) == 0 and mesh.shape["head"] == 4
+    return jax.shard_map(
+        head_body if whole_heads else body,
+        mesh=mesh,
+        in_specs=in_specs,
+        out_specs=out_specs,
+        check_vma=False,
+    )

time: 733 us -> 327 us (0.45)
  waiting for transfers between devices: 411 us -> 125 us
  local copies, waits for them, and re-layouts: 233 us -> 61.3 us
  Pallas kernels: 0 us -> 88.2 us
  matrix products: 36.8 us -> 10.4 us
  between operations: 14 us -> 1.29 us
    all_to_all x5 -> x2, waiting for transfers between devices: 287 us -> 68.1 us  [the longest x1 68.1 us: head_body(): pair = lax.all_to_all(pair, 'ctx', split_axis=0, concat_axis=0, tiled=True)]
    reduce_scatter x2 -> x0, waiting for transfers between devices: 123 us -> none  [the longest x1 123 us: body(): lax.psum_scatter(lax.dot_general(out_weight, attended, (((0,), (1,)), (()...]
    gather x1 -> x0, local copies, waits for them, and re-layouts: 95.3 us -> none  [body(): rows_back[target, head_ids].reshape(tok_rows, head_rows * head_size)]
    pallas_call x0 -> x5, Pallas kernels: none -> 88.2 us  [the longest x1 31.3 us: place_pair(): pl.pallas_call(place_pair_kernel, grid=(ranks,), in_specs=[pl.BlockSpec((...]
    unnamed x27 -> x53, local copies, waits for them, and re-layouts: 105 us -> 20.5 us
    ppermute x0 -> x19, waiting for transfers between devices: none -> 57.2 us  [the longest x7 28.6 us: head_body(): got[d] = lax.ppermute(block, 'ctx', [(i, i ^ d) for i in range(ranks)])]
    ppermute x0 -> x19, starting transfers between devices: none -> 20.6 us  [the longest x7 14.4 us: head_body(): got[d] = lax.ppermute(block, 'ctx', [(i, i ^ d) for i in range(ranks)])]
    slice x0 -> x15, local copies, waits for them, and re-layouts: none -> 16.9 us  [the longest x8 16.3 us: head_body(): w[first:first + 128 * len(some)]]
  transfers between devices with their start and end apart: 8 -> 21, of which waited for: 5 -> 9; matrix products, arithmetic and copies ran while one was open for 31% -> 16% of each run, Pallas kernels for 0% -> 27%
where the time goes in v1:
time: 327 us; the launch traced here: 325 us
  waiting for transfers between devices  125 us (38%)
  Pallas kernels  88.2 us (27%)
  local copies, waits for them, and re-layouts  61.3 us (19%)
  starting transfers between devices  31.5 us (10%)
  matrix products  10.4 us (3%)
  other arithmetic  6.89 us (2%)
    all_to_all x1, waiting for transfers between devices, head_body(): pair = lax.all_to_all(pair, 'ctx', split_axis=0, concat_axis=0, tiled=True)  68.1 us
    pallas_call x1, Pallas kernels, place_pair(): pl.pallas_call(place_pair_kernel, grid=(ranks,), in_specs=[pl.BlockSpec((...  31.3 us
    ppermute x7, waiting for transfers between devices, head_body(): got[d] = lax.ppermute(block, 'ctx', [(i, i ^ d) for i in range(ranks)])  28.6 us
    ppermute x4, waiting for transfers between devices, swap_y(): return lax.ppermute(x, 'head', [(0, 2), (1, 3), (2, 0), (3, 1)])  27.2 us
    unnamed x53, local copies, waits for them, and re-layouts  20.5 us
    pallas_call x1, Pallas kernels, unplace(): pl.pallas_call(unplace_kernel, grid=(ranks,), in_specs=[pl.BlockSpec((1,...  17.5 us
    pallas_call x1, Pallas kernels, weigh(): pl.pallas_call(weigh_kernel, grid=(groups // step,), in_specs=[spec, spec...  16.4 us
    slice x8, local copies, waits for them, and re-layouts, head_body(): w[first:first + 128 * len(some)]  16.3 us
  transfers between devices with their start and end apart: 21, of which 9 were waited for; matrix products, arithmetic and copies ran while one was open for 16% of the time, Pallas kernels for 27%

profile of v1, /device:TPU:0, one launch (start us, length us, event | category | flops | bytes accessed | tf_op | source)
XLA Modules:
  0.0 324.8 jit_solution(13404713443695289533)
XLA Ops:
  2.2 2.9 copy.11
  7.4 2.9 copy.9
  12.7 3.6 %pad_maximum_fusion = bf16[8,2064,128]{2,1,0:T(8,128)(2,1)} fusion(bf16[8,8,128]{2,1,0:T(8,128)(2,1)S(1)} %get-tuple-element.43, bf16[8,8,128]{2,1,0:T(8,128)(2,1)S(1)} %get-tuple-element.44, bf16[8,1024,128]{2,1,0:T(8,128)(2,1)} %bitcast.81, bf16[8,1024,128]{2,1,0:T(8,128)(2,1)} %bitcast.82), kind=kLoop, calls=%fused_computation | loop fusion | flops 16908288 | bytes 8454144 | tf_op jit(solution)/shard_map/concatenate | solution.py:377
  16.3 7.3 %all-to-all-start = ((bf16[8,2064,128]{2,1,0:T(8,128)(2,1)}), bf16[8,2064,128]{2,1,0:T(8,128)(2,1)}, u32[]{:S(2)}, u32[]{:S(2)}) async-start(bf16[8,2064,128]{2,1,0:T(8,128)(2,1)} %pad_maximum_fusion), calls=%async_computation | async-start | bytes 8454144 | tf_op jit(solution)/shard_map/all_to_all | solution.py:378
  40.1 4.1 %constant_dynamic-slice_fusion.3 = bf16[1024,1024]{1,0:T(8,128)(2,1)} fusion(bf16[1024,4096]{1,0:T(8,128)(2,1)} %copy-done.1, s32[]{:T(128)S(6)} %dynamic_slice.111), kind=kLoop, calls=%fused_computation.97 | loop fusion | bytes 4194308 | tf_op jit(solution)/shard_map/dynamic_slice | solution.py:392
  44.2 2.9 copy.13
  49.5 68.1 %all-to-all-done.q_ref.k_ref = bf16[8,2064,128]{2,1,0:T(8,128)(2,1)} async-done(((bf16[8,2064,128]{2,1,0:T(8,128)(2,1)}), bf16[8,2064,128]{2,1,0:T(8,128)(2,1)}, u32[]{:S(2)}, u32[]{:S(2)}) %all-to-all-start) | async-done | bytes 4227104 | tf_op jit(solution)/shard_map/all_to_all | solution.py:378
  117.6 3.6 %all-to-all-start.1 = ((bf16[8,1024,128]{2,1,0:T(8,128)(2,1)}), bf16[8,1024,128]{2,1,0:T(8,128)(2,1)S(1)}, u32[]{:S(2)}, u32[]{:S(2)}) async-start(bf16[8,1024,128]{2,1,0:T(8,128)(2,1)} %bitcast.77), calls=%async_computation.1 | async-start | bytes 4194304 | tf_op jit(solution)/shard_map/all_to_all | solution.py:379
  131.0 3.1 constant_dynamic-slice_fusion.2
  139.3 5.3 %reshape.59.target_ref = s32[8,1024,1]{2,1,0:T(8,128)} reshape(s32[8,8,128]{2,1,0:T(8,128)S(1)} %slice_add_fusion.1) | data formatting | bytes 65536 | tf_op jit(solution)/shard_map/reshape | solution.py:398
  144.6 31.3 %shard_map.86 = (bf16[256,64,128]{2,1,0:T(8,128)(2,1)S(1)}, bf16[256,64,128]{2,1,0:T(8,128)(2,1)S(1)}, f32[256,64,128]{2,1,0:T(8,128)}) custom-call(s32[8,1,1024]{2,1,0:T(1,128)S(1)} %bitcast.73, bf16[8,2064,128]{2,1,0:T(8,128)(2,1)} %all-to-all-done.q_ref.k_ref, bf16[8,2064,128]{2,1,0:T(8,128)(2,1)} %all-to-all-done.q_ref.k_ref), custom_call_target="tpu_custom_call" | custom-call | flops 17179869184 | bytes 16777216 | tf_op jit(solution)/shard_map/pallas_call | solution.py:176
  175.9 16.4 %shard_map.87 = (bf16[64,256,256]{2,1,0:T(8,128)(2,1)}, f32[64,4,128]{2,1,0:T(4,128)S(1)}) custom-call(bf16[64,256,128]{2,1,0:T(8,128)(2,1)S(1)} %bitcast.69, bf16[64,256,128]{2,1,0:T(8,128)(2,1)S(1)} %bitcast.70, f32[64,256,128]{2,1,0:T(8,128)} %bitcast.76), custom_call_target="tpu_custom_call" | custom-call | flops 2147483648 | bytes 25165824 | tf_op jit(solution)/shard_map/pallas_call | solution.py:262
  192.3 15.4 %shard_map.88 = bf16[256,64,128]{2,1,0:T(8,128)(2,1)S(1)} custom-call(s32[8,1,1024]{2,1,0:T(1,128)S(1)} %bitcast.74, bf16[8,1024,128]{2,1,0:T(8,128)(2,1)S(1)} %all-to-all-done.1.v_ref), custom_call_target="tpu_custom_call" | custom-call | flops 8589934592 | bytes 6291456 | tf_op jit(solution)/shard_map/pallas_call | solution.py:217
  207.7 7.6 %shard_map.89 = bf16[64,256,128]{2,1,0:T(8,128)(2,1)S(1)} custom-call(bf16[64,256,256]{2,1,0:T(8,128)(2,1)} %get-tuple-element.10.w_ref, bf16[64,256,128]{2,1,0:T(8,128)(2,1)S(1)} %bitcast.72), custom_call_target="tpu_custom_call" | custom-call | flops 2147483648 | bytes 16777216 | tf_op jit(solution)/shard_map/pallas_call | solution.py:296
  215.3 17.5 %shard_map.90 = bf16[8,1088,128]{2,1,0:T(8,128)(2,1)S(1)} custom-call(s32[8,1024,1]{2,1,0:T(8,128)S(1)} %copy-done, bf16[256,64,128]{2,1,0:T(8,128)(2,1)S(1)} %bitcast.71, f32[8,32,128]{2,1,0:T(8,128)S(1)} %bitcast.75), custom_call_target="tpu_custom_call" | custom-call | flops 8589934592 | bytes 6291456 | tf_op jit(solution)/shard_map/pallas_call | solution.py:339
  239.2 3.5 %collective-permute-start.10 = (bf16[1088,128]{1,0:T(8,128)(2,1)S(1)}, bf16[1088,128]{1,0:T(8,128)(2,1)S(1)}, u32[]{:S(2)}, u32[]{:S(2)}) collective-permute-start(bf16[1088,128]{1,0:T(8,128)(2,1)S(1)} %get-tuple-element.20), channel_id=1, source_target_pairs={{0,20},{4,16},{8,28},{12,24},{16,4},{20,0},{24,12},{28,8},{1,21},{... | collective-permute-start | bytes 835592 | tf_op jit(solution)/shard_map/ppermute | solution.py:412
  243.4 7.5 %collective-permute-done = bf16[1088,128]{1,0:T(8,128)(2,1)S(1)} collective-permute-done((bf16[1088,128]{1,0:T(8,128)(2,1)S(1)}, bf16[1088,128]{1,0:T(8,128)(2,1)S(1)}, u32[]{:S(2)}, u32[]{:S(2)}) %collective-permute-start) | collective-permute-done | bytes 278560 | tf_op jit(solution)/shard_map/ppermute | solution.py:412
  250.9 5.0 %collective-permute-start.15 = (bf16[1088,128]{1,0:T(8,128)(2,1)S(1)}, bf16[1088,128]{1,0:T(8,128)(2,1)S(1)}, u32[]{:S(2)}, u32[]{:S(2)}) collective-permute-start(bf16[1088,128]{1,0:T(8,128)(2,1)S(1)} %get-tuple-element.18), channel_id=1, source_target_pairs={{0,28},{4,24},{8,20},{12,16},{16,12},{20,8},{24,4},{28,0},{1,29},{... | collective-permute-start | bytes 835592 | tf_op jit(solution)/shard_map/ppermute | solution.py:412
  256.0 6.6 %collective-permute-done.1 = bf16[1088,128]{1,0:T(8,128)(2,1)S(1)} collective-permute-done((bf16[1088,128]{1,0:T(8,128)(2,1)S(1)}, bf16[1088,128]{1,0:T(8,128)(2,1)S(1)}, u32[]{:S(2)}, u32[]{:S(2)}) %collective-permute-start.1) | collective-permute-done | bytes 278560 | tf_op jit(solution)/shard_map/ppermute | solution.py:412
  266.2 14.5 %collective-permute-done.9 = bf16[1088,128]{1,0:T(8,128)(2,1)S(1)} collective-permute-done((bf16[1088,128]{1,0:T(8,128)(2,1)S(1)}, bf16[1088,128]{1,0:T(8,128)(2,1)S(1)}, u32[]{:S(2)}, u32[]{:S(2)}) %collective-permute-start.9) | collective-permute-done | bytes 278560 | tf_op jit(solution)/shard_map/ppermute | solution.py:412
  283.8 18.1 %collective-permute-done.11 = bf16[1024,256]{1,0:T(8,128)(2,1)S(1)} collective-permute-done((bf16[1024,256]{1,0:T(8,128)(2,1)S(1)}, bf16[1024,256]{1,0:T(8,128)(2,1)S(1)}, u32[]{:S(2)}, u32[]{:S(2)}) %collective-permute-start.11) | collective-permute-done | bytes 524320 | tf_op jit(solution)/shard_map/ppermute | solution.py:368
  302.7 8.6 %collective-permute-done.16 = bf16[1024,256]{1,0:T(8,128)(2,1)S(1)} collective-permute-done((bf16[1024,256]{1,0:T(8,128)(2,1)S(1)}, bf16[1024,256]{1,0:T(8,128)(2,1)S(1)}, u32[]{:S(2)}, u32[]{:S(2)}) %collective-permute-start.16) | collective-permute-done | bytes 524320 | tf_op jit(solution)/shard_map/ppermute | solution.py:368
  316.6 4.5 %fusion = f32[1024,1024]{1,0:T(8,128)S(1)} fusion(bf16[1024,2048]{1,0:T(8,128)(2,1)S(1)} %constant_dynamic-update-slice_fusion, bf16[512,1024]{1,0:T(8,128)(2,1)S(1)} %slice.144, bf16[512,1024]{1,0:T(8,128)(2,1)S(1)} %copy-done.3, bf16[512,1024]{1,0:T(8,128)(2,1)S(1)} %copy-done.2, bf16[512,1024]{1,0:T(8,128)(2,1)S(1)} %constant_dynamic-slice_fusion.1), kind=kOutput, calls=%fused_computation.1 | convolution fusion | flops 4311744512 | bytes 12582912 | tf_op jit(solution)/shard_map/dot_general | solution.py:422
  321.2 3.6 %add_convert_fusion = bf16[1024,1024]{1,0:T(8,128)(2,1)} fusion(f32[1024,1024]{1,0:T(8,128)S(1)} %fusion, f32[1024,1024]{1,0:T(8,128)S(1)} %fusion.8, bf16[1024,1024]{1,0:T(8,128)(2,1)S(1)} %constant_dynamic-update-slice_fusion.12, bf16[256,1024]{1,0:T(8,128)(2,1)S(1)} %get-tuple-element.27, bf16[256,1024]{1,0:T(8,128)(2,1)S(1)} %copy-done.5, ...), kind=kOutput, calls=%fused_computation.9 | convolution fusion | flops 2159017984 | bytes 14680064 | tf_op jit(solution)/shard_map/dot_general | solution.py:422
  (120 shorter events, 59.8 us)
Async XLA Ops:
  16.3 101.2 %all-to-all-start = ((bf16[8,2064,128]{2,1,0:T(8,128)(2,1)}), bf16[8,2064,128]{2,1,0:T(8,128)(2,1)}, u32[]{:S(2)}, u32[]{:S(2)}) async-start(bf16[8,2064,128]{2,1,0:T(8,128)(2,1)} %pad_maximum_fusion), calls=%async_computation | async-start | bytes 8454144 | tf_op jit(solution)/shard_map/all_to_all | solution.py:378
  34.0 4.6 %copy-start.1 = (bf16[1024,4096]{1,0:T(8,128)(2,1)}, bf16[1024,4096]{1,0:T(8,128)(2,1)S(1)}, u32[]{:S(2)}) copy-start(bf16[1024,4096]{1,0:T(8,128)(2,1)S(1)} %dynamic-slice_dynamic-update-slice_fusion) | copy-start | bytes 25165828
  38.6 92.3 %collective-permute-start.6 = (bf16[1024,2048]{1,0:T(8,128)(2,1)}, bf16[1024,2048]{1,0:T(8,128)(2,1)}, u32[]{:S(2)}, u32[]{:S(2)}) collective-permute-start(bf16[1024,2048]{1,0:T(8,128)(2,1)} %constant_dynamic-slice_fusion.4), channel_id=1, source_target_pairs={{0,2},{1,3},{2,0},{3,1},{4,6},{5,7},{6,4},{7,5},{8,10},{9,11},{10,... | collective-permute-start | bytes 12582920 | tf_op jit(solution)/shard_map/ppermute | solution.py:368
  44.2 81.7 %collective-permute-start.7 = (bf16[1024,1024]{1,0:T(8,128)(2,1)}, bf16[1024,1024]{1,0:T(8,128)(2,1)}, u32[]{:S(2)}, u32[]{:S(2)}) collective-permute-start(bf16[1024,1024]{1,0:T(8,128)(2,1)} %constant_dynamic-slice_fusion.3), channel_id=1, source_target_pairs={{0,1},{1,0},{2,3},{3,2},{4,5},{5,4},{6,7},{7,6},{8,9},{9,8},{10,11... | collective-permute-start | bytes 6291464 | tf_op jit(solution)/shard_map/ppermute | solution.py:371
  117.6 74.7 %all-to-all-start.1 = ((bf16[8,1024,128]{2,1,0:T(8,128)(2,1)}), bf16[8,1024,128]{2,1,0:T(8,128)(2,1)S(1)}, u32[]{:S(2)}, u32[]{:S(2)}) async-start(bf16[8,1024,128]{2,1,0:T(8,128)(2,1)} %bitcast.77), calls=%async_computation.1 | async-start | bytes 4194304 | tf_op jit(solution)/shard_map/all_to_all | solution.py:379
  134.1 100.7 %collective-permute-start.8 = (bf16[1024,1024]{1,0:T(8,128)(2,1)}, bf16[1024,1024]{1,0:T(8,128)(2,1)}, u32[]{:S(2)}, u32[]{:S(2)}) collective-permute-start(bf16[1024,1024]{1,0:T(8,128)(2,1)} %constant_dynamic-slice_fusion.2), channel_id=1, source_target_pairs={{0,1},{1,0},{2,3},{3,2},{4,5},{5,4},{6,7},{7,6},{8,9},{9,8},{10,11... | collective-permute-start | bytes 6291464 | tf_op jit(solution)/shard_map/ppermute | solution.py:371
  207.7 7.6 %copy-start = (s32[8,1024,1]{2,1,0:T(8,128)S(1)}, s32[8,1024,1]{2,1,0:T(8,128)}, u32[]{:S(2)}) copy-start(s32[8,1024,1]{2,1,0:T(8,128)} %reshape.59.target_ref) | copy-start | bytes 98308
  233.0 17.9 %collective-permute-start = (bf16[1088,128]{1,0:T(8,128)(2,1)S(1)}, bf16[1088,128]{1,0:T(8,128)(2,1)S(1)}, u32[]{:S(2)}, u32[]{:S(2)}) collective-permute-start(bf16[1088,128]{1,0:T(8,128)(2,1)S(1)} %get-tuple-element.24), channel_id=1, source_target_pairs={{0,4},{4,0},{8,12},{12,8},{16,20},{20,16},{24,28},{28,24},{1,5},{5... | collective-permute-start | bytes 835592 | tf_op jit(solution)/shard_map/ppermute | solution.py:412
  237.3 27.0 %collective-permute-start.2 = (bf16[1088,128]{1,0:T(8,128)(2,1)S(1)}, bf16[1088,128]{1,0:T(8,128)(2,1)S(1)}, u32[]{:S(2)}, u32[]{:S(2)}) collective-permute-start(bf16[1088,128]{1,0:T(8,128)(2,1)S(1)} %get-tuple-element.22), channel_id=1, source_target_pairs={{0,12},{4,8},{8,4},{12,0},{16,28},{20,24},{24,20},{28,16},{1,13},{... | collective-permute-start | bytes 835592 | tf_op jit(solution)/shard_map/ppermute | solution.py:412
  238.9 23.7 %collective-permute-start.1 = (bf16[1088,128]{1,0:T(8,128)(2,1)S(1)}, bf16[1088,128]{1,0:T(8,128)(2,1)S(1)}, u32[]{:S(2)}, u32[]{:S(2)}) collective-permute-start(bf16[1088,128]{1,0:T(8,128)(2,1)S(1)} %get-tuple-element.23), channel_id=1, source_target_pairs={{0,8},{4,12},{8,0},{12,4},{16,24},{20,28},{24,16},{28,20},{1,9},{5... | collective-permute-start | bytes 835592 | tf_op jit(solution)/shard_map/ppermute | solution.py:412
  239.2 41.6 %collective-permute-start.10 = (bf16[1088,128]{1,0:T(8,128)(2,1)S(1)}, bf16[1088,128]{1,0:T(8,128)(2,1)S(1)}, u32[]{:S(2)}, u32[]{:S(2)}) collective-permute-start(bf16[1088,128]{1,0:T(8,128)(2,1)S(1)} %get-tuple-element.20), channel_id=1, source_target_pairs={{0,20},{4,16},{8,28},{12,24},{16,4},{20,0},{24,12},{28,8},{1,21},{... | collective-permute-start | bytes 835592 | tf_op jit(solution)/shard_map/ppermute | solution.py:412
  242.7 37.9 %collective-permute-start.9 = (bf16[1088,128]{1,0:T(8,128)(2,1)S(1)}, bf16[1088,128]{1,0:T(8,128)(2,1)S(1)}, u32[]{:S(2)}, u32[]{:S(2)}) collective-permute-start(bf16[1088,128]{1,0:T(8,128)(2,1)S(1)} %get-tuple-element.21), channel_id=1, source_target_pairs={{0,16},{4,20},{8,24},{12,28},{16,0},{20,4},{24,8},{28,12},{1,17},{... | collective-permute-start | bytes 835592 | tf_op jit(solution)/shard_map/ppermute | solution.py:412
  250.9 31.9 %collective-permute-start.15 = (bf16[1088,128]{1,0:T(8,128)(2,1)S(1)}, bf16[1088,128]{1,0:T(8,128)(2,1)S(1)}, u32[]{:S(2)}, u32[]{:S(2)}) collective-permute-start(bf16[1088,128]{1,0:T(8,128)(2,1)S(1)} %get-tuple-element.18), channel_id=1, source_target_pairs={{0,28},{4,24},{8,20},{12,16},{16,12},{20,8},{24,4},{28,0},{1,29},{... | collective-permute-start | bytes 835592 | tf_op jit(solution)/shard_map/ppermute | solution.py:412
  262.5 20.0 %collective-permute-start.14 = (bf16[1088,128]{1,0:T(8,128)(2,1)S(1)}, bf16[1088,128]{1,0:T(8,128)(2,1)S(1)}, u32[]{:S(2)}, u32[]{:S(2)}) collective-permute-start(bf16[1088,128]{1,0:T(8,128)(2,1)S(1)} %get-tuple-element.19), channel_id=1, source_target_pairs={{0,24},{4,28},{8,16},{12,20},{16,8},{20,12},{24,0},{28,4},{1,25},{... | collective-permute-start | bytes 835592 | tf_op jit(solution)/shard_map/ppermute | solution.py:412
  264.5 37.5 %copy-start.10 = (f32[8,32,128]{2,1,0:T(8,128)S(1)}, f32[8,32,128]{2,1,0:T(8,128)}, u32[]{:S(2)}) copy-start(f32[8,32,128]{2,1,0:T(8,128)} %param.12) | copy-start | bytes 393220
  264.6 47.6 %collective-permute-start.3 = (bf16[1024,512]{1,0:T(8,128)(2,1)S(1)}, bf16[1024,512]{1,0:T(8,128)(2,1)S(1)}, u32[]{:S(2)}, u32[]{:S(2)}) collective-permute-start(bf16[1024,512]{1,0:T(8,128)(2,1)S(1)} %pad_maximum_fusion.1), channel_id=1, source_target_pairs={{0,2},{1,3},{2,0},{3,1},{4,6},{5,7},{6,4},{7,5},{8,10},{9,11},{10,... | collective-permute-start | bytes 3145736 | tf_op jit(solution)/shard_map/ppermute | solution.py:368
  280.6 31.7 %collective-permute-start.4 = (bf16[1024,512]{1,0:T(8,128)(2,1)S(1)}, bf16[1024,512]{1,0:T(8,128)(2,1)S(1)}, u32[]{:S(2)}, u32[]{:S(2)}) collective-permute-start(bf16[1024,512]{1,0:T(8,128)(2,1)S(1)} %pad_maximum_fusion.1), channel_id=1, source_target_pairs={{0,1},{1,0},{2,3},{3,2},{4,5},{5,4},{6,7},{7,6},{8,9},{9,8},{10,11... | collective-permute-start | bytes 3145736 | tf_op jit(solution)/shard_map/ppermute | solution.py:371
  280.9 21.1 %collective-permute-start.11 = (bf16[1024,256]{1,0:T(8,128)(2,1)S(1)}, bf16[1024,256]{1,0:T(8,128)(2,1)S(1)}, u32[]{:S(2)}, u32[]{:S(2)}) collective-permute-start(bf16[1024,256]{1,0:T(8,128)(2,1)S(1)} %pad_maximum_fusion.2), channel_id=1, source_target_pairs={{0,2},{1,3},{2,0},{3,1},{4,6},{5,7},{6,4},{7,5},{8,10},{9,11},{10,... | collective-permute-start | bytes 1572872 | tf_op jit(solution)/shard_map/ppermute | solution.py:368
  282.5 28.9 %collective-permute-start.12 = (bf16[1024,256]{1,0:T(8,128)(2,1)S(1)}, bf16[1024,256]{1,0:T(8,128)(2,1)S(1)}, u32[]{:S(2)}, u32[]{:S(2)}) collective-permute-start(bf16[1024,256]{1,0:T(8,128)(2,1)S(1)} %pad_maximum_fusion.2), channel_id=1, source_target_pairs={{0,1},{1,0},{2,3},{3,2},{4,5},{5,4},{6,7},{7,6},{8,9},{9,8},{10,11... | collective-permute-start | bytes 1572872 | tf_op jit(solution)/shard_map/ppermute | solution.py:371
  283.0 28.3 %collective-permute-start.16 = (bf16[1024,256]{1,0:T(8,128)(2,1)S(1)}, bf16[1024,256]{1,0:T(8,128)(2,1)S(1)}, u32[]{:S(2)}, u32[]{:S(2)}) collective-permute-start(bf16[1024,256]{1,0:T(8,128)(2,1)S(1)} %pad_maximum_fusion.3), channel_id=1, source_target_pairs={{0,2},{1,3},{2,0},{3,1},{4,6},{5,7},{6,4},{7,5},{8,10},{9,11},{10,... | collective-permute-start | bytes 1572872 | tf_op jit(solution)/shard_map/ppermute | solution.py:368
  302.0 10.1 %collective-permute-start.17 = (bf16[1024,256]{1,0:T(8,128)(2,1)S(1)}, bf16[1024,256]{1,0:T(8,128)(2,1)S(1)}, u32[]{:S(2)}, u32[]{:S(2)}) collective-permute-start(bf16[1024,256]{1,0:T(8,128)(2,1)S(1)} %pad_maximum_fusion.3), channel_id=1, source_target_pairs={{0,1},{1,0},{2,3},{3,2},{4,5},{5,4},{6,7},{7,6},{8,9},{9,8},{10,11... | collective-permute-start | bytes 1572872 | tf_op jit(solution)/shard_map/ppermute | solution.py:371
  311.3 1.9 collective-permute-start.13
  311.4 2.5 collective-permute-start.18
  312.1 4.3 %collective-permute-start.5 = (bf16[1024,512]{1,0:T(8,128)(2,1)S(1)}, bf16[1024,512]{1,0:T(8,128)(2,1)S(1)}, u32[]{:S(2)}, u32[]{:S(2)}) collective-permute-start(bf16[1024,512]{1,0:T(8,128)(2,1)S(1)} %collective-permute-done.3), channel_id=1, source_target_pairs={{0,1},{1,0},{2,3},{3,2},{4,5},{5,4},{6,7},{7,6},{8,9},{9,8},{10,11... | collective-permute-start | bytes 3145736 | tf_op jit(solution)/shard_map/ppermute | solution.py:371
  (8 other events, 26.7 us)

commit v2 on v0

--- a/solution.py
+++ b/solution.py
@@ -1,8 +1,11 @@
+import functools
 import math
 
 import jax
 import jax.numpy as jnp
 from jax import lax
+from jax.experimental import pallas as pl
+from jax.experimental.pallas import tpu as pltpu
 from jax.sharding import PartitionSpec as P
 
 CLUSTERS = 256
@@ -123,6 +126,407 @@
     return (projected, new_centroids)
 
 
+BF16 = jnp.bfloat16
+F32 = jnp.float32
+PAIR = 2
+EMPTY = 1e9
+
+
+def params(limit):
+    return pltpu.CompilerParams(
+        dimension_semantics=("arbitrary",), vmem_limit_bytes=limit * 1024 * 1024
+    )
+
+
+def cost(flops, nbytes, transcendentals=0):
+    return pl.CostEstimate(
+        flops=flops, bytes_accessed=nbytes, transcendentals=transcendentals
+    )
+
+
+def pack_first_kernel(q_ref, k_ref, v_ref, marks_ref, out_ref):
+    tokens, some = q_ref.shape[0], v_ref.shape[0]
+    out_ref[0, :tokens] = q_ref[...]
+    out_ref[0, tokens : 2 * tokens] = k_ref[...]
+    out_ref[0, 2 * tokens : 2 * tokens + some] = v_ref[...]
+    out_ref[0, 2 * tokens + some :] = marks_ref[0]
+
+
+def pack_first(queries, keys, values, marks, some):
+    tokens, heads = queries.shape[0], marks.shape[0]
+    rows = 2 * tokens + some + marks.shape[1]
+    whole = pl.BlockSpec((tokens, 128), lambda j: (0, j))
+    return pl.pallas_call(
+        pack_first_kernel,
+        grid=(heads,),
+        in_specs=[
+            whole,
+            whole,
+            pl.BlockSpec((some, 128), lambda j: (0, j)),
+            pl.BlockSpec((1, marks.shape[1], 128), lambda j: (j, 0, 0)),
+        ],
+        out_specs=pl.BlockSpec((1, rows, 128), lambda j: (j, 0, 0)),
+        out_shape=jax.ShapeDtypeStruct((heads, rows, 128), BF16),
+        compiler_params=params(60),
+        cost_estimate=cost(0, 2 * heads * rows * 256),
+    )(queries, keys, values, marks)
+
+
+def pack_rest_kernel(v_ref, out_ref):
+    out_ref[0] = v_ref[...]
+
+
+def pack_rest(values, heads, some):
+    rest = values.shape[0] - some
+    return pl.pallas_call(
+        pack_rest_kernel,
+        grid=(heads,),
+        in_specs=[pl.BlockSpec((rest, 128), lambda j: (1, j))],
+        out_specs=pl.BlockSpec((1, rest, 128), lambda j: (j, 0, 0)),
+        out_shape=jax.ShapeDtypeStruct((heads, rest, 128), BF16),
+        compiler_params=params(60),
+        cost_estimate=cost(0, 2 * heads * rest * 256),
+    )(values)
+
+
+def match(first, count, target):
+    rows = first + lax.broadcasted_iota(jnp.int32, (count, target.shape[1]), 0)
+    return rows == target
+
+
+def by_slot(x):
+    return x.reshape(x.shape[0] // SLOTS, SLOTS, 128)
+
+
+def place_pair_kernel(target_ref, q_ref, k_ref, q_out, k_out, p_out, right):
+    tokens = q_ref.shape[1]
+    slots = q_out.shape[0] * SLOTS
+    step = 1024
+    right[:, :128] = q_ref[0]
+    right[:, 128:] = k_ref[0]
+    base = pl.program_id(0) * tokens
+    token = (base + lax.broadcasted_iota(jnp.int32, (1, tokens), 1)).astype(F32)
+    target = target_ref[0]
+
+    def move(i, carry):
+        picked = match(i * step, step, target)
+        out = jnp.dot(picked.astype(BF16), right[...], preferred_element_type=F32)
+        where = pl.ds(i * (step // SLOTS), step // SLOTS)
+        q_out[where] = by_slot(out[:, :128]).astype(BF16)
+        k_out[where] = by_slot(out[:, 128:]).astype(BF16)
+        at = jnp.min(jnp.where(picked, token, EMPTY), axis=1, keepdims=True)
+        p_out[where] = by_slot(jnp.broadcast_to(at, (step, 128)))
+        return carry
+
+    lax.fori_loop(0, slots // step, move, 0)
+
+
+def place_pair(target, first, tokens):
+    ranks = first.shape[0]
+    spec_out = pl.BlockSpec((CLUSTERS, SLOTS, 128), lambda j: (0, j, 0))
+    shape = (CLUSTERS, ranks * SLOTS, 128)
+    return pl.pallas_call(
+        place_pair_kernel,
+        grid=(ranks,),
+        in_specs=[
+            pl.BlockSpec((1, 1, tokens), lambda j: (j, 0, 0)),
+            pl.BlockSpec((1, tokens, 128), lambda j: (j, 0, 0)),
+            pl.BlockSpec((1, tokens, 128), lambda j: (j, 1, 0)),
+        ],
+        out_specs=[spec_out, spec_out, spec_out],
+        out_shape=[
+            jax.ShapeDtypeStruct(shape, BF16),
+            jax.ShapeDtypeStruct(shape, BF16),
+            jax.ShapeDtypeStruct(shape, F32),
+        ],
+        scratch_shapes=[pltpu.VMEM((tokens, 256), BF16)],
+        compiler_params=params(60),
+        cost_estimate=cost(2 * ranks * CLUSTERS * SLOTS * tokens * 256, 16 << 20),
+    )(target, first, first)
+
+
+def place_some_kernel(target_ref, v_ref, v_out):
+    slots = v_out.shape[0] * SLOTS
+    some = v_ref.shape[1]
+    picked = match(0, slots, target_ref[0, :, :some]).astype(BF16)
+    out = jnp.dot(picked, v_ref[0], preferred_element_type=F32)
+    v_out[...] = by_slot(out).astype(BF16)
+
+
+def place_some(target, first, tokens, some):
+    ranks = first.shape[0]
+    block = 2 * tokens // some
+    return pl.pallas_call(
+        place_some_kernel,
+        grid=(ranks,),
+        in_specs=[
+            pl.BlockSpec((1, 1, tokens), lambda j: (j, 0, 0)),
+            pl.BlockSpec((1, some, 128), lambda j: (j, block, 0)),
+        ],
+        out_specs=pl.BlockSpec((CLUSTERS, SLOTS, 128), lambda j: (0, j, 0)),
+        out_shape=jax.ShapeDtypeStruct((CLUSTERS, ranks * SLOTS, 128), BF16),
+        compiler_params=params(24),
+        cost_estimate=cost(2 * ranks * CLUSTERS * SLOTS * some * 256, 6 << 20),
+    )(target, first)
+
+
+def weigh_kernel(q_ref, k_ref, p_ref, w_out, mean_out):
+    count, rows = q_ref.shape[0], q_ref.shape[1]
+    cap = rows // PAIR
+    scale = 1.0 / math.sqrt(q_ref.shape[2])
+    same = (
+        lax.broadcasted_iota(jnp.int32, (rows, rows), 0) // cap
+        == lax.broadcasted_iota(jnp.int32, (rows, rows), 1) // cap
+    )
+    for n in range(count):
+        q, k, own = q_ref[n], k_ref[n], p_ref[n]
+        scores = lax.dot_general(q, k, (((1,), (1,)), ((), ())), preferred_element_type=F32) * scale
+        allowed = same & (jnp.transpose(own) <= own)
+        scores = jnp.where(allowed, scores, neg_fill)
+        top = jnp.max(scores, axis=1, keepdims=True)
+        w_out[n] = jnp.where(allowed, jnp.exp(scores - top), 0.0).astype(BF16)
+    both = (q_ref[...].astype(F32) + k_ref[...].astype(F32)).reshape(count * PAIR, cap, 128)
+    held = (p_ref[...] < EMPTY).astype(F32).reshape(count * PAIR, cap, 128)
+    mean_out[...] = jnp.sum(both, axis=1) / (2.0 * jnp.maximum(jnp.sum(held, axis=1), 1.0))
+
+
+def weigh(q_rows, k_rows, at):
+    groups, rows = q_rows.shape[0], q_rows.shape[1]
+    step = 8
+    spec = pl.BlockSpec((step, rows, 128), lambda i: (i, 0, 0))
+    return pl.pallas_call(
+        weigh_kernel,
+        grid=(groups // step,),
+        in_specs=[spec, spec, spec],
+        out_specs=[
+            pl.BlockSpec((step, rows, rows), lambda i: (i, 0, 0)),
+            pl.BlockSpec((step * PAIR, 128), lambda i: (i, 0)),
+        ],
+        out_shape=[
+            jax.ShapeDtypeStruct((groups, rows, rows), BF16),
+            jax.ShapeDtypeStruct((groups * PAIR, 128), F32),
+        ],
+        compiler_params=params(24),
+        cost_estimate=cost(2 * groups * rows * rows * 256, 20 << 20, groups * rows * rows),
+    )(q_rows, k_rows, at)
+
+
+def mix_kernel(ranks, target_ref, v_ref, part_ref, w_ref, o_out, v_rows):
+    i = pl.program_id(0)
+    slots = part_ref.shape[0] * SLOTS
+    count, rows = w_ref.shape[0], w_ref.shape[1]
+    tokens, rest = target_ref.shape[2], v_ref.shape[1]
+
+    @pl.when(i < ranks)
+    def _():
+        picked = match(0, slots, target_ref[0, :, tokens - rest :]).astype(BF16)
+        out = jnp.dot(picked, v_ref[0], preferred_element_type=F32)
+        where = pl.ds(pl.multiple_of(i * SLOTS, SLOTS), SLOTS)
+        v_rows[:, where, :] = by_slot(out) + part_ref[...].astype(F32)
+
+    @pl.when(i >= ranks)
+    def _():
+        ones = jnp.ones((rows, 128), BF16)
+        for n in range(count):
+            own = v_rows[pl.ds(((i - ranks) * count + n) * PAIR, PAIR)]
+            right = jnp.concatenate([own.reshape(rows, 128).astype(BF16), ones], axis=1)
+            out = jnp.dot(w_ref[n], right, preferred_element_type=F32)
+            total = out[:, 128:]
+            o_out[n] = (out[:, :128] / jnp.where(total > 0.0, total, 1.0)).astype(BF16)
+
+
+def mix(target, rows_v, part, weights):
+    ranks, rest = rows_v.shape[0], rows_v.shape[1]
+    groups, rows = weights.shape[0], weights.shape[1]
+    count = groups // ranks
+
+    def sender(i):
+        return jnp.minimum(i, ranks - 1)
+
+    def group(i):
+        return jnp.maximum(i - ranks, 0)
+
+    return pl.pallas_call(
+        functools.partial(mix_kernel, ranks),
+        grid=(2 * ranks,),
+        in_specs=[
+            pl.BlockSpec((1, 1, target.shape[2]), lambda i: (sender(i), 0, 0)),
+            pl.BlockSpec((1, rest, 128), lambda i: (sender(i), 0, 0)),
+            pl.BlockSpec((CLUSTERS, SLOTS, 128), lambda i: (0, sender(i), 0)),
+            pl.BlockSpec((count, rows, rows), lambda i: (group(i), 0, 0)),
+        ],
+        out_specs=pl.BlockSpec((count, rows, 128), lambda i: (group(i), 0, 0)),
+        out_shape=jax.ShapeDtypeStruct((groups, rows, 128), BF16),
+        scratch_shapes=[pltpu.VMEM((CLUSTERS, ranks * SLOTS, 128), F32)],
+        compiler_params=params(24),
+        cost_estimate=cost(2 * ranks * CLUSTERS * SLOTS * rest * 256, 16 << 20),
+    )(target, rows_v, part, weights)
+
+
+def unplace_kernel(who_ref, target_ref, o_ref, mean_ref, out_ref):
+    tokens = target_ref.shape[2]
+    slots = o_ref.shape[0] * SLOTS
+    right = o_ref[...].astype(F32).reshape(slots, 128).astype(BF16)
+    target = jnp.transpose(jnp.broadcast_to(target_ref[0], (128, tokens)))
+    columns = lax.broadcasted_iota(jnp.int32, (tokens, slots), 1)
+    picked = (columns == jnp.tile(target, (1, slots // 128))).astype(BF16)
+    out_ref[:tokens] = jnp.dot(picked, right, preferred_element_type=F32).astype(BF16)
+    means = mean_ref[...]
+    high = means.astype(BF16)
+    count = means.shape[0]
+    out_ref[tokens : tokens + count] = high
+    out_ref[tokens + count :] = (means - high.astype(F32)).astype(BF16)
+
+
+def unplace(who, target, mixed, means):
+    tokens = target.shape[2]
+    count = CLUSTERS // target.shape[0]
+    return pl.pallas_call(
+        unplace_kernel,
+        grid_spec=pltpu.PrefetchScalarGridSpec(
+            num_scalar_prefetch=1,
+            grid=(1,),
+            in_specs=[
+                pl.BlockSpec((1, 1, tokens), lambda i, who: (who[0], 0, 0)),
+                pl.BlockSpec((CLUSTERS, SLOTS, 128), lambda i, who: (0, who[0], 0)),
+                pl.BlockSpec((count, 128), lambda i, who: (who[0], 0)),
+            ],
+            out_specs=pl.BlockSpec((tokens + 2 * count, 128), lambda i, who: (0, 0)),
+        ),
+        out_shape=jax.ShapeDtypeStruct((tokens + 2 * count, 128), BF16),
+        compiler_params=params(24),
+        cost_estimate=cost(1, 1),
+    )(who, target, mixed, means)
+
+
+def project_kernel(lanes, has_total, *refs):
+    refs = refs[1:]
+    atts, ws = refs[:4], refs[4 : 4 + 4 * lanes]
+    out_ref = refs[-1]
+    left = jnp.concatenate([a[...] for a in atts], axis=1)
+    right = jnp.concatenate([w[...] for w in ws], axis=0)
+    total = jnp.dot(left, right, preferred_element_type=F32)
+    if has_total:
+        total = total + refs[4 + 4 * lanes][...]
+    out_ref[...] = total.astype(out_ref.dtype)
+
+
+def project(where, tokens, atts, weights, columns, total, dtype):
+    lanes = atts[0].shape[1] // 128
+    step = 512
+    cols = out_cols = weights[3].shape[1]
+    in_specs = [pl.BlockSpec((step, 128 * lanes), lambda i, w: (i, 0)) for _ in atts]
+    args = list(atts)
+    for part in range(4):
+        for lane in range(lanes):
+            in_specs.append(
+                pl.BlockSpec(
+                    (128, cols), lambda i, w, lane=lane, part=part: (w[lane], w[lanes + part])
+                )
+            )
+            args.append(weights[part])
+    if total is not None:
+        in_specs.append(pl.BlockSpec((step, out_cols), lambda i, w: (i, 0)))
+        args.append(total)
+    return pl.pallas_call(
+        functools.partial(project_kernel, lanes, total is not None),
+        grid_spec=pltpu.PrefetchScalarGridSpec(
+            num_scalar_prefetch=1,
+            grid=(tokens // step,),
+            in_specs=in_specs,
+            out_specs=pl.BlockSpec((step, out_cols), lambda i, w: (i, 0)),
+        ),
+        out_shape=jax.ShapeDtypeStruct((tokens, out_cols), dtype),
+        compiler_params=params(60),
+        cost_estimate=cost(2 * tokens * 512 * lanes * out_cols, 8 << 20),
+    )(jnp.stack(list(where) + list(columns)), *args)
+
+
+def head_body(queries, keys, values, cluster_of, slot_of, centroids, out_weight):
+    ranks = lax.axis_size("ctx")
+    me = lax.axis_index("ctx")
+    mine = lax.axis_index("head")
+    tokens = queries.shape[0]
+    some = tokens // 2
+    cl_dev = CLUSTERS // ranks
+    cap = ranks * SLOTS
+    y, core = mine // 2, mine % 2
+
+    def swap_y(x):
+        return lax.ppermute(x, "head", [(0, 2), (1, 3), (2, 0), (3, 1)])
+
+    def swap_core(x):
+        return lax.ppermute(x, "head", [(0, 1), (1, 0), (2, 3), (3, 2)])
+
+    marks = [x.astype(BF16).reshape(ranks, tokens // 128, 128) for x in (cluster_of, slot_of)]
+    marks = jnp.concatenate(marks, axis=1)
+    first = pack_first(queries, keys, values, marks, some)
+    first = lax.all_to_all(first, "ctx", split_axis=0, concat_axis=0, tiled=True)
+    rows_v, first = lax.optimization_barrier((pack_rest(values, ranks, some), first))
+    rows_v = lax.all_to_all(rows_v, "ctx", split_axis=0, concat_axis=0, tiled=True)
+
+    cols = out_weight.shape[1] // 4
+    across = swap_y(lax.dynamic_slice_in_dim(out_weight, (1 - y) * 2 * cols, 2 * cols, 1))
+    beside = swap_core(
+        lax.dynamic_slice_in_dim(out_weight, (2 * y + 1 - core) * cols, cols, 1)
+    )
+    corner = swap_core(lax.dynamic_slice_in_dim(across, (1 - core) * cols, cols, 1))
+    w_parts = (out_weight, across, beside, corner)
+    w_columns = (mine, core, jnp.zeros_like(core), jnp.zeros_like(core))
+
+    marks = first[:, 2 * tokens + some :, :].astype(jnp.int32)
+    target = marks[:, : tokens // 128, :] * SLOTS + marks[:, tokens // 128 :, :]
+    target = target.reshape(ranks, 1, tokens)
+    q_rows, k_rows, at = place_pair(target, first, tokens)
+
+    def paired(x):
+        return x.reshape(CLUSTERS // PAIR, PAIR * cap, 128)
+
+    weights, means = weigh(paired(q_rows), paired(k_rows), paired(at))
+    part = place_some(target, first, tokens, some)
+    rows_v, w_parts = lax.optimization_barrier((rows_v, w_parts))
+    mixed = mix(target, rows_v, part, weights).reshape(CLUSTERS, cap, 128)
+
+    got = {}
+    after = {6: 4, 7: 5}
+    for d in (4, 5, 1, 2, 3, 0, 6, 7):
+        who = jnp.reshape(me ^ d, (1,))
+        if d in after:
+            who, got[after[d]] = lax.optimization_barrier((who, got[after[d]]))
+        block = unplace(who, target, mixed, means)
+        got[d] = block
+        if d:
+            got[d] = lax.ppermute(block, "ctx", [(i, i ^ d) for i in range(ranks)])
+
+    total = None
+    splits = ((0, 1, 2, 3), (4, 5), (6,), (7,))
+    for lanes in splits:
+        own = got[lanes[0]]
+        if len(lanes) > 1:
+            own = jnp.concatenate([got[d][:tokens] for d in lanes], axis=1)
+        there = swap_y(own)
+        atts = (own, there, swap_core(own), swap_core(there))
+        last = lanes == splits[-1]
+        total = project(
+            [me ^ d for d in lanes], tokens, atts, w_parts, w_columns, total, BF16 if last else F32
+        )
+
+    sent = jnp.stack([got[d][tokens:] for d in range(ranks)]).astype(F32)
+    sent = sent[:, :cl_dev] + sent[:, cl_dev:]
+    sent = jnp.concatenate(
+        [lax.dynamic_slice_in_dim(sent, me ^ d, 1, 0) for d in range(ranks)], axis=0
+    )
+    new_centroids = mix_rate * centroids + (1.0 - mix_rate) * sent
+    return (total, new_centroids)
+
+
+def dispatch(queries, keys, values, cluster_of, *rest):
+    ranks, heads = lax.axis_size("ctx"), cluster_of.shape[0]
+    whole_heads = ranks == heads == 8 and lax.axis_size("head") == 4
+    step = head_body if whole_heads else body
+    return step(queries, keys, values, cluster_of, *rest)
+
+
 def solution(mesh):
     in_specs = (
         P("ctx", "head"),
@@ -134,4 +538,6 @@
         P("head", None),
     )
     out_specs = (P("ctx", "head"), P("head", "ctx", None))
-    return jax.shard_map(body, mesh=mesh, in_specs=in_specs, out_specs=out_specs, check_vma=False)
+    return jax.shard_map(
+        dispatch, mesh=mesh, in_specs=in_specs, out_specs=out_specs, check_vma=False
+    )

time: 733 us -> 320 us (0.44)
  waiting for transfers between devices: 411 us -> 146 us
  local copies, waits for them, and re-layouts: 233 us -> 32.1 us
  Pallas kernels: 0 us -> 98.8 us
  matrix products: 36.8 us -> 0 us
  between operations: 14 us -> 1.05 us
  starting transfers between devices: 27.8 us -> 36.4 us
    all_to_all x5 -> x2, waiting for transfers between devices: 287 us -> 11 us  [the longest x1 11 us: head_body(): lax.all_to_all(first, 'ctx', split_axis=0, concat_axis=0, tiled=True)]
    ppermute x0 -> x22, waiting for transfers between devices: none -> 135 us  [the longest x5 112 us: swap_y(): return lax.ppermute(x, 'head', [(0, 2), (1, 3), (2, 0), (3, 1)])]
    reduce_scatter x2 -> x0, waiting for transfers between devices: 123 us -> none  [the longest x1 123 us: body(): lax.psum_scatter(lax.dot_general(out_weight, attended, (((0,), (1,)), (()...]
    pallas_call x0 -> x18, Pallas kernels: none -> 98.8 us  [the longest x4 28.4 us: project(): pl.pallas_call(functools.partial(project_kernel, lanes, total is not None...]
    gather x1 -> x0, local copies, waits for them, and re-layouts: 95.3 us -> none  [body(): rows_back[target, head_ids].reshape(tok_rows, head_rows * head_size)]
    unnamed x27 -> x54, local copies, waits for them, and re-layouts: 105 us -> 19.7 us
    ppermute x0 -> x22, starting transfers between devices: none -> 25.5 us  [the longest x7 16.4 us: head_body(): got[d] = lax.ppermute(block, 'ctx', [(i, i ^ d) for i in range(ranks)])]
    dot_general x4 -> x0, matrix products: 24.2 us -> none  [the longest x1 16 us: body(): lax.dot_general(out_weight, attended, (((0,), (1,)), ((), ())), preferred...]
  transfers between devices with their start and end apart: 8 -> 24, of which waited for: 5 -> 9; matrix products, arithmetic and copies ran while one was open for 31% -> 5% of each run, Pallas kernels for 0% -> 23%
where the time goes in v2:
time: 320 us; the launch traced here: 319 us
  waiting for transfers between devices  146 us (46%)
  Pallas kernels  98.8 us (31%)
  starting transfers between devices  36.4 us (11%)
  local copies, waits for them, and re-layouts  32.1 us (10%)
  other arithmetic  5.08 us (2%)
    ppermute x5, waiting for transfers between devices, swap_y(): return lax.ppermute(x, 'head', [(0, 2), (1, 3), (2, 0), (3, 1)])  112 us
    pallas_call x4, Pallas kernels, project(): pl.pallas_call(functools.partial(project_kernel, lanes, total is not None...  28.4 us
    ppermute x7, waiting for transfers between devices, head_body(): got[d] = lax.ppermute(block, 'ctx', [(i, i ^ d) for i in range(ranks)])  22.9 us
    unnamed x54, local copies, waits for them, and re-layouts  19.7 us
    pallas_call x1, Pallas kernels, place_pair(): pl.pallas_call(place_pair_kernel, grid=(ranks,), in_specs=[pl.BlockSpec((...  17.2 us
    ppermute x7, starting transfers between devices, head_body(): got[d] = lax.ppermute(block, 'ctx', [(i, i ^ d) for i in range(ranks)])  16.4 us
    pallas_call x1, Pallas kernels, weigh(): pl.pallas_call(weigh_kernel, grid=(groups // step,), in_specs=[spec, spec...  11 us
    all_to_all x1, waiting for transfers between devices, head_body(): lax.all_to_all(first, 'ctx', split_axis=0, concat_axis=0, tiled=True)  11 us
  transfers between devices with their start and end apart: 24, of which 9 were waited for; matrix products, arithmetic and copies ran while one was open for 5% of the time, Pallas kernels for 23%

profile of v2, /device:TPU:0, one launch (start us, length us, event | category | flops | bytes accessed | tf_op | source)
XLA Modules:
  0.0 319.1 jit_solution(5625575298225045828)
XLA Ops:
  2.8 7.4 %shard_map.87 = bf16[8,2576,128]{2,1,0:T(8,128)(2,1)} custom-call(bf16[1024,1024]{1,0:T(8,128)(2,1)} %q_ref.1, bf16[1024,1024]{1,0:T(8,128)(2,1)} %k_ref.1, bf16[1024,1024]{1,0:T(8,128)(2,1)} %v_ref.3, bf16[8,16,128]{2,1,0:T(8,128)(2,1)} %pad_maximum_fusion.2.marks_ref), custom_call_target="tpu_custom_call" | custom-call | bytes 10551296 | tf_op jit(solution)/shard_map/pallas_call | solution.py:159
  10.2 7.3 %all-to-all-start = ((bf16[8,2576,128]{2,1,0:T(8,128)(2,1)}), bf16[8,2576,128]{2,1,0:T(8,128)(2,1)}, u32[]{:S(2)}, u32[]{:S(2)}) async-start(bf16[8,2576,128]{2,1,0:T(8,128)(2,1)} %shard_map.87), calls=%async_computation | async-start | bytes 10551296 | tf_op jit(solution)/shard_map/all_to_all | solution.py:464
  17.4 4.8 %constant_dynamic-slice_fusion.2 = bf16[1024,2048]{1,0:T(8,128)(2,1)} fusion(bf16[1024,4096]{1,0:T(8,128)(2,1)} %refs_5_.3, s32[]{:T(128)S(6)} %select_n.46), kind=kLoop, calls=%fused_computation.36 | loop fusion | bytes 8388612 | tf_op jit(solution)/shard_map/dynamic_slice | solution.py:469
  26.8 87.7 %collective-permute-done.refs_9_.refs_10_.refs_11_.refs_12_.refs_7_.refs_8_.refs_6_ = bf16[1024,2048]{1,0:T(8,128)(2,1)} collective-permute-done((bf16[1024,2048]{1,0:T(8,128)(2,1)}, bf16[1024,2048]{1,0:T(8,128)(2,1)}, u32[]{:S(2)}, u32[]{:S(2)}) %collective-permute-start) | collective-permute-done | bytes 4194336 | tf_op jit(solution)/shard_map/ppermute | solution.py:456
  117.7 5.2 %shard_map.86 = bf16[8,512,128]{2,1,0:T(8,128)(2,1)} custom-call(bf16[1024,1024]{1,0:T(8,128)(2,1)} %v_ref.3), custom_call_target="tpu_custom_call" | custom-call | bytes 2097152 | tf_op jit(solution)/shard_map/pallas_call | solution.py:181
  122.9 11.0 %all-to-all-done.v_ref.q_ref.k_ref = bf16[8,2576,128]{2,1,0:T(8,128)(2,1)} async-done(((bf16[8,2576,128]{2,1,0:T(8,128)(2,1)}), bf16[8,2576,128]{2,1,0:T(8,128)(2,1)}, u32[]{:S(2)}, u32[]{:S(2)}) %all-to-all-start) | async-done | bytes 5275680 | tf_op jit(solution)/shard_map/all_to_all | solution.py:464
  133.9 3.6 %all-to-all-start.1 = ((bf16[8,512,128]{2,1,0:T(8,128)(2,1)}), bf16[8,512,128]{2,1,0:T(8,128)(2,1)S(1)}, u32[]{:S(2)}, u32[]{:S(2)}) async-start(bf16[8,512,128]{2,1,0:T(8,128)(2,1)} %shard_map.86), calls=%async_computation.1 | async-start | bytes 2097152 | tf_op jit(solution)/shard_map/all_to_all | solution.py:466
  138.9 17.2 %shard_map.89 = (bf16[256,64,128]{2,1,0:T(8,128)(2,1)}, bf16[256,64,128]{2,1,0:T(8,128)(2,1)}, f32[256,64,128]{2,1,0:T(8,128)}) custom-call(s32[8,1,1024]{2,1,0:T(1,128)} %bitcast.62, bf16[8,2576,128]{2,1,0:T(8,128)(2,1)} %all-to-all-done.v_ref.q_ref.k_ref, bf16[8,2576,128]{2,1,0:T(8,128)(2,1)} %all-to-all-done.v_ref.q_ref.k_ref), custom_call_target="tpu_custom_call" | custom-call | flops 8589934592 | bytes 16777216 | tf_op jit(solution)/shard_map/pallas_call | solution.py:228
  163.8 11.0 %shard_map.90 = (bf16[128,128,128]{2,1,0:T(8,128)(2,1)S(1)}, f32[256,128]{1,0:T(8,128)S(1)}) custom-call(bf16[128,128,128]{2,1,0:T(8,128)(2,1)S(1)} %bitcast.60, bf16[128,128,128]{2,1,0:T(8,128)(2,1)S(1)} %bitcast.61, f32[128,128,128]{2,1,0:T(8,128)S(1)} %bitcast.59), custom_call_target="tpu_custom_call" | custom-call | flops 1073741824 | bytes 20971520 | tf_op jit(solution)/shard_map/pallas_call | solution.py:297
  174.9 8.0 %shard_map.88.part_ref = bf16[256,64,128]{2,1,0:T(8,128)(2,1)S(1)} custom-call(s32[8,1,1024]{2,1,0:T(1,128)S(1)} %bitcast.63, bf16[8,2576,128]{2,1,0:T(8,128)(2,1)} %all-to-all-done.v_ref.q_ref.k_ref), custom_call_target="tpu_custom_call" | custom-call | flops 4294967296 | bytes 6291456 | tf_op jit(solution)/shard_map/pallas_call | solution.py:259
  190.1 10.7 %shard_map.91 = bf16[128,128,128]{2,1,0:T(8,128)(2,1)S(1)} custom-call(s32[8,1,1024]{2,1,0:T(1,128)S(1)} %bitcast.64, bf16[8,512,128]{2,1,0:T(8,128)(2,1)S(1)} %all-to-all-done.1.v_ref, bf16[256,64,128]{2,1,0:T(8,128)(2,1)S(1)} %copy-done.9, bf16[128,128,128]{2,1,0:T(8,128)(2,1)S(1)} %copy-done.7), custom_call_target="tpu_custom_call" | custom-call | flops 4294967296 | bytes 16777216 | tf_op jit(solution)/shard_map/pallas_call | solution.py:349
  202.2 3.9 %collective-permute-start.3 = (bf16[1088,128]{1,0:T(8,128)(2,1)S(1)}, bf16[1088,128]{1,0:T(8,128)(2,1)S(1)}, u32[]{:S(2)}, u32[]{:S(2)}) collective-permute-start(bf16[1088,128]{1,0:T(8,128)(2,1)S(1)} %shard_map.92), channel_id=1, source_target_pairs={{0,20},{4,16},{8,28},{12,24},{16,4},{20,0},{24,12},{28,8},{1,21},{... | collective-permute-start | bytes 835592 | tf_op jit(solution)/shard_map/ppermute | solution.py:499
  221.3 4.5 %collective-permute-done.3 = bf16[1088,128]{1,0:T(8,128)(2,1)S(1)} collective-permute-done((bf16[1088,128]{1,0:T(8,128)(2,1)S(1)}, bf16[1088,128]{1,0:T(8,128)(2,1)S(1)}, u32[]{:S(2)}, u32[]{:S(2)}) %collective-permute-start.3) | collective-permute-done | bytes 278560 | tf_op jit(solution)/shard_map/ppermute | solution.py:499
  225.7 5.0 %collective-permute-done.8 = bf16[1088,128]{1,0:T(8,128)(2,1)S(1)} collective-permute-done((bf16[1088,128]{1,0:T(8,128)(2,1)S(1)}, bf16[1088,128]{1,0:T(8,128)(2,1)S(1)}, u32[]{:S(2)}, u32[]{:S(2)}) %collective-permute-start.8) | collective-permute-done | bytes 278560 | tf_op jit(solution)/shard_map/ppermute | solution.py:499
  236.4 4.4 %collective-permute-start.4 = (bf16[1088,128]{1,0:T(8,128)(2,1)S(1)}, bf16[1088,128]{1,0:T(8,128)(2,1)S(1)}, u32[]{:S(2)}, u32[]{:S(2)}) collective-permute-start(bf16[1088,128]{1,0:T(8,128)(2,1)S(1)} %shard_map.93), channel_id=1, source_target_pairs={{0,28},{4,24},{8,20},{12,16},{16,12},{20,8},{24,4},{28,0},{1,29},{... | collective-permute-start | bytes 835592 | tf_op jit(solution)/shard_map/ppermute | solution.py:499
  240.9 7.0 %collective-permute-done.17 = bf16[1088,128]{1,0:T(8,128)(2,1)S(1)} collective-permute-done((bf16[1088,128]{1,0:T(8,128)(2,1)S(1)}, bf16[1088,128]{1,0:T(8,128)(2,1)S(1)}, u32[]{:S(2)}, u32[]{:S(2)}) %collective-permute-start.17) | collective-permute-done | bytes 278560 | tf_op jit(solution)/shard_map/ppermute | solution.py:499
  247.9 3.9 %collective-permute-start.9 = (bf16[1088,128]{1,0:T(8,128)(2,1)S(1)}, bf16[1088,128]{1,0:T(8,128)(2,1)}, u32[]{:S(2)}, u32[]{:S(2)}) collective-permute-start(bf16[1088,128]{1,0:T(8,128)(2,1)S(1)} %shard_map.95), channel_id=1, source_target_pairs={{0,24},{4,28},{8,16},{12,20},{16,8},{20,12},{24,0},{28,4},{1,25},{... | collective-permute-start | bytes 835592 | tf_op jit(solution)/shard_map/ppermute | solution.py:499
  253.6 5.2 %collective-permute-done.9.refs_1_ = bf16[1088,128]{1,0:T(8,128)(2,1)} collective-permute-done((bf16[1088,128]{1,0:T(8,128)(2,1)S(1)}, bf16[1088,128]{1,0:T(8,128)(2,1)}, u32[]{:S(2)}, u32[]{:S(2)}) %collective-permute-start.9) | collective-permute-done | bytes 278560 | tf_op jit(solution)/shard_map/ppermute | solution.py:499
  259.6 17.2 %collective-permute-done.19.refs_2_ = bf16[1024,512]{1,0:T(8,128)(2,1)S(1)} collective-permute-done((bf16[1024,512]{1,0:T(8,128)(2,1)S(1)}, bf16[1024,512]{1,0:T(8,128)(2,1)S(1)}, u32[]{:S(2)}, u32[]{:S(2)}) %collective-permute-start.19) | collective-permute-done | bytes 1048608 | tf_op jit(solution)/shard_map/ppermute | solution.py:456
  279.4 6.8 %collective-permute-done.10.refs_2_ = bf16[1088,128]{1,0:T(8,128)(2,1)} collective-permute-done((bf16[1088,128]{1,0:T(8,128)(2,1)}, bf16[1088,128]{1,0:T(8,128)(2,1)}, u32[]{:S(2)}, u32[]{:S(2)}) %collective-permute-start.10) | collective-permute-done | bytes 278560 | tf_op jit(solution)/shard_map/ppermute | solution.py:456
  289.3 9.9 %shard_map.100.refs_13_ = f32[1024,1024]{1,0:T(8,128)} custom-call(s32[8]{0:T(128)} %stack.82.refs_0_, bf16[1024,512]{1,0:T(8,128)(2,1)} %copy-done.11, bf16[1024,512]{1,0:T(8,128)(2,1)} %copy-done.13, bf16[1024,512]{1,0:T(8,128)(2,1)} %copy-done.14, bf16[1024,512]{1,0:T(8,128)(2,1)} %copy-done.15, bf16[1024,4096]{1,0:T(8,128)(2,1)} %refs_5_.3, ...), custom_call_target="tpu_custom_call" | custom-call | flops 4294967296 | bytes 8388608 | tf_op jit(solution)/shard_map/pallas_call | solution.py:431
  299.8 7.3 %shard_map.101.refs_9_ = f32[1024,1024]{1,0:T(8,128)} custom-call(s32[6]{0:T(128)} %stack.77.refs_0_, bf16[1024,256]{1,0:T(8,128)(2,1)} %copy-done.12, bf16[1024,256]{1,0:T(8,128)(2,1)} %collective-permute-done.13.refs_2_, bf16[1024,256]{1,0:T(8,128)(2,1)} %collective-permute-done.14.refs_3_, bf16[1024,256]{1,0:T(8,128)(2,1)} %collective-permute-done.15.refs_4_, ...), custom_call_target="tpu_custom_call" | custom-call | flops 2147483648 | bytes 8388608 | tf_op jit(solution)/shard_map/pallas_call | solution.py:431
  307.2 5.8 %shard_map.102.refs_9_ = f32[1024,1024]{1,0:T(8,128)} custom-call(s32[5]{0:T(128)} %get-tuple-element.34.refs_0_, bf16[1088,128]{1,0:T(8,128)(2,1)} %collective-permute-done.9.refs_1_, bf16[1088,128]{1,0:T(8,128)(2,1)} %collective-permute-done.10.refs_2_, bf16[1088,128]{1,0:T(8,128)(2,1)} %collective-permute-done.11.refs_3_, ...), custom_call_target="tpu_custom_call" | custom-call | flops 1073741824 | bytes 8388608 | tf_op jit(solution)/shard_map/pallas_call | solution.py:431
  313.8 5.4 %shard_map.103 = bf16[1024,1024]{1,0:T(8,128)(2,1)} custom-call(s32[5]{0:T(128)} %get-tuple-element.35.refs_0_, bf16[1088,128]{1,0:T(8,128)(2,1)} %copy-done.16, bf16[1088,128]{1,0:T(8,128)(2,1)} %collective-permute-done.5.refs_2_, bf16[1088,128]{1,0:T(8,128)(2,1)} %copy-done.17, bf16[1088,128]{1,0:T(8,128)(2,1)} %copy-done.18, bf16[1024,4096]{1,0:T(8,128)(2,1)} %refs_5_.3, ...), custom_call_target="tpu_custom_call" | custom-call | flops 1073741824 | bytes 8388608 | tf_op jit(solution)/shard_map/pallas_call | solution.py:431
  (122 shorter events, 57.8 us)
Async XLA Ops:
  10.2 123.7 %all-to-all-start = ((bf16[8,2576,128]{2,1,0:T(8,128)(2,1)}), bf16[8,2576,128]{2,1,0:T(8,128)(2,1)}, u32[]{:S(2)}, u32[]{:S(2)}) async-start(bf16[8,2576,128]{2,1,0:T(8,128)(2,1)} %shard_map.87), calls=%async_computation | async-start | bytes 10551296 | tf_op jit(solution)/shard_map/all_to_all | solution.py:464
  22.2 92.3 %collective-permute-start = (bf16[1024,2048]{1,0:T(8,128)(2,1)}, bf16[1024,2048]{1,0:T(8,128)(2,1)}, u32[]{:S(2)}, u32[]{:S(2)}) collective-permute-start(bf16[1024,2048]{1,0:T(8,128)(2,1)} %constant_dynamic-slice_fusion.2), channel_id=1, source_target_pairs={{0,2},{1,3},{2,0},{3,1},{4,6},{5,7},{6,4},{7,5},{8,10},{9,11},{10,... | collective-permute-start | bytes 12582920 | tf_op jit(solution)/shard_map/ppermute | solution.py:456
  26.8 158.1 %collective-permute-start.1 = (bf16[1024,1024]{1,0:T(8,128)(2,1)}, bf16[1024,1024]{1,0:T(8,128)(2,1)S(1)}, u32[]{:S(2)}, u32[]{:S(2)}) collective-permute-start(bf16[1024,1024]{1,0:T(8,128)(2,1)} %constant_dynamic-slice_fusion.1), channel_id=1, source_target_pairs={{0,1},{1,0},{2,3},{3,2},{4,5},{5,4},{6,7},{7,6},{8,9},{9,8},{10,11... | collective-permute-start | bytes 6291464 | tf_op jit(solution)/shard_map/ppermute | solution.py:459
  117.7 67.3 %collective-permute-start.2 = (bf16[1024,1024]{1,0:T(8,128)(2,1)}, bf16[1024,1024]{1,0:T(8,128)(2,1)}, u32[]{:S(2)}, u32[]{:S(2)}) collective-permute-start(bf16[1024,1024]{1,0:T(8,128)(2,1)} %constant_dynamic-slice_fusion), channel_id=1, source_target_pairs={{0,1},{1,0},{2,3},{3,2},{4,5},{5,4},{6,7},{7,6},{8,9},{9,8},{10,11... | collective-permute-start | bytes 6291464 | tf_op jit(solution)/shard_map/ppermute | solution.py:459
  133.9 51.1 %all-to-all-start.1 = ((bf16[8,512,128]{2,1,0:T(8,128)(2,1)}), bf16[8,512,128]{2,1,0:T(8,128)(2,1)S(1)}, u32[]{:S(2)}, u32[]{:S(2)}) async-start(bf16[8,512,128]{2,1,0:T(8,128)(2,1)} %shard_map.86), calls=%async_computation.1 | async-start | bytes 2097152 | tf_op jit(solution)/shard_map/all_to_all | solution.py:466
  202.2 23.5 %collective-permute-start.3 = (bf16[1088,128]{1,0:T(8,128)(2,1)S(1)}, bf16[1088,128]{1,0:T(8,128)(2,1)S(1)}, u32[]{:S(2)}, u32[]{:S(2)}) collective-permute-start(bf16[1088,128]{1,0:T(8,128)(2,1)S(1)} %shard_map.92), channel_id=1, source_target_pairs={{0,20},{4,16},{8,28},{12,24},{16,4},{20,0},{24,12},{28,8},{1,21},{... | collective-permute-start | bytes 835592 | tf_op jit(solution)/shard_map/ppermute | solution.py:499
  207.5 23.2 %collective-permute-start.8 = (bf16[1088,128]{1,0:T(8,128)(2,1)S(1)}, bf16[1088,128]{1,0:T(8,128)(2,1)S(1)}, u32[]{:S(2)}, u32[]{:S(2)}) collective-permute-start(bf16[1088,128]{1,0:T(8,128)(2,1)S(1)} %shard_map.94), channel_id=1, source_target_pairs={{0,16},{4,20},{8,24},{12,28},{16,0},{20,4},{24,8},{28,12},{1,17},{... | collective-permute-start | bytes 835592 | tf_op jit(solution)/shard_map/ppermute | solution.py:499
  217.7 18.7 %collective-permute-start.18 = (bf16[1088,128]{1,0:T(8,128)(2,1)S(1)}, bf16[1088,128]{1,0:T(8,128)(2,1)S(1)}, u32[]{:S(2)}, u32[]{:S(2)}) collective-permute-start(bf16[1088,128]{1,0:T(8,128)(2,1)S(1)} %shard_map.99), channel_id=1, source_target_pairs={{0,12},{4,8},{8,4},{12,0},{16,28},{20,24},{24,20},{28,16},{1,13},{... | collective-permute-start | bytes 835592 | tf_op jit(solution)/shard_map/ppermute | solution.py:499
  219.2 28.6 %collective-permute-start.17 = (bf16[1088,128]{1,0:T(8,128)(2,1)S(1)}, bf16[1088,128]{1,0:T(8,128)(2,1)S(1)}, u32[]{:S(2)}, u32[]{:S(2)}) collective-permute-start(bf16[1088,128]{1,0:T(8,128)(2,1)S(1)} %shard_map.98), channel_id=1, source_target_pairs={{0,8},{4,12},{8,0},{12,4},{16,24},{20,28},{24,16},{28,20},{1,9},{5... | collective-permute-start | bytes 835592 | tf_op jit(solution)/shard_map/ppermute | solution.py:499
  219.3 32.5 %collective-permute-start.16 = (bf16[1088,128]{1,0:T(8,128)(2,1)S(1)}, bf16[1088,128]{1,0:T(8,128)(2,1)S(1)}, u32[]{:S(2)}, u32[]{:S(2)}) collective-permute-start(bf16[1088,128]{1,0:T(8,128)(2,1)S(1)} %shard_map.97), channel_id=1, source_target_pairs={{0,4},{4,0},{8,12},{12,8},{16,20},{20,16},{24,28},{28,24},{1,5},{5... | collective-permute-start | bytes 835592 | tf_op jit(solution)/shard_map/ppermute | solution.py:499
  230.9 47.7 %collective-permute-start.13 = (bf16[1024,256]{1,0:T(8,128)(2,1)S(1)}, bf16[1024,256]{1,0:T(8,128)(2,1)}, u32[]{:S(2)}, u32[]{:S(2)}) collective-permute-start(bf16[1024,256]{1,0:T(8,128)(2,1)S(1)} %pad_maximum_fusion.1.refs_1_), channel_id=1, source_target_pairs={{0,2},{1,3},{2,0},{3,1},{4,6},{5,7},{6,4},{7,5},{8,10},{9,11},{10,... | collective-permute-start | bytes 1572872 | tf_op jit(solution)/shard_map/ppermute | solution.py:456
  232.4 66.8 %collective-permute-start.14 = (bf16[1024,256]{1,0:T(8,128)(2,1)S(1)}, bf16[1024,256]{1,0:T(8,128)(2,1)}, u32[]{:S(2)}, u32[]{:S(2)}) collective-permute-start(bf16[1024,256]{1,0:T(8,128)(2,1)S(1)} %pad_maximum_fusion.1.refs_1_), channel_id=1, source_target_pairs={{0,1},{1,0},{2,3},{3,2},{4,5},{5,4},{6,7},{7,6},{8,9},{9,8},{10,11... | collective-permute-start | bytes 1572872 | tf_op jit(solution)/shard_map/ppermute | solution.py:459
  236.4 23.2 %collective-permute-start.4 = (bf16[1088,128]{1,0:T(8,128)(2,1)S(1)}, bf16[1088,128]{1,0:T(8,128)(2,1)S(1)}, u32[]{:S(2)}, u32[]{:S(2)}) collective-permute-start(bf16[1088,128]{1,0:T(8,128)(2,1)S(1)} %shard_map.93), channel_id=1, source_target_pairs={{0,28},{4,24},{8,20},{12,16},{16,12},{20,8},{24,4},{28,0},{1,29},{... | collective-permute-start | bytes 835592 | tf_op jit(solution)/shard_map/ppermute | solution.py:499
  247.9 11.0 %collective-permute-start.9 = (bf16[1088,128]{1,0:T(8,128)(2,1)S(1)}, bf16[1088,128]{1,0:T(8,128)(2,1)}, u32[]{:S(2)}, u32[]{:S(2)}) collective-permute-start(bf16[1088,128]{1,0:T(8,128)(2,1)S(1)} %shard_map.95), channel_id=1, source_target_pairs={{0,24},{4,28},{8,16},{12,20},{16,8},{20,12},{24,0},{28,4},{1,25},{... | collective-permute-start | bytes 835592 | tf_op jit(solution)/shard_map/ppermute | solution.py:499
  252.0 24.9 %collective-permute-start.19 = (bf16[1024,512]{1,0:T(8,128)(2,1)S(1)}, bf16[1024,512]{1,0:T(8,128)(2,1)S(1)}, u32[]{:S(2)}, u32[]{:S(2)}) collective-permute-start(bf16[1024,512]{1,0:T(8,128)(2,1)S(1)} %pad_maximum_fusion.refs_1_), channel_id=1, source_target_pairs={{0,2},{1,3},{2,0},{3,1},{4,6},{5,7},{6,4},{7,5},{8,10},{9,11},{10,... | collective-permute-start | bytes 3145736 | tf_op jit(solution)/shard_map/ppermute | solution.py:456
  258.8 28.9 %collective-permute-start.20 = (bf16[1024,512]{1,0:T(8,128)(2,1)S(1)}, bf16[1024,512]{1,0:T(8,128)(2,1)S(1)}, u32[]{:S(2)}, u32[]{:S(2)}) collective-permute-start(bf16[1024,512]{1,0:T(8,128)(2,1)S(1)} %pad_maximum_fusion.refs_1_), channel_id=1, source_target_pairs={{0,1},{1,0},{2,3},{3,2},{4,5},{5,4},{6,7},{7,6},{8,9},{9,8},{10,11... | collective-permute-start | bytes 3145736 | tf_op jit(solution)/shard_map/ppermute | solution.py:459
  276.9 10.9 %collective-permute-start.21 = (bf16[1024,512]{1,0:T(8,128)(2,1)S(1)}, bf16[1024,512]{1,0:T(8,128)(2,1)S(1)}, u32[]{:S(2)}, u32[]{:S(2)}) collective-permute-start(bf16[1024,512]{1,0:T(8,128)(2,1)S(1)} %collective-permute-done.19.refs_2_), channel_id=1, source_target_pairs={{0,1},{1,0},{2,3},{3,2},{4,5},{5,4},{6,7},{7,6},{8,9},{9,8},{10,11... | collective-permute-start | bytes 3145736 | tf_op jit(solution)/shard_map/ppermute | solution.py:459
  276.9 9.4 %collective-permute-start.10 = (bf16[1088,128]{1,0:T(8,128)(2,1)}, bf16[1088,128]{1,0:T(8,128)(2,1)}, u32[]{:S(2)}, u32[]{:S(2)}) collective-permute-start(bf16[1088,128]{1,0:T(8,128)(2,1)} %collective-permute-done.9.refs_1_), channel_id=1, source_target_pairs={{0,2},{1,3},{2,0},{3,1},{4,6},{5,7},{6,4},{7,5},{8,10},{9,11},{10,... | collective-permute-start | bytes 835592 | tf_op jit(solution)/shard_map/ppermute | solution.py:456
  278.5 21.3 %collective-permute-start.15 = (bf16[1024,256]{1,0:T(8,128)(2,1)}, bf16[1024,256]{1,0:T(8,128)(2,1)}, u32[]{:S(2)}, u32[]{:S(2)}) collective-permute-start(bf16[1024,256]{1,0:T(8,128)(2,1)} %collective-permute-done.13.refs_2_), channel_id=1, source_target_pairs={{0,1},{1,0},{2,3},{3,2},{4,5},{5,4},{6,7},{7,6},{8,9},{9,8},{10,11... | collective-permute-start | bytes 1572872 | tf_op jit(solution)/shard_map/ppermute | solution.py:459
  286.3 13.1 %collective-permute-start.5 = (bf16[1088,128]{1,0:T(8,128)(2,1)S(1)}, bf16[1088,128]{1,0:T(8,128)(2,1)}, u32[]{:S(2)}, u32[]{:S(2)}) collective-permute-start(bf16[1088,128]{1,0:T(8,128)(2,1)S(1)} %collective-permute-done.4.refs_1_), channel_id=1, source_target_pairs={{0,2},{1,3},{2,0},{3,1},{4,6},{5,7},{6,4},{7,5},{8,10},{9,11},{10,... | collective-permute-start | bytes 835592 | tf_op jit(solution)/shard_map/ppermute | solution.py:456
  287.8 19.4 %collective-permute-start.11 = (bf16[1088,128]{1,0:T(8,128)(2,1)}, bf16[1088,128]{1,0:T(8,128)(2,1)}, u32[]{:S(2)}, u32[]{:S(2)}) collective-permute-start(bf16[1088,128]{1,0:T(8,128)(2,1)} %collective-permute-done.9.refs_1_), channel_id=1, source_target_pairs={{0,1},{1,0},{2,3},{3,2},{4,5},{5,4},{6,7},{7,6},{8,9},{9,8},{10,11... | collective-permute-start | bytes 835592 | tf_op jit(solution)/shard_map/ppermute | solution.py:459
  288.8 18.3 %collective-permute-start.12 = (bf16[1088,128]{1,0:T(8,128)(2,1)}, bf16[1088,128]{1,0:T(8,128)(2,1)}, u32[]{:S(2)}, u32[]{:S(2)}) collective-permute-start(bf16[1088,128]{1,0:T(8,128)(2,1)} %collective-permute-done.10.refs_2_), channel_id=1, source_target_pairs={{0,1},{1,0},{2,3},{3,2},{4,5},{5,4},{6,7},{7,6},{8,9},{9,8},{10,11... | collective-permute-start | bytes 835592 | tf_op jit(solution)/shard_map/ppermute | solution.py:459
  299.2 13.7 %collective-permute-start.6 = (bf16[1088,128]{1,0:T(8,128)(2,1)S(1)}, bf16[1088,128]{1,0:T(8,128)(2,1)S(1)}, u32[]{:S(2)}, u32[]{:S(2)}) collective-permute-start(bf16[1088,128]{1,0:T(8,128)(2,1)S(1)} %collective-permute-done.4.refs_1_), channel_id=1, source_target_pairs={{0,1},{1,0},{2,3},{3,2},{4,5},{5,4},{6,7},{7,6},{8,9},{9,8},{10,11... | collective-permute-start | bytes 835592 | tf_op jit(solution)/shard_map/ppermute | solution.py:459
  299.4 13.6 %collective-permute-start.7 = (bf16[1088,128]{1,0:T(8,128)(2,1)}, bf16[1088,128]{1,0:T(8,128)(2,1)S(1)}, u32[]{:S(2)}, u32[]{:S(2)}) collective-permute-start(bf16[1088,128]{1,0:T(8,128)(2,1)} %collective-permute-done.5.refs_2_), channel_id=1, source_target_pairs={{0,1},{1,0},{2,3},{3,2},{4,5},{5,4},{6,7},{7,6},{8,9},{9,8},{10,11... | collective-permute-start | bytes 835592 | tf_op jit(solution)/shard_map/ppermute | solution.py:459
  (20 other events, 201.4 us)

commit v3 on v2

--- a/solution.py
+++ b/solution.py
@@ -144,48 +144,57 @@
     )
 
 
-def pack_first_kernel(q_ref, k_ref, v_ref, marks_ref, out_ref):
-    tokens, some = q_ref.shape[0], v_ref.shape[0]
-    out_ref[0, :tokens] = q_ref[...]
-    out_ref[0, tokens : 2 * tokens] = k_ref[...]
-    out_ref[0, 2 * tokens : 2 * tokens + some] = v_ref[...]
-    out_ref[0, 2 * tokens + some :] = marks_ref[0]
-
-
-def pack_first(queries, keys, values, marks, some):
-    tokens, heads = queries.shape[0], marks.shape[0]
-    rows = 2 * tokens + some + marks.shape[1]
-    whole = pl.BlockSpec((tokens, 128), lambda j: (0, j))
-    return pl.pallas_call(
-        pack_first_kernel,
+def pack_kernel(count, *refs):
+    sources, marks_ref = refs[:count], refs[count]
+    out_ref, sems = refs[count + 1], refs[count + 2]
+    tokens, heads = sources[0].shape[0], out_ref.shape[0]
+    copies = []
+    for n, source in enumerate(sources):
+        for j in range(heads):
+            copies.append(
+                pltpu.make_async_copy(
+                    source.at[:, pl.ds(j * 128, 128)],
+                    out_ref.at[j, pl.ds(n * tokens, tokens)],
+                    sems.at[len(copies)],
+                )
+            )
+    marked = out_ref.at[:, pl.ds(count * tokens, marks_ref.shape[1])]
+    copies.append(pltpu.make_async_copy(marks_ref, marked, sems.at[len(copies)]))
+    for copy in copies:
+        copy.start()
+    for copy in copies:
+        copy.wait()
+
+
+def pack(sources, marks):
+    tokens, heads = sources[0].shape[0], marks.shape[0]
+    rows = len(sources) * tokens + marks.shape[1]
+    anywhere = pl.BlockSpec(memory_space=pl.ANY)
+    return pl.pallas_call(
+        functools.partial(pack_kernel, len(sources)),
+        in_specs=[anywhere] * (len(sources) + 1),
+        out_specs=anywhere,
+        out_shape=jax.ShapeDtypeStruct((heads, rows, 128), BF16),
+        scratch_shapes=[pltpu.SemaphoreType.DMA((len(sources) * heads + 1,))],
+        compiler_params=pltpu.CompilerParams(vmem_limit_bytes=60 * 1024 * 1024),
+        cost_estimate=cost(0, 2 * heads * rows * 256),
+    )(*sources, marks)
+
+
+def split_kernel(v_ref, out_ref):
+    out_ref[0] = v_ref[...]
+
+
+def split(values, heads):
+    tokens = values.shape[0]
+    return pl.pallas_call(
+        split_kernel,
         grid=(heads,),
-        in_specs=[
-            whole,
-            whole,
-            pl.BlockSpec((some, 128), lambda j: (0, j)),
-            pl.BlockSpec((1, marks.shape[1], 128), lambda j: (j, 0, 0)),
-        ],
-        out_specs=pl.BlockSpec((1, rows, 128), lambda j: (j, 0, 0)),
-        out_shape=jax.ShapeDtypeStruct((heads, rows, 128), BF16),
-        compiler_params=params(60),
-        cost_estimate=cost(0, 2 * heads * rows * 256),
-    )(queries, keys, values, marks)
-
-
-def pack_rest_kernel(v_ref, out_ref):
-    out_ref[0] = v_ref[...]
-
-
-def pack_rest(values, heads, some):
-    rest = values.shape[0] - some
-    return pl.pallas_call(
-        pack_rest_kernel,
-        grid=(heads,),
-        in_specs=[pl.BlockSpec((rest, 128), lambda j: (1, j))],
-        out_specs=pl.BlockSpec((1, rest, 128), lambda j: (j, 0, 0)),
-        out_shape=jax.ShapeDtypeStruct((heads, rest, 128), BF16),
-        compiler_params=params(60),
-        cost_estimate=cost(0, 2 * heads * rest * 256),
+        in_specs=[pl.BlockSpec((tokens, 128), lambda j: (0, j))],
+        out_specs=pl.BlockSpec((1, tokens, 128), lambda j: (j, 0, 0)),
+        out_shape=jax.ShapeDtypeStruct((heads, tokens, 128), BF16),
+        compiler_params=params(60),
+        cost_estimate=cost(0, 2 * heads * tokens * 256),
     )(values)
 
 
@@ -241,33 +250,43 @@
         ],
         scratch_shapes=[pltpu.VMEM((tokens, 256), BF16)],
         compiler_params=params(60),
-        cost_estimate=cost(2 * ranks * CLUSTERS * SLOTS * tokens * 256, 16 << 20),
+        cost_estimate=cost(1, 1),
     )(target, first, first)
 
 
-def place_some_kernel(target_ref, v_ref, v_out):
+def place_one_kernel(who_ref, target_ref, v_ref, *refs):
+    v_out = refs[-1]
     slots = v_out.shape[0] * SLOTS
-    some = v_ref.shape[1]
-    picked = match(0, slots, target_ref[0, :, :some]).astype(BF16)
-    out = jnp.dot(picked, v_ref[0], preferred_element_type=F32)
+    picked = match(0, slots, target_ref[0]).astype(BF16)
+    out = jnp.dot(picked, v_ref[...], preferred_element_type=F32)
     v_out[...] = by_slot(out).astype(BF16)
 
 
-def place_some(target, first, tokens, some):
-    ranks = first.shape[0]
-    block = 2 * tokens // some
-    return pl.pallas_call(
-        place_some_kernel,
-        grid=(ranks,),
-        in_specs=[
-            pl.BlockSpec((1, 1, tokens), lambda j: (j, 0, 0)),
-            pl.BlockSpec((1, some, 128), lambda j: (j, block, 0)),
-        ],
-        out_specs=pl.BlockSpec((CLUSTERS, SLOTS, 128), lambda j: (0, j, 0)),
+def place_one(who, target, rows, placed):
+    ranks, tokens = target.shape[0], target.shape[2]
+    in_specs = [
+        pl.BlockSpec((1, 1, tokens), lambda i, who: (who[0], 0, 0)),
+        pl.BlockSpec((tokens, 128), lambda i, who: (0, 0)),
+    ]
+    args = [who, target, rows]
+    aliases = {}
+    if placed is not None:
+        in_specs.append(pl.BlockSpec(memory_space=pl.ANY))
+        args.append(placed)
+        aliases = {3: 0}
+    return pl.pallas_call(
+        place_one_kernel,
+        grid_spec=pltpu.PrefetchScalarGridSpec(
+            num_scalar_prefetch=1,
+            grid=(1,),
+            in_specs=in_specs,
+            out_specs=pl.BlockSpec((CLUSTERS, SLOTS, 128), lambda i, who: (0, who[0], 0)),
+        ),
         out_shape=jax.ShapeDtypeStruct((CLUSTERS, ranks * SLOTS, 128), BF16),
-        compiler_params=params(24),
-        cost_estimate=cost(2 * ranks * CLUSTERS * SLOTS * some * 256, 6 << 20),
-    )(target, first)
+        input_output_aliases=aliases,
+        compiler_params=params(60),
+        cost_estimate=cost(1, 1),
+    )(*args)
 
 
 def weigh_kernel(q_ref, k_ref, p_ref, w_out, mean_out):
@@ -306,61 +325,37 @@
             jax.ShapeDtypeStruct((groups, rows, rows), BF16),
             jax.ShapeDtypeStruct((groups * PAIR, 128), F32),
         ],
-        compiler_params=params(24),
-        cost_estimate=cost(2 * groups * rows * rows * 256, 20 << 20, groups * rows * rows),
+        compiler_params=params(60),
+        cost_estimate=cost(1, 1),
     )(q_rows, k_rows, at)
 
 
-def mix_kernel(ranks, target_ref, v_ref, part_ref, w_ref, o_out, v_rows):
-    i = pl.program_id(0)
-    slots = part_ref.shape[0] * SLOTS
+def mix_kernel(w_ref, v_ref, o_out):
     count, rows = w_ref.shape[0], w_ref.shape[1]
-    tokens, rest = target_ref.shape[2], v_ref.shape[1]
-
-    @pl.when(i < ranks)
-    def _():
-        picked = match(0, slots, target_ref[0, :, tokens - rest :]).astype(BF16)
-        out = jnp.dot(picked, v_ref[0], preferred_element_type=F32)
-        where = pl.ds(pl.multiple_of(i * SLOTS, SLOTS), SLOTS)
-        v_rows[:, where, :] = by_slot(out) + part_ref[...].astype(F32)
-
-    @pl.when(i >= ranks)
-    def _():
-        ones = jnp.ones((rows, 128), BF16)
-        for n in range(count):
-            own = v_rows[pl.ds(((i - ranks) * count + n) * PAIR, PAIR)]
-            right = jnp.concatenate([own.reshape(rows, 128).astype(BF16), ones], axis=1)
-            out = jnp.dot(w_ref[n], right, preferred_element_type=F32)
-            total = out[:, 128:]
-            o_out[n] = (out[:, :128] / jnp.where(total > 0.0, total, 1.0)).astype(BF16)
-
-
-def mix(target, rows_v, part, weights):
-    ranks, rest = rows_v.shape[0], rows_v.shape[1]
+    ones = jnp.ones((rows, 128), BF16)
+    for n in range(count):
+        right = jnp.concatenate([v_ref[n], ones], axis=1)
+        out = jnp.dot(w_ref[n], right, preferred_element_type=F32)
+        total = out[:, 128:]
+        o_out[n] = (out[:, :128] / jnp.where(total > 0.0, total, 1.0)).astype(BF16)
+
+
+def mix(weights, v_rows):
     groups, rows = weights.shape[0], weights.shape[1]
-    count = groups // ranks
-
-    def sender(i):
-        return jnp.minimum(i, ranks - 1)
-
-    def group(i):
-        return jnp.maximum(i - ranks, 0)
-
-    return pl.pallas_call(
-        functools.partial(mix_kernel, ranks),
-        grid=(2 * ranks,),
-        in_specs=[
-            pl.BlockSpec((1, 1, target.shape[2]), lambda i: (sender(i), 0, 0)),
-            pl.BlockSpec((1, rest, 128), lambda i: (sender(i), 0, 0)),
-            pl.BlockSpec((CLUSTERS, SLOTS, 128), lambda i: (0, sender(i), 0)),
-            pl.BlockSpec((count, rows, rows), lambda i: (group(i), 0, 0)),
-        ],
-        out_specs=pl.BlockSpec((count, rows, 128), lambda i: (group(i), 0, 0)),
+    step = 16
+
+    def spec(width):
+        return pl.BlockSpec((step, rows, width), lambda i: (i, 0, 0))
+
+    return pl.pallas_call(
+        mix_kernel,
+        grid=(groups // step,),
+        in_specs=[spec(rows), spec(128)],
+        out_specs=spec(128),
         out_shape=jax.ShapeDtypeStruct((groups, rows, 128), BF16),
-        scratch_shapes=[pltpu.VMEM((CLUSTERS, ranks * SLOTS, 128), F32)],
-        compiler_params=params(24),
-        cost_estimate=cost(2 * ranks * CLUSTERS * SLOTS * rest * 256, 16 << 20),
-    )(target, rows_v, part, weights)
+        compiler_params=params(60),
+        cost_estimate=cost(1, 1),
+    )(weights, v_rows)
 
 
 def unplace_kernel(who_ref, target_ref, o_ref, mean_ref, out_ref):
@@ -394,29 +389,29 @@
             out_specs=pl.BlockSpec((tokens + 2 * count, 128), lambda i, who: (0, 0)),
         ),
         out_shape=jax.ShapeDtypeStruct((tokens + 2 * count, 128), BF16),
-        compiler_params=params(24),
+        compiler_params=params(60),
         cost_estimate=cost(1, 1),
     )(who, target, mixed, means)
 
 
-def project_kernel(lanes, has_total, *refs):
+def project_kernel(pieces, lanes, has_total, *refs):
     refs = refs[1:]
-    atts, ws = refs[:4], refs[4 : 4 + 4 * lanes]
+    atts, ws = refs[:pieces], refs[pieces : pieces + 4 * lanes]
     out_ref = refs[-1]
     left = jnp.concatenate([a[...] for a in atts], axis=1)
     right = jnp.concatenate([w[...] for w in ws], axis=0)
     total = jnp.dot(left, right, preferred_element_type=F32)
     if has_total:
-        total = total + refs[4 + 4 * lanes][...]
+        total = total + refs[pieces + 4 * lanes][...]
     out_ref[...] = total.astype(out_ref.dtype)
 
 
 def project(where, tokens, atts, weights, columns, total, dtype):
-    lanes = atts[0].shape[1] // 128
-    step = 512
-    cols = out_cols = weights[3].shape[1]
-    in_specs = [pl.BlockSpec((step, 128 * lanes), lambda i, w: (i, 0)) for _ in atts]
-    args = list(atts)
+    lanes, pieces = len(where), sum(len(group) for group in atts)
+    step = 256
+    cols = weights[3].shape[1]
+    args = [a for group in atts for a in group]
+    in_specs = [pl.BlockSpec((step, a.shape[1]), lambda i, w: (i, 0)) for a in args]
     for part in range(4):
         for lane in range(lanes):
             in_specs.append(
@@ -426,19 +421,19 @@
             )
             args.append(weights[part])
     if total is not None:
-        in_specs.append(pl.BlockSpec((step, out_cols), lambda i, w: (i, 0)))
+        in_specs.append(pl.BlockSpec((step, cols), lambda i, w: (i, 0)))
         args.append(total)
     return pl.pallas_call(
-        functools.partial(project_kernel, lanes, total is not None),
+        functools.partial(project_kernel, pieces, lanes, total is not None),
         grid_spec=pltpu.PrefetchScalarGridSpec(
             num_scalar_prefetch=1,
             grid=(tokens // step,),
             in_specs=in_specs,
-            out_specs=pl.BlockSpec((step, out_cols), lambda i, w: (i, 0)),
+            out_specs=pl.BlockSpec((step, cols), lambda i, w: (i, 0)),
         ),
-        out_shape=jax.ShapeDtypeStruct((tokens, out_cols), dtype),
-        compiler_params=params(60),
-        cost_estimate=cost(2 * tokens * 512 * lanes * out_cols, 8 << 20),
+        out_shape=jax.ShapeDtypeStruct((tokens, cols), dtype),
+        compiler_params=params(60),
+        cost_estimate=cost(1, 1),
     )(jnp.stack(list(where) + list(columns)), *args)
 
 
@@ -447,7 +442,6 @@
     me = lax.axis_index("ctx")
     mine = lax.axis_index("head")
     tokens = queries.shape[0]
-    some = tokens // 2
     cl_dev = CLUSTERS // ranks
     cap = ranks * SLOTS
     y, core = mine // 2, mine % 2
@@ -458,12 +452,20 @@
     def swap_core(x):
         return lax.ppermute(x, "head", [(0, 1), (1, 0), (2, 3), (3, 2)])
 
+    def swap_ctx(x, d):
+        return lax.ppermute(x, "ctx", [(i, i ^ d) for i in range(ranks)])
+
+    def who(d):
+        return jnp.reshape(me ^ d, (1,))
+
+    def after(x, other):
+        return lax.optimization_barrier((x, other))[0]
+
     marks = [x.astype(BF16).reshape(ranks, tokens // 128, 128) for x in (cluster_of, slot_of)]
-    marks = jnp.concatenate(marks, axis=1)
-    first = pack_first(queries, keys, values, marks, some)
+    first = pack((queries, keys), jnp.concatenate(marks, axis=1))
     first = lax.all_to_all(first, "ctx", split_axis=0, concat_axis=0, tiled=True)
-    rows_v, first = lax.optimization_barrier((pack_rest(values, ranks, some), first))
-    rows_v = lax.all_to_all(rows_v, "ctx", split_axis=0, concat_axis=0, tiled=True)
+    v_heads = split(values, ranks)
+    v_heads = {d: lax.dynamic_index_in_dim(v_heads, me ^ d, 0, False) for d in range(ranks)}
 
     cols = out_weight.shape[1] // 4
     across = swap_y(lax.dynamic_slice_in_dim(out_weight, (1 - y) * 2 * cols, 2 * cols, 1))
@@ -471,10 +473,14 @@
         lax.dynamic_slice_in_dim(out_weight, (2 * y + 1 - core) * cols, cols, 1)
     )
     corner = swap_core(lax.dynamic_slice_in_dim(across, (1 - core) * cols, cols, 1))
-    w_parts = (out_weight, across, beside, corner)
     w_columns = (mine, core, jnp.zeros_like(core), jnp.zeros_like(core))
 
-    marks = first[:, 2 * tokens + some :, :].astype(jnp.int32)
+    v_heads = after(v_heads, (first, across, beside))
+    rows_v = {0: v_heads[0]}
+    for d in (4, 5, 6, 1):
+        rows_v[d] = swap_ctx(v_heads[d], d)
+
+    marks = first[:, 2 * tokens :, :].astype(jnp.int32)
     target = marks[:, : tokens // 128, :] * SLOTS + marks[:, tokens // 128 :, :]
     target = target.reshape(ranks, 1, tokens)
     q_rows, k_rows, at = place_pair(target, first, tokens)
@@ -482,34 +488,57 @@
     def paired(x):
         return x.reshape(CLUSTERS // PAIR, PAIR * cap, 128)
 
+    rows_v[2] = swap_ctx(after(v_heads[2], (rows_v[1], q_rows)), 2)
+    q_rows = after(q_rows, corner)
     weights, means = weigh(paired(q_rows), paired(k_rows), paired(at))
-    part = place_some(target, first, tokens, some)
-    rows_v, w_parts = lax.optimization_barrier((rows_v, w_parts))
-    mixed = mix(target, rows_v, part, weights).reshape(CLUSTERS, cap, 128)
-
-    got = {}
-    after = {6: 4, 7: 5}
-    for d in (4, 5, 1, 2, 3, 0, 6, 7):
-        who = jnp.reshape(me ^ d, (1,))
-        if d in after:
-            who, got[after[d]] = lax.optimization_barrier((who, got[after[d]]))
-        block = unplace(who, target, mixed, means)
-        got[d] = block
-        if d:
-            got[d] = lax.ppermute(block, "ctx", [(i, i ^ d) for i in range(ranks)])
-
-    total = None
-    splits = ((0, 1, 2, 3), (4, 5), (6,), (7,))
-    for lanes in splits:
-        own = got[lanes[0]]
-        if len(lanes) > 1:
-            own = jnp.concatenate([got[d][:tokens] for d in lanes], axis=1)
-        there = swap_y(own)
-        atts = (own, there, swap_core(own), swap_core(there))
-        last = lanes == splits[-1]
-        total = project(
-            [me ^ d for d in lanes], tokens, atts, w_parts, w_columns, total, BF16 if last else F32
-        )
+    for d in (7, 3):
+        rows_v[d] = swap_ctx(after(v_heads[d], (rows_v[2], weights)), d)
+    placed = None
+    for d in (0, 1, 2, 4, 5, 3, 6, 7):
+        placed = place_one(who(d), target, rows_v[d], placed)
+    w_parts = (out_weight, across, beside, corner)
+    mixed = mix(weights, paired(placed)).reshape(CLUSTERS, cap, 128)
+
+    def leave(d, *others):
+        return unplace(after(who(d), others) if others else who(d), target, mixed, means)
+
+    def side(blocks):
+        return jnp.concatenate([block[:tokens] for block in blocks], axis=1)
+
+    got = {d: swap_ctx(leave(d), d) for d in (4, 5)}
+    got[0] = leave(0)
+    y_0 = swap_y(got[0])
+    got[1] = swap_ctx(leave(1), 1)
+    got[2] = swap_ctx(leave(2, y_0), 2)
+    got[3] = swap_ctx(leave(3, got[1]), 3)
+    own_123 = side([got[d] for d in (1, 2, 3)])
+    y_123 = swap_y(own_123)
+    got[6] = swap_ctx(leave(6, got[4], got[3]), 6)
+    got[7] = swap_ctx(leave(7, got[5]), 7)
+    own_45 = side([got[d] for d in (4, 5)])
+    y_45 = swap_y(own_45)
+    own_0123 = side([got[0], own_123])
+    core_0123 = swap_core(after(own_0123, y_123))
+    both_0123 = side([y_0, y_123])
+    core_both_0123 = swap_core(both_0123)
+    y_6 = swap_y(after(got[6], y_123))
+    core_45 = swap_core(after(own_45, core_both_0123))
+    y_7 = swap_y(got[7])
+    core_both_45 = swap_core(after(y_45, core_45))
+
+    def add(total, lanes, atts, dtype):
+        heads = [me ^ d for d in lanes]
+        return project(heads, tokens, atts, w_parts, w_columns, total, dtype)
+
+    total = add(
+        None, (0, 1, 2, 3), [[own_0123], [both_0123], [core_0123], [core_both_0123]], F32
+    )
+    total = add(total, (4, 5), [[own_45], [y_45], [core_45], [core_both_45]], F32)
+    core_67 = swap_core(side([got[6], got[7]]))
+    core_y_6, core_y_7 = swap_core(y_6), swap_core(y_7)
+    total = add(
+        total, (6, 7), [[got[6], got[7]], [y_6, y_7], [core_67], [core_y_6, core_y_7]], BF16
+    )
 
     sent = jnp.stack([got[d][tokens:] for d in range(ranks)]).astype(F32)
     sent = sent[:, :cl_dev] + sent[:, cl_dev:]

time: 320 us -> 455 us (1.42)
  Pallas kernels: 98.8 us -> 253 us
  waiting for transfers between devices: 146 us -> 132 us
  local copies, waits for them, and re-layouts: 32.1 us -> 24.4 us
    pallas_call x8 -> x14, Pallas kernels: 59.7 us -> 194 us  [the longest x1 129 us: pack(): pl.pallas_call(functools.partial(pack_kernel, len(sources)), in_specs=[an...]
    pallas_call x8, Pallas kernels: 10.9 us -> 24.6 us  [unplace(): pl.pallas_call(unplace_kernel, grid_spec=pltpu.PrefetchScalarGridSpec(num...]
    unnamed x54 -> x64, local copies, waits for them, and re-layouts: 19.7 us -> 8.11 us
    all_to_all x1, waiting for transfers between devices: 11 us -> 0.01 us  [head_body(): lax.all_to_all(first, 'ctx', split_axis=0, concat_axis=0, tiled=True)]
    pallas_call x1, Pallas kernels: 11 us -> 17 us  [weigh(): pl.pallas_call(weigh_kernel, grid=(groups // step,), in_specs=[spec, spec...]
    ppermute x7 -> x14, starting transfers between devices: 16.4 us -> 21.9 us  [swap_ctx(): return lax.ppermute(x, 'ctx', [(i, i ^ d) for i in range(ranks)])]
    ppermute x5 -> x6, waiting for transfers between devices: 112 us -> 109 us  [swap_y(): return lax.ppermute(x, 'head', [(0, 2), (1, 3), (2, 0), (3, 1)])]
    ppermute x7 -> x14, waiting for transfers between devices: 22.9 us -> 22.4 us  [swap_ctx(): return lax.ppermute(x, 'ctx', [(i, i ^ d) for i in range(ranks)])]
  transfers between devices with their start and end apart: 24 -> 30, of which waited for: 9 -> 10; matrix products, arithmetic and copies ran while one was open for 5% -> 5% of each run, Pallas kernels for 23% -> 22%
where the time goes in v3:
time: 455 us; the launch traced here: 453 us
  Pallas kernels  253 us (56%)
  waiting for transfers between devices  132 us (29%)
  starting transfers between devices  35.9 us (8%)
  local copies, waits for them, and re-layouts  24.4 us (5%)
  other arithmetic  6.76 us (1%)
    pallas_call x1, Pallas kernels, pack(): pl.pallas_call(functools.partial(pack_kernel, len(sources)), in_specs=[an...  129 us
    ppermute x6, waiting for transfers between devices, swap_y(): return lax.ppermute(x, 'head', [(0, 2), (1, 3), (2, 0), (3, 1)])  109 us
    pallas_call x3, Pallas kernels, project(): pl.pallas_call(functools.partial(project_kernel, pieces, lanes, total is...  25.8 us
    pallas_call x8, Pallas kernels, unplace(): pl.pallas_call(unplace_kernel, grid_spec=pltpu.PrefetchScalarGridSpec(num...  24.6 us
    pallas_call x8, Pallas kernels, place_one(): pl.pallas_call(place_one_kernel, grid_spec=pltpu.PrefetchScalarGridSpec(n...  24.5 us
    ppermute x14, waiting for transfers between devices, swap_ctx(): return lax.ppermute(x, 'ctx', [(i, i ^ d) for i in range(ranks)])  22.4 us
    ppermute x14, starting transfers between devices, swap_ctx(): return lax.ppermute(x, 'ctx', [(i, i ^ d) for i in range(ranks)])  21.9 us
    pallas_call x1, Pallas kernels, place_pair(): pl.pallas_call(place_pair_kernel, grid=(ranks,), in_specs=[pl.BlockSpec((...  17.2 us
  transfers between devices with their start and end apart: 30, of which 10 were waited for; matrix products, arithmetic and copies ran while one was open for 5% of the time, Pallas kernels for 22%

profile of v3, /device:TPU:0, one launch (start us, length us, event | category | flops | bytes accessed | tf_op | source)
XLA Modules:
  0.0 453.2 jit_solution(15001504744026557231)
XLA Ops:
  2.8 129.3 %shard_map.86 = bf16[8,2064,128]{2,1,0:T(8,128)(2,1)} custom-call(bf16[1024,1024]{1,0:T(8,128)(2,1)} %refs_0_.1, bf16[1024,1024]{1,0:T(8,128)(2,1)} %refs_1_.1, bf16[8,16,128]{2,1,0:T(8,128)(2,1)} %pad_maximum_fusion.5.refs_2_), custom_call_target="tpu_custom_call" | custom-call | bytes 8454144 | tf_op jit(solution)/shard_map/pallas_call | solution.py:173
  132.1 7.3 %all-to-all-start = ((bf16[8,2064,128]{2,1,0:T(8,128)(2,1)}), bf16[8,2064,128]{2,1,0:T(8,128)(2,1)}, u32[]{:S(2)}, u32[]{:S(2)}) async-start(bf16[8,2064,128]{2,1,0:T(8,128)(2,1)} %shard_map.86), calls=%async_computation | async-start | bytes 8454144 | tf_op jit(solution)/shard_map/all_to_all | solution.py:466
  139.4 4.8 %constant_dynamic-slice_fusion.2 = bf16[1024,2048]{1,0:T(8,128)(2,1)} fusion(bf16[1024,4096]{1,0:T(8,128)(2,1)} %refs_9_.1, s32[]{:T(128)S(6)} %select_n.55), kind=kLoop, calls=%fused_computation.49 | loop fusion | bytes 8388612 | tf_op jit(solution)/shard_map/dynamic_slice | solution.py:471
  145.7 3.2 constant_dynamic-slice_fusion
  148.8 87.6 %collective-permute-done.refs_9_.refs_10_.refs_11_.refs_12_.refs_7_.refs_8_ = bf16[1024,2048]{1,0:T(8,128)(2,1)} collective-permute-done((bf16[1024,2048]{1,0:T(8,128)(2,1)}, bf16[1024,2048]{1,0:T(8,128)(2,1)}, u32[]{:S(2)}, u32[]{:S(2)}) %collective-permute-start) | collective-permute-done | bytes 4194336 | tf_op jit(solution)/shard_map/ppermute | solution.py:450
  239.5 5.6 %shard_map.89 = bf16[8,1024,128]{2,1,0:T(8,128)(2,1)} custom-call(bf16[1024,1024]{1,0:T(8,128)(2,1)} %v_ref.1), custom_call_target="tpu_custom_call" | custom-call | bytes 4194304 | tf_op jit(solution)/shard_map/pallas_call | solution.py:190
  250.8 17.2 %shard_map.87 = (bf16[256,64,128]{2,1,0:T(8,128)(2,1)}, bf16[256,64,128]{2,1,0:T(8,128)(2,1)}, f32[256,64,128]{2,1,0:T(8,128)}) custom-call(s32[8,1,1024]{2,1,0:T(1,128)} %bitcast.81, bf16[8,2064,128]{2,1,0:T(8,128)(2,1)} %all-to-all-done.q_ref.k_ref, bf16[8,2064,128]{2,1,0:T(8,128)(2,1)} %all-to-all-done.q_ref.k_ref), custom_call_target="tpu_custom_call" | custom-call | flops 1 | bytes 1 | tf_op jit(solution)/shard_map/pallas_call | solution.py:237
  272.6 17.0 %shard_map.88 = (bf16[128,128,128]{2,1,0:T(8,128)(2,1)}, f32[256,128]{1,0:T(8,128)}) custom-call(bf16[128,128,128]{2,1,0:T(8,128)(2,1)} %bitcast.99, bf16[128,128,128]{2,1,0:T(8,128)(2,1)} %bitcast.100, f32[128,128,128]{2,1,0:T(8,128)} %bitcast.98), custom_call_target="tpu_custom_call" | custom-call | flops 1 | bytes 1 | tf_op jit(solution)/shard_map/pallas_call | solution.py:316
  291.1 3.3 collective-permute-start.6
  294.7 3.1 shard_map.90.refs_0_
  324.6 8.8 %shard_map.98 = bf16[128,128,128]{2,1,0:T(8,128)(2,1)} custom-call(bf16[128,128,128]{2,1,0:T(8,128)(2,1)} %get-tuple-element.31.w_ref, bf16[128,128,128]{2,1,0:T(8,128)(2,1)} %bitcast.80), custom_call_target="tpu_custom_call" | custom-call | flops 1 | bytes 1 | tf_op jit(solution)/shard_map/pallas_call | solution.py:350
  348.2 3.3 collective-permute-start.10
  357.5 3.1 shard_map.106
  362.5 4.0 collective-permute-done.14
  366.5 3.2 shard_map.104
  372.2 12.2 %collective-permute-done.12 = bf16[1088,128]{1,0:T(8,128)(2,1)S(1)} collective-permute-done((bf16[1088,128]{1,0:T(8,128)(2,1)}, bf16[1088,128]{1,0:T(8,128)(2,1)S(1)}, u32[]{:S(2)}, u32[]{:S(2)}) %collective-permute-start.12) | collective-permute-done | bytes 278560 | tf_op jit(solution)/shard_map/ppermute | solution.py:456
  384.4 4.1 collective-permute-done.17
  390.0 3.1 shard_map.102
  397.0 11.1 %collective-permute-done.18 = bf16[1024,384]{1,0:T(8,128)(2,1)} collective-permute-done((bf16[1024,384]{1,0:T(8,128)(2,1)S(1)}, bf16[1024,384]{1,0:T(8,128)(2,1)}, u32[]{:S(2)}, u32[]{:S(2)}) %collective-permute-start.18) | collective-permute-done | bytes 786464 | tf_op jit(solution)/shard_map/ppermute | solution.py:450
  414.2 5.1 %collective-permute-done.20.refs_4_ = bf16[1088,128]{1,0:T(8,128)(2,1)} collective-permute-done((bf16[1088,128]{1,0:T(8,128)(2,1)S(1)}, bf16[1088,128]{1,0:T(8,128)(2,1)}, u32[]{:S(2)}, u32[]{:S(2)}) %collective-permute-start.20) | collective-permute-done | bytes 278560 | tf_op jit(solution)/shard_map/ppermute | solution.py:450
  419.8 5.0 %collective-permute-done.19.refs_3_ = bf16[1088,128]{1,0:T(8,128)(2,1)} collective-permute-done((bf16[1088,128]{1,0:T(8,128)(2,1)S(1)}, bf16[1088,128]{1,0:T(8,128)(2,1)}, u32[]{:S(2)}, u32[]{:S(2)}) %collective-permute-start.19) | collective-permute-done | bytes 278560 | tf_op jit(solution)/shard_map/ppermute | solution.py:450
  425.6 9.9 %shard_map.107.refs_13_ = f32[1024,1024]{1,0:T(8,128)} custom-call(s32[8]{0:T(128)} %stack.64.refs_0_, bf16[1024,512]{1,0:T(8,128)(2,1)} %copy-done.2, bf16[1024,512]{1,0:T(8,128)(2,1)} %copy-done.1, bf16[1024,512]{1,0:T(8,128)(2,1)} %collective-permute-done.28.refs_3_, bf16[1024,512]{1,0:T(8,128)(2,1)} %copy-done.7, bf16[1024,4096]{1,0:T(8,128)(2,1)} %refs_9_.1, ...), custom_call_target="tpu_custom_call" | custom-call | flops 1 | bytes 1 | tf_op jit(solution)/shard_map/pallas_call | solution.py:426
  436.2 8.3 %shard_map.108.refs_16_ = f32[1024,1024]{1,0:T(8,128)} custom-call(s32[6]{0:T(128)} %stack.63.refs_0_, bf16[1024,256]{1,0:T(8,128)(2,1)} %copy-done.3, bf16[1024,256]{1,0:T(8,128)(2,1)} %collective-permute-done.24.refs_2_, bf16[1024,256]{1,0:T(8,128)(2,1)} %copy-done.10, bf16[1024,256]{1,0:T(8,128)(2,1)} %copy-done.12, bf16[1024,4096]{1,0:T(8,128)(2,1)} %refs_9_.1, ...), custom_call_target="tpu_custom_call" | custom-call | flops 1 | bytes 1 | tf_op jit(solution)/shard_map/pallas_call | solution.py:426
  445.4 7.6 %shard_map.109 = bf16[1024,1024]{1,0:T(8,128)(2,1)} custom-call(s32[6]{0:T(128)} %stack.62.refs_0_, bf16[1088,128]{1,0:T(8,128)(2,1)} %copy-done.6, bf16[1088,128]{1,0:T(8,128)(2,1)} %copy-done.5, bf16[1088,128]{1,0:T(8,128)(2,1)} %collective-permute-done.19.refs_3_, bf16[1088,128]{1,0:T(8,128)(2,1)} %collective-permute-done.20.refs_4_, ...), custom_call_target="tpu_custom_call" | custom-call | flops 1 | bytes 1 | tf_op jit(solution)/shard_map/pallas_call | solution.py:426
  (158 shorter events, 84.8 us)
Async XLA Ops:
  132.1 115.5 %all-to-all-start = ((bf16[8,2064,128]{2,1,0:T(8,128)(2,1)}), bf16[8,2064,128]{2,1,0:T(8,128)(2,1)}, u32[]{:S(2)}, u32[]{:S(2)}) async-start(bf16[8,2064,128]{2,1,0:T(8,128)(2,1)} %shard_map.86), calls=%async_computation | async-start | bytes 8454144 | tf_op jit(solution)/shard_map/all_to_all | solution.py:466
  144.1 92.3 %collective-permute-start = (bf16[1024,2048]{1,0:T(8,128)(2,1)}, bf16[1024,2048]{1,0:T(8,128)(2,1)}, u32[]{:S(2)}, u32[]{:S(2)}) collective-permute-start(bf16[1024,2048]{1,0:T(8,128)(2,1)} %constant_dynamic-slice_fusion.2), channel_id=1, source_target_pairs={{0,2},{1,3},{2,0},{3,1},{4,6},{5,7},{6,4},{7,5},{8,10},{9,11},{10,... | collective-permute-start | bytes 12582920 | tf_op jit(solution)/shard_map/ppermute | solution.py:450
  148.8 98.8 %collective-permute-start.2 = (bf16[1024,1024]{1,0:T(8,128)(2,1)}, bf16[1024,1024]{1,0:T(8,128)(2,1)S(1)}, u32[]{:S(2)}, u32[]{:S(2)}) collective-permute-start(bf16[1024,1024]{1,0:T(8,128)(2,1)} %constant_dynamic-slice_fusion), channel_id=1, source_target_pairs={{0,1},{1,0},{2,3},{3,2},{4,5},{5,4},{6,7},{7,6},{8,9},{9,8},{10,11... | collective-permute-start | bytes 6291464 | tf_op jit(solution)/shard_map/ppermute | solution.py:453
  239.5 30.1 %collective-permute-start.1 = (bf16[1024,1024]{1,0:T(8,128)(2,1)}, bf16[1024,1024]{1,0:T(8,128)(2,1)}, u32[]{:S(2)}, u32[]{:S(2)}) collective-permute-start(bf16[1024,1024]{1,0:T(8,128)(2,1)} %constant_dynamic-slice_fusion.1), channel_id=1, source_target_pairs={{0,1},{1,0},{2,3},{3,2},{4,5},{5,4},{6,7},{7,6},{8,9},{9,8},{10,11... | collective-permute-start | bytes 6291464 | tf_op jit(solution)/shard_map/ppermute | solution.py:453
  247.6 20.4 %collective-permute-start.3 = (bf16[1024,128]{1,0:T(8,128)(2,1)}, bf16[1024,128]{1,0:T(8,128)(2,1)S(1)}, u32[]{:S(2)}, u32[]{:S(2)}) collective-permute-start(bf16[1024,128]{1,0:T(8,128)(2,1)} %get-tuple-element.34), channel_id=1, source_target_pairs={{0,4},{4,0},{8,12},{12,8},{16,20},{20,16},{24,28},{28,24},{1,5},{5... | collective-permute-start | bytes 786440 | tf_op jit(solution)/shard_map/ppermute | solution.py:456
  268.1 21.5 %collective-permute-start.4 = (bf16[1024,128]{1,0:T(8,128)(2,1)S(1)}, bf16[1024,128]{1,0:T(8,128)(2,1)S(1)}, u32[]{:S(2)}, u32[]{:S(2)}) collective-permute-start(bf16[1024,128]{1,0:T(8,128)(2,1)S(1)} %copy-done.16), channel_id=1, source_target_pairs={{0,8},{4,12},{8,0},{12,4},{16,24},{20,28},{24,16},{28,20},{1,9},{5... | collective-permute-start | bytes 786440 | tf_op jit(solution)/shard_map/ppermute | solution.py:456
  269.6 38.0 %collective-permute-start.8 = (bf16[1024,128]{1,0:T(8,128)(2,1)S(1)}, bf16[1024,128]{1,0:T(8,128)(2,1)S(1)}, u32[]{:S(2)}, u32[]{:S(2)}) collective-permute-start(bf16[1024,128]{1,0:T(8,128)(2,1)S(1)} %get-tuple-element.40), channel_id=1, source_target_pairs={{0,20},{4,16},{8,28},{12,24},{16,4},{20,0},{24,12},{28,8},{1,21},{... | collective-permute-start | bytes 786440 | tf_op jit(solution)/shard_map/ppermute | solution.py:456
  272.0 31.9 %collective-permute-start.9 = (bf16[1024,128]{1,0:T(8,128)(2,1)S(1)}, bf16[1024,128]{1,0:T(8,128)(2,1)S(1)}, u32[]{:S(2)}, u32[]{:S(2)}) collective-permute-start(bf16[1024,128]{1,0:T(8,128)(2,1)S(1)} %get-tuple-element.41), channel_id=1, source_target_pairs={{0,16},{4,20},{8,24},{12,28},{16,0},{20,4},{24,8},{28,12},{1,17},{... | collective-permute-start | bytes 786440 | tf_op jit(solution)/shard_map/ppermute | solution.py:456
  289.6 23.7 %collective-permute-start.7 = (bf16[1024,128]{1,0:T(8,128)(2,1)S(1)}, bf16[1024,128]{1,0:T(8,128)(2,1)S(1)}, u32[]{:S(2)}, u32[]{:S(2)}) collective-permute-start(bf16[1024,128]{1,0:T(8,128)(2,1)S(1)} %get-tuple-element.39), channel_id=1, source_target_pairs={{0,12},{4,8},{8,4},{12,0},{16,28},{20,24},{24,20},{28,16},{1,13},{... | collective-permute-start | bytes 786440 | tf_op jit(solution)/shard_map/ppermute | solution.py:456
  291.1 26.0 %collective-permute-start.6 = (bf16[1024,128]{1,0:T(8,128)(2,1)S(1)}, bf16[1024,128]{1,0:T(8,128)(2,1)S(1)}, u32[]{:S(2)}, u32[]{:S(2)}) collective-permute-start(bf16[1024,128]{1,0:T(8,128)(2,1)S(1)} %get-tuple-element.37), channel_id=1, source_target_pairs={{0,24},{4,28},{8,16},{12,20},{16,8},{20,12},{24,0},{28,4},{1,25},{... | collective-permute-start | bytes 786440 | tf_op jit(solution)/shard_map/ppermute | solution.py:456
  294.4 26.5 %collective-permute-start.5 = (bf16[1024,128]{1,0:T(8,128)(2,1)S(1)}, bf16[1024,128]{1,0:T(8,128)(2,1)S(1)}, u32[]{:S(2)}, u32[]{:S(2)}) collective-permute-start(bf16[1024,128]{1,0:T(8,128)(2,1)S(1)} %get-tuple-element.36), channel_id=1, source_target_pairs={{0,28},{4,24},{8,20},{12,16},{16,12},{20,8},{24,4},{28,0},{1,29},{... | collective-permute-start | bytes 786440 | tf_op jit(solution)/shard_map/ppermute | solution.py:456
  336.5 17.8 %collective-permute-start.11 = (bf16[1088,128]{1,0:T(8,128)(2,1)}, bf16[1088,128]{1,0:T(8,128)(2,1)S(1)}, u32[]{:S(2)}, u32[]{:S(2)}) collective-permute-start(bf16[1088,128]{1,0:T(8,128)(2,1)} %shard_map.100), channel_id=1, source_target_pairs={{0,4},{4,0},{8,12},{12,8},{16,20},{20,16},{24,28},{28,24},{1,5},{5... | collective-permute-start | bytes 835592 | tf_op jit(solution)/shard_map/ppermute | solution.py:456
  340.1 17.4 %collective-permute-start.16 = (bf16[1088,128]{1,0:T(8,128)(2,1)}, bf16[1088,128]{1,0:T(8,128)(2,1)S(1)}, u32[]{:S(2)}, u32[]{:S(2)}) collective-permute-start(bf16[1088,128]{1,0:T(8,128)(2,1)} %shard_map.105), channel_id=1, source_target_pairs={{0,2},{1,3},{2,0},{3,1},{4,6},{5,7},{6,4},{7,5},{8,10},{9,11},{10,... | collective-permute-start | bytes 835592 | tf_op jit(solution)/shard_map/ppermute | solution.py:450
  344.7 21.9 %collective-permute-start.14 = (bf16[1088,128]{1,0:T(8,128)(2,1)}, bf16[1088,128]{1,0:T(8,128)(2,1)S(1)}, u32[]{:S(2)}, u32[]{:S(2)}) collective-permute-start(bf16[1088,128]{1,0:T(8,128)(2,1)} %shard_map.103), channel_id=1, source_target_pairs={{0,20},{4,16},{8,28},{12,24},{16,4},{20,0},{24,12},{28,8},{1,21},{... | collective-permute-start | bytes 835592 | tf_op jit(solution)/shard_map/ppermute | solution.py:456
  348.2 23.3 %collective-permute-start.10 = (bf16[1088,128]{1,0:T(8,128)(2,1)}, bf16[1088,128]{1,0:T(8,128)(2,1)S(1)}, u32[]{:S(2)}, u32[]{:S(2)}) collective-permute-start(bf16[1088,128]{1,0:T(8,128)(2,1)} %shard_map.99), channel_id=1, source_target_pairs={{0,16},{4,20},{8,24},{12,28},{16,0},{20,4},{24,8},{28,12},{1,17},{... | collective-permute-start | bytes 835592 | tf_op jit(solution)/shard_map/ppermute | solution.py:456
  357.3 27.1 %collective-permute-start.12 = (bf16[1088,128]{1,0:T(8,128)(2,1)}, bf16[1088,128]{1,0:T(8,128)(2,1)S(1)}, u32[]{:S(2)}, u32[]{:S(2)}) collective-permute-start(bf16[1088,128]{1,0:T(8,128)(2,1)} %shard_map.101), channel_id=1, source_target_pairs={{0,12},{4,8},{8,4},{12,0},{16,28},{20,24},{24,20},{28,16},{1,13},{... | collective-permute-start | bytes 835592 | tf_op jit(solution)/shard_map/ppermute | solution.py:456
  360.6 27.9 %collective-permute-start.17 = (bf16[1088,128]{1,0:T(8,128)(2,1)}, bf16[1088,128]{1,0:T(8,128)(2,1)S(1)}, u32[]{:S(2)}, u32[]{:S(2)}) collective-permute-start(bf16[1088,128]{1,0:T(8,128)(2,1)} %shard_map.106), channel_id=1, source_target_pairs={{0,8},{4,12},{8,0},{12,4},{16,24},{20,28},{24,16},{28,20},{1,9},{5... | collective-permute-start | bytes 835592 | tf_op jit(solution)/shard_map/ppermute | solution.py:456
  369.7 39.9 %collective-permute-start.15 = (bf16[1088,128]{1,0:T(8,128)(2,1)}, bf16[1088,128]{1,0:T(8,128)(2,1)S(1)}, u32[]{:S(2)}, u32[]{:S(2)}) collective-permute-start(bf16[1088,128]{1,0:T(8,128)(2,1)} %shard_map.104), channel_id=1, source_target_pairs={{0,28},{4,24},{8,20},{12,16},{16,12},{20,8},{24,4},{28,0},{1,29},{... | collective-permute-start | bytes 835592 | tf_op jit(solution)/shard_map/ppermute | solution.py:456
  371.7 42.5 %collective-permute-start.24 = (bf16[1024,256]{1,0:T(8,128)(2,1)S(1)}, bf16[1024,256]{1,0:T(8,128)(2,1)}, u32[]{:S(2)}, u32[]{:S(2)}) collective-permute-start(bf16[1024,256]{1,0:T(8,128)(2,1)S(1)} %pad_maximum_fusion.4.refs_1_), channel_id=1, source_target_pairs={{0,2},{1,3},{2,0},{3,1},{4,6},{5,7},{6,4},{7,5},{8,10},{9,11},{10,... | collective-permute-start | bytes 1572872 | tf_op jit(solution)/shard_map/ppermute | solution.py:450
  389.4 18.8 %collective-permute-start.18 = (bf16[1024,384]{1,0:T(8,128)(2,1)S(1)}, bf16[1024,384]{1,0:T(8,128)(2,1)}, u32[]{:S(2)}, u32[]{:S(2)}) collective-permute-start(bf16[1024,384]{1,0:T(8,128)(2,1)S(1)} %pad_maximum_fusion.2), channel_id=1, source_target_pairs={{0,2},{1,3},{2,0},{3,1},{4,6},{5,7},{6,4},{7,5},{8,10},{9,11},{10,... | collective-permute-start | bytes 2359304 | tf_op jit(solution)/shard_map/ppermute | solution.py:450
  393.1 17.9 %collective-permute-start.13 = (bf16[1088,128]{1,0:T(8,128)(2,1)}, bf16[1088,128]{1,0:T(8,128)(2,1)S(1)}, u32[]{:S(2)}, u32[]{:S(2)}) collective-permute-start(bf16[1088,128]{1,0:T(8,128)(2,1)} %shard_map.102), channel_id=1, source_target_pairs={{0,24},{4,28},{8,16},{12,20},{16,8},{20,12},{24,0},{28,4},{1,25},{... | collective-permute-start | bytes 835592 | tf_op jit(solution)/shard_map/ppermute | solution.py:456
  414.2 30.4 %collective-permute-start.21 = (bf16[1024,256]{1,0:T(8,128)(2,1)}, bf16[1024,256]{1,0:T(8,128)(2,1)S(1)}, u32[]{:S(2)}, u32[]{:S(2)}) collective-permute-start(bf16[1024,256]{1,0:T(8,128)(2,1)} %pad_maximum_fusion.3), channel_id=1, source_target_pairs={{0,1},{1,0},{2,3},{3,2},{4,5},{5,4},{6,7},{7,6},{8,9},{9,8},{10,11... | collective-permute-start | bytes 1572872 | tf_op jit(solution)/shard_map/ppermute | solution.py:453
  419.3 25.3 %collective-permute-start.23 = (bf16[1088,128]{1,0:T(8,128)(2,1)}, bf16[1088,128]{1,0:T(8,128)(2,1)}, u32[]{:S(2)}, u32[]{:S(2)}) collective-permute-start(bf16[1088,128]{1,0:T(8,128)(2,1)} %collective-permute-done.20.refs_4_), channel_id=1, source_target_pairs={{0,1},{1,0},{2,3},{3,2},{4,5},{5,4},{6,7},{7,6},{8,9},{9,8},{10,11... | collective-permute-start | bytes 835592 | tf_op jit(solution)/shard_map/ppermute | solution.py:453
  424.8 19.7 %collective-permute-start.22 = (bf16[1088,128]{1,0:T(8,128)(2,1)}, bf16[1088,128]{1,0:T(8,128)(2,1)}, u32[]{:S(2)}, u32[]{:S(2)}) collective-permute-start(bf16[1088,128]{1,0:T(8,128)(2,1)} %collective-permute-done.19.refs_3_), channel_id=1, source_target_pairs={{0,1},{1,0},{2,3},{3,2},{4,5},{5,4},{6,7},{7,6},{8,9},{9,8},{10,11... | collective-permute-start | bytes 835592 | tf_op jit(solution)/shard_map/ppermute | solution.py:453
  (32 other events, 364.6 us)

commit v4 on v2

--- a/solution.py
+++ b/solution.py
@@ -240,7 +240,7 @@
             jax.ShapeDtypeStruct(shape, F32),
         ],
         scratch_shapes=[pltpu.VMEM((tokens, 256), BF16)],
-        compiler_params=params(60),
+        compiler_params=params(16),
         cost_estimate=cost(2 * ranks * CLUSTERS * SLOTS * tokens * 256, 16 << 20),
     )(target, first, first)
 
@@ -264,8 +264,8 @@
             pl.BlockSpec((1, some, 128), lambda j: (j, block, 0)),
         ],
         out_specs=pl.BlockSpec((CLUSTERS, SLOTS, 128), lambda j: (0, j, 0)),
-        out_shape=jax.ShapeDtypeStruct((CLUSTERS, ranks * SLOTS, 128), BF16),
-        compiler_params=params(24),
+        out_shape=pltpu.HBM((CLUSTERS, ranks * SLOTS, 128), BF16),
+        compiler_params=params(10),
         cost_estimate=cost(2 * ranks * CLUSTERS * SLOTS * some * 256, 6 << 20),
     )(target, first)
 
@@ -303,10 +303,10 @@
             pl.BlockSpec((step * PAIR, 128), lambda i: (i, 0)),
         ],
         out_shape=[
-            jax.ShapeDtypeStruct((groups, rows, rows), BF16),
+            pltpu.HBM((groups, rows, rows), BF16),
             jax.ShapeDtypeStruct((groups * PAIR, 128), F32),
         ],
-        compiler_params=params(24),
+        compiler_params=params(12),
         cost_estimate=cost(2 * groups * rows * rows * 256, 20 << 20, groups * rows * rows),
     )(q_rows, k_rows, at)
 
@@ -358,7 +358,7 @@
         out_specs=pl.BlockSpec((count, rows, 128), lambda i: (group(i), 0, 0)),
         out_shape=jax.ShapeDtypeStruct((groups, rows, 128), BF16),
         scratch_shapes=[pltpu.VMEM((CLUSTERS, ranks * SLOTS, 128), F32)],
-        compiler_params=params(24),
+        compiler_params=params(18),
         cost_estimate=cost(2 * ranks * CLUSTERS * SLOTS * rest * 256, 16 << 20),
     )(target, rows_v, part, weights)
 
@@ -370,76 +370,33 @@
     target = jnp.transpose(jnp.broadcast_to(target_ref[0], (128, tokens)))
     columns = lax.broadcasted_iota(jnp.int32, (tokens, slots), 1)
     picked = (columns == jnp.tile(target, (1, slots // 128))).astype(BF16)
-    out_ref[:tokens] = jnp.dot(picked, right, preferred_element_type=F32).astype(BF16)
+    out_ref[0, :tokens] = jnp.dot(picked, right, preferred_element_type=F32).astype(BF16)
     means = mean_ref[...]
     high = means.astype(BF16)
     count = means.shape[0]
-    out_ref[tokens : tokens + count] = high
-    out_ref[tokens + count :] = (means - high.astype(F32)).astype(BF16)
+    out_ref[0, tokens : tokens + count] = high
+    out_ref[0, tokens + count :] = (means - high.astype(F32)).astype(BF16)
 
 
 def unplace(who, target, mixed, means):
-    tokens = target.shape[2]
+    tokens, partners = target.shape[2], who.shape[0]
     count = CLUSTERS // target.shape[0]
     return pl.pallas_call(
         unplace_kernel,
         grid_spec=pltpu.PrefetchScalarGridSpec(
             num_scalar_prefetch=1,
-            grid=(1,),
+            grid=(partners,),
             in_specs=[
-                pl.BlockSpec((1, 1, tokens), lambda i, who: (who[0], 0, 0)),
-                pl.BlockSpec((CLUSTERS, SLOTS, 128), lambda i, who: (0, who[0], 0)),
-                pl.BlockSpec((count, 128), lambda i, who: (who[0], 0)),
+                pl.BlockSpec((1, 1, tokens), lambda i, who: (who[i], 0, 0)),
+                pl.BlockSpec((CLUSTERS, SLOTS, 128), lambda i, who: (0, who[i], 0)),
+                pl.BlockSpec((count, 128), lambda i, who: (who[i], 0)),
             ],
-            out_specs=pl.BlockSpec((tokens + 2 * count, 128), lambda i, who: (0, 0)),
+            out_specs=pl.BlockSpec((1, tokens + 2 * count, 128), lambda i, who: (i, 0, 0)),
         ),
-        out_shape=jax.ShapeDtypeStruct((tokens + 2 * count, 128), BF16),
-        compiler_params=params(24),
+        out_shape=jax.ShapeDtypeStruct((partners, tokens + 2 * count, 128), BF16),
+        compiler_params=params(12),
         cost_estimate=cost(1, 1),
     )(who, target, mixed, means)
-
-
-def project_kernel(lanes, has_total, *refs):
-    refs = refs[1:]
-    atts, ws = refs[:4], refs[4 : 4 + 4 * lanes]
-    out_ref = refs[-1]
-    left = jnp.concatenate([a[...] for a in atts], axis=1)
-    right = jnp.concatenate([w[...] for w in ws], axis=0)
-    total = jnp.dot(left, right, preferred_element_type=F32)
-    if has_total:
-        total = total + refs[4 + 4 * lanes][...]
-    out_ref[...] = total.astype(out_ref.dtype)
-
-
-def project(where, tokens, atts, weights, columns, total, dtype):
-    lanes = atts[0].shape[1] // 128
-    step = 512
-    cols = out_cols = weights[3].shape[1]
-    in_specs = [pl.BlockSpec((step, 128 * lanes), lambda i, w: (i, 0)) for _ in atts]
-    args = list(atts)
-    for part in range(4):
-        for lane in range(lanes):
-            in_specs.append(
-                pl.BlockSpec(
-                    (128, cols), lambda i, w, lane=lane, part=part: (w[lane], w[lanes + part])
-                )
-            )
-            args.append(weights[part])
-    if total is not None:
-        in_specs.append(pl.BlockSpec((step, out_cols), lambda i, w: (i, 0)))
-        args.append(total)
-    return pl.pallas_call(
-        functools.partial(project_kernel, lanes, total is not None),
-        grid_spec=pltpu.PrefetchScalarGridSpec(
-            num_scalar_prefetch=1,
-            grid=(tokens // step,),
-            in_specs=in_specs,
-            out_specs=pl.BlockSpec((step, out_cols), lambda i, w: (i, 0)),
-        ),
-        out_shape=jax.ShapeDtypeStruct((tokens, out_cols), dtype),
-        compiler_params=params(60),
-        cost_estimate=cost(2 * tokens * 512 * lanes * out_cols, 8 << 20),
-    )(jnp.stack(list(where) + list(columns)), *args)
 
 
 def head_body(queries, keys, values, cluster_of, slot_of, centroids, out_weight):
@@ -448,6 +405,7 @@
     mine = lax.axis_index("head")
     tokens = queries.shape[0]
     some = tokens // 2
+    near = ranks // 2
     cl_dev = CLUSTERS // ranks
     cap = ranks * SLOTS
     y, core = mine // 2, mine % 2
@@ -457,13 +415,14 @@
 
     def swap_core(x):
         return lax.ppermute(x, "head", [(0, 1), (1, 0), (2, 3), (3, 2)])
+
+    def after(x, *others):
+        return lax.optimization_barrier((x, others))[0]
 
     marks = [x.astype(BF16).reshape(ranks, tokens // 128, 128) for x in (cluster_of, slot_of)]
     marks = jnp.concatenate(marks, axis=1)
     first = pack_first(queries, keys, values, marks, some)
     first = lax.all_to_all(first, "ctx", split_axis=0, concat_axis=0, tiled=True)
-    rows_v, first = lax.optimization_barrier((pack_rest(values, ranks, some), first))
-    rows_v = lax.all_to_all(rows_v, "ctx", split_axis=0, concat_axis=0, tiled=True)
 
     cols = out_weight.shape[1] // 4
     across = swap_y(lax.dynamic_slice_in_dim(out_weight, (1 - y) * 2 * cols, 2 * cols, 1))
@@ -471,8 +430,20 @@
         lax.dynamic_slice_in_dim(out_weight, (2 * y + 1 - core) * cols, cols, 1)
     )
     corner = swap_core(lax.dynamic_slice_in_dim(across, (1 - core) * cols, cols, 1))
-    w_parts = (out_weight, across, beside, corner)
-    w_columns = (mine, core, jnp.zeros_like(core), jnp.zeros_like(core))
+    w_parts = ((out_weight, mine * cols), (across, core * cols), (beside, 0), (corner, 0))
+
+    def w_rows(*lanes):
+        picked = [
+            lax.dynamic_slice(w, ((me ^ d) * 128, column), (128, cols))
+            for w, column in w_parts
+            for d in lanes
+        ]
+        return jnp.concatenate(picked, axis=0)
+
+    w_first, w_second, w_third = w_rows(0, 1, 2, 3), w_rows(4, 5), w_rows(6, 7)
+
+    rows_v = after(pack_rest(values, ranks, some), first, w_first, w_second, w_third)
+    rows_v = lax.all_to_all(rows_v, "ctx", split_axis=0, concat_axis=0, tiled=True)
 
     marks = first[:, 2 * tokens + some :, :].astype(jnp.int32)
     target = marks[:, : tokens // 128, :] * SLOTS + marks[:, tokens // 128 :, :]
@@ -484,40 +455,73 @@
 
     weights, means = weigh(paired(q_rows), paired(k_rows), paired(at))
     part = place_some(target, first, tokens, some)
-    rows_v, w_parts = lax.optimization_barrier((rows_v, w_parts))
+    part, weights = (pltpu.with_memory_space_constraint(x, pltpu.HBM) for x in (part, weights))
     mixed = mix(target, rows_v, part, weights).reshape(CLUSTERS, cap, 128)
 
     got = {}
-    after = {6: 4, 7: 5}
-    for d in (4, 5, 1, 2, 3, 0, 6, 7):
-        who = jnp.reshape(me ^ d, (1,))
-        if d in after:
-            who, got[after[d]] = lax.optimization_barrier((who, got[after[d]]))
-        block = unplace(who, target, mixed, means)
-        got[d] = block
-        if d:
-            got[d] = lax.ppermute(block, "ctx", [(i, i ^ d) for i in range(ranks)])
-
-    total = None
-    splits = ((0, 1, 2, 3), (4, 5), (6,), (7,))
-    for lanes in splits:
-        own = got[lanes[0]]
-        if len(lanes) > 1:
-            own = jnp.concatenate([got[d][:tokens] for d in lanes], axis=1)
-        there = swap_y(own)
-        atts = (own, there, swap_core(own), swap_core(there))
-        last = lanes == splits[-1]
-        total = project(
-            [me ^ d for d in lanes], tokens, atts, w_parts, w_columns, total, BF16 if last else F32
-        )
-
-    sent = jnp.stack([got[d][tokens:] for d in range(ranks)]).astype(F32)
-    sent = sent[:, :cl_dev] + sent[:, cl_dev:]
-    sent = jnp.concatenate(
-        [lax.dynamic_slice_in_dim(sent, me ^ d, 1, 0) for d in range(ranks)], axis=0
-    )
+    previous = mixed
+    base = me // near * near
+
+    def far(d):
+        block = unplace(after(jnp.reshape(me ^ d, (1,)), previous), target, mixed, means)
+        block = block.reshape(block.shape[1:])
+        got[d] = lax.ppermute(block, "ctx", [(i, i ^ d) for i in range(ranks)])
+        return block
+
+    previous = far(4)
+    previous = far(5)
+    close = after(base + jnp.arange(near, dtype=jnp.int32), previous)
+    close = unplace(close, target, mixed, means)
+    previous = close
+    own_0 = lax.dynamic_index_in_dim(close, me % near, 0, False)[:tokens]
+    halves = [list(range(h * near, (h + 1) * near)) for h in range(2)]
+    close = lax.all_to_all(
+        close, "ctx", split_axis=0, concat_axis=0, axis_index_groups=halves, tiled=True
+    )
+    y_0 = swap_y(own_0)
+
+    def side(*blocks):
+        return jnp.concatenate([block[:tokens] for block in blocks], axis=1)
+
+    own_123 = side(
+        *[lax.dynamic_index_in_dim(close, (me % near) ^ d, 0, False) for d in (1, 2, 3)]
+    )
+    y_123 = swap_y(own_123)
+    previous = own_123
+    previous = far(6)
+    far(7)
+    own_45 = side(got[4], got[5])
+    y_45 = swap_y(after(own_45, own_123))
+    core_a = swap_core(side(own_0, own_123, y_0))
+    own_67 = side(got[6], got[7])
+    y_67 = swap_y(own_67)
+    core_67 = swap_core(own_67)
+    core_b = swap_core(y_123)
+
+    def dot(left, right):
+        return jnp.dot(left, right, preferred_element_type=F32)
+
+    total = dot(side(own_0, own_123, y_0, y_123, core_a, core_b), w_first)
+    more_45 = side(own_45, y_45)
+    total = total + dot(side(more_45, swap_core(more_45)), w_second)
+    most = 6 * 128
+    total = total + dot(side(own_67, y_67, core_67), w_third[:most])
+    total = total + dot(swap_core(y_67), w_third[most:])
+    projected = total.astype(BF16)
+
+    def tails(blocks):
+        sent = blocks[:, tokens:].astype(F32)
+        return sent[:, :cl_dev] + sent[:, cl_dev:]
+
+    other = tails(jnp.stack([got[d] for d in (4, 5, 6, 7)]))
+    other = jnp.concatenate(
+        [lax.dynamic_slice_in_dim(other, (me % near) ^ j, 1, 0) for j in range(near)], axis=0
+    )
+    this = tails(close)
+    low = base == 0
+    sent = jnp.concatenate([jnp.where(low, this, other), jnp.where(low, other, this)], axis=0)
     new_centroids = mix_rate * centroids + (1.0 - mix_rate) * sent
-    return (total, new_centroids)
+    return (projected, new_centroids)
 
 
 def dispatch(queries, keys, values, cluster_of, *rest):

time: 320 us -> 314 us (0.981)
  the two profiles are of different devices: /device:TPU:0 before, /device:TPU:9 now
where the time goes in v4:
time: 314 us; the launch traced here: 312 us
  waiting for transfers between devices  134 us (43%)
  Pallas kernels  78.8 us (25%)
  local copies, waits for them, and re-layouts  46.2 us (15%)
  starting transfers between devices  33.5 us (11%)
  matrix products  14.1 us (4%)
  other arithmetic  4.76 us (2%)
    ppermute x5, waiting for transfers between devices, swap_y(): return lax.ppermute(x, 'head', [(0, 2), (1, 3), (2, 0), (3, 1)])  96.8 us
    ppermute x4, waiting for transfers between devices, far(): got[d] = lax.ppermute(block, 'ctx', [(i, i ^ d) for i in range(ranks)])  37.2 us
    unnamed x41, local copies, waits for them, and re-layouts  32.9 us
    pallas_call x1, Pallas kernels, place_pair(): pl.pallas_call(place_pair_kernel, grid=(ranks,), in_specs=[pl.BlockSpec((...  19.3 us
    pallas_call x1, Pallas kernels, mix(): pl.pallas_call(functools.partial(mix_kernel, ranks), grid=(2 * ranks,), i...  14.1 us
    dot_general x4, matrix products, dot(): return jnp.dot(left, right, preferred_element_type=F32)  14.1 us
    pallas_call x5, Pallas kernels, unplace(): pl.pallas_call(unplace_kernel, grid_spec=pltpu.PrefetchScalarGridSpec(num...  12.5 us
    pallas_call x1, Pallas kernels, weigh(): pl.pallas_call(weigh_kernel, grid=(groups // step,), in_specs=[spec, spec...  11.6 us
  transfers between devices with their start and end apart: 19, of which 5 were waited for; matrix products, arithmetic and copies ran while one was open for 19% of the time, Pallas kernels for 15%

profile of v4, /device:TPU:9, one launch (start us, length us, event | category | flops | bytes accessed | tf_op | source)
XLA Modules:
  0.0 312.3 jit_solution(1534217283000997983)
XLA Ops:
  2.8 7.4 %shard_map.86 = bf16[8,2576,128]{2,1,0:T(8,128)(2,1)} custom-call(bf16[1024,1024]{1,0:T(8,128)(2,1)} %q_ref.1, bf16[1024,1024]{1,0:T(8,128)(2,1)} %k_ref.1, bf16[1024,1024]{1,0:T(8,128)(2,1)} %v_ref.3, bf16[8,16,128]{2,1,0:T(8,128)(2,1)} %pad_maximum_fusion.8.marks_ref), custom_call_target="tpu_custom_call" | custom-call | bytes 10551296 | tf_op jit(solution)/shard_map/pallas_call | solution.py:159
  10.2 5.7 %all-to-all-start = ((bf16[8,2576,128]{2,1,0:T(8,128)(2,1)}), bf16[8,2576,128]{2,1,0:T(8,128)(2,1)}, u32[]{:S(2)}, u32[]{:S(2)}) async-start(bf16[8,2576,128]{2,1,0:T(8,128)(2,1)} %shard_map.86), calls=%async_computation | async-start | bytes 10551296 | tf_op jit(solution)/shard_map/all_to_all | solution.py:425
  15.8 4.7 %constant_dynamic-slice_fusion.8 = bf16[1024,2048]{1,0:T(8,128)(2,1)} fusion(bf16[1024,4096]{1,0:T(8,128)(2,1)} %param.13, s32[]{:T(128)S(6)} %select_n.145), kind=kLoop, calls=%fused_computation.99 | loop fusion | bytes 8388612 | tf_op jit(solution)/shard_map/dynamic_slice | solution.py:428
  21.8 3.1 %constant_dynamic-slice_fusion.7 = bf16[1024,1024]{1,0:T(8,128)(2,1)} fusion(bf16[1024,4096]{1,0:T(8,128)(2,1)} %param.13, s32[]{:T(128)S(6)} %select_n.148), kind=kLoop, calls=%fused_computation.98 | loop fusion | bytes 4194308 | tf_op jit(solution)/shard_map/dynamic_slice | solution.py:430
  26.5 85.2 %collective-permute-done = bf16[1024,2048]{1,0:T(8,128)(2,1)} collective-permute-done((bf16[1024,2048]{1,0:T(8,128)(2,1)}, bf16[1024,2048]{1,0:T(8,128)(2,1)}, u32[]{:S(2)}, u32[]{:S(2)}) %collective-permute-start) | collective-permute-done | bytes 4194336 | tf_op jit(solution)/shard_map/ppermute | solution.py:414
  111.7 3.1 constant_dynamic-slice_fusion.6
  117.0 5.2 %shard_map.87 = bf16[8,512,128]{2,1,0:T(8,128)(2,1)} custom-call(bf16[1024,1024]{1,0:T(8,128)(2,1)} %v_ref.3), custom_call_target="tpu_custom_call" | custom-call | bytes 2097152 | tf_op jit(solution)/shard_map/pallas_call | solution.py:181
  147.1 5.4 %all-to-all-start.1 = ((bf16[8,512,128]{2,1,0:T(8,128)(2,1)}), bf16[8,512,128]{2,1,0:T(8,128)(2,1)S(1)}, u32[]{:S(2)}, u32[]{:S(2)}) async-start(bf16[8,512,128]{2,1,0:T(8,128)(2,1)} %shard_map.87), calls=%async_computation.1 | async-start | bytes 2097152 | tf_op jit(solution)/shard_map/all_to_all | solution.py:446
  153.3 19.3 %shard_map.89 = (bf16[256,64,128]{2,1,0:T(8,128)(2,1)S(1)}, bf16[256,64,128]{2,1,0:T(8,128)(2,1)S(1)}, f32[256,64,128]{2,1,0:T(8,128)S(1)}) custom-call(s32[8,1,1024]{2,1,0:T(1,128)S(1)} %bitcast.50, bf16[8,2576,128]{2,1,0:T(8,128)(2,1)} %all-to-all-done.v_ref.q_ref.k_ref, bf16[8,2576,128]{2,1,0:T(8,128)(2,1)} %all-to-all-done.v_ref.q_ref.k_ref), custom_call_target="tpu_custom_call" | custom-call | flops 8589934592 | bytes 16777216 | tf_op jit(solution)/shard_map/pallas_call | solution.py:228
  172.7 11.6 %shard_map.90 = (bf16[128,128,128]{2,1,0:T(8,128)(2,1)}, f32[256,128]{1,0:T(8,128)S(1)}) custom-call(bf16[128,128,128]{2,1,0:T(8,128)(2,1)S(1)} %bitcast.48, bf16[128,128,128]{2,1,0:T(8,128)(2,1)S(1)} %bitcast.49, f32[128,128,128]{2,1,0:T(8,128)S(1)} %bitcast.47), custom_call_target="tpu_custom_call" | custom-call | flops 1073741824 | bytes 20971520 | tf_op jit(solution)/shard_map/pallas_call | solution.py:297
  184.3 8.7 %shard_map.88.part_ref = bf16[256,64,128]{2,1,0:T(8,128)(2,1)} custom-call(s32[8,1,1024]{2,1,0:T(1,128)S(1)} %bitcast.51, bf16[8,2576,128]{2,1,0:T(8,128)(2,1)} %all-to-all-done.v_ref.q_ref.k_ref), custom_call_target="tpu_custom_call" | custom-call | flops 4294967296 | bytes 6291456 | tf_op jit(solution)/shard_map/pallas_call | solution.py:259
  192.9 14.1 %shard_map.91 = bf16[128,128,128]{2,1,0:T(8,128)(2,1)S(1)} custom-call(s32[8,1,1024]{2,1,0:T(1,128)S(1)} %bitcast.52, bf16[8,512,128]{2,1,0:T(8,128)(2,1)S(1)} %all-to-all-done.1.v_ref, bf16[256,64,128]{2,1,0:T(8,128)(2,1)} %shard_map.88.part_ref, bf16[128,128,128]{2,1,0:T(8,128)(2,1)} %get-tuple-element.18.w_ref), custom_call_target="tpu_custom_call" | custom-call | flops 4294967296 | bytes 16777216 | tf_op jit(solution)/shard_map/pallas_call | solution.py:349
  209.8 7.1 %shard_map.94 = bf16[4,1088,128]{2,1,0:T(8,128)(2,1)} custom-call(s32[4]{0:T(128)S(1)} %iota_add_fusion.who_ref, s32[8,1,1024]{2,1,0:T(1,128)S(1)} %bitcast.55, bf16[256,64,128]{2,1,0:T(8,128)(2,1)S(1)} %bitcast.44, f32[256,128]{1,0:T(8,128)S(1)} %get-tuple-element.20.mean_ref), custom_call_target="tpu_custom_call" | custom-call | flops 1 | bytes 1 | tf_op jit(solution)/shard_map/pallas_call | solution.py:384
  216.9 3.7 %all-to-all-start.2 = ((bf16[4,1088,128]{2,1,0:T(8,128)(2,1)}), bf16[4,1088,128]{2,1,0:T(8,128)(2,1)S(1)}, u32[]{:S(2)}, u32[]{:S(2)}) async-start(bf16[4,1088,128]{2,1,0:T(8,128)(2,1)} %shard_map.94), calls=%async_computation.2 | async-start | bytes 2228224 | tf_op jit(solution)/shard_map/all_to_all | solution.py:478
  220.6 3.1 collective-permute-start.8
  228.8 13.1 %collective-permute-done.8 = bf16[1088,128]{1,0:T(8,128)(2,1)S(1)} collective-permute-done((bf16[1088,128]{1,0:T(8,128)(2,1)S(1)}, bf16[1088,128]{1,0:T(8,128)(2,1)S(1)}, u32[]{:S(2)}, u32[]{:S(2)}) %collective-permute-start.8) | collective-permute-done | bytes 278560 | tf_op jit(solution)/shard_map/ppermute | solution.py:468
  241.9 5.1 %collective-permute-done.7 = bf16[1088,128]{1,0:T(8,128)(2,1)S(1)} collective-permute-done((bf16[1088,128]{1,0:T(8,128)(2,1)S(1)}, bf16[1088,128]{1,0:T(8,128)(2,1)S(1)}, u32[]{:S(2)}, u32[]{:S(2)}) %collective-permute-start.7) | collective-permute-done | bytes 278560 | tf_op jit(solution)/shard_map/ppermute | solution.py:468
  251.6 2.2 copy-done.1
  256.6 2.4 collective-permute-start.12
  260.4 2.5 collective-permute-start.5
  263.2 19.0 %collective-permute-done.12 = bf16[1088,128]{1,0:T(8,128)(2,1)S(1)} collective-permute-done((bf16[1088,128]{1,0:T(8,128)(2,1)S(1)}, bf16[1088,128]{1,0:T(8,128)(2,1)S(1)}, u32[]{:S(2)}, u32[]{:S(2)}) %collective-permute-start.12) | collective-permute-done | bytes 278560 | tf_op jit(solution)/shard_map/ppermute | solution.py:468
  285.2 11.6 %collective-permute-done.13 = bf16[1024,256]{1,0:T(8,128)(2,1)S(1)} collective-permute-done((bf16[1024,256]{1,0:T(8,128)(2,1)S(1)}, bf16[1024,256]{1,0:T(8,128)(2,1)S(1)}, u32[]{:S(2)}, u32[]{:S(2)}) %collective-permute-start.13) | collective-permute-done | bytes 524320 | tf_op jit(solution)/shard_map/ppermute | solution.py:414
  299.9 6.3 %fusion.26 = f32[1024,1024]{1,0:T(8,128)S(1)} fusion(bf16[1024,2048]{1,0:T(8,128)(2,1)S(1)} %constant_dynamic-update-slice_fusion.5, bf16[2048,1024]{1,0:T(8,128)(2,1)} %get-tuple-element.49), kind=kOutput, calls=%fused_computation.104 | convolution fusion | flops 4294967296 | bytes 12582912 | tf_op jit(solution)/shard_map/dot_general | solution.py:502
  306.3 3.9 %fusion = f32[1024,1024]{1,0:T(8,128)S(1)} fusion(bf16[1024,1024]{1,0:T(8,128)(2,1)} %get-tuple-element.48, bf16[1024,512]{1,0:T(8,128)(2,1)S(1)} %collective-permute-done.10, bf16[1024,256]{1,0:T(8,128)(2,1)S(1)} %collective-permute-done.9, bf16[1024,128]{1,0:T(8,128)(2,1)S(1)} %slice.92, bf16[1024,128]{1,0:T(8,128)(2,1)S(1)} %slice.91), kind=kOutput, calls=%fused_computation.1 | convolution fusion | flops 2155872256 | bytes 8388608 | tf_op jit(solution)/shard_map/dot_general | solution.py:502
  (97 shorter events, 57.9 us)
Async XLA Ops:
  10.2 137.0 %all-to-all-start = ((bf16[8,2576,128]{2,1,0:T(8,128)(2,1)}), bf16[8,2576,128]{2,1,0:T(8,128)(2,1)}, u32[]{:S(2)}, u32[]{:S(2)}) async-start(bf16[8,2576,128]{2,1,0:T(8,128)(2,1)} %shard_map.86), calls=%async_computation | async-start | bytes 10551296 | tf_op jit(solution)/shard_map/all_to_all | solution.py:425
  20.6 91.1 %collective-permute-start = (bf16[1024,2048]{1,0:T(8,128)(2,1)}, bf16[1024,2048]{1,0:T(8,128)(2,1)}, u32[]{:S(2)}, u32[]{:S(2)}) collective-permute-start(bf16[1024,2048]{1,0:T(8,128)(2,1)} %constant_dynamic-slice_fusion.8), channel_id=1, source_target_pairs={{0,2},{1,3},{2,0},{3,1},{4,6},{5,7},{6,4},{7,5},{8,10},{9,11},{10,... | collective-permute-start | bytes 12582920 | tf_op jit(solution)/shard_map/ppermute | solution.py:414
  25.0 111.6 %collective-permute-start.1 = (bf16[1024,1024]{1,0:T(8,128)(2,1)}, bf16[1024,1024]{1,0:T(8,128)(2,1)}, u32[]{:S(2)}, u32[]{:S(2)}) collective-permute-start(bf16[1024,1024]{1,0:T(8,128)(2,1)} %constant_dynamic-slice_fusion.7), channel_id=1, source_target_pairs={{0,1},{1,0},{2,3},{3,2},{4,5},{5,4},{6,7},{7,6},{8,9},{9,8},{10,11... | collective-permute-start | bytes 6291464 | tf_op jit(solution)/shard_map/ppermute | solution.py:417
  114.8 29.0 %collective-permute-start.2 = (bf16[1024,1024]{1,0:T(8,128)(2,1)}, bf16[1024,1024]{1,0:T(8,128)(2,1)S(1)}, u32[]{:S(2)}, u32[]{:S(2)}) collective-permute-start(bf16[1024,1024]{1,0:T(8,128)(2,1)} %constant_dynamic-slice_fusion.6), channel_id=1, source_target_pairs={{0,1},{1,0},{2,3},{3,2},{4,5},{5,4},{6,7},{7,6},{8,9},{9,8},{10,11... | collective-permute-start | bytes 6291464 | tf_op jit(solution)/shard_map/ppermute | solution.py:417
  147.1 45.8 %all-to-all-start.1 = ((bf16[8,512,128]{2,1,0:T(8,128)(2,1)}), bf16[8,512,128]{2,1,0:T(8,128)(2,1)S(1)}, u32[]{:S(2)}, u32[]{:S(2)}) async-start(bf16[8,512,128]{2,1,0:T(8,128)(2,1)} %shard_map.87), calls=%async_computation.1 | async-start | bytes 2097152 | tf_op jit(solution)/shard_map/all_to_all | solution.py:446
  216.9 30.9 %all-to-all-start.2 = ((bf16[4,1088,128]{2,1,0:T(8,128)(2,1)}), bf16[4,1088,128]{2,1,0:T(8,128)(2,1)S(1)}, u32[]{:S(2)}, u32[]{:S(2)}) async-start(bf16[4,1088,128]{2,1,0:T(8,128)(2,1)} %shard_map.94), calls=%async_computation.2 | async-start | bytes 2228224 | tf_op jit(solution)/shard_map/all_to_all | solution.py:478
  220.6 21.3 %collective-permute-start.8 = (bf16[1088,128]{1,0:T(8,128)(2,1)S(1)}, bf16[1088,128]{1,0:T(8,128)(2,1)S(1)}, u32[]{:S(2)}, u32[]{:S(2)}) collective-permute-start(bf16[1088,128]{1,0:T(8,128)(2,1)S(1)} %bitcast.59), channel_id=1, source_target_pairs={{0,20},{4,16},{8,28},{12,24},{16,4},{20,0},{24,12},{28,8},{1,21},{... | collective-permute-start | bytes 835592 | tf_op jit(solution)/shard_map/ppermute | solution.py:468
  223.7 23.3 %collective-permute-start.7 = (bf16[1088,128]{1,0:T(8,128)(2,1)S(1)}, bf16[1088,128]{1,0:T(8,128)(2,1)S(1)}, u32[]{:S(2)}, u32[]{:S(2)}) collective-permute-start(bf16[1088,128]{1,0:T(8,128)(2,1)S(1)} %bitcast.58), channel_id=1, source_target_pairs={{0,16},{4,20},{8,24},{12,28},{16,0},{20,4},{24,8},{28,12},{1,17},{... | collective-permute-start | bytes 835592 | tf_op jit(solution)/shard_map/ppermute | solution.py:468
  225.8 33.5 %collective-permute-start.3 = (bf16[1024,128]{1,0:T(8,128)(2,1)}, bf16[1024,128]{1,0:T(8,128)(2,1)}, u32[]{:S(2)}, u32[]{:S(2)}) collective-permute-start(bf16[1024,128]{1,0:T(8,128)(2,1)} %get-tuple-element.33), channel_id=1, source_target_pairs={{0,2},{1,3},{2,0},{3,1},{4,6},{5,7},{6,4},{7,5},{8,10},{9,11},{10,... | collective-permute-start | bytes 786440 | tf_op jit(solution)/shard_map/ppermute | solution.py:414
  250.3 34.0 %collective-permute-start.4 = (bf16[1024,384]{1,0:T(8,128)(2,1)S(1)}, bf16[1024,384]{1,0:T(8,128)(2,1)S(1)}, u32[]{:S(2)}, u32[]{:S(2)}) collective-permute-start(bf16[1024,384]{1,0:T(8,128)(2,1)S(1)} %pad_maximum_fusion.1), channel_id=1, source_target_pairs={{0,2},{1,3},{2,0},{3,1},{4,6},{5,7},{6,4},{7,5},{8,10},{9,11},{10,... | collective-permute-start | bytes 2359304 | tf_op jit(solution)/shard_map/ppermute | solution.py:414
  253.8 5.3 %copy-start.7 = (bf16[1024,2048]{1,0:T(8,128)(2,1)S(1)}, bf16[1024,2048]{1,0:T(8,128)(2,1)}, u32[]{:S(2)}) copy-start(bf16[1024,2048]{1,0:T(8,128)(2,1)} %constant_dynamic-update-slice_fusion.12) | copy-start | bytes 12582916
  255.1 4.2 %copy-start.4 = (bf16[1024,640]{1,0:T(8,128)(2,1)S(1)}, bf16[1024,640]{1,0:T(8,128)(2,1)}, u32[]{:S(2)}) copy-start(bf16[1024,640]{1,0:T(8,128)(2,1)} %get-tuple-element.26) | copy-start | bytes 3932164
  255.1 7.8 %copy-start.2 = (bf16[1024,256]{1,0:T(8,128)(2,1)S(1)}, bf16[1024,256]{1,0:T(8,128)(2,1)}, u32[]{:S(2)}) copy-start(bf16[1024,256]{1,0:T(8,128)(2,1)} %pad_maximum_fusion.2) | copy-start | bytes 1572868
  255.1 27.0 %collective-permute-start.11 = (bf16[1088,128]{1,0:T(8,128)(2,1)S(1)}, bf16[1088,128]{1,0:T(8,128)(2,1)S(1)}, u32[]{:S(2)}, u32[]{:S(2)}) collective-permute-start(bf16[1088,128]{1,0:T(8,128)(2,1)S(1)} %bitcast.60), channel_id=1, source_target_pairs={{0,24},{4,28},{8,16},{12,20},{16,8},{20,12},{24,0},{28,4},{1,25},{... | collective-permute-start | bytes 835592 | tf_op jit(solution)/shard_map/ppermute | solution.py:468
  256.6 27.0 %copy-start.3 = (f32[8,32,128]{2,1,0:T(8,128)S(1)}, f32[8,32,128]{2,1,0:T(8,128)}, u32[]{:S(2)}) copy-start(f32[8,32,128]{2,1,0:T(8,128)} %param.12) | copy-start | bytes 393220
  256.6 25.5 %collective-permute-start.12 = (bf16[1088,128]{1,0:T(8,128)(2,1)S(1)}, bf16[1088,128]{1,0:T(8,128)(2,1)S(1)}, u32[]{:S(2)}, u32[]{:S(2)}) collective-permute-start(bf16[1088,128]{1,0:T(8,128)(2,1)S(1)} %bitcast.61), channel_id=1, source_target_pairs={{0,28},{4,24},{8,20},{12,16},{16,12},{20,8},{24,4},{28,0},{1,29},{... | collective-permute-start | bytes 835592 | tf_op jit(solution)/shard_map/ppermute | solution.py:468
  260.4 37.2 %copy-start.6 = (bf16[768,1024]{1,0:T(8,128)(2,1)S(1)}, bf16[768,1024]{1,0:T(8,128)(2,1)}, u32[]{:S(2)}) copy-start(bf16[768,1024]{1,0:T(8,128)(2,1)} %copy-done.5) | copy-start | bytes 4718596
  260.4 39.0 %collective-permute-start.5 = (bf16[1024,640]{1,0:T(8,128)(2,1)S(1)}, bf16[1024,640]{1,0:T(8,128)(2,1)S(1)}, u32[]{:S(2)}, u32[]{:S(2)}) collective-permute-start(bf16[1024,640]{1,0:T(8,128)(2,1)S(1)} %get-tuple-element.58), channel_id=1, source_target_pairs={{0,1},{1,0},{2,3},{3,2},{4,5},{5,4},{6,7},{7,6},{8,9},{9,8},{10,11... | collective-permute-start | bytes 3932168 | tf_op jit(solution)/shard_map/ppermute | solution.py:417
  262.9 21.7 %collective-permute-start.9 = (bf16[1024,256]{1,0:T(8,128)(2,1)S(1)}, bf16[1024,256]{1,0:T(8,128)(2,1)S(1)}, u32[]{:S(2)}, u32[]{:S(2)}) collective-permute-start(bf16[1024,256]{1,0:T(8,128)(2,1)S(1)} %copy-done.2), channel_id=1, source_target_pairs={{0,2},{1,3},{2,0},{3,1},{4,6},{5,7},{6,4},{7,5},{8,10},{9,11},{10,... | collective-permute-start | bytes 1572872 | tf_op jit(solution)/shard_map/ppermute | solution.py:414
  282.2 15.4 %collective-permute-start.14 = (bf16[1024,256]{1,0:T(8,128)(2,1)S(1)}, bf16[1024,256]{1,0:T(8,128)(2,1)S(1)}, u32[]{:S(2)}, u32[]{:S(2)}) collective-permute-start(bf16[1024,256]{1,0:T(8,128)(2,1)S(1)} %pad_maximum_fusion.3), channel_id=1, source_target_pairs={{0,1},{1,0},{2,3},{3,2},{4,5},{5,4},{6,7},{7,6},{8,9},{9,8},{10,11... | collective-permute-start | bytes 1572872 | tf_op jit(solution)/shard_map/ppermute | solution.py:417
  283.3 13.5 %collective-permute-start.13 = (bf16[1024,256]{1,0:T(8,128)(2,1)S(1)}, bf16[1024,256]{1,0:T(8,128)(2,1)S(1)}, u32[]{:S(2)}, u32[]{:S(2)}) collective-permute-start(bf16[1024,256]{1,0:T(8,128)(2,1)S(1)} %pad_maximum_fusion.3), channel_id=1, source_target_pairs={{0,2},{1,3},{2,0},{3,1},{4,6},{5,7},{6,4},{7,5},{8,10},{9,11},{10,... | collective-permute-start | bytes 1572872 | tf_op jit(solution)/shard_map/ppermute | solution.py:414
  284.3 15.4 %collective-permute-start.6 = (bf16[1024,384]{1,0:T(8,128)(2,1)S(1)}, bf16[1024,384]{1,0:T(8,128)(2,1)S(1)}, u32[]{:S(2)}, u32[]{:S(2)}) collective-permute-start(bf16[1024,384]{1,0:T(8,128)(2,1)S(1)} %collective-permute-done.4), channel_id=1, source_target_pairs={{0,1},{1,0},{2,3},{3,2},{4,5},{5,4},{6,7},{7,6},{8,9},{9,8},{10,11... | collective-permute-start | bytes 2359304 | tf_op jit(solution)/shard_map/ppermute | solution.py:417
  284.7 21.5 %collective-permute-start.10 = (bf16[1024,512]{1,0:T(8,128)(2,1)S(1)}, bf16[1024,512]{1,0:T(8,128)(2,1)S(1)}, u32[]{:S(2)}, u32[]{:S(2)}) collective-permute-start(bf16[1024,512]{1,0:T(8,128)(2,1)S(1)} %pad_maximum_fusion), channel_id=1, source_target_pairs={{0,1},{1,0},{2,3},{3,2},{4,5},{5,4},{6,7},{7,6},{8,9},{9,8},{10,11... | collective-permute-start | bytes 3145736 | tf_op jit(solution)/shard_map/ppermute | solution.py:417
  296.8 13.4 %collective-permute-start.15 = (bf16[1024,256]{1,0:T(8,128)(2,1)S(1)}, bf16[1024,256]{1,0:T(8,128)(2,1)S(1)}, u32[]{:S(2)}, u32[]{:S(2)}) collective-permute-start(bf16[1024,256]{1,0:T(8,128)(2,1)S(1)} %collective-permute-done.13), channel_id=1, source_target_pairs={{0,1},{1,0},{2,3},{3,2},{4,5},{5,4},{6,7},{7,6},{8,9},{9,8},{10,11... | collective-permute-start | bytes 1572872 | tf_op jit(solution)/shard_map/ppermute | solution.py:417
  (3 other events, 7.3 us)

commit v5 on v4

--- a/solution.py
+++ b/solution.py
@@ -144,49 +144,80 @@
     )
 
 
-def pack_first_kernel(q_ref, k_ref, v_ref, marks_ref, out_ref):
-    tokens, some = q_ref.shape[0], v_ref.shape[0]
-    out_ref[0, :tokens] = q_ref[...]
-    out_ref[0, tokens : 2 * tokens] = k_ref[...]
-    out_ref[0, 2 * tokens : 2 * tokens + some] = v_ref[...]
-    out_ref[0, 2 * tokens + some :] = marks_ref[0]
-
-
-def pack_first(queries, keys, values, marks, some):
-    tokens, heads = queries.shape[0], marks.shape[0]
-    rows = 2 * tokens + some + marks.shape[1]
-    whole = pl.BlockSpec((tokens, 128), lambda j: (0, j))
-    return pl.pallas_call(
-        pack_first_kernel,
-        grid=(heads,),
-        in_specs=[
-            whole,
-            whole,
-            pl.BlockSpec((some, 128), lambda j: (0, j)),
-            pl.BlockSpec((1, marks.shape[1], 128), lambda j: (j, 0, 0)),
-        ],
-        out_specs=pl.BlockSpec((1, rows, 128), lambda j: (j, 0, 0)),
-        out_shape=jax.ShapeDtypeStruct((heads, rows, 128), BF16),
+def pack_kernel(steps, *refs):
+    out_ref = refs[-1]
+    i = pl.program_id(0)
+    for n, source in enumerate(refs[:-1]):
+
+        @pl.when(i // steps == n)
+        def _(source=source):
+            for j in range(out_ref.shape[0]):
+                out_ref[j] = source[:, j * 128 : (j + 1) * 128]
+
+
+def pack(sources):
+    tokens, width = sources[0].shape
+    heads, rows = width // 128, 256
+    steps = tokens // rows
+
+    def block(n):
+        return lambda i: (jnp.clip(i - n * steps, 0, steps - 1), 0)
+
+    total = len(sources) * tokens
+    return pl.pallas_call(
+        functools.partial(pack_kernel, steps),
+        grid=(len(sources) * steps,),
+        in_specs=[pl.BlockSpec((rows, width), block(n)) for n in range(len(sources))],
+        out_specs=pl.BlockSpec((heads, rows, 128), lambda i: (0, i, 0)),
+        out_shape=pltpu.HBM((heads, total, 128), BF16),
         compiler_params=params(60),
-        cost_estimate=cost(0, 2 * heads * rows * 256),
-    )(queries, keys, values, marks)
-
-
-def pack_rest_kernel(v_ref, out_ref):
-    out_ref[0] = v_ref[...]
-
-
-def pack_rest(values, heads, some):
-    rest = values.shape[0] - some
-    return pl.pallas_call(
-        pack_rest_kernel,
-        grid=(heads,),
-        in_specs=[pl.BlockSpec((rest, 128), lambda j: (1, j))],
-        out_specs=pl.BlockSpec((1, rest, 128), lambda j: (j, 0, 0)),
-        out_shape=jax.ShapeDtypeStruct((heads, rest, 128), BF16),
+        cost_estimate=cost(0, 2 * heads * total * 256),
+    )(*sources)
+
+
+def pick_kernel(where_ref, one_ref, two_ref, out_ref):
+    i = pl.program_id(0)
+    steps = pl.num_programs(0)
+
+    @pl.when(where_ref[2 * steps + i] == 0)
+    def _():
+        out_ref[...] = one_ref[...]
+
+    @pl.when(where_ref[2 * steps + i] == 1)
+    def _():
+        out_ref[...] = two_ref[...]
+
+
+def pick(heads, one, two, columns, groups, cols):
+    first, second, which = [], [], []
+    for group in groups:
+        first += list(group) + [group[-1]] * len(group)
+        second += [group[0]] * len(group) + list(group)
+        which += [0] * len(group) + [1] * len(group)
+    steps = len(which)
+    table = jnp.concatenate(
+        [
+            heads[jnp.array(first)],
+            heads[jnp.array(second)],
+            jnp.array(which, jnp.int32),
+            jnp.stack(columns),
+        ]
+    )
+    return pl.pallas_call(
+        pick_kernel,
+        grid_spec=pltpu.PrefetchScalarGridSpec(
+            num_scalar_prefetch=1,
+            grid=(steps,),
+            in_specs=[
+                pl.BlockSpec((128, cols), lambda i, w: (w[i], w[3 * steps])),
+                pl.BlockSpec((128, cols), lambda i, w: (w[steps + i], w[3 * steps + 1])),
+            ],
+            out_specs=pl.BlockSpec((128, cols), lambda i, w: (i, 0)),
+        ),
+        out_shape=pltpu.HBM((128 * steps, cols), BF16),
         compiler_params=params(60),
-        cost_estimate=cost(0, 2 * heads * rest * 256),
-    )(values)
+        cost_estimate=cost(1, 1),
+    )(table, one, two)
 
 
 def match(first, count, target):
@@ -198,24 +229,50 @@
     return x.reshape(x.shape[0] // SLOTS, SLOTS, 128)
 
 
-def place_pair_kernel(target_ref, q_ref, k_ref, q_out, k_out, p_out, right):
-    tokens = q_ref.shape[1]
+def positions_kernel(target_ref, p_out):
+    slots = p_out.shape[0] * SLOTS
+    tokens = target_ref.shape[2]
+    step = 512
+    base = pl.program_id(0) * tokens
+    token = (base + lax.broadcasted_iota(jnp.int32, (1, tokens), 1)).astype(F32)
+    target = target_ref[0]
+
+    def move(i, carry):
+        at = jnp.where(match(i * step, step, target), token, EMPTY)
+        at = jnp.min(at, axis=1, keepdims=True)
+        where = pl.ds(i * (step // SLOTS), step // SLOTS)
+        p_out[where] = by_slot(jnp.broadcast_to(at, (step, 128)))
+        return carry
+
+    lax.fori_loop(0, slots // step, move, 0)
+
+
+def positions(target):
+    ranks, tokens = target.shape[0], target.shape[2]
+    return pl.pallas_call(
+        positions_kernel,
+        grid=(ranks,),
+        in_specs=[pl.BlockSpec((1, 1, tokens), lambda j: (j, 0, 0))],
+        out_specs=pl.BlockSpec((CLUSTERS, SLOTS, 128), lambda j: (0, j, 0)),
+        out_shape=pltpu.HBM((CLUSTERS, ranks * SLOTS, 128), F32),
+        compiler_params=params(16),
+        cost_estimate=cost(1, 1),
+    )(target)
+
+
+def place_pair_kernel(target_ref, q_ref, k_ref, q_out, k_out, right):
     slots = q_out.shape[0] * SLOTS
     step = 1024
     right[:, :128] = q_ref[0]
     right[:, 128:] = k_ref[0]
-    base = pl.program_id(0) * tokens
-    token = (base + lax.broadcasted_iota(jnp.int32, (1, tokens), 1)).astype(F32)
     target = target_ref[0]
 
     def move(i, carry):
-        picked = match(i * step, step, target)
-        out = jnp.dot(picked.astype(BF16), right[...], preferred_element_type=F32)
+        picked = match(i * step, step, target).astype(BF16)
+        out = jnp.dot(picked, right[...], preferred_element_type=F32)
         where = pl.ds(i * (step // SLOTS), step // SLOTS)
         q_out[where] = by_slot(out[:, :128]).astype(BF16)
         k_out[where] = by_slot(out[:, 128:]).astype(BF16)
-        at = jnp.min(jnp.where(picked, token, EMPTY), axis=1, keepdims=True)
-        p_out[where] = by_slot(jnp.broadcast_to(at, (step, 128)))
         return carry
 
     lax.fori_loop(0, slots // step, move, 0)
@@ -233,41 +290,12 @@
             pl.BlockSpec((1, tokens, 128), lambda j: (j, 0, 0)),
             pl.BlockSpec((1, tokens, 128), lambda j: (j, 1, 0)),
         ],
-        out_specs=[spec_out, spec_out, spec_out],
-        out_shape=[
-            jax.ShapeDtypeStruct(shape, BF16),
-            jax.ShapeDtypeStruct(shape, BF16),
-            jax.ShapeDtypeStruct(shape, F32),
-        ],
+        out_specs=[spec_out, spec_out],
+        out_shape=[jax.ShapeDtypeStruct(shape, BF16), jax.ShapeDtypeStruct(shape, BF16)],
         scratch_shapes=[pltpu.VMEM((tokens, 256), BF16)],
         compiler_params=params(16),
-        cost_estimate=cost(2 * ranks * CLUSTERS * SLOTS * tokens * 256, 16 << 20),
+        cost_estimate=cost(1, 1),
     )(target, first, first)
-
-
-def place_some_kernel(target_ref, v_ref, v_out):
-    slots = v_out.shape[0] * SLOTS
-    some = v_ref.shape[1]
-    picked = match(0, slots, target_ref[0, :, :some]).astype(BF16)
-    out = jnp.dot(picked, v_ref[0], preferred_element_type=F32)
-    v_out[...] = by_slot(out).astype(BF16)
-
-
-def place_some(target, first, tokens, some):
-    ranks = first.shape[0]
-    block = 2 * tokens // some
-    return pl.pallas_call(
-        place_some_kernel,
-        grid=(ranks,),
-        in_specs=[
-            pl.BlockSpec((1, 1, tokens), lambda j: (j, 0, 0)),
-            pl.BlockSpec((1, some, 128), lambda j: (j, block, 0)),
-        ],
-        out_specs=pl.BlockSpec((CLUSTERS, SLOTS, 128), lambda j: (0, j, 0)),
-        out_shape=pltpu.HBM((CLUSTERS, ranks * SLOTS, 128), BF16),
-        compiler_params=params(10),
-        cost_estimate=cost(2 * ranks * CLUSTERS * SLOTS * some * 256, 6 << 20),
-    )(target, first)
 
 
 def weigh_kernel(q_ref, k_ref, p_ref, w_out, mean_out):
@@ -307,22 +335,21 @@
             jax.ShapeDtypeStruct((groups * PAIR, 128), F32),
         ],
         compiler_params=params(12),
-        cost_estimate=cost(2 * groups * rows * rows * 256, 20 << 20, groups * rows * rows),
+        cost_estimate=cost(1, 1),
     )(q_rows, k_rows, at)
 
 
-def mix_kernel(ranks, target_ref, v_ref, part_ref, w_ref, o_out, v_rows):
+def mix_kernel(ranks, target_ref, v_ref, w_ref, o_out, v_rows):
     i = pl.program_id(0)
-    slots = part_ref.shape[0] * SLOTS
+    slots = v_rows.shape[0] * SLOTS
     count, rows = w_ref.shape[0], w_ref.shape[1]
-    tokens, rest = target_ref.shape[2], v_ref.shape[1]
 
     @pl.when(i < ranks)
     def _():
-        picked = match(0, slots, target_ref[0, :, tokens - rest :]).astype(BF16)
+        picked = match(0, slots, target_ref[0]).astype(BF16)
         out = jnp.dot(picked, v_ref[0], preferred_element_type=F32)
         where = pl.ds(pl.multiple_of(i * SLOTS, SLOTS), SLOTS)
-        v_rows[:, where, :] = by_slot(out) + part_ref[...].astype(F32)
+        v_rows[:, where, :] = by_slot(out)
 
     @pl.when(i >= ranks)
     def _():
@@ -335,8 +362,8 @@
             o_out[n] = (out[:, :128] / jnp.where(total > 0.0, total, 1.0)).astype(BF16)
 
 
-def mix(target, rows_v, part, weights):
-    ranks, rest = rows_v.shape[0], rows_v.shape[1]
+def mix(target, rows_v, weights):
+    ranks, tokens = rows_v.shape[0], rows_v.shape[1]
     groups, rows = weights.shape[0], weights.shape[1]
     count = groups // ranks
 
@@ -350,17 +377,16 @@
         functools.partial(mix_kernel, ranks),
         grid=(2 * ranks,),
         in_specs=[
-            pl.BlockSpec((1, 1, target.shape[2]), lambda i: (sender(i), 0, 0)),
-            pl.BlockSpec((1, rest, 128), lambda i: (sender(i), 0, 0)),
-            pl.BlockSpec((CLUSTERS, SLOTS, 128), lambda i: (0, sender(i), 0)),
+            pl.BlockSpec((1, 1, tokens), lambda i: (sender(i), 0, 0)),
+            pl.BlockSpec((1, tokens, 128), lambda i: (sender(i), 0, 0)),
             pl.BlockSpec((count, rows, rows), lambda i: (group(i), 0, 0)),
         ],
         out_specs=pl.BlockSpec((count, rows, 128), lambda i: (group(i), 0, 0)),
         out_shape=jax.ShapeDtypeStruct((groups, rows, 128), BF16),
         scratch_shapes=[pltpu.VMEM((CLUSTERS, ranks * SLOTS, 128), F32)],
-        compiler_params=params(18),
-        cost_estimate=cost(2 * ranks * CLUSTERS * SLOTS * rest * 256, 16 << 20),
-    )(target, rows_v, part, weights)
+        compiler_params=params(20),
+        cost_estimate=cost(1, 1),
+    )(target, rows_v, weights)
 
 
 def unplace_kernel(who_ref, target_ref, o_ref, mean_ref, out_ref):
@@ -404,8 +430,6 @@
     me = lax.axis_index("ctx")
     mine = lax.axis_index("head")
     tokens = queries.shape[0]
-    some = tokens // 2
-    near = ranks // 2
     cl_dev = CLUSTERS // ranks
     cap = ranks * SLOTS
     y, core = mine // 2, mine % 2
@@ -419,108 +443,98 @@
     def after(x, *others):
         return lax.optimization_barrier((x, others))[0]
 
-    marks = [x.astype(BF16).reshape(ranks, tokens // 128, 128) for x in (cluster_of, slot_of)]
-    marks = jnp.concatenate(marks, axis=1)
-    first = pack_first(queries, keys, values, marks, some)
-    first = lax.all_to_all(first, "ctx", split_axis=0, concat_axis=0, tiled=True)
+    def swap_ctx(x, d):
+        return lax.ppermute(x, "ctx", [(i, i ^ d) for i in range(ranks)])
+
+    def exchange(x):
+        return lax.all_to_all(x, "ctx", split_axis=0, concat_axis=0, tiled=True)
+
+    places = lax.all_gather(cluster_of * SLOTS + slot_of, "ctx", axis=0, tiled=False)
+    target = lax.dynamic_index_in_dim(places, me, 1, True)
+    first = exchange(pack((queries, keys)))
+    at = positions(target)
 
     cols = out_weight.shape[1] // 4
+    heads = me ^ jnp.arange(ranks, dtype=jnp.int32)
     across = swap_y(lax.dynamic_slice_in_dim(out_weight, (1 - y) * 2 * cols, 2 * cols, 1))
     beside = swap_core(
         lax.dynamic_slice_in_dim(out_weight, (2 * y + 1 - core) * cols, cols, 1)
     )
     corner = swap_core(lax.dynamic_slice_in_dim(across, (1 - core) * cols, cols, 1))
-    w_parts = ((out_weight, mine * cols), (across, core * cols), (beside, 0), (corner, 0))
-
-    def w_rows(*lanes):
-        picked = [
-            lax.dynamic_slice(w, ((me ^ d) * 128, column), (128, cols))
-            for w, column in w_parts
-            for d in lanes
-        ]
-        return jnp.concatenate(picked, axis=0)
-
-    w_first, w_second, w_third = w_rows(0, 1, 2, 3), w_rows(4, 5), w_rows(6, 7)
-
-    rows_v = after(pack_rest(values, ranks, some), first, w_first, w_second, w_third)
-    rows_v = lax.all_to_all(rows_v, "ctx", split_axis=0, concat_axis=0, tiled=True)
-
-    marks = first[:, 2 * tokens + some :, :].astype(jnp.int32)
-    target = marks[:, : tokens // 128, :] * SLOTS + marks[:, tokens // 128 :, :]
-    target = target.reshape(ranks, 1, tokens)
-    q_rows, k_rows, at = place_pair(target, first, tokens)
+    groups = ((0, 1, 2, 3), (4, 5), (6, 7))
+    w_same = pick(heads, out_weight, across, (mine, core), groups, cols)
+    w_core = pick(heads, beside, corner, (0 * core, 0 * core), groups, cols)
+
+    rows_v = exchange(after(pack((values,)), first, at))
 
     def paired(x):
         return x.reshape(CLUSTERS // PAIR, PAIR * cap, 128)
 
-    weights, means = weigh(paired(q_rows), paired(k_rows), paired(at))
-    part = place_some(target, first, tokens, some)
-    part, weights = (pltpu.with_memory_space_constraint(x, pltpu.HBM) for x in (part, weights))
-    mixed = mix(target, rows_v, part, weights).reshape(CLUSTERS, cap, 128)
-
-    got = {}
-    previous = mixed
-    base = me // near * near
-
-    def far(d):
-        block = unplace(after(jnp.reshape(me ^ d, (1,)), previous), target, mixed, means)
-        block = block.reshape(block.shape[1:])
-        got[d] = lax.ppermute(block, "ctx", [(i, i ^ d) for i in range(ranks)])
-        return block
-
-    previous = far(4)
-    previous = far(5)
-    close = after(base + jnp.arange(near, dtype=jnp.int32), previous)
-    close = unplace(close, target, mixed, means)
-    previous = close
-    own_0 = lax.dynamic_index_in_dim(close, me % near, 0, False)[:tokens]
-    halves = [list(range(h * near, (h + 1) * near)) for h in range(2)]
-    close = lax.all_to_all(
-        close, "ctx", split_axis=0, concat_axis=0, axis_index_groups=halves, tiled=True
-    )
-    y_0 = swap_y(own_0)
+    q_rows, k_rows = place_pair(target, first, tokens)
+    at = pltpu.with_memory_space_constraint(paired(at), pltpu.HBM)
+    weights, means = weigh(paired(q_rows), paired(k_rows), at)
+    weights = pltpu.with_memory_space_constraint(weights, pltpu.HBM)
+    rows_v = after(rows_v, w_same, w_core)
+    mixed = mix(target, rows_v, weights).reshape(CLUSTERS, cap, 128)
+
+    got, sent = {}, {}
+
+    def leave(d, *others):
+        block = unplace(after(jnp.reshape(me ^ d, (1,)), *others), target, mixed, means)
+        sent[d] = block.reshape(block.shape[1:])
+
+    def go(d):
+        got[d] = swap_ctx(sent[d], d)
 
     def side(*blocks):
         return jnp.concatenate([block[:tokens] for block in blocks], axis=1)
 
-    own_123 = side(
-        *[lax.dynamic_index_in_dim(close, (me % near) ^ d, 0, False) for d in (1, 2, 3)]
-    )
+    leave(4)
+    go(4)
+    leave(5, sent[4])
+    go(5)
+    leave(0, sent[5])
+    got[0] = sent[0]
+    y_0 = swap_y(got[0])
+    leave(1, sent[0])
+    go(1)
+    leave(2, sent[1])
+    go(2)
+    leave(3, sent[2], y_0)
+    go(3)
+    leave(6, sent[3], got[4])
+    go(6)
+    own_123 = side(*[got[d] for d in (1, 2, 3)])
+    leave(7, sent[6], got[5], own_123)
+    go(7)
+    own, there = {}, {}
     y_123 = swap_y(own_123)
-    previous = own_123
-    previous = far(6)
-    far(7)
-    own_45 = side(got[4], got[5])
-    y_45 = swap_y(after(own_45, own_123))
-    core_a = swap_core(side(own_0, own_123, y_0))
-    own_67 = side(got[6], got[7])
-    y_67 = swap_y(own_67)
-    core_67 = swap_core(own_67)
-    core_b = swap_core(y_123)
-
-    def dot(left, right):
-        return jnp.dot(left, right, preferred_element_type=F32)
-
-    total = dot(side(own_0, own_123, y_0, y_123, core_a, core_b), w_first)
-    more_45 = side(own_45, y_45)
-    total = total + dot(side(more_45, swap_core(more_45)), w_second)
-    most = 6 * 128
-    total = total + dot(side(own_67, y_67, core_67), w_third[:most])
-    total = total + dot(swap_core(y_67), w_third[most:])
-    projected = total.astype(BF16)
-
-    def tails(blocks):
-        sent = blocks[:, tokens:].astype(F32)
-        return sent[:, :cl_dev] + sent[:, cl_dev:]
-
-    other = tails(jnp.stack([got[d] for d in (4, 5, 6, 7)]))
-    other = jnp.concatenate(
-        [lax.dynamic_slice_in_dim(other, (me % near) ^ j, 1, 0) for j in range(near)], axis=0
-    )
-    this = tails(close)
-    low = base == 0
-    sent = jnp.concatenate([jnp.where(low, this, other), jnp.where(low, other, this)], axis=0)
-    new_centroids = mix_rate * centroids + (1.0 - mix_rate) * sent
+    own[2] = side(got[4], got[5])
+    there[2] = swap_y(own[2])
+    own[3] = side(got[6], got[7])
+    there[3] = swap_y(own[3])
+    same = {1: side(got[0], own_123, y_0, y_123), 2: side(own[2], there[2])}
+
+    def add(total, left, weight, row):
+        more = jnp.dot(left, weight[row : row + left.shape[1]], preferred_element_type=F32)
+        return more if total is None else total + more
+
+    total = None
+    for n, row in ((1, 0), (2, 1024)):
+        total = add(total, same[n], w_same, row)
+        total = add(total, swap_core(same[n]), w_core, row)
+    row = 1536
+    total = add(total, swap_core(own[3]), w_core, row)
+    last = swap_core(after(there[3], total))
+    total = add(total, side(own[3], there[3]), w_same, row)
+    projected = add(total, last, w_core, row + 256).astype(BF16)
+
+    tails = jnp.stack([got[d][tokens:] for d in range(ranks)]).astype(F32)
+    tails = tails[:, :cl_dev] + tails[:, cl_dev:]
+    tails = jnp.concatenate(
+        [lax.dynamic_slice_in_dim(tails, me ^ d, 1, 0) for d in range(ranks)], axis=0
+    )
+    new_centroids = mix_rate * centroids + (1.0 - mix_rate) * tails
     return (projected, new_centroids)
 
 

time: 314 us -> 307 us (0.978)
  the two profiles are of different devices: /device:TPU:9 before, /device:TPU:0 now
where the time goes in v5:
time: 307 us; the launch traced here: 305 us
  blocking collectives  107 us (35%)
  Pallas kernels  103 us (34%)
  starting transfers between devices  33.9 us (11%)
  waiting for transfers between devices  32 us (10%)
  local copies, waits for them, and re-layouts  14 us (5%)
  matrix products  11.8 us (4%)
    all_gather x1, blocking collectives, head_body(): lax.all_gather(cluster_of * SLOTS + slot_of, 'ctx', axis=0, tiled=False)  107 us
    ppermute x7, waiting for transfers between devices, swap_ctx(): return lax.ppermute(x, 'ctx', [(i, i ^ d) for i in range(ranks)])  22.7 us
    pallas_call x2, Pallas kernels, pick(): pl.pallas_call(pick_kernel, grid_spec=pltpu.PrefetchScalarGridSpec(num_sc...  22.5 us
    pallas_call x1, Pallas kernels, mix(): pl.pallas_call(functools.partial(mix_kernel, ranks), grid=(2 * ranks,), i...  17.4 us
    pallas_call x1, Pallas kernels, place_pair(): pl.pallas_call(place_pair_kernel, grid=(ranks,), in_specs=[pl.BlockSpec((...  15.6 us
    pallas_call x1, Pallas kernels, weigh(): pl.pallas_call(weigh_kernel, grid=(groups // step,), in_specs=[spec, spec...  15.5 us
    ppermute x7, starting transfers between devices, swap_ctx(): return lax.ppermute(x, 'ctx', [(i, i ^ d) for i in range(ranks)])  15.5 us
    dot_general x7, matrix products, add(): jnp.dot(left, weight[row:row + left.shape[1]], preferred_element_type=F32)  11.8 us
  transfers between devices with their start and end apart: 20, of which 9 were waited for; matrix products, arithmetic and copies ran while one was open for 8% of the time, Pallas kernels for 25%

profile of v5, /device:TPU:0, one launch (start us, length us, event | category | flops | bytes accessed | tf_op | source)
XLA Modules:
  0.0 305.4 jit_solution(3506235320526759552)
XLA Ops:
  0.6 7.1 %shard_map.141 = bf16[8,2048,128]{2,1,0:T(8,128)(2,1)} custom-call(bf16[1024,1024]{1,0:T(8,128)(2,1)} %refs_0_.3, bf16[1024,1024]{1,0:T(8,128)(2,1)} %refs_1_.1), custom_call_target="tpu_custom_call" | custom-call | bytes 8388608 | tf_op jit(solution)/shard_map/pallas_call | solution.py:167
  7.7 7.3 %all-to-all-start = ((bf16[8,2048,128]{2,1,0:T(8,128)(2,1)}), bf16[8,2048,128]{2,1,0:T(8,128)(2,1)}, u32[]{:S(2)}, u32[]{:S(2)}) async-start(bf16[8,2048,128]{2,1,0:T(8,128)(2,1)} %shard_map.141), calls=%async_computation | async-start | bytes 8388608 | tf_op jit(solution)/shard_map/all_to_all | solution.py:450
  15.0 4.8 %constant_dynamic-slice_fusion.2 = bf16[1024,2048]{1,0:T(8,128)(2,1)} fusion(bf16[1024,4096]{1,0:T(8,128)(2,1)} %one_ref.1, s32[]{:T(128)S(6)} %select_n.63), kind=kLoop, calls=%fused_computation.64 | loop fusion | bytes 8388612 | tf_op jit(solution)/shard_map/dynamic_slice | solution.py:459
  21.3 107.3 %all-gather = s32[64,1024]{1,0:T(8,128)S(1)} all-gather(s32[8,1024]{1,0:T(8,128)S(1)} %multiply_add_fusion), channel_id=2, replica_groups=mesh['ctx'=8,'head'=4] {'ctx'}, dimensions={0}, use_global_device_ids=true | all-gather | bytes 294912 | tf_op jit(solution)/shard_map/all_gather | solution.py:452
  128.7 10.4 %shard_map.142 = f32[256,64,128]{2,1,0:T(8,128)} custom-call(s32[8,1,1024]{2,1,0:T(1,128)S(1)} %constant_dynamic-slice_fusion.3.target_ref), custom_call_target="tpu_custom_call" | custom-call | flops 1 | bytes 1 | tf_op jit(solution)/shard_map/pallas_call | solution.py:252
  139.1 3.9 %shard_map.140 = bf16[8,1024,128]{2,1,0:T(8,128)(2,1)} custom-call(bf16[1024,1024]{1,0:T(8,128)(2,1)} %refs_0_.2), custom_call_target="tpu_custom_call" | custom-call | bytes 4194304 | tf_op jit(solution)/shard_map/pallas_call | solution.py:167
  143.0 3.8 %all-to-all-start.1 = ((bf16[8,1024,128]{2,1,0:T(8,128)(2,1)}), bf16[8,1024,128]{2,1,0:T(8,128)(2,1)S(1)}, u32[]{:S(2)}, u32[]{:S(2)}) async-start(bf16[8,1024,128]{2,1,0:T(8,128)(2,1)} %shard_map.140), calls=%async_computation.1 | async-start | bytes 4194304 | tf_op jit(solution)/shard_map/all_to_all | solution.py:450
  146.8 3.2 %constant_dynamic-slice_fusion.1 = bf16[1024,1024]{1,0:T(8,128)(2,1)} fusion(bf16[1024,4096]{1,0:T(8,128)(2,1)} %one_ref.1, s32[]{:T(128)S(6)} %select_n.66), kind=kLoop, calls=%fused_computation.63 | loop fusion | bytes 4194308 | tf_op jit(solution)/shard_map/dynamic_slice | solution.py:461
  150.0 3.2 %constant_dynamic-slice_fusion = bf16[1024,1024]{1,0:T(8,128)(2,1)} fusion(bf16[1024,2048]{1,0:T(8,128)(2,1)} %collective-permute-done.two_ref, s32[]{:T(128)S(6)} %select_n.67), kind=kLoop, calls=%fused_computation.62 | loop fusion | bytes 4194308 | tf_op jit(solution)/shard_map/dynamic_slice | solution.py:463
  156.3 11.2 %shard_map.143 = bf16[2048,1024]{1,0:T(8,128)(2,1)} custom-call(s32[50]{0:T(128)} %concatenate.30.where_ref, bf16[1024,4096]{1,0:T(8,128)(2,1)} %one_ref.1, bf16[1024,2048]{1,0:T(8,128)(2,1)} %collective-permute-done.two_ref), custom_call_target="tpu_custom_call" | custom-call | flops 1 | bytes 1 | tf_op jit(solution)/shard_map/pallas_call | solution.py:206
  167.5 11.2 %shard_map.144 = bf16[2048,1024]{1,0:T(8,128)(2,1)} custom-call(s32[50]{0:T(128)} %pad_add_fusion.where_ref, bf16[1024,1024]{1,0:T(8,128)(2,1)} %collective-permute-done.1.one_ref, bf16[1024,1024]{1,0:T(8,128)(2,1)} %collective-permute-done.2.two_ref), custom_call_target="tpu_custom_call" | custom-call | flops 1 | bytes 1 | tf_op jit(solution)/shard_map/pallas_call | solution.py:206
  178.8 15.6 %shard_map.145 = (bf16[256,64,128]{2,1,0:T(8,128)(2,1)S(1)}, bf16[256,64,128]{2,1,0:T(8,128)(2,1)S(1)}) custom-call(s32[8,1,1024]{2,1,0:T(1,128)S(1)} %constant_dynamic-slice_fusion.3.target_ref, bf16[8,2048,128]{2,1,0:T(8,128)(2,1)} %all-to-all-done.q_ref.k_ref, bf16[8,2048,128]{2,1,0:T(8,128)(2,1)} %all-to-all-done.q_ref.k_ref), custom_call_target="tpu_custom_call" | custom-call | flops 1 | bytes 1 | tf_op jit(solution)/shard_map/pallas_call | solution.py:285
  194.4 15.5 %shard_map.146 = (bf16[128,128,128]{2,1,0:T(8,128)(2,1)}, f32[256,128]{1,0:T(8,128)S(1)}) custom-call(bf16[128,128,128]{2,1,0:T(8,128)(2,1)S(1)} %bitcast.68, bf16[128,128,128]{2,1,0:T(8,128)(2,1)S(1)} %bitcast.69, f32[128,128,128]{2,1,0:T(8,128)} %bitcast.78), custom_call_target="tpu_custom_call" | custom-call | flops 1 | bytes 1 | tf_op jit(solution)/shard_map/pallas_call | solution.py:325
  209.9 17.4 %shard_map.147 = bf16[128,128,128]{2,1,0:T(8,128)(2,1)S(1)} custom-call(s32[8,1,1024]{2,1,0:T(1,128)S(1)} %constant_dynamic-slice_fusion.3.target_ref, bf16[8,1024,128]{2,1,0:T(8,128)(2,1)S(1)} %all-to-all-done.1.v_ref, bf16[128,128,128]{2,1,0:T(8,128)(2,1)} %get-tuple-element.20.w_ref), custom_call_target="tpu_custom_call" | custom-call | flops 1 | bytes 1 | tf_op jit(solution)/shard_map/pallas_call | solution.py:376
  228.7 3.0 collective-permute-start.9
  246.9 4.3 %collective-permute-done.9 = bf16[1088,128]{1,0:T(8,128)(2,1)S(1)} collective-permute-done((bf16[1088,128]{1,0:T(8,128)(2,1)S(1)}, bf16[1088,128]{1,0:T(8,128)(2,1)S(1)}, u32[]{:S(2)}, u32[]{:S(2)}) %collective-permute-start.9) | collective-permute-done | bytes 278560 | tf_op jit(solution)/shard_map/ppermute | solution.py:447
  252.5 3.1 %collective-permute-start.13 = (bf16[1088,128]{1,0:T(8,128)(2,1)S(1)}, bf16[1088,128]{1,0:T(8,128)(2,1)S(1)}, u32[]{:S(2)}, u32[]{:S(2)}) collective-permute-start(bf16[1088,128]{1,0:T(8,128)(2,1)S(1)} %bitcast.71), channel_id=1, source_target_pairs={{0,24},{4,28},{8,16},{12,20},{16,8},{20,12},{24,0},{28,4},{1,25},{... | collective-permute-start | bytes 835592 | tf_op jit(solution)/shard_map/ppermute | solution.py:447
  255.6 3.8 %collective-permute-done.10 = bf16[1088,128]{1,0:T(8,128)(2,1)S(1)} collective-permute-done((bf16[1088,128]{1,0:T(8,128)(2,1)S(1)}, bf16[1088,128]{1,0:T(8,128)(2,1)S(1)}, u32[]{:S(2)}, u32[]{:S(2)}) %collective-permute-start.10) | collective-permute-done | bytes 278560 | tf_op jit(solution)/shard_map/ppermute | solution.py:447
  261.2 5.4 %collective-permute-done.4 = bf16[1088,128]{1,0:T(8,128)(2,1)S(1)} collective-permute-done((bf16[1088,128]{1,0:T(8,128)(2,1)S(1)}, bf16[1088,128]{1,0:T(8,128)(2,1)S(1)}, u32[]{:S(2)}, u32[]{:S(2)}) %collective-permute-start.4) | collective-permute-done | bytes 278560 | tf_op jit(solution)/shard_map/ppermute | solution.py:447
  266.8 5.4 %collective-permute-done.6 = bf16[1088,128]{1,0:T(8,128)(2,1)S(1)} collective-permute-done((bf16[1088,128]{1,0:T(8,128)(2,1)S(1)}, bf16[1088,128]{1,0:T(8,128)(2,1)S(1)}, u32[]{:S(2)}, u32[]{:S(2)}) %collective-permute-start.6) | collective-permute-done | bytes 278560 | tf_op jit(solution)/shard_map/ppermute | solution.py:447
  274.4 4.2 %collective-permute-start.14 = (bf16[1088,128]{1,0:T(8,128)(2,1)S(1)}, bf16[1088,128]{1,0:T(8,128)(2,1)S(1)}, u32[]{:S(2)}, u32[]{:S(2)}) collective-permute-start(bf16[1088,128]{1,0:T(8,128)(2,1)S(1)} %bitcast.76), channel_id=1, source_target_pairs={{0,28},{4,24},{8,20},{12,16},{16,12},{20,8},{24,4},{28,0},{1,29},{... | collective-permute-start | bytes 835592 | tf_op jit(solution)/shard_map/ppermute | solution.py:447
  280.2 3.7 %collective-permute-done.14 = bf16[1088,128]{1,0:T(8,128)(2,1)S(1)} collective-permute-done((bf16[1088,128]{1,0:T(8,128)(2,1)S(1)}, bf16[1088,128]{1,0:T(8,128)(2,1)S(1)}, u32[]{:S(2)}, u32[]{:S(2)}) %collective-permute-start.14) | collective-permute-done | bytes 278560 | tf_op jit(solution)/shard_map/ppermute | solution.py:447
  285.4 7.1 %collective-permute-done.7 = bf16[1024,384]{1,0:T(8,128)(2,1)S(1)} collective-permute-done((bf16[1024,384]{1,0:T(8,128)(2,1)S(1)}, bf16[1024,384]{1,0:T(8,128)(2,1)S(1)}, u32[]{:S(2)}, u32[]{:S(2)}) %collective-permute-start.7) | collective-permute-done | bytes 786464 | tf_op jit(solution)/shard_map/ppermute | solution.py:438
  293.3 2.3 fusion.2
  (101 shorter events, 40.0 us)
Async XLA Ops:
  7.7 135.3 %all-to-all-start = ((bf16[8,2048,128]{2,1,0:T(8,128)(2,1)}), bf16[8,2048,128]{2,1,0:T(8,128)(2,1)}, u32[]{:S(2)}, u32[]{:S(2)}) async-start(bf16[8,2048,128]{2,1,0:T(8,128)(2,1)} %shard_map.141), calls=%async_computation | async-start | bytes 8388608 | tf_op jit(solution)/shard_map/all_to_all | solution.py:450
  15.0 6.4 %copy-start.3 = (s32[8,1024]{1,0:T(8,128)S(1)}, s32[8,1024]{1,0:T(8,128)}, u32[]{:S(2)}) copy-start(s32[8,1024]{1,0:T(8,128)} %param.17) | copy-start | bytes 98308
  15.0 6.4 %copy-start.4 = (s32[8,1024]{1,0:T(8,128)S(1)}, s32[8,1024]{1,0:T(8,128)}, u32[]{:S(2)}) copy-start(s32[8,1024]{1,0:T(8,128)} %param.16) | copy-start | bytes 98308
  19.8 130.2 %collective-permute-start = (bf16[1024,2048]{1,0:T(8,128)(2,1)}, bf16[1024,2048]{1,0:T(8,128)(2,1)}, u32[]{:S(2)}, u32[]{:S(2)}) collective-permute-start(bf16[1024,2048]{1,0:T(8,128)(2,1)} %constant_dynamic-slice_fusion.2), channel_id=1, source_target_pairs={{0,2},{1,3},{2,0},{3,1},{4,6},{5,7},{6,4},{7,5},{8,10},{9,11},{10,... | collective-permute-start | bytes 12582920 | tf_op jit(solution)/shard_map/ppermute | solution.py:438
  143.0 66.9 %all-to-all-start.1 = ((bf16[8,1024,128]{2,1,0:T(8,128)(2,1)}), bf16[8,1024,128]{2,1,0:T(8,128)(2,1)S(1)}, u32[]{:S(2)}, u32[]{:S(2)}) async-start(bf16[8,1024,128]{2,1,0:T(8,128)(2,1)} %shard_map.140), calls=%async_computation.1 | async-start | bytes 4194304 | tf_op jit(solution)/shard_map/all_to_all | solution.py:450
  150.0 17.6 %collective-permute-start.1 = (bf16[1024,1024]{1,0:T(8,128)(2,1)}, bf16[1024,1024]{1,0:T(8,128)(2,1)}, u32[]{:S(2)}, u32[]{:S(2)}) collective-permute-start(bf16[1024,1024]{1,0:T(8,128)(2,1)} %constant_dynamic-slice_fusion.1), channel_id=1, source_target_pairs={{0,1},{1,0},{2,3},{3,2},{4,5},{5,4},{6,7},{7,6},{8,9},{9,8},{10,11... | collective-permute-start | bytes 6291464 | tf_op jit(solution)/shard_map/ppermute | solution.py:441
  150.0 5.1 %copy-start.5 = (s32[16]{0:T(128)S(1)}, s32[16]{0:T(128)}, u32[]{:S(2)}) copy-start(s32[16]{0:T(128)} %constant.72.clone) | copy-start | bytes 196
  153.2 14.4 %collective-permute-start.2 = (bf16[1024,1024]{1,0:T(8,128)(2,1)}, bf16[1024,1024]{1,0:T(8,128)(2,1)}, u32[]{:S(2)}, u32[]{:S(2)}) collective-permute-start(bf16[1024,1024]{1,0:T(8,128)(2,1)} %constant_dynamic-slice_fusion), channel_id=1, source_target_pairs={{0,1},{1,0},{2,3},{3,2},{4,5},{5,4},{6,7},{7,6},{8,9},{9,8},{10,11... | collective-permute-start | bytes 6291464 | tf_op jit(solution)/shard_map/ppermute | solution.py:441
  228.7 22.5 %collective-permute-start.9 = (bf16[1088,128]{1,0:T(8,128)(2,1)S(1)}, bf16[1088,128]{1,0:T(8,128)(2,1)S(1)}, u32[]{:S(2)}, u32[]{:S(2)}) collective-permute-start(bf16[1088,128]{1,0:T(8,128)(2,1)S(1)} %bitcast.77), channel_id=1, source_target_pairs={{0,16},{4,20},{8,24},{12,28},{16,0},{20,4},{24,8},{28,12},{1,17},{... | collective-permute-start | bytes 835592 | tf_op jit(solution)/shard_map/ppermute | solution.py:447
  233.0 26.4 %collective-permute-start.10 = (bf16[1088,128]{1,0:T(8,128)(2,1)S(1)}, bf16[1088,128]{1,0:T(8,128)(2,1)S(1)}, u32[]{:S(2)}, u32[]{:S(2)}) collective-permute-start(bf16[1088,128]{1,0:T(8,128)(2,1)S(1)} %bitcast.74), channel_id=1, source_target_pairs={{0,20},{4,16},{8,28},{12,24},{16,4},{20,0},{24,12},{28,8},{1,21},{... | collective-permute-start | bytes 835592 | tf_op jit(solution)/shard_map/ppermute | solution.py:447
  235.9 8.1 %collective-permute-start.5 = (bf16[1088,128]{1,0:T(8,128)(2,1)S(1)}, bf16[1088,128]{1,0:T(8,128)(2,1)S(1)}, u32[]{:S(2)}, u32[]{:S(2)}) collective-permute-start(bf16[1088,128]{1,0:T(8,128)(2,1)S(1)} %bitcast.70), channel_id=1, source_target_pairs={{0,2},{1,3},{2,0},{3,1},{4,6},{5,7},{6,4},{7,5},{8,10},{9,11},{10,... | collective-permute-start | bytes 835592 | tf_op jit(solution)/shard_map/ppermute | solution.py:438
  238.9 22.2 %collective-permute-start.3 = (bf16[1088,128]{1,0:T(8,128)(2,1)S(1)}, bf16[1088,128]{1,0:T(8,128)(2,1)S(1)}, u32[]{:S(2)}, u32[]{:S(2)}) collective-permute-start(bf16[1088,128]{1,0:T(8,128)(2,1)S(1)} %bitcast.75), channel_id=1, source_target_pairs={{0,4},{4,0},{8,12},{12,8},{16,20},{20,16},{24,28},{28,24},{1,5},{5... | collective-permute-start | bytes 835592 | tf_op jit(solution)/shard_map/ppermute | solution.py:447
  240.4 26.3 %collective-permute-start.4 = (bf16[1088,128]{1,0:T(8,128)(2,1)S(1)}, bf16[1088,128]{1,0:T(8,128)(2,1)S(1)}, u32[]{:S(2)}, u32[]{:S(2)}) collective-permute-start(bf16[1088,128]{1,0:T(8,128)(2,1)S(1)} %bitcast.72), channel_id=1, source_target_pairs={{0,8},{4,12},{8,0},{12,4},{16,24},{20,28},{24,16},{28,20},{1,9},{5... | collective-permute-start | bytes 835592 | tf_op jit(solution)/shard_map/ppermute | solution.py:447
  245.3 26.8 %collective-permute-start.6 = (bf16[1088,128]{1,0:T(8,128)(2,1)S(1)}, bf16[1088,128]{1,0:T(8,128)(2,1)S(1)}, u32[]{:S(2)}, u32[]{:S(2)}) collective-permute-start(bf16[1088,128]{1,0:T(8,128)(2,1)S(1)} %bitcast.73), channel_id=1, source_target_pairs={{0,12},{4,8},{8,4},{12,0},{16,28},{20,24},{24,20},{28,16},{1,13},{... | collective-permute-start | bytes 835592 | tf_op jit(solution)/shard_map/ppermute | solution.py:447
  252.5 26.1 %collective-permute-start.13 = (bf16[1088,128]{1,0:T(8,128)(2,1)S(1)}, bf16[1088,128]{1,0:T(8,128)(2,1)S(1)}, u32[]{:S(2)}, u32[]{:S(2)}) collective-permute-start(bf16[1088,128]{1,0:T(8,128)(2,1)S(1)} %bitcast.71), channel_id=1, source_target_pairs={{0,24},{4,28},{8,16},{12,20},{16,8},{20,12},{24,0},{28,4},{1,25},{... | collective-permute-start | bytes 835592 | tf_op jit(solution)/shard_map/ppermute | solution.py:447
  259.5 19.2 %collective-permute-start.11 = (bf16[1024,256]{1,0:T(8,128)(2,1)S(1)}, bf16[1024,256]{1,0:T(8,128)(2,1)S(1)}, u32[]{:S(2)}, u32[]{:S(2)}) collective-permute-start(bf16[1024,256]{1,0:T(8,128)(2,1)S(1)} %pad_maximum_fusion.2), channel_id=1, source_target_pairs={{0,2},{1,3},{2,0},{3,1},{4,6},{5,7},{6,4},{7,5},{8,10},{9,11},{10,... | collective-permute-start | bytes 1572872 | tf_op jit(solution)/shard_map/ppermute | solution.py:438
  272.4 20.1 %collective-permute-start.7 = (bf16[1024,384]{1,0:T(8,128)(2,1)S(1)}, bf16[1024,384]{1,0:T(8,128)(2,1)S(1)}, u32[]{:S(2)}, u32[]{:S(2)}) collective-permute-start(bf16[1024,384]{1,0:T(8,128)(2,1)S(1)} %pad_maximum_fusion.1), channel_id=1, source_target_pairs={{0,2},{1,3},{2,0},{3,1},{4,6},{5,7},{6,4},{7,5},{8,10},{9,11},{10,... | collective-permute-start | bytes 2359304 | tf_op jit(solution)/shard_map/ppermute | solution.py:438
  273.0 5.9 %copy-start.1 = (bf16[2048,1024]{1,0:T(8,128)(2,1)S(1)}, bf16[2048,1024]{1,0:T(8,128)(2,1)}, u32[]{:S(2)}) copy-start(bf16[2048,1024]{1,0:T(8,128)(2,1)} %shard_map.143) | copy-start | bytes 12582916
  274.4 9.6 %collective-permute-start.14 = (bf16[1088,128]{1,0:T(8,128)(2,1)S(1)}, bf16[1088,128]{1,0:T(8,128)(2,1)S(1)}, u32[]{:S(2)}, u32[]{:S(2)}) collective-permute-start(bf16[1088,128]{1,0:T(8,128)(2,1)S(1)} %bitcast.76), channel_id=1, source_target_pairs={{0,28},{4,24},{8,20},{12,16},{16,12},{20,8},{24,4},{28,0},{1,29},{... | collective-permute-start | bytes 835592 | tf_op jit(solution)/shard_map/ppermute | solution.py:447
  278.8 16.8 %collective-permute-start.12 = (bf16[1024,512]{1,0:T(8,128)(2,1)S(1)}, bf16[1024,512]{1,0:T(8,128)(2,1)S(1)}, u32[]{:S(2)}, u32[]{:S(2)}) collective-permute-start(bf16[1024,512]{1,0:T(8,128)(2,1)S(1)} %pad_maximum_fusion), channel_id=1, source_target_pairs={{0,1},{1,0},{2,3},{3,2},{4,5},{5,4},{6,7},{7,6},{8,9},{9,8},{10,11... | collective-permute-start | bytes 3145736 | tf_op jit(solution)/shard_map/ppermute | solution.py:441
  284.0 15.3 %collective-permute-start.15 = (bf16[1024,256]{1,0:T(8,128)(2,1)S(1)}, bf16[1024,256]{1,0:T(8,128)(2,1)S(1)}, u32[]{:S(2)}, u32[]{:S(2)}) collective-permute-start(bf16[1024,256]{1,0:T(8,128)(2,1)S(1)} %pad_maximum_fusion.3), channel_id=1, source_target_pairs={{0,1},{1,0},{2,3},{3,2},{4,5},{5,4},{6,7},{7,6},{8,9},{9,8},{10,11... | collective-permute-start | bytes 1572872 | tf_op jit(solution)/shard_map/ppermute | solution.py:441
  284.1 17.0 %collective-permute-start.16 = (bf16[1024,256]{1,0:T(8,128)(2,1)S(1)}, bf16[1024,256]{1,0:T(8,128)(2,1)S(1)}, u32[]{:S(2)}, u32[]{:S(2)}) collective-permute-start(bf16[1024,256]{1,0:T(8,128)(2,1)S(1)} %pad_maximum_fusion.3), channel_id=1, source_target_pairs={{0,2},{1,3},{2,0},{3,1},{4,6},{5,7},{6,4},{7,5},{8,10},{9,11},{10,... | collective-permute-start | bytes 1572872 | tf_op jit(solution)/shard_map/ppermute | solution.py:438
  292.7 4.2 %collective-permute-start.8 = (bf16[1024,1024]{1,0:T(8,128)(2,1)S(1)}, bf16[1024,1024]{1,0:T(8,128)(2,1)S(1)}, u32[]{:S(2)}, u32[]{:S(2)}) collective-permute-start(bf16[1024,1024]{1,0:T(8,128)(2,1)S(1)} %constant_dynamic-update-slice_fusion), channel_id=1, source_target_pairs={{0,1},{1,0},{2,3},{3,2},{4,5},{5,4},{6,7},{7,6},{8,9},{9,8},{10,11... | collective-permute-start | bytes 6291464 | tf_op jit(solution)/shard_map/ppermute | solution.py:441
  301.1 1.9 collective-permute-start.17
  (4 other events, 11.6 us)

commit v6 on v5

--- a/solution.py
+++ b/solution.py
@@ -144,80 +144,105 @@
     )
 
 
-def pack_kernel(steps, *refs):
-    out_ref = refs[-1]
-    i = pl.program_id(0)
-    for n, source in enumerate(refs[:-1]):
-
-        @pl.when(i // steps == n)
-        def _(source=source):
-            for j in range(out_ref.shape[0]):
-                out_ref[j] = source[:, j * 128 : (j + 1) * 128]
-
-
-def pack(sources):
+def pack_kernel(count, marked, *refs):
+    sources = refs[:count]
+    out_ref, held, sems_in, sems_out = refs[count + marked :]
+    heads = out_ref.shape[0]
+    tokens = sources[0].shape[0]
+    parts = 2
+    rows = tokens // parts
+    reads = []
+    for n, source in enumerate(sources):
+        for p in range(parts):
+            here = pl.ds(p * rows, rows)
+            reads.append(
+                pltpu.make_async_copy(
+                    source.at[here], held.at[n, here], sems_in.at[n * parts + p]
+                )
+            )
+    for copy in reads:
+        copy.start()
+    writes = []
+    if marked:
+        marks_ref = refs[count]
+        there = out_ref.at[:, pl.ds(count * tokens, marks_ref.shape[1])]
+        writes.append(pltpu.make_async_copy(marks_ref, there, sems_out.at[0]))
+        writes[0].start()
+    for n in range(count):
+        for p in range(parts):
+            reads[n * parts + p].wait()
+            for j in range(heads):
+                copy = pltpu.make_async_copy(
+                    held.at[n, pl.ds(p * rows, rows), pl.ds(j * 128, 128)],
+                    out_ref.at[j, pl.ds(n * tokens + p * rows, rows)],
+                    sems_out.at[1 + (n * parts + p) * heads + j],
+                )
+                copy.start()
+                writes.append(copy)
+    for copy in writes:
+        copy.wait()
+
+
+def pack(sources, marks=None):
     tokens, width = sources[0].shape
-    heads, rows = width // 128, 256
-    steps = tokens // rows
-
-    def block(n):
-        return lambda i: (jnp.clip(i - n * steps, 0, steps - 1), 0)
-
-    total = len(sources) * tokens
+    heads, count = width // 128, len(sources)
+    marked = marks is not None
+    rows = count * tokens + (marks.shape[1] if marked else 0)
+    anywhere = pl.BlockSpec(memory_space=pl.ANY)
+    args = list(sources)
+    in_specs = [anywhere] * count
+    if marked:
+        args.append(marks)
+        in_specs.append(pl.BlockSpec(memory_space=pltpu.VMEM))
     return pl.pallas_call(
-        functools.partial(pack_kernel, steps),
-        grid=(len(sources) * steps,),
-        in_specs=[pl.BlockSpec((rows, width), block(n)) for n in range(len(sources))],
-        out_specs=pl.BlockSpec((heads, rows, 128), lambda i: (0, i, 0)),
-        out_shape=pltpu.HBM((heads, total, 128), BF16),
-        compiler_params=params(60),
-        cost_estimate=cost(0, 2 * heads * total * 256),
-    )(*sources)
-
-
-def pick_kernel(where_ref, one_ref, two_ref, out_ref):
-    i = pl.program_id(0)
-    steps = pl.num_programs(0)
-
-    @pl.when(where_ref[2 * steps + i] == 0)
-    def _():
-        out_ref[...] = one_ref[...]
-
-    @pl.when(where_ref[2 * steps + i] == 1)
-    def _():
-        out_ref[...] = two_ref[...]
-
-
-def pick(heads, one, two, columns, groups, cols):
-    first, second, which = [], [], []
-    for group in groups:
-        first += list(group) + [group[-1]] * len(group)
-        second += [group[0]] * len(group) + list(group)
-        which += [0] * len(group) + [1] * len(group)
-    steps = len(which)
-    table = jnp.concatenate(
-        [
-            heads[jnp.array(first)],
-            heads[jnp.array(second)],
-            jnp.array(which, jnp.int32),
-            jnp.stack(columns),
-        ]
-    )
+        functools.partial(pack_kernel, count, marked),
+        in_specs=in_specs,
+        out_specs=anywhere,
+        out_shape=pltpu.HBM((heads, rows, 128), BF16),
+        scratch_shapes=[
+            pltpu.VMEM((count, tokens, width), BF16),
+            pltpu.SemaphoreType.DMA((2 * count,)),
+            pltpu.SemaphoreType.DMA((2 * count * heads + 1,)),
+        ],
+        compiler_params=pltpu.CompilerParams(vmem_limit_bytes=60 * 1024 * 1024),
+        cost_estimate=cost(0, 2 * heads * rows * 256),
+    )(*args)
+
+
+def pick_kernel(plan, where_ref, *refs):
+    sources, out_ref, sems = refs[:-2], refs[-2], refs[-1]
+    count = where_ref.shape[0] - len(sources)
+    cols = out_ref.shape[1]
+    copies = []
+    for n, (part, lane) in enumerate(plan):
+        row = pl.multiple_of(where_ref[lane] * 128, 128)
+        column = pl.multiple_of(where_ref[count + part] * cols, cols)
+        copies.append(
+            pltpu.make_async_copy(
+                sources[part].at[pl.ds(row, 128), pl.ds(column, cols)],
+                out_ref.at[pl.ds(n * 128, 128)],
+                sems.at[n],
+            )
+        )
+    for copy in copies:
+        copy.start()
+    for copy in copies:
+        copy.wait()
+
+
+def pick(heads, weights, columns, groups, cols):
+    plan = [(part, d) for group in groups for part in range(len(weights)) for d in group]
+    where = jnp.concatenate([heads, jnp.stack(columns)])
     return pl.pallas_call(
-        pick_kernel,
-        grid_spec=pltpu.PrefetchScalarGridSpec(
-            num_scalar_prefetch=1,
-            grid=(steps,),
-            in_specs=[
-                pl.BlockSpec((128, cols), lambda i, w: (w[i], w[3 * steps])),
-                pl.BlockSpec((128, cols), lambda i, w: (w[steps + i], w[3 * steps + 1])),
-            ],
-            out_specs=pl.BlockSpec((128, cols), lambda i, w: (i, 0)),
-        ),
-        out_shape=pltpu.HBM((128 * steps, cols), BF16),
-        compiler_params=params(60),
+        functools.partial(pick_kernel, plan),
+        in_specs=[pl.BlockSpec(memory_space=pltpu.SMEM)]
+        + [pl.BlockSpec(memory_space=pl.ANY)] * len(weights),
+        out_specs=pl.BlockSpec(memory_space=pltpu.VMEM),
+        out_shape=jax.ShapeDtypeStruct((128 * len(plan), cols), BF16),
+        scratch_shapes=[pltpu.SemaphoreType.DMA((len(plan),))],
+        compiler_params=pltpu.CompilerParams(vmem_limit_bytes=56 * 1024 * 1024),
         cost_estimate=cost(1, 1),
-    )(table, one, two)
+    )(where, *weights)
 
 
 def match(first, count, target):
@@ -229,50 +254,24 @@
     return x.reshape(x.shape[0] // SLOTS, SLOTS, 128)
 
 
-def positions_kernel(target_ref, p_out):
-    slots = p_out.shape[0] * SLOTS
-    tokens = target_ref.shape[2]
-    step = 512
-    base = pl.program_id(0) * tokens
-    token = (base + lax.broadcasted_iota(jnp.int32, (1, tokens), 1)).astype(F32)
-    target = target_ref[0]
-
-    def move(i, carry):
-        at = jnp.where(match(i * step, step, target), token, EMPTY)
-        at = jnp.min(at, axis=1, keepdims=True)
-        where = pl.ds(i * (step // SLOTS), step // SLOTS)
-        p_out[where] = by_slot(jnp.broadcast_to(at, (step, 128)))
-        return carry
-
-    lax.fori_loop(0, slots // step, move, 0)
-
-
-def positions(target):
-    ranks, tokens = target.shape[0], target.shape[2]
-    return pl.pallas_call(
-        positions_kernel,
-        grid=(ranks,),
-        in_specs=[pl.BlockSpec((1, 1, tokens), lambda j: (j, 0, 0))],
-        out_specs=pl.BlockSpec((CLUSTERS, SLOTS, 128), lambda j: (0, j, 0)),
-        out_shape=pltpu.HBM((CLUSTERS, ranks * SLOTS, 128), F32),
-        compiler_params=params(16),
-        cost_estimate=cost(1, 1),
-    )(target)
-
-
-def place_pair_kernel(target_ref, q_ref, k_ref, q_out, k_out, right):
+def place_pair_kernel(target_ref, q_ref, k_ref, q_out, k_out, p_out, right):
+    tokens = q_ref.shape[1]
     slots = q_out.shape[0] * SLOTS
     step = 1024
     right[:, :128] = q_ref[0]
     right[:, 128:] = k_ref[0]
+    base = pl.program_id(0) * tokens
+    token = (base + lax.broadcasted_iota(jnp.int32, (1, tokens), 1)).astype(F32)
     target = target_ref[0]
 
     def move(i, carry):
-        picked = match(i * step, step, target).astype(BF16)
-        out = jnp.dot(picked, right[...], preferred_element_type=F32)
+        picked = match(i * step, step, target)
+        out = jnp.dot(picked.astype(BF16), right[...], preferred_element_type=F32)
         where = pl.ds(i * (step // SLOTS), step // SLOTS)
         q_out[where] = by_slot(out[:, :128]).astype(BF16)
         k_out[where] = by_slot(out[:, 128:]).astype(BF16)
+        at = jnp.min(jnp.where(picked, token, EMPTY), axis=1, keepdims=True)
+        p_out[where] = by_slot(jnp.broadcast_to(at, (step, 128)))
         return carry
 
     lax.fori_loop(0, slots // step, move, 0)
@@ -290,8 +289,12 @@
             pl.BlockSpec((1, tokens, 128), lambda j: (j, 0, 0)),
             pl.BlockSpec((1, tokens, 128), lambda j: (j, 1, 0)),
         ],
-        out_specs=[spec_out, spec_out],
-        out_shape=[jax.ShapeDtypeStruct(shape, BF16), jax.ShapeDtypeStruct(shape, BF16)],
+        out_specs=[spec_out, spec_out, spec_out],
+        out_shape=[
+            jax.ShapeDtypeStruct(shape, BF16),
+            jax.ShapeDtypeStruct(shape, BF16),
+            jax.ShapeDtypeStruct(shape, F32),
+        ],
         scratch_shapes=[pltpu.VMEM((tokens, 256), BF16)],
         compiler_params=params(16),
         cost_estimate=cost(1, 1),
@@ -449,10 +452,11 @@
     def exchange(x):
         return lax.all_to_all(x, "ctx", split_axis=0, concat_axis=0, tiled=True)
 
-    places = lax.all_gather(cluster_of * SLOTS + slot_of, "ctx", axis=0, tiled=False)
-    target = lax.dynamic_index_in_dim(places, me, 1, True)
-    first = exchange(pack((queries, keys)))
-    at = positions(target)
+    marks = [x.astype(BF16).reshape(ranks, tokens // 128, 128) for x in (cluster_of, slot_of)]
+    first = exchange(pack((queries, keys), jnp.concatenate(marks, axis=1)))
+    marks = first[:, 2 * tokens :, :].astype(jnp.int32)
+    target = marks[:, : tokens // 128, :] * SLOTS + marks[:, tokens // 128 :, :]
+    target = target.reshape(ranks, 1, tokens)
 
     cols = out_weight.shape[1] // 4
     heads = me ^ jnp.arange(ranks, dtype=jnp.int32)
@@ -462,19 +466,19 @@
     )
     corner = swap_core(lax.dynamic_slice_in_dim(across, (1 - core) * cols, cols, 1))
     groups = ((0, 1, 2, 3), (4, 5), (6, 7))
-    w_same = pick(heads, out_weight, across, (mine, core), groups, cols)
-    w_core = pick(heads, beside, corner, (0 * core, 0 * core), groups, cols)
-
-    rows_v = exchange(after(pack((values,)), first, at))
+    zero = jnp.zeros_like(core)
+    weight = pick(
+        heads, (out_weight, across, beside, corner), (mine, core, zero, zero), groups, cols
+    )
+    rows_v = exchange(after(pack((values,)), first))
 
     def paired(x):
         return x.reshape(CLUSTERS // PAIR, PAIR * cap, 128)
 
-    q_rows, k_rows = place_pair(target, first, tokens)
-    at = pltpu.with_memory_space_constraint(paired(at), pltpu.HBM)
-    weights, means = weigh(paired(q_rows), paired(k_rows), at)
+    q_rows, k_rows, at = place_pair(target, first, tokens)
+    weights, means = weigh(paired(q_rows), paired(k_rows), paired(at))
     weights = pltpu.with_memory_space_constraint(weights, pltpu.HBM)
-    rows_v = after(rows_v, w_same, w_core)
+    rows_v = after(rows_v, weight)
     mixed = mix(target, rows_v, weights).reshape(CLUSTERS, cap, 128)
 
     got, sent = {}, {}
@@ -515,19 +519,18 @@
     there[3] = swap_y(own[3])
     same = {1: side(got[0], own_123, y_0, y_123), 2: side(own[2], there[2])}
 
-    def add(total, left, weight, row):
+    def add(total, left, row):
         more = jnp.dot(left, weight[row : row + left.shape[1]], preferred_element_type=F32)
         return more if total is None else total + more
 
     total = None
-    for n, row in ((1, 0), (2, 1024)):
-        total = add(total, same[n], w_same, row)
-        total = add(total, swap_core(same[n]), w_core, row)
-    row = 1536
-    total = add(total, swap_core(own[3]), w_core, row)
+    for n, row in ((1, 0), (2, 2048)):
+        total = add(total, jnp.concatenate([same[n], swap_core(same[n])], axis=1), row)
+    row = 3072
+    total = add(total, swap_core(own[3]), row + 512)
     last = swap_core(after(there[3], total))
-    total = add(total, side(own[3], there[3]), w_same, row)
-    projected = add(total, last, w_core, row + 256).astype(BF16)
+    total = add(total, side(own[3], there[3]), row)
+    projected = add(total, last, row + 768).astype(BF16)
 
     tails = jnp.stack([got[d][tokens:] for d in range(ranks)]).astype(F32)
     tails = tails[:, :cl_dev] + tails[:, cl_dev:]

time: 307 us -> 264 us (0.86)
  blocking collectives: 107 us -> 0 us
  waiting for transfers between devices: 32 us -> 126 us
  Pallas kernels: 103 us -> 73.8 us
    all_gather x1 -> x0, blocking collectives: 107 us -> none  [head_body(): lax.all_gather(cluster_of * SLOTS + slot_of, 'ctx', axis=0, tiled=False)]
    all_to_all x2, waiting for transfers between devices: 0.01 us -> 85 us  [exchange(): return lax.all_to_all(x, 'ctx', split_axis=0, concat_axis=0, tiled=True)]
    pallas_call x5 -> x3, Pallas kernels: 43.9 us -> 14.6 us  [the longest x1 7.54 us: pick(): pl.pallas_call(functools.partial(pick_kernel, plan), in_specs=[pl.BlockSp...]
    ppermute x6, waiting for transfers between devices: 0.1 us -> 7.28 us  [swap_core(): return lax.ppermute(x, 'head', [(0, 1), (1, 0), (2, 3), (3, 2)])]
    ppermute x5, waiting for transfers between devices: 9.28 us -> 14.7 us  [swap_y(): return lax.ppermute(x, 'head', [(0, 2), (1, 3), (2, 0), (3, 1)])]
    ppermute x7, waiting for transfers between devices: 22.7 us -> 18.6 us  [swap_ctx(): return lax.ppermute(x, 'ctx', [(i, i ^ d) for i in range(ranks)])]
    pallas_call x1, Pallas kernels: 15.5 us -> 11.6 us  [weigh(): pl.pallas_call(weigh_kernel, grid=(groups // step,), in_specs=[spec, spec...]
    pallas_call x1, Pallas kernels: 15.6 us -> 19.3 us  [place_pair(): pl.pallas_call(place_pair_kernel, grid=(ranks,), in_specs=[pl.BlockSpec((...]
  transfers between devices with their start and end apart: 20 -> 20, of which waited for: 9 -> 11; matrix products, arithmetic and copies ran while one was open for 8% -> 9% of each run, Pallas kernels for 25% -> 19%
where the time goes in v6:
time: 264 us; the launch traced here: 263 us
  waiting for transfers between devices  126 us (48%)
  Pallas kernels  73.8 us (28%)
  starting transfers between devices  34 us (13%)
  local copies, waits for them, and re-layouts  12.6 us (5%)
  matrix products  11.1 us (4%)
  other arithmetic  4.62 us (2%)
    all_to_all x2, waiting for transfers between devices, exchange(): return lax.all_to_all(x, 'ctx', split_axis=0, concat_axis=0, tiled=True)  85 us
    pallas_call x1, Pallas kernels, place_pair(): pl.pallas_call(place_pair_kernel, grid=(ranks,), in_specs=[pl.BlockSpec((...  19.3 us
    ppermute x7, waiting for transfers between devices, swap_ctx(): return lax.ppermute(x, 'ctx', [(i, i ^ d) for i in range(ranks)])  18.6 us
    pallas_call x1, Pallas kernels, mix(): pl.pallas_call(functools.partial(mix_kernel, ranks), grid=(2 * ranks,), i...  17.4 us
    ppermute x7, starting transfers between devices, swap_ctx(): return lax.ppermute(x, 'ctx', [(i, i ^ d) for i in range(ranks)])  15.8 us
    ppermute x5, waiting for transfers between devices, swap_y(): return lax.ppermute(x, 'head', [(0, 2), (1, 3), (2, 0), (3, 1)])  14.7 us
    pallas_call x1, Pallas kernels, weigh(): pl.pallas_call(weigh_kernel, grid=(groups // step,), in_specs=[spec, spec...  11.6 us
    dot_general x5, matrix products, add(): jnp.dot(left, weight[row:row + left.shape[1]], preferred_element_type=F32)  11.1 us
  transfers between devices with their start and end apart: 20, of which 11 were waited for; matrix products, arithmetic and copies ran while one was open for 9% of the time, Pallas kernels for 19%

profile of v6, /device:TPU:0, one launch (start us, length us, event | category | flops | bytes accessed | tf_op | source)
XLA Modules:
  0.0 262.6 jit_solution(12105087814385183014)
XLA Ops:
  2.8 4.4 %shard_map.86 = bf16[8,2064,128]{2,1,0:T(8,128)(2,1)} custom-call(bf16[1024,1024]{1,0:T(8,128)(2,1)} %refs_0_.3, bf16[1024,1024]{1,0:T(8,128)(2,1)} %refs_1_.1, bf16[8,16,128]{2,1,0:T(8,128)(2,1)} %pad_maximum_fusion.4.refs_2_), custom_call_target="tpu_custom_call" | custom-call | bytes 8454144 | tf_op jit(solution)/shard_map/pallas_call | solution.py:197
  7.2 7.3 %all-to-all-start = ((bf16[8,2064,128]{2,1,0:T(8,128)(2,1)}), bf16[8,2064,128]{2,1,0:T(8,128)(2,1)}, u32[]{:S(2)}, u32[]{:S(2)}) async-start(bf16[8,2064,128]{2,1,0:T(8,128)(2,1)} %shard_map.86), calls=%async_computation | async-start | bytes 8454144 | tf_op jit(solution)/shard_map/all_to_all | solution.py:453
  14.5 4.7 %constant_dynamic-slice_fusion.2 = bf16[1024,2048]{1,0:T(8,128)(2,1)} fusion(bf16[1024,4096]{1,0:T(8,128)(2,1)} %refs_0_.5, s32[]{:T(128)S(6)} %select_n.46), kind=kLoop, calls=%fused_computation.77 | loop fusion | bytes 8388612 | tf_op jit(solution)/shard_map/dynamic_slice | solution.py:463
  20.7 2.7 %shard_map.87 = bf16[8,1024,128]{2,1,0:T(8,128)(2,1)} custom-call(bf16[1024,1024]{1,0:T(8,128)(2,1)} %refs_0_.4), custom_call_target="tpu_custom_call" | custom-call | bytes 4194304 | tf_op jit(solution)/shard_map/pallas_call | solution.py:197
  23.4 85.0 %all-to-all-done.q_ref.k_ref = bf16[8,2064,128]{2,1,0:T(8,128)(2,1)} async-done(((bf16[8,2064,128]{2,1,0:T(8,128)(2,1)}), bf16[8,2064,128]{2,1,0:T(8,128)(2,1)}, u32[]{:S(2)}, u32[]{:S(2)}) %all-to-all-start) | async-done | bytes 4227104 | tf_op jit(solution)/shard_map/all_to_all | solution.py:453
  108.4 3.6 %all-to-all-start.1 = ((bf16[8,1024,128]{2,1,0:T(8,128)(2,1)}), bf16[8,1024,128]{2,1,0:T(8,128)(2,1)S(1)}, u32[]{:S(2)}, u32[]{:S(2)}) async-start(bf16[8,1024,128]{2,1,0:T(8,128)(2,1)} %shard_map.87), calls=%async_computation.1 | async-start | bytes 4194304 | tf_op jit(solution)/shard_map/all_to_all | solution.py:453
  112.1 3.1 %constant_dynamic-slice_fusion.1 = bf16[1024,1024]{1,0:T(8,128)(2,1)} fusion(bf16[1024,4096]{1,0:T(8,128)(2,1)} %refs_0_.5, s32[]{:T(128)S(6)} %select_n.47), kind=kLoop, calls=%fused_computation.76 | loop fusion | bytes 4194308 | tf_op jit(solution)/shard_map/dynamic_slice | solution.py:465
  115.1 3.1 %constant_dynamic-slice_fusion = bf16[1024,1024]{1,0:T(8,128)(2,1)} fusion(bf16[1024,2048]{1,0:T(8,128)(2,1)} %collective-permute-done.refs_1_, s32[]{:T(128)S(6)} %select_n.48), kind=kLoop, calls=%fused_computation.75 | loop fusion | bytes 4194308 | tf_op jit(solution)/shard_map/dynamic_slice | solution.py:467
  119.6 3.2 %collective-permute-done.2.refs_3_ = bf16[1024,1024]{1,0:T(8,128)(2,1)} collective-permute-done((bf16[1024,1024]{1,0:T(8,128)(2,1)}, bf16[1024,1024]{1,0:T(8,128)(2,1)}, u32[]{:S(2)}, u32[]{:S(2)}) %collective-permute-start.2) | collective-permute-done | bytes 2097184 | tf_op jit(solution)/shard_map/ppermute | solution.py:444
  122.8 7.5 %shard_map.88 = bf16[4096,1024]{1,0:T(8,128)(2,1)} custom-call(s32[12]{0:T(128)} %pad_add_fusion.where_ref, bf16[1024,4096]{1,0:T(8,128)(2,1)} %refs_0_.5, bf16[1024,2048]{1,0:T(8,128)(2,1)} %collective-permute-done.refs_1_, bf16[1024,1024]{1,0:T(8,128)(2,1)} %collective-permute-done.1.refs_2_, bf16[1024,1024]{1,0:T(8,128)(2,1)} %collective-permute-done.2.refs_3_), custom_call_target="tpu_custom_call" | custom-call | flops 1 | bytes 1 | tf_op jit(solution)/shard_map/pallas_call | solution.py:236
  131.2 19.3 %shard_map.89 = (bf16[256,64,128]{2,1,0:T(8,128)(2,1)S(1)}, bf16[256,64,128]{2,1,0:T(8,128)(2,1)S(1)}, f32[256,64,128]{2,1,0:T(8,128)S(1)}) custom-call(s32[8,1,1024]{2,1,0:T(1,128)S(1)} %bitcast.79, bf16[8,2064,128]{2,1,0:T(8,128)(2,1)} %all-to-all-done.q_ref.k_ref, bf16[8,2064,128]{2,1,0:T(8,128)(2,1)} %all-to-all-done.q_ref.k_ref), custom_call_target="tpu_custom_call" | custom-call | flops 1 | bytes 1 | tf_op jit(solution)/shard_map/pallas_call | solution.py:284
  150.5 11.6 %shard_map.90 = (bf16[128,128,128]{2,1,0:T(8,128)(2,1)}, f32[256,128]{1,0:T(8,128)S(1)}) custom-call(bf16[128,128,128]{2,1,0:T(8,128)(2,1)S(1)} %bitcast.77, bf16[128,128,128]{2,1,0:T(8,128)(2,1)S(1)} %bitcast.78, f32[128,128,128]{2,1,0:T(8,128)S(1)} %bitcast.76), custom_call_target="tpu_custom_call" | custom-call | flops 1 | bytes 1 | tf_op jit(solution)/shard_map/pallas_call | solution.py:328
  162.1 17.4 %shard_map.91 = bf16[128,128,128]{2,1,0:T(8,128)(2,1)S(1)} custom-call(s32[8,1,1024]{2,1,0:T(1,128)S(1)} %bitcast.80, bf16[8,1024,128]{2,1,0:T(8,128)(2,1)S(1)} %all-to-all-done.1.v_ref, bf16[128,128,128]{2,1,0:T(8,128)(2,1)} %get-tuple-element.22.w_ref), custom_call_target="tpu_custom_call" | custom-call | flops 1 | bytes 1 | tf_op jit(solution)/shard_map/pallas_call | solution.py:379
  180.9 3.0 %collective-permute-start.9 = (bf16[1088,128]{1,0:T(8,128)(2,1)S(1)}, bf16[1088,128]{1,0:T(8,128)(2,1)S(1)}, u32[]{:S(2)}, u32[]{:S(2)}) collective-permute-start(bf16[1088,128]{1,0:T(8,128)(2,1)S(1)} %bitcast.95), channel_id=1, source_target_pairs={{0,16},{4,20},{8,24},{12,28},{16,0},{20,4},{24,8},{28,12},{1,17},{... | collective-permute-start | bytes 835592 | tf_op jit(solution)/shard_map/ppermute | solution.py:450
  199.5 4.0 %collective-permute-done.9 = bf16[1088,128]{1,0:T(8,128)(2,1)S(1)} collective-permute-done((bf16[1088,128]{1,0:T(8,128)(2,1)S(1)}, bf16[1088,128]{1,0:T(8,128)(2,1)S(1)}, u32[]{:S(2)}, u32[]{:S(2)}) %collective-permute-start.9) | collective-permute-done | bytes 278560 | tf_op jit(solution)/shard_map/ppermute | solution.py:450
  204.8 3.3 %collective-permute-start.13 = (bf16[1088,128]{1,0:T(8,128)(2,1)S(1)}, bf16[1088,128]{1,0:T(8,128)(2,1)S(1)}, u32[]{:S(2)}, u32[]{:S(2)}) collective-permute-start(bf16[1088,128]{1,0:T(8,128)(2,1)S(1)} %bitcast.90), channel_id=1, source_target_pairs={{0,24},{4,28},{8,16},{12,20},{16,8},{20,12},{24,0},{28,4},{1,25},{... | collective-permute-start | bytes 835592 | tf_op jit(solution)/shard_map/ppermute | solution.py:450
  208.1 2.7 %collective-permute-done.10 = bf16[1088,128]{1,0:T(8,128)(2,1)S(1)} collective-permute-done((bf16[1088,128]{1,0:T(8,128)(2,1)S(1)}, bf16[1088,128]{1,0:T(8,128)(2,1)S(1)}, u32[]{:S(2)}, u32[]{:S(2)}) %collective-permute-start.10) | collective-permute-done | bytes 278560 | tf_op jit(solution)/shard_map/ppermute | solution.py:450
  212.7 6.2 %collective-permute-done.4 = bf16[1088,128]{1,0:T(8,128)(2,1)S(1)} collective-permute-done((bf16[1088,128]{1,0:T(8,128)(2,1)S(1)}, bf16[1088,128]{1,0:T(8,128)(2,1)S(1)}, u32[]{:S(2)}, u32[]{:S(2)}) %collective-permute-start.4) | collective-permute-done | bytes 278560 | tf_op jit(solution)/shard_map/ppermute | solution.py:450
  219.1 5.7 %collective-permute-done.6 = bf16[1088,128]{1,0:T(8,128)(2,1)S(1)} collective-permute-done((bf16[1088,128]{1,0:T(8,128)(2,1)S(1)}, bf16[1088,128]{1,0:T(8,128)(2,1)S(1)}, u32[]{:S(2)}, u32[]{:S(2)}) %collective-permute-start.6) | collective-permute-done | bytes 278560 | tf_op jit(solution)/shard_map/ppermute | solution.py:450
  227.0 4.3 %collective-permute-start.14 = (bf16[1088,128]{1,0:T(8,128)(2,1)S(1)}, bf16[1088,128]{1,0:T(8,128)(2,1)S(1)}, u32[]{:S(2)}, u32[]{:S(2)}) collective-permute-start(bf16[1088,128]{1,0:T(8,128)(2,1)S(1)} %bitcast.91), channel_id=1, source_target_pairs={{0,28},{4,24},{8,20},{12,16},{16,12},{20,8},{24,4},{28,0},{1,29},{... | collective-permute-start | bytes 835592 | tf_op jit(solution)/shard_map/ppermute | solution.py:450
  231.6 11.4 %collective-permute-done.7 = bf16[1024,384]{1,0:T(8,128)(2,1)S(1)} collective-permute-done((bf16[1024,384]{1,0:T(8,128)(2,1)S(1)}, bf16[1024,384]{1,0:T(8,128)(2,1)S(1)}, u32[]{:S(2)}, u32[]{:S(2)}) %collective-permute-start.7) | collective-permute-done | bytes 786464 | tf_op jit(solution)/shard_map/ppermute | solution.py:441
  245.3 3.8 %collective-permute-done.12 = bf16[1024,512]{1,0:T(8,128)(2,1)S(1)} collective-permute-done((bf16[1024,512]{1,0:T(8,128)(2,1)S(1)}, bf16[1024,512]{1,0:T(8,128)(2,1)S(1)}, u32[]{:S(2)}, u32[]{:S(2)}) %collective-permute-start.12) | collective-permute-done | bytes 1048608 | tf_op jit(solution)/shard_map/ppermute | solution.py:444
  249.1 2.6 fusion.2
  251.9 4.5 %fusion = f32[1024,1024]{1,0:T(8,128)S(1)} fusion(bf16[1024,2048]{1,0:T(8,128)(2,1)S(1)} %constant_dynamic-update-slice_fusion.4, bf16[4096,1024]{1,0:T(8,128)(2,1)S(1)} %bitcast.98), kind=kOutput, calls=%fused_computation | convolution fusion | flops 4294967296 | bytes 12582912 | tf_op jit(solution)/shard_map/dot_general | solution.py:523
  (88 shorter events, 37.3 us)
Async XLA Ops:
  7.2 101.3 %all-to-all-start = ((bf16[8,2064,128]{2,1,0:T(8,128)(2,1)}), bf16[8,2064,128]{2,1,0:T(8,128)(2,1)}, u32[]{:S(2)}, u32[]{:S(2)}) async-start(bf16[8,2064,128]{2,1,0:T(8,128)(2,1)} %shard_map.86), calls=%async_computation | async-start | bytes 8454144 | tf_op jit(solution)/shard_map/all_to_all | solution.py:453
  19.2 95.9 %collective-permute-start = (bf16[1024,2048]{1,0:T(8,128)(2,1)}, bf16[1024,2048]{1,0:T(8,128)(2,1)}, u32[]{:S(2)}, u32[]{:S(2)}) collective-permute-start(bf16[1024,2048]{1,0:T(8,128)(2,1)} %constant_dynamic-slice_fusion.2), channel_id=1, source_target_pairs={{0,2},{1,3},{2,0},{3,1},{4,6},{5,7},{6,4},{7,5},{8,10},{9,11},{10,... | collective-permute-start | bytes 12582920 | tf_op jit(solution)/shard_map/ppermute | solution.py:441
  108.4 53.7 %all-to-all-start.1 = ((bf16[8,1024,128]{2,1,0:T(8,128)(2,1)}), bf16[8,1024,128]{2,1,0:T(8,128)(2,1)S(1)}, u32[]{:S(2)}, u32[]{:S(2)}) async-start(bf16[8,1024,128]{2,1,0:T(8,128)(2,1)} %shard_map.87), calls=%async_computation.1 | async-start | bytes 4194304 | tf_op jit(solution)/shard_map/all_to_all | solution.py:453
  115.1 4.5 %collective-permute-start.1 = (bf16[1024,1024]{1,0:T(8,128)(2,1)}, bf16[1024,1024]{1,0:T(8,128)(2,1)}, u32[]{:S(2)}, u32[]{:S(2)}) collective-permute-start(bf16[1024,1024]{1,0:T(8,128)(2,1)} %constant_dynamic-slice_fusion.1), channel_id=1, source_target_pairs={{0,1},{1,0},{2,3},{3,2},{4,5},{5,4},{6,7},{7,6},{8,9},{9,8},{10,11... | collective-permute-start | bytes 6291464 | tf_op jit(solution)/shard_map/ppermute | solution.py:444
  118.2 4.6 %collective-permute-start.2 = (bf16[1024,1024]{1,0:T(8,128)(2,1)}, bf16[1024,1024]{1,0:T(8,128)(2,1)}, u32[]{:S(2)}, u32[]{:S(2)}) collective-permute-start(bf16[1024,1024]{1,0:T(8,128)(2,1)} %constant_dynamic-slice_fusion), channel_id=1, source_target_pairs={{0,1},{1,0},{2,3},{3,2},{4,5},{5,4},{6,7},{7,6},{8,9},{9,8},{10,11... | collective-permute-start | bytes 6291464 | tf_op jit(solution)/shard_map/ppermute | solution.py:444
  180.9 22.5 %collective-permute-start.9 = (bf16[1088,128]{1,0:T(8,128)(2,1)S(1)}, bf16[1088,128]{1,0:T(8,128)(2,1)S(1)}, u32[]{:S(2)}, u32[]{:S(2)}) collective-permute-start(bf16[1088,128]{1,0:T(8,128)(2,1)S(1)} %bitcast.95), channel_id=1, source_target_pairs={{0,16},{4,20},{8,24},{12,28},{16,0},{20,4},{24,8},{28,12},{1,17},{... | collective-permute-start | bytes 835592 | tf_op jit(solution)/shard_map/ppermute | solution.py:450
  185.2 25.6 %collective-permute-start.10 = (bf16[1088,128]{1,0:T(8,128)(2,1)S(1)}, bf16[1088,128]{1,0:T(8,128)(2,1)S(1)}, u32[]{:S(2)}, u32[]{:S(2)}) collective-permute-start(bf16[1088,128]{1,0:T(8,128)(2,1)S(1)} %bitcast.94), channel_id=1, source_target_pairs={{0,20},{4,16},{8,28},{12,24},{16,4},{20,0},{24,12},{28,8},{1,21},{... | collective-permute-start | bytes 835592 | tf_op jit(solution)/shard_map/ppermute | solution.py:450
  188.1 8.4 %collective-permute-start.5 = (bf16[1088,128]{1,0:T(8,128)(2,1)S(1)}, bf16[1088,128]{1,0:T(8,128)(2,1)S(1)}, u32[]{:S(2)}, u32[]{:S(2)}) collective-permute-start(bf16[1088,128]{1,0:T(8,128)(2,1)S(1)} %bitcast.89), channel_id=1, source_target_pairs={{0,2},{1,3},{2,0},{3,1},{4,6},{5,7},{6,4},{7,5},{8,10},{9,11},{10,... | collective-permute-start | bytes 835592 | tf_op jit(solution)/shard_map/ppermute | solution.py:441
  191.2 21.3 %collective-permute-start.3 = (bf16[1088,128]{1,0:T(8,128)(2,1)S(1)}, bf16[1088,128]{1,0:T(8,128)(2,1)S(1)}, u32[]{:S(2)}, u32[]{:S(2)}) collective-permute-start(bf16[1088,128]{1,0:T(8,128)(2,1)S(1)} %bitcast.96), channel_id=1, source_target_pairs={{0,4},{4,0},{8,12},{12,8},{16,20},{20,16},{24,28},{28,24},{1,5},{5... | collective-permute-start | bytes 835592 | tf_op jit(solution)/shard_map/ppermute | solution.py:450
  192.7 26.2 %collective-permute-start.4 = (bf16[1088,128]{1,0:T(8,128)(2,1)S(1)}, bf16[1088,128]{1,0:T(8,128)(2,1)S(1)}, u32[]{:S(2)}, u32[]{:S(2)}) collective-permute-start(bf16[1088,128]{1,0:T(8,128)(2,1)S(1)} %bitcast.93), channel_id=1, source_target_pairs={{0,8},{4,12},{8,0},{12,4},{16,24},{20,28},{24,16},{28,20},{1,9},{5... | collective-permute-start | bytes 835592 | tf_op jit(solution)/shard_map/ppermute | solution.py:450
  197.9 26.9 %collective-permute-start.6 = (bf16[1088,128]{1,0:T(8,128)(2,1)S(1)}, bf16[1088,128]{1,0:T(8,128)(2,1)S(1)}, u32[]{:S(2)}, u32[]{:S(2)}) collective-permute-start(bf16[1088,128]{1,0:T(8,128)(2,1)S(1)} %bitcast.92), channel_id=1, source_target_pairs={{0,12},{4,8},{8,4},{12,0},{16,28},{20,24},{24,20},{28,16},{1,13},{... | collective-permute-start | bytes 835592 | tf_op jit(solution)/shard_map/ppermute | solution.py:450
  204.8 26.5 %collective-permute-start.13 = (bf16[1088,128]{1,0:T(8,128)(2,1)S(1)}, bf16[1088,128]{1,0:T(8,128)(2,1)S(1)}, u32[]{:S(2)}, u32[]{:S(2)}) collective-permute-start(bf16[1088,128]{1,0:T(8,128)(2,1)S(1)} %bitcast.90), channel_id=1, source_target_pairs={{0,24},{4,28},{8,16},{12,20},{16,8},{20,12},{24,0},{28,4},{1,25},{... | collective-permute-start | bytes 835592 | tf_op jit(solution)/shard_map/ppermute | solution.py:450
  210.9 32.5 %collective-permute-start.11 = (bf16[1024,256]{1,0:T(8,128)(2,1)S(1)}, bf16[1024,256]{1,0:T(8,128)(2,1)S(1)}, u32[]{:S(2)}, u32[]{:S(2)}) collective-permute-start(bf16[1024,256]{1,0:T(8,128)(2,1)S(1)} %pad_maximum_fusion.2), channel_id=1, source_target_pairs={{0,2},{1,3},{2,0},{3,1},{4,6},{5,7},{6,4},{7,5},{8,10},{9,11},{10,... | collective-permute-start | bytes 1572872 | tf_op jit(solution)/shard_map/ppermute | solution.py:441
  224.8 24.3 %slice-start = ((s8[8388608]{0:T(1024)(128)(4,1)}), s8[4194304]{0:T(1024)(128)(4,1)S(1)}, s32[]{:S(2)}) async-start(s8[8388608]{0:T(1024)(128)(4,1)} %bitcast.97), calls=%async_computation.2 | async-start | bytes 8388608
  225.1 17.8 %collective-permute-start.7 = (bf16[1024,384]{1,0:T(8,128)(2,1)S(1)}, bf16[1024,384]{1,0:T(8,128)(2,1)S(1)}, u32[]{:S(2)}, u32[]{:S(2)}) collective-permute-start(bf16[1024,384]{1,0:T(8,128)(2,1)S(1)} %pad_maximum_fusion.1), channel_id=1, source_target_pairs={{0,2},{1,3},{2,0},{3,1},{4,6},{5,7},{6,4},{7,5},{8,10},{9,11},{10,... | collective-permute-start | bytes 2359304 | tf_op jit(solution)/shard_map/ppermute | solution.py:441
  227.0 17.1 %collective-permute-start.14 = (bf16[1088,128]{1,0:T(8,128)(2,1)S(1)}, bf16[1088,128]{1,0:T(8,128)(2,1)S(1)}, u32[]{:S(2)}, u32[]{:S(2)}) collective-permute-start(bf16[1088,128]{1,0:T(8,128)(2,1)S(1)} %bitcast.91), channel_id=1, source_target_pairs={{0,28},{4,24},{8,20},{12,16},{16,12},{20,8},{24,4},{28,0},{1,29},{... | collective-permute-start | bytes 835592 | tf_op jit(solution)/shard_map/ppermute | solution.py:450
  231.3 17.8 %slice-start.1 = ((s8[8388608]{0:T(1024)(128)(4,1)}), s8[4194304]{0:T(1024)(128)(4,1)S(1)}, s32[]{:S(2)}) async-start(s8[8388608]{0:T(1024)(128)(4,1)} %bitcast.97), calls=%async_computation.3 | async-start | bytes 8388608
  243.4 8.3 %collective-permute-start.8 = (bf16[1024,1024]{1,0:T(8,128)(2,1)S(1)}, bf16[1024,1024]{1,0:T(8,128)(2,1)S(1)}, u32[]{:S(2)}, u32[]{:S(2)}) collective-permute-start(bf16[1024,1024]{1,0:T(8,128)(2,1)S(1)} %get-tuple-element.32), channel_id=1, source_target_pairs={{0,1},{1,0},{2,3},{3,2},{4,5},{5,4},{6,7},{7,6},{8,9},{9,8},{10,11... | collective-permute-start | bytes 6291464 | tf_op jit(solution)/shard_map/ppermute | solution.py:444
  243.6 5.5 %collective-permute-start.12 = (bf16[1024,512]{1,0:T(8,128)(2,1)S(1)}, bf16[1024,512]{1,0:T(8,128)(2,1)S(1)}, u32[]{:S(2)}, u32[]{:S(2)}) collective-permute-start(bf16[1024,512]{1,0:T(8,128)(2,1)S(1)} %pad_maximum_fusion), channel_id=1, source_target_pairs={{0,1},{1,0},{2,3},{3,2},{4,5},{5,4},{6,7},{7,6},{8,9},{9,8},{10,11... | collective-permute-start | bytes 3145736 | tf_op jit(solution)/shard_map/ppermute | solution.py:444
  244.2 12.2 %collective-permute-start.15 = (bf16[1024,256]{1,0:T(8,128)(2,1)S(1)}, bf16[1024,256]{1,0:T(8,128)(2,1)S(1)}, u32[]{:S(2)}, u32[]{:S(2)}) collective-permute-start(bf16[1024,256]{1,0:T(8,128)(2,1)S(1)} %pad_maximum_fusion.3), channel_id=1, source_target_pairs={{0,1},{1,0},{2,3},{3,2},{4,5},{5,4},{6,7},{7,6},{8,9},{9,8},{10,11... | collective-permute-start | bytes 1572872 | tf_op jit(solution)/shard_map/ppermute | solution.py:444
  244.3 14.3 %collective-permute-start.16 = (bf16[1024,256]{1,0:T(8,128)(2,1)S(1)}, bf16[1024,256]{1,0:T(8,128)(2,1)S(1)}, u32[]{:S(2)}, u32[]{:S(2)}) collective-permute-start(bf16[1024,256]{1,0:T(8,128)(2,1)S(1)} %pad_maximum_fusion.3), channel_id=1, source_target_pairs={{0,2},{1,3},{2,0},{3,1},{4,6},{5,7},{6,4},{7,5},{8,10},{9,11},{10,... | collective-permute-start | bytes 1572872 | tf_op jit(solution)/shard_map/ppermute | solution.py:441
  256.4 2.2 copy-start
  258.6 1.9 collective-permute-start.17

commit v7 on v6

--- a/solution.py
+++ b/solution.py
@@ -301,7 +301,7 @@
     )(target, first, first)
 
 
-def weigh_kernel(q_ref, k_ref, p_ref, w_out, mean_out):
+def weigh_kernel(tokens, q_ref, k_ref, p_ref, w_out, mean_out, early_out):
     count, rows = q_ref.shape[0], q_ref.shape[1]
     cap = rows // PAIR
     scale = 1.0 / math.sqrt(q_ref.shape[2])
@@ -316,43 +316,52 @@
         scores = jnp.where(allowed, scores, neg_fill)
         top = jnp.max(scores, axis=1, keepdims=True)
         w_out[n] = jnp.where(allowed, jnp.exp(scores - top), 0.0).astype(BF16)
+    share = p_ref[...] * (1.0 / tokens)
+    early_out[...] = (share - jnp.floor(share) < 0.5).astype(BF16)
     both = (q_ref[...].astype(F32) + k_ref[...].astype(F32)).reshape(count * PAIR, cap, 128)
     held = (p_ref[...] < EMPTY).astype(F32).reshape(count * PAIR, cap, 128)
     mean_out[...] = jnp.sum(both, axis=1) / (2.0 * jnp.maximum(jnp.sum(held, axis=1), 1.0))
 
 
-def weigh(q_rows, k_rows, at):
+def weigh(q_rows, k_rows, at, tokens):
     groups, rows = q_rows.shape[0], q_rows.shape[1]
     step = 8
     spec = pl.BlockSpec((step, rows, 128), lambda i: (i, 0, 0))
     return pl.pallas_call(
-        weigh_kernel,
+        functools.partial(weigh_kernel, tokens),
         grid=(groups // step,),
         in_specs=[spec, spec, spec],
         out_specs=[
             pl.BlockSpec((step, rows, rows), lambda i: (i, 0, 0)),
             pl.BlockSpec((step * PAIR, 128), lambda i: (i, 0)),
+            spec,
         ],
         out_shape=[
             pltpu.HBM((groups, rows, rows), BF16),
             jax.ShapeDtypeStruct((groups * PAIR, 128), F32),
+            pltpu.HBM((groups, rows, 128), BF16),
         ],
         compiler_params=params(12),
         cost_estimate=cost(1, 1),
     )(q_rows, k_rows, at)
 
 
-def mix_kernel(ranks, target_ref, v_ref, w_ref, o_out, v_rows):
+def mix_kernel(ranks, target_ref, v_ref, early_ref, w_ref, o_out, v_rows):
     i = pl.program_id(0)
     slots = v_rows.shape[0] * SLOTS
     count, rows = w_ref.shape[0], w_ref.shape[1]
+    tokens = v_ref.shape[1]
+    half = tokens // 2
 
     @pl.when(i < ranks)
     def _():
-        picked = match(0, slots, target_ref[0]).astype(BF16)
-        out = jnp.dot(picked, v_ref[0], preferred_element_type=F32)
+        target = target_ref[0]
+        picked = match(0, slots, target[:, :half]) | match(0, slots, target[:, half:])
+        both = jnp.concatenate([v_ref[0, :half], v_ref[0, half:]], axis=1)
+        out = jnp.dot(picked.astype(BF16), both, preferred_element_type=F32)
+        early = early_ref[...].astype(F32) > 0.0
         where = pl.ds(pl.multiple_of(i * SLOTS, SLOTS), SLOTS)
-        v_rows[:, where, :] = by_slot(out)
+        v_rows[:, where, :] = jnp.where(early, by_slot(out[:, :128]), by_slot(out[:, 128:]))
 
     @pl.when(i >= ranks)
     def _():
@@ -365,7 +374,7 @@
             o_out[n] = (out[:, :128] / jnp.where(total > 0.0, total, 1.0)).astype(BF16)
 
 
-def mix(target, rows_v, weights):
+def mix(target, rows_v, early, weights):
     ranks, tokens = rows_v.shape[0], rows_v.shape[1]
     groups, rows = weights.shape[0], weights.shape[1]
     count = groups // ranks
@@ -382,6 +391,7 @@
         in_specs=[
             pl.BlockSpec((1, 1, tokens), lambda i: (sender(i), 0, 0)),
             pl.BlockSpec((1, tokens, 128), lambda i: (sender(i), 0, 0)),
+            pl.BlockSpec((CLUSTERS, SLOTS, 128), lambda i: (0, sender(i), 0)),
             pl.BlockSpec((count, rows, rows), lambda i: (group(i), 0, 0)),
         ],
         out_specs=pl.BlockSpec((count, rows, 128), lambda i: (group(i), 0, 0)),
@@ -389,17 +399,20 @@
         scratch_shapes=[pltpu.VMEM((CLUSTERS, ranks * SLOTS, 128), F32)],
         compiler_params=params(20),
         cost_estimate=cost(1, 1),
-    )(target, rows_v, weights)
+    )(target, rows_v, early, weights)
 
 
 def unplace_kernel(who_ref, target_ref, o_ref, mean_ref, out_ref):
     tokens = target_ref.shape[2]
-    slots = o_ref.shape[0] * SLOTS
-    right = o_ref[...].astype(F32).reshape(slots, 128).astype(BF16)
+    half = o_ref.shape[0] // 2 * SLOTS
+    right = o_ref[...].astype(F32).reshape(2 * half, 128).astype(BF16)
+    right = jnp.concatenate([right[:half], right[half:]], axis=1)
     target = jnp.transpose(jnp.broadcast_to(target_ref[0], (128, tokens)))
-    columns = lax.broadcasted_iota(jnp.int32, (tokens, slots), 1)
-    picked = (columns == jnp.tile(target, (1, slots // 128))).astype(BF16)
-    out_ref[0, :tokens] = jnp.dot(picked, right, preferred_element_type=F32).astype(BF16)
+    low = jnp.where(target < half, target, target - half)
+    columns = lax.broadcasted_iota(jnp.int32, (tokens, half), 1)
+    picked = (columns == jnp.tile(low, (1, half // 128))).astype(BF16)
+    out = jnp.dot(picked, right, preferred_element_type=F32)
+    out_ref[0, :tokens] = jnp.where(target < half, out[:, :128], out[:, 128:]).astype(BF16)
     means = mean_ref[...]
     high = means.astype(BF16)
     count = means.shape[0]
@@ -465,10 +478,17 @@
         lax.dynamic_slice_in_dim(out_weight, (2 * y + 1 - core) * cols, cols, 1)
     )
     corner = swap_core(lax.dynamic_slice_in_dim(across, (1 - core) * cols, cols, 1))
-    groups = ((0, 1, 2, 3), (4, 5), (6, 7))
+    groups = ((0, 2, 3, 1), (4, 5), (6, 7))
     zero = jnp.zeros_like(core)
     weight = pick(
-        heads, (out_weight, across, beside, corner), (mine, core, zero, zero), groups, cols
+        heads,
+        [
+            pltpu.with_memory_space_constraint(w, pltpu.HBM)
+            for w in (out_weight, across, beside, corner)
+        ],
+        (mine, core, zero, zero),
+        groups,
+        cols,
     )
     rows_v = exchange(after(pack((values,)), first))
 
@@ -476,10 +496,11 @@
         return x.reshape(CLUSTERS // PAIR, PAIR * cap, 128)
 
     q_rows, k_rows, at = place_pair(target, first, tokens)
-    weights, means = weigh(paired(q_rows), paired(k_rows), paired(at))
-    weights = pltpu.with_memory_space_constraint(weights, pltpu.HBM)
+    weights, means, early = weigh(paired(q_rows), paired(k_rows), paired(at), tokens)
+    early = early.reshape(CLUSTERS, cap, 128)
+    early, weights = (pltpu.with_memory_space_constraint(x, pltpu.HBM) for x in (early, weights))
     rows_v = after(rows_v, weight)
-    mixed = mix(target, rows_v, weights).reshape(CLUSTERS, cap, 128)
+    mixed = mix(target, rows_v, early, weights).reshape(CLUSTERS, cap, 128)
 
     got, sent = {}, {}
 
@@ -500,24 +521,24 @@
     leave(0, sent[5])
     got[0] = sent[0]
     y_0 = swap_y(got[0])
-    leave(1, sent[0])
+    leave(2, sent[0])
+    go(2)
+    leave(3, sent[2])
+    go(3)
+    leave(1, sent[3], y_0)
     go(1)
-    leave(2, sent[1])
-    go(2)
-    leave(3, sent[2], y_0)
-    go(3)
-    leave(6, sent[3], got[4])
+    leave(6, sent[1], got[4])
     go(6)
-    own_123 = side(*[got[d] for d in (1, 2, 3)])
-    leave(7, sent[6], got[5], own_123)
+    own_231 = side(*[got[d] for d in (2, 3, 1)])
+    leave(7, sent[6], got[5], own_231)
     go(7)
     own, there = {}, {}
-    y_123 = swap_y(own_123)
+    y_231 = swap_y(own_231)
     own[2] = side(got[4], got[5])
     there[2] = swap_y(own[2])
     own[3] = side(got[6], got[7])
     there[3] = swap_y(own[3])
-    same = {1: side(got[0], own_123, y_0, y_123), 2: side(own[2], there[2])}
+    same = {1: side(got[0], own_231, y_0, y_231), 2: side(own[2], there[2])}
 
     def add(total, left, row):
         more = jnp.dot(left, weight[row : row + left.shape[1]], preferred_element_type=F32)

time: 264 us -> 262 us (level)
  Pallas kernels: 73.8 us -> 71 us
    pallas_call x8, Pallas kernels: 10.9 us -> 6.63 us  [unplace(): pl.pallas_call(unplace_kernel, grid_spec=pltpu.PrefetchScalarGridSpec(num...]
    pallas_call x1, Pallas kernels: 11.6 us -> 14.8 us  [weigh(): pl.pallas_call(functools.partial(weigh_kernel, tokens), grid=(groups // s...]
    ppermute x5, waiting for transfers between devices: 14.7 us -> 17.4 us  [swap_y(): return lax.ppermute(x, 'head', [(0, 2), (1, 3), (2, 0), (3, 1)])]
  transfers between devices with their start and end apart: 20 -> 20, of which waited for: 11 -> 10; matrix products, arithmetic and copies ran while one was open for 9% -> 9% of each run, Pallas kernels for 19% -> 19%
where the time goes in v7:
time: 262 us; the launch traced here: 261 us
  waiting for transfers between devices  127 us (48%)
  Pallas kernels  71 us (27%)
  starting transfers between devices  33.9 us (13%)
  local copies, waits for them, and re-layouts  12.6 us (5%)
  matrix products  11.1 us (4%)
  other arithmetic  4.56 us (2%)
    all_to_all x2, waiting for transfers between devices, exchange(): return lax.all_to_all(x, 'ctx', split_axis=0, concat_axis=0, tiled=True)  85.1 us
    pallas_call x1, Pallas kernels, place_pair(): pl.pallas_call(place_pair_kernel, grid=(ranks,), in_specs=[pl.BlockSpec((...  19.3 us
    ppermute x7, waiting for transfers between devices, swap_ctx(): return lax.ppermute(x, 'ctx', [(i, i ^ d) for i in range(ranks)])  18 us
    ppermute x5, waiting for transfers between devices, swap_y(): return lax.ppermute(x, 'head', [(0, 2), (1, 3), (2, 0), (3, 1)])  17.4 us
    pallas_call x1, Pallas kernels, mix(): pl.pallas_call(functools.partial(mix_kernel, ranks), grid=(2 * ranks,), i...  15.6 us
    ppermute x7, starting transfers between devices, swap_ctx(): return lax.ppermute(x, 'ctx', [(i, i ^ d) for i in range(ranks)])  15.1 us
    pallas_call x1, Pallas kernels, weigh(): pl.pallas_call(functools.partial(weigh_kernel, tokens), grid=(groups // s...  14.8 us
    dot_general x5, matrix products, add(): jnp.dot(left, weight[row:row + left.shape[1]], preferred_element_type=F32)  11.1 us
  transfers between devices with their start and end apart: 20, of which 10 were waited for; matrix products, arithmetic and copies ran while one was open for 9% of the time, Pallas kernels for 19%

profile of v7, /device:TPU:0, one launch (start us, length us, event | category | flops | bytes accessed | tf_op | source)
XLA Modules:
  0.0 261.1 jit_solution(5799022588907461256)
XLA Ops:
  2.8 4.3 %shard_map.86 = bf16[8,2064,128]{2,1,0:T(8,128)(2,1)} custom-call(bf16[1024,1024]{1,0:T(8,128)(2,1)} %refs_0_.3, bf16[1024,1024]{1,0:T(8,128)(2,1)} %refs_1_.1, bf16[8,16,128]{2,1,0:T(8,128)(2,1)} %pad_maximum_fusion.4.refs_2_), custom_call_target="tpu_custom_call" | custom-call | bytes 8454144 | tf_op jit(solution)/shard_map/pallas_call | solution.py:197
  7.1 7.3 %all-to-all-start = ((bf16[8,2064,128]{2,1,0:T(8,128)(2,1)}), bf16[8,2064,128]{2,1,0:T(8,128)(2,1)}, u32[]{:S(2)}, u32[]{:S(2)}) async-start(bf16[8,2064,128]{2,1,0:T(8,128)(2,1)} %shard_map.86), calls=%async_computation | async-start | bytes 8454144 | tf_op jit(solution)/shard_map/all_to_all | solution.py:466
  14.4 4.7 %constant_dynamic-slice_fusion.2 = bf16[1024,2048]{1,0:T(8,128)(2,1)} fusion(bf16[1024,4096]{1,0:T(8,128)(2,1)} %refs_0_.5, s32[]{:T(128)S(6)} %select_n.46), kind=kLoop, calls=%fused_computation.77 | loop fusion | bytes 8388612 | tf_op jit(solution)/shard_map/dynamic_slice | solution.py:476
  20.6 2.7 %shard_map.87 = bf16[8,1024,128]{2,1,0:T(8,128)(2,1)} custom-call(bf16[1024,1024]{1,0:T(8,128)(2,1)} %refs_0_.4), custom_call_target="tpu_custom_call" | custom-call | bytes 4194304 | tf_op jit(solution)/shard_map/pallas_call | solution.py:197
  23.3 85.1 %all-to-all-done.q_ref.k_ref = bf16[8,2064,128]{2,1,0:T(8,128)(2,1)} async-done(((bf16[8,2064,128]{2,1,0:T(8,128)(2,1)}), bf16[8,2064,128]{2,1,0:T(8,128)(2,1)}, u32[]{:S(2)}, u32[]{:S(2)}) %all-to-all-start) | async-done | bytes 4227104 | tf_op jit(solution)/shard_map/all_to_all | solution.py:466
  108.3 3.6 %all-to-all-start.1 = ((bf16[8,1024,128]{2,1,0:T(8,128)(2,1)}), bf16[8,1024,128]{2,1,0:T(8,128)(2,1)S(1)}, u32[]{:S(2)}, u32[]{:S(2)}) async-start(bf16[8,1024,128]{2,1,0:T(8,128)(2,1)} %shard_map.87), calls=%async_computation.1 | async-start | bytes 4194304 | tf_op jit(solution)/shard_map/all_to_all | solution.py:466
  112.0 3.2 %constant_dynamic-slice_fusion.1 = bf16[1024,1024]{1,0:T(8,128)(2,1)} fusion(bf16[1024,4096]{1,0:T(8,128)(2,1)} %refs_0_.5, s32[]{:T(128)S(6)} %select_n.47), kind=kLoop, calls=%fused_computation.76 | loop fusion | bytes 4194308 | tf_op jit(solution)/shard_map/dynamic_slice | solution.py:478
  115.1 3.0 %constant_dynamic-slice_fusion = bf16[1024,1024]{1,0:T(8,128)(2,1)} fusion(bf16[1024,2048]{1,0:T(8,128)(2,1)} %collective-permute-done.refs_1_, s32[]{:T(128)S(6)} %select_n.48), kind=kLoop, calls=%fused_computation.75 | loop fusion | bytes 4194308 | tf_op jit(solution)/shard_map/dynamic_slice | solution.py:480
  119.6 3.2 %collective-permute-done.2.refs_3_ = bf16[1024,1024]{1,0:T(8,128)(2,1)} collective-permute-done((bf16[1024,1024]{1,0:T(8,128)(2,1)}, bf16[1024,1024]{1,0:T(8,128)(2,1)}, u32[]{:S(2)}, u32[]{:S(2)}) %collective-permute-start.2) | collective-permute-done | bytes 2097184 | tf_op jit(solution)/shard_map/ppermute | solution.py:457
  122.8 7.8 %shard_map.88 = bf16[4096,1024]{1,0:T(8,128)(2,1)} custom-call(s32[12]{0:T(128)} %pad_add_fusion.where_ref, bf16[1024,4096]{1,0:T(8,128)(2,1)} %refs_0_.5, bf16[1024,2048]{1,0:T(8,128)(2,1)} %collective-permute-done.refs_1_, bf16[1024,1024]{1,0:T(8,128)(2,1)} %collective-permute-done.1.refs_2_, bf16[1024,1024]{1,0:T(8,128)(2,1)} %collective-permute-done.2.refs_3_), custom_call_target="tpu_custom_call" | custom-call | flops 1 | bytes 1 | tf_op jit(solution)/shard_map/pallas_call | solution.py:236
  131.4 19.3 %shard_map.89 = (bf16[256,64,128]{2,1,0:T(8,128)(2,1)S(1)}, bf16[256,64,128]{2,1,0:T(8,128)(2,1)S(1)}, f32[256,64,128]{2,1,0:T(8,128)S(1)}) custom-call(s32[8,1,1024]{2,1,0:T(1,128)S(1)} %bitcast.80, bf16[8,2064,128]{2,1,0:T(8,128)(2,1)} %all-to-all-done.q_ref.k_ref, bf16[8,2064,128]{2,1,0:T(8,128)(2,1)} %all-to-all-done.q_ref.k_ref), custom_call_target="tpu_custom_call" | custom-call | flops 1 | bytes 1 | tf_op jit(solution)/shard_map/pallas_call | solution.py:284
  150.7 14.8 %shard_map.90 = (bf16[128,128,128]{2,1,0:T(8,128)(2,1)}, f32[256,128]{1,0:T(8,128)S(1)}, bf16[128,128,128]{2,1,0:T(8,128)(2,1)}) custom-call(bf16[128,128,128]{2,1,0:T(8,128)(2,1)S(1)} %bitcast.78, bf16[128,128,128]{2,1,0:T(8,128)(2,1)S(1)} %bitcast.79, f32[128,128,128]{2,1,0:T(8,128)S(1)} %bitcast.77), custom_call_target="tpu_custom_call" | custom-call | flops 1 | bytes 1 | tf_op jit(solution)/shard_map/pallas_call | solution.py:330
  165.5 15.6 %shard_map.91 = bf16[128,128,128]{2,1,0:T(8,128)(2,1)S(1)} custom-call(s32[8,1,1024]{2,1,0:T(1,128)S(1)} %bitcast.81, bf16[8,1024,128]{2,1,0:T(8,128)(2,1)S(1)} %all-to-all-done.1.v_ref, bf16[256,64,128]{2,1,0:T(8,128)(2,1)} %bitcast.100, bf16[128,128,128]{2,1,0:T(8,128)(2,1)} %get-tuple-element.24.w_ref), custom_call_target="tpu_custom_call" | custom-call | flops 1 | bytes 1 | tf_op jit(solution)/shard_map/pallas_call | solution.py:388
  181.9 3.0 %collective-permute-start.9 = (bf16[1088,128]{1,0:T(8,128)(2,1)S(1)}, bf16[1088,128]{1,0:T(8,128)(2,1)S(1)}, u32[]{:S(2)}, u32[]{:S(2)}) collective-permute-start(bf16[1088,128]{1,0:T(8,128)(2,1)S(1)} %bitcast.96), channel_id=1, source_target_pairs={{0,16},{4,20},{8,24},{12,28},{16,0},{20,4},{24,8},{28,12},{1,17},{... | collective-permute-start | bytes 835592 | tf_op jit(solution)/shard_map/ppermute | solution.py:463
  193.0 3.4 %collective-permute-done.5 = bf16[1088,128]{1,0:T(8,128)(2,1)S(1)} collective-permute-done((bf16[1088,128]{1,0:T(8,128)(2,1)S(1)}, bf16[1088,128]{1,0:T(8,128)(2,1)S(1)}, u32[]{:S(2)}, u32[]{:S(2)}) %collective-permute-start.5) | collective-permute-done | bytes 278560 | tf_op jit(solution)/shard_map/ppermute | solution.py:454
  197.6 6.8 %collective-permute-done.9 = bf16[1088,128]{1,0:T(8,128)(2,1)S(1)} collective-permute-done((bf16[1088,128]{1,0:T(8,128)(2,1)S(1)}, bf16[1088,128]{1,0:T(8,128)(2,1)S(1)}, u32[]{:S(2)}, u32[]{:S(2)}) %collective-permute-start.9) | collective-permute-done | bytes 278560 | tf_op jit(solution)/shard_map/ppermute | solution.py:463
  205.2 3.3 %collective-permute-start.13 = (bf16[1088,128]{1,0:T(8,128)(2,1)S(1)}, bf16[1088,128]{1,0:T(8,128)(2,1)S(1)}, u32[]{:S(2)}, u32[]{:S(2)}) collective-permute-start(bf16[1088,128]{1,0:T(8,128)(2,1)S(1)} %bitcast.91), channel_id=1, source_target_pairs={{0,24},{4,28},{8,16},{12,20},{16,8},{20,12},{24,0},{28,4},{1,25},{... | collective-permute-start | bytes 835592 | tf_op jit(solution)/shard_map/ppermute | solution.py:463
  208.5 3.7 %collective-permute-done.10 = bf16[1088,128]{1,0:T(8,128)(2,1)S(1)} collective-permute-done((bf16[1088,128]{1,0:T(8,128)(2,1)S(1)}, bf16[1088,128]{1,0:T(8,128)(2,1)S(1)}, u32[]{:S(2)}, u32[]{:S(2)}) %collective-permute-start.10) | collective-permute-done | bytes 278560 | tf_op jit(solution)/shard_map/ppermute | solution.py:463
  213.8 7.5 %collective-permute-done.4 = bf16[1088,128]{1,0:T(8,128)(2,1)S(1)} collective-permute-done((bf16[1088,128]{1,0:T(8,128)(2,1)S(1)}, bf16[1088,128]{1,0:T(8,128)(2,1)S(1)}, u32[]{:S(2)}, u32[]{:S(2)}) %collective-permute-start.4) | collective-permute-done | bytes 278560 | tf_op jit(solution)/shard_map/ppermute | solution.py:463
  223.3 5.4 %collective-permute-start.14 = (bf16[1088,128]{1,0:T(8,128)(2,1)S(1)}, bf16[1088,128]{1,0:T(8,128)(2,1)S(1)}, u32[]{:S(2)}, u32[]{:S(2)}) collective-permute-start(bf16[1088,128]{1,0:T(8,128)(2,1)S(1)} %bitcast.92), channel_id=1, source_target_pairs={{0,28},{4,24},{8,20},{12,16},{16,12},{20,8},{24,4},{28,0},{1,29},{... | collective-permute-start | bytes 835592 | tf_op jit(solution)/shard_map/ppermute | solution.py:463
  228.9 12.5 %collective-permute-done.7 = bf16[1024,384]{1,0:T(8,128)(2,1)S(1)} collective-permute-done((bf16[1024,384]{1,0:T(8,128)(2,1)S(1)}, bf16[1024,384]{1,0:T(8,128)(2,1)S(1)}, u32[]{:S(2)}, u32[]{:S(2)}) %collective-permute-start.7) | collective-permute-done | bytes 786464 | tf_op jit(solution)/shard_map/ppermute | solution.py:454
  244.6 2.9 %collective-permute-done.12 = bf16[1024,512]{1,0:T(8,128)(2,1)S(1)} collective-permute-done((bf16[1024,512]{1,0:T(8,128)(2,1)S(1)}, bf16[1024,512]{1,0:T(8,128)(2,1)S(1)}, u32[]{:S(2)}, u32[]{:S(2)}) %collective-permute-start.12) | collective-permute-done | bytes 1048608 | tf_op jit(solution)/shard_map/ppermute | solution.py:457
  247.6 2.3 fusion.2
  250.1 4.7 %fusion = f32[1024,1024]{1,0:T(8,128)S(1)} fusion(bf16[1024,2048]{1,0:T(8,128)(2,1)S(1)} %constant_dynamic-update-slice_fusion.4, bf16[4096,1024]{1,0:T(8,128)(2,1)S(1)} %bitcast.99), kind=kOutput, calls=%fused_computation | convolution fusion | flops 4294967296 | bytes 12582912 | tf_op jit(solution)/shard_map/dot_general | solution.py:544
  (88 shorter events, 30.1 us)
Async XLA Ops:
  7.1 101.3 %all-to-all-start = ((bf16[8,2064,128]{2,1,0:T(8,128)(2,1)}), bf16[8,2064,128]{2,1,0:T(8,128)(2,1)}, u32[]{:S(2)}, u32[]{:S(2)}) async-start(bf16[8,2064,128]{2,1,0:T(8,128)(2,1)} %shard_map.86), calls=%async_computation | async-start | bytes 8454144 | tf_op jit(solution)/shard_map/all_to_all | solution.py:466
  19.1 96.1 %collective-permute-start = (bf16[1024,2048]{1,0:T(8,128)(2,1)}, bf16[1024,2048]{1,0:T(8,128)(2,1)}, u32[]{:S(2)}, u32[]{:S(2)}) collective-permute-start(bf16[1024,2048]{1,0:T(8,128)(2,1)} %constant_dynamic-slice_fusion.2), channel_id=1, source_target_pairs={{0,2},{1,3},{2,0},{3,1},{4,6},{5,7},{6,4},{7,5},{8,10},{9,11},{10,... | collective-permute-start | bytes 12582920 | tf_op jit(solution)/shard_map/ppermute | solution.py:454
  108.3 57.2 %all-to-all-start.1 = ((bf16[8,1024,128]{2,1,0:T(8,128)(2,1)}), bf16[8,1024,128]{2,1,0:T(8,128)(2,1)S(1)}, u32[]{:S(2)}, u32[]{:S(2)}) async-start(bf16[8,1024,128]{2,1,0:T(8,128)(2,1)} %shard_map.87), calls=%async_computation.1 | async-start | bytes 4194304 | tf_op jit(solution)/shard_map/all_to_all | solution.py:466
  115.1 4.5 %collective-permute-start.1 = (bf16[1024,1024]{1,0:T(8,128)(2,1)}, bf16[1024,1024]{1,0:T(8,128)(2,1)}, u32[]{:S(2)}, u32[]{:S(2)}) collective-permute-start(bf16[1024,1024]{1,0:T(8,128)(2,1)} %constant_dynamic-slice_fusion.1), channel_id=1, source_target_pairs={{0,1},{1,0},{2,3},{3,2},{4,5},{5,4},{6,7},{7,6},{8,9},{9,8},{10,11... | collective-permute-start | bytes 6291464 | tf_op jit(solution)/shard_map/ppermute | solution.py:457
  118.2 4.6 %collective-permute-start.2 = (bf16[1024,1024]{1,0:T(8,128)(2,1)}, bf16[1024,1024]{1,0:T(8,128)(2,1)}, u32[]{:S(2)}, u32[]{:S(2)}) collective-permute-start(bf16[1024,1024]{1,0:T(8,128)(2,1)} %constant_dynamic-slice_fusion), channel_id=1, source_target_pairs={{0,1},{1,0},{2,3},{3,2},{4,5},{5,4},{6,7},{7,6},{8,9},{9,8},{10,11... | collective-permute-start | bytes 6291464 | tf_op jit(solution)/shard_map/ppermute | solution.py:457
  181.9 22.5 %collective-permute-start.9 = (bf16[1088,128]{1,0:T(8,128)(2,1)S(1)}, bf16[1088,128]{1,0:T(8,128)(2,1)S(1)}, u32[]{:S(2)}, u32[]{:S(2)}) collective-permute-start(bf16[1088,128]{1,0:T(8,128)(2,1)S(1)} %bitcast.96), channel_id=1, source_target_pairs={{0,16},{4,20},{8,24},{12,28},{16,0},{20,4},{24,8},{28,12},{1,17},{... | collective-permute-start | bytes 835592 | tf_op jit(solution)/shard_map/ppermute | solution.py:463
  185.7 26.5 %collective-permute-start.10 = (bf16[1088,128]{1,0:T(8,128)(2,1)S(1)}, bf16[1088,128]{1,0:T(8,128)(2,1)S(1)}, u32[]{:S(2)}, u32[]{:S(2)}) collective-permute-start(bf16[1088,128]{1,0:T(8,128)(2,1)S(1)} %bitcast.93), channel_id=1, source_target_pairs={{0,20},{4,16},{8,28},{12,24},{16,4},{20,0},{24,12},{28,8},{1,21},{... | collective-permute-start | bytes 835592 | tf_op jit(solution)/shard_map/ppermute | solution.py:463
  188.1 8.3 %collective-permute-start.5 = (bf16[1088,128]{1,0:T(8,128)(2,1)S(1)}, bf16[1088,128]{1,0:T(8,128)(2,1)S(1)}, u32[]{:S(2)}, u32[]{:S(2)}) collective-permute-start(bf16[1088,128]{1,0:T(8,128)(2,1)S(1)} %bitcast.90), channel_id=1, source_target_pairs={{0,2},{1,3},{2,0},{3,1},{4,6},{5,7},{6,4},{7,5},{8,10},{9,11},{10,... | collective-permute-start | bytes 835592 | tf_op jit(solution)/shard_map/ppermute | solution.py:454
  190.6 23.1 %collective-permute-start.3 = (bf16[1088,128]{1,0:T(8,128)(2,1)S(1)}, bf16[1088,128]{1,0:T(8,128)(2,1)S(1)}, u32[]{:S(2)}, u32[]{:S(2)}) collective-permute-start(bf16[1088,128]{1,0:T(8,128)(2,1)S(1)} %bitcast.97), channel_id=1, source_target_pairs={{0,8},{4,12},{8,0},{12,4},{16,24},{20,28},{24,16},{28,20},{1,9},{5... | collective-permute-start | bytes 835592 | tf_op jit(solution)/shard_map/ppermute | solution.py:463
  192.9 28.4 %collective-permute-start.4 = (bf16[1088,128]{1,0:T(8,128)(2,1)S(1)}, bf16[1088,128]{1,0:T(8,128)(2,1)S(1)}, u32[]{:S(2)}, u32[]{:S(2)}) collective-permute-start(bf16[1088,128]{1,0:T(8,128)(2,1)S(1)} %bitcast.94), channel_id=1, source_target_pairs={{0,12},{4,8},{8,4},{12,0},{16,28},{20,24},{24,20},{28,16},{1,13},{... | collective-permute-start | bytes 835592 | tf_op jit(solution)/shard_map/ppermute | solution.py:463
  197.2 24.3 %collective-permute-start.6 = (bf16[1088,128]{1,0:T(8,128)(2,1)S(1)}, bf16[1088,128]{1,0:T(8,128)(2,1)S(1)}, u32[]{:S(2)}, u32[]{:S(2)}) collective-permute-start(bf16[1088,128]{1,0:T(8,128)(2,1)S(1)} %bitcast.95), channel_id=1, source_target_pairs={{0,4},{4,0},{8,12},{12,8},{16,20},{20,16},{24,28},{28,24},{1,5},{5... | collective-permute-start | bytes 835592 | tf_op jit(solution)/shard_map/ppermute | solution.py:463
  205.2 23.5 %collective-permute-start.13 = (bf16[1088,128]{1,0:T(8,128)(2,1)S(1)}, bf16[1088,128]{1,0:T(8,128)(2,1)S(1)}, u32[]{:S(2)}, u32[]{:S(2)}) collective-permute-start(bf16[1088,128]{1,0:T(8,128)(2,1)S(1)} %bitcast.91), channel_id=1, source_target_pairs={{0,24},{4,28},{8,16},{12,20},{16,8},{20,12},{24,0},{28,4},{1,25},{... | collective-permute-start | bytes 835592 | tf_op jit(solution)/shard_map/ppermute | solution.py:463
  212.3 29.6 %collective-permute-start.11 = (bf16[1024,256]{1,0:T(8,128)(2,1)S(1)}, bf16[1024,256]{1,0:T(8,128)(2,1)S(1)}, u32[]{:S(2)}, u32[]{:S(2)}) collective-permute-start(bf16[1024,256]{1,0:T(8,128)(2,1)S(1)} %pad_maximum_fusion.2), channel_id=1, source_target_pairs={{0,2},{1,3},{2,0},{3,1},{4,6},{5,7},{6,4},{7,5},{8,10},{9,11},{10,... | collective-permute-start | bytes 1572872 | tf_op jit(solution)/shard_map/ppermute | solution.py:454
  221.5 26.0 %slice-start = ((s8[8388608]{0:T(1024)(128)(4,1)}), s8[4194304]{0:T(1024)(128)(4,1)S(1)}, s32[]{:S(2)}) async-start(s8[8388608]{0:T(1024)(128)(4,1)} %bitcast.98), calls=%async_computation.2 | async-start | bytes 8388608
  221.9 19.6 %collective-permute-start.7 = (bf16[1024,384]{1,0:T(8,128)(2,1)S(1)}, bf16[1024,384]{1,0:T(8,128)(2,1)S(1)}, u32[]{:S(2)}, u32[]{:S(2)}) collective-permute-start(bf16[1024,384]{1,0:T(8,128)(2,1)S(1)} %pad_maximum_fusion.1), channel_id=1, source_target_pairs={{0,2},{1,3},{2,0},{3,1},{4,6},{5,7},{6,4},{7,5},{8,10},{9,11},{10,... | collective-permute-start | bytes 2359304 | tf_op jit(solution)/shard_map/ppermute | solution.py:454
  223.3 19.3 %collective-permute-start.14 = (bf16[1088,128]{1,0:T(8,128)(2,1)S(1)}, bf16[1088,128]{1,0:T(8,128)(2,1)S(1)}, u32[]{:S(2)}, u32[]{:S(2)}) collective-permute-start(bf16[1088,128]{1,0:T(8,128)(2,1)S(1)} %bitcast.92), channel_id=1, source_target_pairs={{0,28},{4,24},{8,20},{12,16},{16,12},{20,8},{24,4},{28,0},{1,29},{... | collective-permute-start | bytes 835592 | tf_op jit(solution)/shard_map/ppermute | solution.py:463
  228.7 18.9 %slice-start.1 = ((s8[8388608]{0:T(1024)(128)(4,1)}), s8[4194304]{0:T(1024)(128)(4,1)S(1)}, s32[]{:S(2)}) async-start(s8[8388608]{0:T(1024)(128)(4,1)} %bitcast.98), calls=%async_computation.3 | async-start | bytes 8388608
  241.8 8.1 %collective-permute-start.8 = (bf16[1024,1024]{1,0:T(8,128)(2,1)S(1)}, bf16[1024,1024]{1,0:T(8,128)(2,1)S(1)}, u32[]{:S(2)}, u32[]{:S(2)}) collective-permute-start(bf16[1024,1024]{1,0:T(8,128)(2,1)S(1)} %get-tuple-element.34), channel_id=1, source_target_pairs={{0,1},{1,0},{2,3},{3,2},{4,5},{5,4},{6,7},{7,6},{8,9},{9,8},{10,11... | collective-permute-start | bytes 6291464 | tf_op jit(solution)/shard_map/ppermute | solution.py:457
  242.0 5.5 %collective-permute-start.12 = (bf16[1024,512]{1,0:T(8,128)(2,1)S(1)}, bf16[1024,512]{1,0:T(8,128)(2,1)S(1)}, u32[]{:S(2)}, u32[]{:S(2)}) collective-permute-start(bf16[1024,512]{1,0:T(8,128)(2,1)S(1)} %pad_maximum_fusion), channel_id=1, source_target_pairs={{0,1},{1,0},{2,3},{3,2},{4,5},{5,4},{6,7},{7,6},{8,9},{9,8},{10,11... | collective-permute-start | bytes 3145736 | tf_op jit(solution)/shard_map/ppermute | solution.py:457
  242.7 12.2 %collective-permute-start.15 = (bf16[1024,256]{1,0:T(8,128)(2,1)S(1)}, bf16[1024,256]{1,0:T(8,128)(2,1)S(1)}, u32[]{:S(2)}, u32[]{:S(2)}) collective-permute-start(bf16[1024,256]{1,0:T(8,128)(2,1)S(1)} %pad_maximum_fusion.3), channel_id=1, source_target_pairs={{0,1},{1,0},{2,3},{3,2},{4,5},{5,4},{6,7},{7,6},{8,9},{9,8},{10,11... | collective-permute-start | bytes 1572872 | tf_op jit(solution)/shard_map/ppermute | solution.py:457
  242.8 14.3 %collective-permute-start.16 = (bf16[1024,256]{1,0:T(8,128)(2,1)S(1)}, bf16[1024,256]{1,0:T(8,128)(2,1)S(1)}, u32[]{:S(2)}, u32[]{:S(2)}) collective-permute-start(bf16[1024,256]{1,0:T(8,128)(2,1)S(1)} %pad_maximum_fusion.3), channel_id=1, source_target_pairs={{0,2},{1,3},{2,0},{3,1},{4,6},{5,7},{6,4},{7,5},{8,10},{9,11},{10,... | collective-permute-start | bytes 1572872 | tf_op jit(solution)/shard_map/ppermute | solution.py:454
  254.9 2.2 copy-start
  257.1 1.9 collective-permute-start.17

commit v8 on v7

--- a/solution.py
+++ b/solution.py
@@ -130,6 +130,7 @@
 F32 = jnp.float32
 PAIR = 2
 EMPTY = 1e9
+LANES = (0, 2, 3, 1, 4, 5, 6, 7)
 
 
 def params(limit):
@@ -209,40 +210,39 @@
     )(*args)
 
 
-def pick_kernel(plan, where_ref, *refs):
-    sources, out_ref, sems = refs[:-2], refs[-2], refs[-1]
-    count = where_ref.shape[0] - len(sources)
-    cols = out_ref.shape[1]
+def pick_kernel(where_ref, weight_ref, *refs):
+    outs, sems = refs[:-1], refs[-1]
+    heads, cols = where_ref.shape[0] - len(refs[:-1]), outs[0].shape[1]
     copies = []
-    for n, (part, lane) in enumerate(plan):
-        row = pl.multiple_of(where_ref[lane] * 128, 128)
-        column = pl.multiple_of(where_ref[count + part] * cols, cols)
-        copies.append(
-            pltpu.make_async_copy(
-                sources[part].at[pl.ds(row, 128), pl.ds(column, cols)],
-                out_ref.at[pl.ds(n * 128, 128)],
-                sems.at[n],
+    for n, out_ref in enumerate(outs):
+        column = pl.multiple_of(where_ref[heads + n] * cols, cols)
+        for lane in range(heads):
+            row = pl.multiple_of(where_ref[lane] * 128, 128)
+            copies.append(
+                pltpu.make_async_copy(
+                    weight_ref.at[pl.ds(row, 128), pl.ds(column, cols)],
+                    out_ref.at[pl.ds(lane * 128, 128)],
+                    sems.at[len(copies)],
+                )
             )
-        )
     for copy in copies:
         copy.start()
     for copy in copies:
         copy.wait()
 
 
-def pick(heads, weights, columns, groups, cols):
-    plan = [(part, d) for group in groups for part in range(len(weights)) for d in group]
+def pick(heads, weight, columns, cols):
     where = jnp.concatenate([heads, jnp.stack(columns)])
+    shape = jax.ShapeDtypeStruct((weight.shape[0], cols), BF16)
     return pl.pallas_call(
-        functools.partial(pick_kernel, plan),
-        in_specs=[pl.BlockSpec(memory_space=pltpu.SMEM)]
-        + [pl.BlockSpec(memory_space=pl.ANY)] * len(weights),
-        out_specs=pl.BlockSpec(memory_space=pltpu.VMEM),
-        out_shape=jax.ShapeDtypeStruct((128 * len(plan), cols), BF16),
-        scratch_shapes=[pltpu.SemaphoreType.DMA((len(plan),))],
-        compiler_params=pltpu.CompilerParams(vmem_limit_bytes=56 * 1024 * 1024),
+        pick_kernel,
+        in_specs=[pl.BlockSpec(memory_space=pltpu.SMEM), pl.BlockSpec(memory_space=pl.ANY)],
+        out_specs=[pl.BlockSpec(memory_space=pltpu.VMEM)] * len(columns),
+        out_shape=[shape] * len(columns),
+        scratch_shapes=[pltpu.SemaphoreType.DMA((heads.shape[0] * len(columns),))],
+        compiler_params=pltpu.CompilerParams(vmem_limit_bytes=8 * 1024 * 1024),
         cost_estimate=cost(1, 1),
-    )(where, *weights)
+    )(where, pltpu.with_memory_space_constraint(weight, pltpu.HBM))
 
 
 def match(first, count, target):
@@ -472,24 +472,13 @@
     target = target.reshape(ranks, 1, tokens)
 
     cols = out_weight.shape[1] // 4
-    heads = me ^ jnp.arange(ranks, dtype=jnp.int32)
-    across = swap_y(lax.dynamic_slice_in_dim(out_weight, (1 - y) * 2 * cols, 2 * cols, 1))
-    beside = swap_core(
-        lax.dynamic_slice_in_dim(out_weight, (2 * y + 1 - core) * cols, cols, 1)
-    )
-    corner = swap_core(lax.dynamic_slice_in_dim(across, (1 - core) * cols, cols, 1))
-    groups = ((0, 2, 3, 1), (4, 5), (6, 7))
-    zero = jnp.zeros_like(core)
-    weight = pick(
-        heads,
-        [
-            pltpu.with_memory_space_constraint(w, pltpu.HBM)
-            for w in (out_weight, across, beside, corner)
-        ],
-        (mine, core, zero, zero),
-        groups,
-        cols,
-    )
+    heads = me ^ jnp.array(LANES, jnp.int32)
+    far = 2 * (1 - y)
+    corner, across = pick(heads, out_weight, (far + 1 - core, far + core), cols)
+    corner, across = swap_y(corner), swap_y(across)
+    w_own, beside = pick(heads, out_weight, (mine, 2 * y + 1 - core), cols)
+    w_beside, w_corner, w_across = swap_core(beside), swap_core(corner), across
+    values = after(values, w_beside, w_corner)
     rows_v = exchange(after(pack((values,)), first))
 
     def paired(x):
@@ -499,7 +488,7 @@
     weights, means, early = weigh(paired(q_rows), paired(k_rows), paired(at), tokens)
     early = early.reshape(CLUSTERS, cap, 128)
     early, weights = (pltpu.with_memory_space_constraint(x, pltpu.HBM) for x in (early, weights))
-    rows_v = after(rows_v, weight)
+    rows_v = after(rows_v, w_across)
     mixed = mix(target, rows_v, early, weights).reshape(CLUSTERS, cap, 128)
 
     got, sent = {}, {}
@@ -514,44 +503,49 @@
     def side(*blocks):
         return jnp.concatenate([block[:tokens] for block in blocks], axis=1)
 
-    leave(4)
-    go(4)
-    leave(5, sent[4])
-    go(5)
-    leave(0, sent[5])
-    got[0] = sent[0]
-    y_0 = swap_y(got[0])
-    leave(2, sent[0])
-    go(2)
-    leave(3, sent[2])
-    go(3)
-    leave(1, sent[3], y_0)
-    go(1)
-    leave(6, sent[1], got[4])
-    go(6)
-    own_231 = side(*[got[d] for d in (2, 3, 1)])
-    leave(7, sent[6], got[5], own_231)
-    go(7)
+    plan = (4, 2, 0, 3, 1, 5, 6, 7)
+    waits = {5: (0,), 6: (4,), 7: (5, 9)}
+    ends = {}
+    for n, d in enumerate(plan):
+        if d == 7:
+            own_near = side(*[got[d] for d in LANES[1:4]])
+            ends[9] = own_near
+        others = [ends[k] for k in waits.get(d, ())]
+        if n:
+            others = [sent[plan[n - 1]]] + others
+        leave(d, *others)
+        if d:
+            go(d)
+            ends[d] = got[d]
+        else:
+            got[0] = sent[0]
+            y_0 = ends[0] = swap_y(got[0])
     own, there = {}, {}
-    y_231 = swap_y(own_231)
+    y_near = swap_y(own_near)
     own[2] = side(got[4], got[5])
     there[2] = swap_y(own[2])
     own[3] = side(got[6], got[7])
     there[3] = swap_y(own[3])
-    same = {1: side(got[0], own_231, y_0, y_231), 2: side(own[2], there[2])}
-
-    def add(total, left, row):
+    own[1], there[1] = side(got[0], own_near), side(y_0, y_near)
+
+    def add(total, left, weight, row):
         more = jnp.dot(left, weight[row : row + left.shape[1]], preferred_element_type=F32)
         return more if total is None else total + more
 
     total = None
-    for n, row in ((1, 0), (2, 2048)):
-        total = add(total, jnp.concatenate([same[n], swap_core(same[n])], axis=1), row)
-    row = 3072
-    total = add(total, swap_core(own[3]), row + 512)
+    for n, row in ((1, 0), (2, 512)):
+        width = own[n].shape[1]
+        total = add(total, own[n], w_own, row)
+        total = add(total, there[n], w_across, row)
+        moved = swap_core(side(own[n], there[n]))
+        total = add(total, moved[:, :width], w_beside, row)
+        total = add(total, moved[:, width:], w_corner, row)
+    row = 768
+    total = add(total, own[3], w_own, row)
+    total = add(total, swap_core(own[3]), w_beside, row)
     last = swap_core(after(there[3], total))
-    total = add(total, side(own[3], there[3]), row)
-    projected = add(total, last, row + 768).astype(BF16)
+    total = add(total, there[3], w_across, row)
+    projected = add(total, last, w_corner, row).astype(BF16)
 
     tails = jnp.stack([got[d][tokens:] for d in range(ranks)]).astype(F32)
     tails = tails[:, :cl_dev] + tails[:, cl_dev:]

time: 262 us -> 274 us (1.046)
  matrix products: 11.1 us -> 42.1 us
  local copies, waits for them, and re-layouts: 12.6 us -> 5.33 us
  waiting for transfers between devices: 127 us -> 120 us
  starting transfers between devices: 33.9 us -> 29.8 us
    all_to_all x2, waiting for transfers between devices: 85.1 us -> 36.5 us  [exchange(): return lax.all_to_all(x, 'ctx', split_axis=0, concat_axis=0, tiled=True)]
    ppermute x5 -> x6, waiting for transfers between devices: 17.4 us -> 56.1 us  [swap_y(): return lax.ppermute(x, 'head', [(0, 2), (1, 3), (2, 0), (3, 1)])]
    dot_general x5 -> x12, matrix products: 11.1 us -> 42.1 us  [add(): jnp.dot(left, weight[row:row + left.shape[1]], preferred_element_type=F32)]
    dynamic_slice x3 -> x0, local copies, waits for them, and re-layouts: 10.9 us -> none  [the longest x1 4.7 us: head_body(): lax.dynamic_slice_in_dim(out_weight, (1 - y) * 2 * cols, 2 * cols, 1)]
    ppermute x7, waiting for transfers between devices: 18 us -> 24.7 us  [swap_ctx(): return lax.ppermute(x, 'ctx', [(i, i ^ d) for i in range(ranks)])]
    ppermute x7, starting transfers between devices: 15.1 us -> 8.63 us  [swap_ctx(): return lax.ppermute(x, 'ctx', [(i, i ^ d) for i in range(ranks)])]
    unnamed x25 -> x36, local copies, waits for them, and re-layouts: 1 us -> 4.91 us
    ppermute x6, waiting for transfers between devices: 6.47 us -> 2.96 us  [swap_core(): return lax.ppermute(x, 'head', [(0, 1), (1, 0), (2, 3), (3, 2)])]
  transfers between devices with their start and end apart: 20 -> 21, of which waited for: 10 -> 12; matrix products, arithmetic and copies ran while one was open for 9% -> 16% of each run, Pallas kernels for 19% -> 18%
where the time goes in v8:
time: 274 us; the launch traced here: 272 us
  waiting for transfers between devices  120 us (44%)
  Pallas kernels  69 us (25%)
  matrix products  42.1 us (15%)
  starting transfers between devices  29.8 us (11%)
  local copies, waits for them, and re-layouts  5.33 us (2%)
  other arithmetic  4.83 us (2%)
    ppermute x6, waiting for transfers between devices, swap_y(): return lax.ppermute(x, 'head', [(0, 2), (1, 3), (2, 0), (3, 1)])  56.1 us
    dot_general x12, matrix products, add(): jnp.dot(left, weight[row:row + left.shape[1]], preferred_element_type=F32)  42.1 us
    all_to_all x2, waiting for transfers between devices, exchange(): return lax.all_to_all(x, 'ctx', split_axis=0, concat_axis=0, tiled=True)  36.5 us
    ppermute x7, waiting for transfers between devices, swap_ctx(): return lax.ppermute(x, 'ctx', [(i, i ^ d) for i in range(ranks)])  24.7 us
    pallas_call x1, Pallas kernels, place_pair(): pl.pallas_call(place_pair_kernel, grid=(ranks,), in_specs=[pl.BlockSpec((...  19.3 us
    pallas_call x1, Pallas kernels, mix(): pl.pallas_call(functools.partial(mix_kernel, ranks), grid=(2 * ranks,), i...  15.6 us
    pallas_call x1, Pallas kernels, weigh(): pl.pallas_call(functools.partial(weigh_kernel, tokens), grid=(groups // s...  14.8 us
    all_to_all x2, starting transfers between devices, exchange(): return lax.all_to_all(x, 'ctx', split_axis=0, concat_axis=0, tiled=True)  10.9 us
  transfers between devices with their start and end apart: 21, of which 12 were waited for; matrix products, arithmetic and copies ran while one was open for 16% of the time, Pallas kernels for 18%

profile of v8, /device:TPU:0, one launch (start us, length us, event | category | flops | bytes accessed | tf_op | source)
XLA Modules:
  0.0 272.3 jit_solution(5782200660843390549)
XLA Ops:
  2.8 4.4 %shard_map.95 = bf16[8,2064,128]{2,1,0:T(8,128)(2,1)} custom-call(bf16[1024,1024]{1,0:T(8,128)(2,1)} %refs_0_.1, bf16[1024,1024]{1,0:T(8,128)(2,1)} %refs_1_.1, bf16[8,16,128]{2,1,0:T(8,128)(2,1)} %pad_maximum_fusion.4.refs_2_), custom_call_target="tpu_custom_call" | custom-call | bytes 8454144 | tf_op jit(solution)/shard_map/pallas_call | solution.py:198
  7.2 7.3 %all-to-all-start = ((bf16[8,2064,128]{2,1,0:T(8,128)(2,1)}), bf16[8,2064,128]{2,1,0:T(8,128)(2,1)}, u32[]{:S(2)}, u32[]{:S(2)}) async-start(bf16[8,2064,128]{2,1,0:T(8,128)(2,1)} %shard_map.95), calls=%async_computation | async-start | bytes 8454144 | tf_op jit(solution)/shard_map/all_to_all | solution.py:466
  14.5 2.8 %shard_map.97 = (bf16[1024,1024]{1,0:T(8,128)(2,1)S(1)}, bf16[1024,1024]{1,0:T(8,128)(2,1)S(1)}) custom-call(s32[10]{0:T(128)S(1)} %get-tuple-element.52.where_ref, bf16[1024,4096]{1,0:T(8,128)(2,1)} %weight_ref.3), custom_call_target="tpu_custom_call" | custom-call | flops 1 | bytes 1 | tf_op jit(solution)/shard_map/pallas_call | solution.py:237
  20.2 2.8 %shard_map.96 = (bf16[1024,1024]{1,0:T(8,128)(2,1)S(1)}, bf16[1024,1024]{1,0:T(8,128)(2,1)S(1)}) custom-call(s32[10]{0:T(128)S(1)} %get-tuple-element.53.where_ref, bf16[1024,4096]{1,0:T(8,128)(2,1)} %weight_ref.3), custom_call_target="tpu_custom_call" | custom-call | flops 1 | bytes 1 | tf_op jit(solution)/shard_map/pallas_call | solution.py:237
  24.4 41.3 %collective-permute-done.1 = bf16[1024,1024]{1,0:T(8,128)(2,1)S(1)} collective-permute-done((bf16[1024,1024]{1,0:T(8,128)(2,1)S(1)}, bf16[1024,1024]{1,0:T(8,128)(2,1)S(1)}, u32[]{:S(2)}, u32[]{:S(2)}) %collective-permute-start.1) | collective-permute-done | bytes 2097184 | tf_op jit(solution)/shard_map/ppermute | solution.py:454
  67.1 2.9 %collective-permute-done.2 = bf16[1024,1024]{1,0:T(8,128)(2,1)} collective-permute-done((bf16[1024,1024]{1,0:T(8,128)(2,1)S(1)}, bf16[1024,1024]{1,0:T(8,128)(2,1)}, u32[]{:S(2)}, u32[]{:S(2)}) %collective-permute-start.2) | collective-permute-done | bytes 2097184 | tf_op jit(solution)/shard_map/ppermute | solution.py:457
  72.7 35.7 %all-to-all-done.q_ref.k_ref = bf16[8,2064,128]{2,1,0:T(8,128)(2,1)} async-done(((bf16[8,2064,128]{2,1,0:T(8,128)(2,1)}), bf16[8,2064,128]{2,1,0:T(8,128)(2,1)}, u32[]{:S(2)}, u32[]{:S(2)}) %all-to-all-start) | async-done | bytes 4227104 | tf_op jit(solution)/shard_map/all_to_all | solution.py:466
  108.4 3.6 %all-to-all-start.1 = ((bf16[8,1024,128]{2,1,0:T(8,128)(2,1)}), bf16[8,1024,128]{2,1,0:T(8,128)(2,1)S(1)}, u32[]{:S(2)}, u32[]{:S(2)}) async-start(bf16[8,1024,128]{2,1,0:T(8,128)(2,1)} %shard_map.98), calls=%async_computation.1 | async-start | bytes 4194304 | tf_op jit(solution)/shard_map/all_to_all | solution.py:466
  114.4 19.3 %shard_map.99 = (bf16[256,64,128]{2,1,0:T(8,128)(2,1)S(1)}, bf16[256,64,128]{2,1,0:T(8,128)(2,1)S(1)}, f32[256,64,128]{2,1,0:T(8,128)S(1)}) custom-call(s32[8,1,1024]{2,1,0:T(1,128)S(1)} %bitcast.81, bf16[8,2064,128]{2,1,0:T(8,128)(2,1)} %all-to-all-done.q_ref.k_ref, bf16[8,2064,128]{2,1,0:T(8,128)(2,1)} %all-to-all-done.q_ref.k_ref), custom_call_target="tpu_custom_call" | custom-call | flops 1 | bytes 1 | tf_op jit(solution)/shard_map/pallas_call | solution.py:284
  133.7 14.8 %shard_map.100 = (bf16[128,128,128]{2,1,0:T(8,128)(2,1)}, f32[256,128]{1,0:T(8,128)S(1)}, bf16[128,128,128]{2,1,0:T(8,128)(2,1)}) custom-call(bf16[128,128,128]{2,1,0:T(8,128)(2,1)S(1)} %bitcast.79, bf16[128,128,128]{2,1,0:T(8,128)(2,1)S(1)} %bitcast.80, f32[128,128,128]{2,1,0:T(8,128)S(1)} %bitcast.78), custom_call_target="tpu_custom_call" | custom-call | flops 1 | bytes 1 | tf_op jit(solution)/shard_map/pallas_call | solution.py:330
  148.5 11.1 %collective-permute-done.3 = bf16[1024,1024]{1,0:T(8,128)(2,1)} collective-permute-done((bf16[1024,1024]{1,0:T(8,128)(2,1)}, bf16[1024,1024]{1,0:T(8,128)(2,1)}, u32[]{:S(2)}, u32[]{:S(2)}) %collective-permute-start.3) | collective-permute-done | bytes 2097184 | tf_op jit(solution)/shard_map/ppermute | solution.py:454
  160.5 15.6 %shard_map.101 = bf16[128,128,128]{2,1,0:T(8,128)(2,1)S(1)} custom-call(s32[8,1,1024]{2,1,0:T(1,128)S(1)} %bitcast.82, bf16[8,1024,128]{2,1,0:T(8,128)(2,1)S(1)} %all-to-all-done.1.v_ref, bf16[256,64,128]{2,1,0:T(8,128)(2,1)} %bitcast.99, bf16[128,128,128]{2,1,0:T(8,128)(2,1)} %get-tuple-element.33.w_ref), custom_call_target="tpu_custom_call" | custom-call | flops 1 | bytes 1 | tf_op jit(solution)/shard_map/pallas_call | solution.py:388
  194.7 3.7 %collective-permute-done.4 = bf16[1088,128]{1,0:T(8,128)(2,1)S(1)} collective-permute-done((bf16[1088,128]{1,0:T(8,128)(2,1)S(1)}, bf16[1088,128]{1,0:T(8,128)(2,1)S(1)}, u32[]{:S(2)}, u32[]{:S(2)}) %collective-permute-start.4) | collective-permute-done | bytes 278560 | tf_op jit(solution)/shard_map/ppermute | solution.py:463
  198.5 6.5 %collective-permute-done.5 = bf16[1088,128]{1,0:T(8,128)(2,1)S(1)} collective-permute-done((bf16[1088,128]{1,0:T(8,128)(2,1)S(1)}, bf16[1088,128]{1,0:T(8,128)(2,1)S(1)}, u32[]{:S(2)}, u32[]{:S(2)}) %collective-permute-start.5) | collective-permute-done | bytes 278560 | tf_op jit(solution)/shard_map/ppermute | solution.py:463
  206.9 3.2 %fusion.8 = f32[1024,1024]{1,0:T(8,128)} fusion(bf16[1024,128]{1,0:T(8,128)(2,1)S(1)} %get-tuple-element.47, bf16[1024,128]{1,0:T(8,128)(2,1)S(1)} %get-tuple-element.49, bf16[1024,128]{1,0:T(8,128)(2,1)S(1)} %get-tuple-element.51, bf16[1024,128]{1,0:T(8,128)(2,1)S(1)} %slice_bitcast_fusion, bf16[1024,1024]{1,0:T(8,128)(2,1)S(1)} %copy-done.1), kind=kOutput, calls=%fused_computation.10 | convolution fusion | flops 1077936128 | bytes 6291456 | tf_op jit(solution)/shard_map/dot_general | solution.py:532
  210.3 6.5 %collective-permute-done.11 = bf16[1088,128]{1,0:T(8,128)(2,1)S(1)} collective-permute-done((bf16[1088,128]{1,0:T(8,128)(2,1)S(1)}, bf16[1088,128]{1,0:T(8,128)(2,1)S(1)}, u32[]{:S(2)}, u32[]{:S(2)}) %collective-permute-start.11) | collective-permute-done | bytes 278560 | tf_op jit(solution)/shard_map/ppermute | solution.py:463
  220.2 7.7 %collective-permute-done.15 = bf16[1088,128]{1,0:T(8,128)(2,1)S(1)} collective-permute-done((bf16[1088,128]{1,0:T(8,128)(2,1)S(1)}, bf16[1088,128]{1,0:T(8,128)(2,1)S(1)}, u32[]{:S(2)}, u32[]{:S(2)}) %collective-permute-start.15) | collective-permute-done | bytes 278560 | tf_op jit(solution)/shard_map/ppermute | solution.py:463
  233.3 4.5 %fusion.6 = f32[1024,1024]{1,0:T(8,128)} fusion(bf16[1024,1024]{1,0:T(8,128)(2,1)} %collective-permute-done.3, bf16[1024,384]{1,0:T(8,128)(2,1)S(1)} %collective-permute-done.8, bf16[1024,128]{1,0:T(8,128)(2,1)S(1)} %get-tuple-element.44), kind=kOutput, calls=%fused_computation.8 | convolution fusion | flops 1075838976 | bytes 6291456 | tf_op jit(solution)/shard_map/dot_general | solution.py:532
  239.7 3.0 %fusion.26 = f32[1024,1024]{1,0:T(8,128)} fusion(bf16[1024,256]{1,0:T(8,128)(2,1)S(1)} %collective-permute-done.16, bf16[1024,1024]{1,0:T(8,128)(2,1)S(1)} %copy-done.6), kind=kOutput, calls=%fused_computation.28 | convolution fusion | flops 536870912 | bytes 5242880 | tf_op jit(solution)/shard_map/dot_general | solution.py:532
  242.7 2.7 %fusion.30 = f32[1024,1024]{1,0:T(8,128)} fusion(bf16[1024,1024]{1,0:T(8,128)(2,1)S(1)} %copy-done.6, bf16[1024,512]{1,0:T(8,128)(2,1)S(1)} %collective-permute-done.13), kind=kOutput, calls=%fused_computation.32 | convolution fusion | flops 536870912 | bytes 5242880 | tf_op jit(solution)/shard_map/dot_general | solution.py:532
  245.4 3.3 %fusion.3 = f32[1024,1024]{1,0:T(8,128)} fusion(bf16[1024,1024]{1,0:T(8,128)(2,1)S(1)} %copy-done.6, bf16[1024,1024]{1,0:T(8,128)(2,1)S(1)} %collective-permute-done.9), kind=kOutput, calls=%fused_computation.5 | convolution fusion | flops 1073741824 | bytes 6291456 | tf_op jit(solution)/shard_map/dot_general | solution.py:532
  248.7 4.4 %fusion = f32[1024,1024]{1,0:T(8,128)} fusion(bf16[1024,1024]{1,0:T(8,128)(2,1)} %collective-permute-done.2, bf16[1024,1024]{1,0:T(8,128)(2,1)S(1)} %collective-permute-done.9), kind=kOutput, calls=%fused_computation.2 | convolution fusion | flops 1073741824 | bytes 6291456 | tf_op jit(solution)/shard_map/dot_general | solution.py:532
  253.1 12.5 %add_add_fusion = f32[1024,1024]{1,0:T(8,128)} fusion(f32[1024,1024]{1,0:T(8,128)} %fusion.26, f32[1024,1024]{1,0:T(8,128)S(1)} %fusion.35, f32[1024,1024]{1,0:T(8,128)} %fusion.30, f32[1024,1024]{1,0:T(8,128)S(1)} %fusion.33, f32[1024,1024]{1,0:T(8,128)S(1)} %fusion.37, f32[1024,1024]{1,0:T(8,128)} %fusion, f32[1024,1024]{1,0:T(8,128)} %fusion.3, ...), kind=kOutput, calls=%fused_computation.1 | convolution fusion | flops 546308096 | bytes 42991616 | tf_op jit(solution)/shard_map/dot_general | solution.py:532
  269.2 3.1 %add_convert_fusion = bf16[1024,1024]{1,0:T(8,128)(2,1)} fusion(f32[1024,1024]{1,0:T(8,128)S(1)} %copy-done.3, f32[1024,1024]{1,0:T(8,128)S(1)} %fusion.24, bf16[1024,256]{1,0:T(8,128)(2,1)S(1)} %collective-permute-done.18, bf16[1024,1024]{1,0:T(8,128)(2,1)} %collective-permute-done.2), kind=kOutput, calls=%fused_computation | convolution fusion | flops 540016640 | bytes 11534336 | tf_op jit(solution)/shard_map/dot_general | solution.py:532
  (105 shorter events, 48.5 us)
Async XLA Ops:
  7.2 7.3 %copy-start.8 = (s32[8]{0:T(128)S(1)}, s32[8]{0:T(128)}, u32[]{:S(2)}) copy-start(s32[8]{0:T(128)} %constant.52.clone) | copy-start | bytes 100
  7.2 101.3 %all-to-all-start = ((bf16[8,2064,128]{2,1,0:T(8,128)(2,1)}), bf16[8,2064,128]{2,1,0:T(8,128)(2,1)}, u32[]{:S(2)}, u32[]{:S(2)}) async-start(bf16[8,2064,128]{2,1,0:T(8,128)(2,1)} %shard_map.95), calls=%async_computation | async-start | bytes 8454144 | tf_op jit(solution)/shard_map/all_to_all | solution.py:466
  18.7 47.1 %collective-permute-start.1 = (bf16[1024,1024]{1,0:T(8,128)(2,1)S(1)}, bf16[1024,1024]{1,0:T(8,128)(2,1)S(1)}, u32[]{:S(2)}, u32[]{:S(2)}) collective-permute-start(bf16[1024,1024]{1,0:T(8,128)(2,1)S(1)} %get-tuple-element.24), channel_id=1, source_target_pairs={{0,2},{1,3},{2,0},{3,1},{4,6},{5,7},{6,4},{7,5},{8,10},{9,11},{10,... | collective-permute-start | bytes 6291464 | tf_op jit(solution)/shard_map/ppermute | solution.py:454
  24.4 41.3 %collective-permute-start = (bf16[1024,1024]{1,0:T(8,128)(2,1)S(1)}, bf16[1024,1024]{1,0:T(8,128)(2,1)S(1)}, u32[]{:S(2)}, u32[]{:S(2)}) collective-permute-start(bf16[1024,1024]{1,0:T(8,128)(2,1)S(1)} %get-tuple-element.23), channel_id=1, source_target_pairs={{0,1},{1,0},{2,3},{3,2},{4,5},{5,4},{6,7},{7,6},{8,9},{9,8},{10,11... | collective-permute-start | bytes 6291464 | tf_op jit(solution)/shard_map/ppermute | solution.py:457
  65.8 4.3 %collective-permute-start.2 = (bf16[1024,1024]{1,0:T(8,128)(2,1)S(1)}, bf16[1024,1024]{1,0:T(8,128)(2,1)}, u32[]{:S(2)}, u32[]{:S(2)}) collective-permute-start(bf16[1024,1024]{1,0:T(8,128)(2,1)S(1)} %collective-permute-done.1), channel_id=1, source_target_pairs={{0,1},{1,0},{2,3},{3,2},{4,5},{5,4},{6,7},{7,6},{8,9},{9,8},{10,11... | collective-permute-start | bytes 6291464 | tf_op jit(solution)/shard_map/ppermute | solution.py:457
  108.4 52.1 %all-to-all-start.1 = ((bf16[8,1024,128]{2,1,0:T(8,128)(2,1)}), bf16[8,1024,128]{2,1,0:T(8,128)(2,1)S(1)}, u32[]{:S(2)}, u32[]{:S(2)}) async-start(bf16[8,1024,128]{2,1,0:T(8,128)(2,1)} %shard_map.98), calls=%async_computation.1 | async-start | bytes 4194304 | tf_op jit(solution)/shard_map/all_to_all | solution.py:466
  112.1 47.6 %collective-permute-start.3 = (bf16[1024,1024]{1,0:T(8,128)(2,1)}, bf16[1024,1024]{1,0:T(8,128)(2,1)}, u32[]{:S(2)}, u32[]{:S(2)}) collective-permute-start(bf16[1024,1024]{1,0:T(8,128)(2,1)} %copy-done.2), channel_id=1, source_target_pairs={{0,2},{1,3},{2,0},{3,1},{4,6},{5,7},{6,4},{7,5},{8,10},{9,11},{10,... | collective-permute-start | bytes 6291464 | tf_op jit(solution)/shard_map/ppermute | solution.py:454
  176.9 14.5 %collective-permute-start.10 = (bf16[1088,128]{1,0:T(8,128)(2,1)S(1)}, bf16[1088,128]{1,0:T(8,128)(2,1)S(1)}, u32[]{:S(2)}, u32[]{:S(2)}) collective-permute-start(bf16[1088,128]{1,0:T(8,128)(2,1)S(1)} %bitcast.95), channel_id=1, source_target_pairs={{0,16},{4,20},{8,24},{12,28},{16,0},{20,4},{24,8},{28,12},{1,17},{... | collective-permute-start | bytes 835592 | tf_op jit(solution)/shard_map/ppermute | solution.py:463
  179.6 18.8 %collective-permute-start.4 = (bf16[1088,128]{1,0:T(8,128)(2,1)S(1)}, bf16[1088,128]{1,0:T(8,128)(2,1)S(1)}, u32[]{:S(2)}, u32[]{:S(2)}) collective-permute-start(bf16[1088,128]{1,0:T(8,128)(2,1)S(1)} %bitcast.94), channel_id=1, source_target_pairs={{0,8},{4,12},{8,0},{12,4},{16,24},{20,28},{24,16},{28,20},{1,9},{5... | collective-permute-start | bytes 835592 | tf_op jit(solution)/shard_map/ppermute | solution.py:463
  182.0 7.6 %collective-permute-start.7 = (bf16[1088,128]{1,0:T(8,128)(2,1)S(1)}, bf16[1088,128]{1,0:T(8,128)(2,1)S(1)}, u32[]{:S(2)}, u32[]{:S(2)}) collective-permute-start(bf16[1088,128]{1,0:T(8,128)(2,1)S(1)} %bitcast.91), channel_id=1, source_target_pairs={{0,2},{1,3},{2,0},{3,1},{4,6},{5,7},{6,4},{7,5},{8,10},{9,11},{10,... | collective-permute-start | bytes 835592 | tf_op jit(solution)/shard_map/ppermute | solution.py:454
  184.5 20.5 %collective-permute-start.5 = (bf16[1088,128]{1,0:T(8,128)(2,1)S(1)}, bf16[1088,128]{1,0:T(8,128)(2,1)S(1)}, u32[]{:S(2)}, u32[]{:S(2)}) collective-permute-start(bf16[1088,128]{1,0:T(8,128)(2,1)S(1)} %bitcast.97), channel_id=1, source_target_pairs={{0,12},{4,8},{8,4},{12,0},{16,28},{20,24},{24,20},{28,16},{1,13},{... | collective-permute-start | bytes 835592 | tf_op jit(solution)/shard_map/ppermute | solution.py:463
  186.8 18.3 %collective-permute-start.6 = (bf16[1088,128]{1,0:T(8,128)(2,1)S(1)}, bf16[1088,128]{1,0:T(8,128)(2,1)S(1)}, u32[]{:S(2)}, u32[]{:S(2)}) collective-permute-start(bf16[1088,128]{1,0:T(8,128)(2,1)S(1)} %bitcast.96), channel_id=1, source_target_pairs={{0,4},{4,0},{8,12},{12,8},{16,20},{20,16},{24,28},{28,24},{1,5},{5... | collective-permute-start | bytes 835592 | tf_op jit(solution)/shard_map/ppermute | solution.py:463
  190.5 26.3 %collective-permute-start.11 = (bf16[1088,128]{1,0:T(8,128)(2,1)S(1)}, bf16[1088,128]{1,0:T(8,128)(2,1)S(1)}, u32[]{:S(2)}, u32[]{:S(2)}) collective-permute-start(bf16[1088,128]{1,0:T(8,128)(2,1)S(1)} %bitcast.93), channel_id=1, source_target_pairs={{0,20},{4,16},{8,28},{12,24},{16,4},{20,0},{24,12},{28,8},{1,21},{... | collective-permute-start | bytes 835592 | tf_op jit(solution)/shard_map/ppermute | solution.py:463
  192.2 14.7 %copy-start.1 = (bf16[1024,1024]{1,0:T(8,128)(2,1)S(1)}, bf16[1024,1024]{1,0:T(8,128)(2,1)}, u32[]{:S(2)}) copy-start(bf16[1024,1024]{1,0:T(8,128)(2,1)} %copy-done) | copy-start | bytes 6291460
  192.2 27.9 %collective-permute-start.14 = (bf16[1088,128]{1,0:T(8,128)(2,1)S(1)}, bf16[1088,128]{1,0:T(8,128)(2,1)S(1)}, u32[]{:S(2)}, u32[]{:S(2)}) collective-permute-start(bf16[1088,128]{1,0:T(8,128)(2,1)S(1)} %bitcast.92), channel_id=1, source_target_pairs={{0,24},{4,28},{8,16},{12,20},{16,8},{20,12},{24,0},{28,4},{1,25},{... | collective-permute-start | bytes 835592 | tf_op jit(solution)/shard_map/ppermute | solution.py:463
  205.3 25.1 %collective-permute-start.8 = (bf16[1024,384]{1,0:T(8,128)(2,1)S(1)}, bf16[1024,384]{1,0:T(8,128)(2,1)S(1)}, u32[]{:S(2)}, u32[]{:S(2)}) collective-permute-start(bf16[1024,384]{1,0:T(8,128)(2,1)S(1)} %pad_maximum_fusion.1), channel_id=1, source_target_pairs={{0,2},{1,3},{2,0},{3,1},{4,6},{5,7},{6,4},{7,5},{8,10},{9,11},{10,... | collective-permute-start | bytes 2359304 | tf_op jit(solution)/shard_map/ppermute | solution.py:454
  218.4 9.4 %collective-permute-start.15 = (bf16[1088,128]{1,0:T(8,128)(2,1)S(1)}, bf16[1088,128]{1,0:T(8,128)(2,1)S(1)}, u32[]{:S(2)}, u32[]{:S(2)}) collective-permute-start(bf16[1088,128]{1,0:T(8,128)(2,1)S(1)} %bitcast.98), channel_id=1, source_target_pairs={{0,28},{4,24},{8,20},{12,16},{16,12},{20,8},{24,4},{28,0},{1,29},{... | collective-permute-start | bytes 835592 | tf_op jit(solution)/shard_map/ppermute | solution.py:463
  218.5 14.6 %collective-permute-start.12 = (bf16[1024,256]{1,0:T(8,128)(2,1)S(1)}, bf16[1024,256]{1,0:T(8,128)(2,1)S(1)}, u32[]{:S(2)}, u32[]{:S(2)}) collective-permute-start(bf16[1024,256]{1,0:T(8,128)(2,1)S(1)} %pad_maximum_fusion.2), channel_id=1, source_target_pairs={{0,2},{1,3},{2,0},{3,1},{4,6},{5,7},{6,4},{7,5},{8,10},{9,11},{10,... | collective-permute-start | bytes 1572872 | tf_op jit(solution)/shard_map/ppermute | solution.py:454
  228.7 10.9 %collective-permute-start.16 = (bf16[1024,256]{1,0:T(8,128)(2,1)}, bf16[1024,256]{1,0:T(8,128)(2,1)S(1)}, u32[]{:S(2)}, u32[]{:S(2)}) collective-permute-start(bf16[1024,256]{1,0:T(8,128)(2,1)} %pad_maximum_fusion.3), channel_id=1, source_target_pairs={{0,1},{1,0},{2,3},{3,2},{4,5},{5,4},{6,7},{7,6},{8,9},{9,8},{10,11... | collective-permute-start | bytes 1572872 | tf_op jit(solution)/shard_map/ppermute | solution.py:457
  228.7 36.8 %collective-permute-start.17 = (bf16[1024,256]{1,0:T(8,128)(2,1)}, bf16[1024,256]{1,0:T(8,128)(2,1)}, u32[]{:S(2)}, u32[]{:S(2)}) collective-permute-start(bf16[1024,256]{1,0:T(8,128)(2,1)} %pad_maximum_fusion.3), channel_id=1, source_target_pairs={{0,2},{1,3},{2,0},{3,1},{4,6},{5,7},{6,4},{7,5},{8,10},{9,11},{10,... | collective-permute-start | bytes 1572872 | tf_op jit(solution)/shard_map/ppermute | solution.py:454
  230.7 14.7 %collective-permute-start.9 = (bf16[1024,1024]{1,0:T(8,128)(2,1)S(1)}, bf16[1024,1024]{1,0:T(8,128)(2,1)S(1)}, u32[]{:S(2)}, u32[]{:S(2)}) collective-permute-start(bf16[1024,1024]{1,0:T(8,128)(2,1)S(1)} %constant_dynamic-update-slice_fusion), channel_id=1, source_target_pairs={{0,1},{1,0},{2,3},{3,2},{4,5},{5,4},{6,7},{7,6},{8,9},{9,8},{10,11... | collective-permute-start | bytes 6291464 | tf_op jit(solution)/shard_map/ppermute | solution.py:457
  233.2 9.5 %collective-permute-start.13 = (bf16[1024,512]{1,0:T(8,128)(2,1)S(1)}, bf16[1024,512]{1,0:T(8,128)(2,1)S(1)}, u32[]{:S(2)}, u32[]{:S(2)}) collective-permute-start(bf16[1024,512]{1,0:T(8,128)(2,1)S(1)} %pad_maximum_fusion), channel_id=1, source_target_pairs={{0,1},{1,0},{2,3},{3,2},{4,5},{5,4},{6,7},{7,6},{8,9},{9,8},{10,11... | collective-permute-start | bytes 3145736 | tf_op jit(solution)/shard_map/ppermute | solution.py:457
  253.1 13.0 %copy-start.7 = (f32[8,32,128]{2,1,0:T(8,128)S(1)}, f32[8,32,128]{2,1,0:T(8,128)}, u32[]{:S(2)}) copy-start(f32[8,32,128]{2,1,0:T(8,128)} %param.13) | copy-start | bytes 393220
  265.5 3.2 %collective-permute-start.18 = (bf16[1024,256]{1,0:T(8,128)(2,1)}, bf16[1024,256]{1,0:T(8,128)(2,1)S(1)}, u32[]{:S(2)}, u32[]{:S(2)}) collective-permute-start(bf16[1024,256]{1,0:T(8,128)(2,1)} %collective-permute-done.17), channel_id=1, source_target_pairs={{0,1},{1,0},{2,3},{3,2},{4,5},{5,4},{6,7},{7,6},{8,9},{9,8},{10,11... | collective-permute-start | bytes 1572872 | tf_op jit(solution)/shard_map/ppermute | solution.py:457
  (6 other events, 11.2 us)

commit v9 on v8

--- a/solution.py
+++ b/solution.py
@@ -210,18 +210,17 @@
     )(*args)
 
 
-def pick_kernel(where_ref, weight_ref, *refs):
-    outs, sems = refs[:-1], refs[-1]
-    heads, cols = where_ref.shape[0] - len(refs[:-1]), outs[0].shape[1]
+def pick_kernel(count, where_ref, weight_ref, out_ref, sems):
+    heads, cols = where_ref.shape[0] - count, out_ref.shape[1]
     copies = []
-    for n, out_ref in enumerate(outs):
+    for n in range(count):
         column = pl.multiple_of(where_ref[heads + n] * cols, cols)
         for lane in range(heads):
             row = pl.multiple_of(where_ref[lane] * 128, 128)
             copies.append(
                 pltpu.make_async_copy(
                     weight_ref.at[pl.ds(row, 128), pl.ds(column, cols)],
-                    out_ref.at[pl.ds(lane * 128, 128)],
+                    out_ref.at[pl.ds((n * heads + lane) * 128, 128)],
                     sems.at[len(copies)],
                 )
             )
@@ -232,17 +231,49 @@
 
 
 def pick(heads, weight, columns, cols):
+    count = len(columns)
     where = jnp.concatenate([heads, jnp.stack(columns)])
-    shape = jax.ShapeDtypeStruct((weight.shape[0], cols), BF16)
     return pl.pallas_call(
-        pick_kernel,
+        functools.partial(pick_kernel, count),
         in_specs=[pl.BlockSpec(memory_space=pltpu.SMEM), pl.BlockSpec(memory_space=pl.ANY)],
-        out_specs=[pl.BlockSpec(memory_space=pltpu.VMEM)] * len(columns),
-        out_shape=[shape] * len(columns),
-        scratch_shapes=[pltpu.SemaphoreType.DMA((heads.shape[0] * len(columns),))],
-        compiler_params=pltpu.CompilerParams(vmem_limit_bytes=8 * 1024 * 1024),
+        out_specs=pl.BlockSpec(memory_space=pltpu.VMEM),
+        out_shape=pltpu.HBM((count * weight.shape[0], cols), BF16),
+        scratch_shapes=[pltpu.SemaphoreType.DMA((heads.shape[0] * count,))],
+        compiler_params=pltpu.CompilerParams(vmem_limit_bytes=56 * 1024 * 1024),
         cost_estimate=cost(1, 1),
     )(where, pltpu.with_memory_space_constraint(weight, pltpu.HBM))
+
+
+def join_kernel(plan, *refs):
+    sources, out_ref, sems = refs[:-2], refs[-2], refs[-1]
+    copies, row = [], 0
+    for part, first, count in plan:
+        copies.append(
+            pltpu.make_async_copy(
+                sources[part].at[pl.ds(first, count)],
+                out_ref.at[pl.ds(row, count)],
+                sems.at[len(copies)],
+            )
+        )
+        row += count
+    for copy in copies:
+        copy.start()
+    for copy in copies:
+        copy.wait()
+
+
+def join(sources, starts, groups):
+    plan = [(part, at + first, count) for first, count in groups for part, at in enumerate(starts)]
+    rows, cols = sum(count for _, _, count in plan), sources[0].shape[1]
+    return pl.pallas_call(
+        functools.partial(join_kernel, plan),
+        in_specs=[pl.BlockSpec(memory_space=pl.ANY)] * len(sources),
+        out_specs=pl.BlockSpec(memory_space=pltpu.VMEM),
+        out_shape=pltpu.HBM((rows, cols), BF16),
+        scratch_shapes=[pltpu.SemaphoreType.DMA((len(plan),))],
+        compiler_params=pltpu.CompilerParams(vmem_limit_bytes=56 * 1024 * 1024),
+        cost_estimate=cost(1, 1),
+    )(*sources)
 
 
 def match(first, count, target):
@@ -474,11 +505,17 @@
     cols = out_weight.shape[1] // 4
     heads = me ^ jnp.array(LANES, jnp.int32)
     far = 2 * (1 - y)
-    corner, across = pick(heads, out_weight, (far + 1 - core, far + core), cols)
-    corner, across = swap_y(corner), swap_y(across)
-    w_own, beside = pick(heads, out_weight, (mine, 2 * y + 1 - core), cols)
-    w_beside, w_corner, w_across = swap_core(beside), swap_core(corner), across
-    values = after(values, w_beside, w_corner)
+    both = pick(heads, out_weight, (far + 1 - core, far + core), cols)
+    both = swap_y(both)
+    w_own = pick(heads, out_weight, (mine,), cols)
+    beside = pick(heads, out_weight, (2 * y + 1 - core,), cols)
+    beside, corner = swap_core(beside), swap_core(both[: both.shape[0] // 2])
+    values = after(values, beside, w_own)
+    weight = join(
+        (w_own, both, beside, corner),
+        (0, both.shape[0] // 2, 0, 0),
+        ((0, 512), (512, 256), (768, 256)),
+    )
     rows_v = exchange(after(pack((values,)), first))
 
     def paired(x):
@@ -488,7 +525,7 @@
     weights, means, early = weigh(paired(q_rows), paired(k_rows), paired(at), tokens)
     early = early.reshape(CLUSTERS, cap, 128)
     early, weights = (pltpu.with_memory_space_constraint(x, pltpu.HBM) for x in (early, weights))
-    rows_v = after(rows_v, w_across)
+    rows_v = after(rows_v, weight)
     mixed = mix(target, rows_v, early, weights).reshape(CLUSTERS, cap, 128)
 
     got, sent = {}, {}
@@ -526,26 +563,20 @@
     there[2] = swap_y(own[2])
     own[3] = side(got[6], got[7])
     there[3] = swap_y(own[3])
-    own[1], there[1] = side(got[0], own_near), side(y_0, y_near)
-
-    def add(total, left, weight, row):
+    same = {1: side(got[0], own_near, y_0, y_near), 2: side(own[2], there[2])}
+
+    def add(total, left, row):
         more = jnp.dot(left, weight[row : row + left.shape[1]], preferred_element_type=F32)
         return more if total is None else total + more
 
     total = None
-    for n, row in ((1, 0), (2, 512)):
-        width = own[n].shape[1]
-        total = add(total, own[n], w_own, row)
-        total = add(total, there[n], w_across, row)
-        moved = swap_core(side(own[n], there[n]))
-        total = add(total, moved[:, :width], w_beside, row)
-        total = add(total, moved[:, width:], w_corner, row)
-    row = 768
-    total = add(total, own[3], w_own, row)
-    total = add(total, swap_core(own[3]), w_beside, row)
+    for n, row in ((1, 0), (2, 2048)):
+        total = add(total, jnp.concatenate([same[n], swap_core(same[n])], axis=1), row)
+    row = 3072
+    total = add(total, swap_core(own[3]), row + 512)
     last = swap_core(after(there[3], total))
-    total = add(total, there[3], w_across, row)
-    projected = add(total, last, w_corner, row).astype(BF16)
+    total = add(total, side(own[3], there[3]), row)
+    projected = add(total, last, row + 768).astype(BF16)
 
     tails = jnp.stack([got[d][tokens:] for d in range(ranks)]).astype(F32)
     tails = tails[:, :cl_dev] + tails[:, cl_dev:]

time: 274 us -> 255 us (0.931)
  matrix products: 42.1 us -> 11.1 us
  Pallas kernels: 69 us -> 82.1 us
    ppermute x6 -> x5, waiting for transfers between devices: 56.1 us -> 9.98 us  [swap_y(): return lax.ppermute(x, 'head', [(0, 2), (1, 3), (2, 0), (3, 1)])]
    all_to_all x2, waiting for transfers between devices: 36.5 us -> 75.4 us  [exchange(): return lax.all_to_all(x, 'ctx', split_axis=0, concat_axis=0, tiled=True)]
    dot_general x12 -> x5, matrix products: 42.1 us -> 11.1 us  [add(): jnp.dot(left, weight[row:row + left.shape[1]], preferred_element_type=F32)]
    pallas_call x2 -> x4, Pallas kernels: 5.68 us -> 18.8 us  [the longest x3 12.1 us: pick(): pl.pallas_call(functools.partial(pick_kernel, count), in_specs=[pl.BlockS...]
    ppermute x6, waiting for transfers between devices: 2.96 us -> 7.86 us  [swap_core(): return lax.ppermute(x, 'head', [(0, 1), (1, 0), (2, 3), (3, 2)])]
    unnamed x36 -> x27, local copies, waits for them, and re-layouts: 4.91 us -> 1 us
    ppermute x7, starting transfers between devices: 8.63 us -> 12.4 us  [swap_ctx(): return lax.ppermute(x, 'ctx', [(i, i ^ d) for i in range(ranks)])]
    slice x0 -> x1, local copies, waits for them, and re-layouts: none -> 3.09 us  [head_body(): beside, corner = (swap_core(beside), swap_core(both[:both.shape[0] // 2]))]
  transfers between devices with their start and end apart: 21 -> 20, of which waited for: 12 -> 11; matrix products, arithmetic and copies ran while one was open for 16% -> 7% of each run, Pallas kernels for 18% -> 24%
where the time goes in v9:
time: 255 us; the launch traced here: 254 us
  waiting for transfers between devices  118 us (46%)
  Pallas kernels  82.1 us (32%)
  starting transfers between devices  31.7 us (12%)
  matrix products  11.1 us (4%)
  other arithmetic  5.26 us (2%)
  local copies, waits for them, and re-layouts  4.85 us (2%)
    all_to_all x2, waiting for transfers between devices, exchange(): return lax.all_to_all(x, 'ctx', split_axis=0, concat_axis=0, tiled=True)  75.4 us
    ppermute x7, waiting for transfers between devices, swap_ctx(): return lax.ppermute(x, 'ctx', [(i, i ^ d) for i in range(ranks)])  25.1 us
    pallas_call x1, Pallas kernels, place_pair(): pl.pallas_call(place_pair_kernel, grid=(ranks,), in_specs=[pl.BlockSpec((...  19.3 us
    pallas_call x1, Pallas kernels, mix(): pl.pallas_call(functools.partial(mix_kernel, ranks), grid=(2 * ranks,), i...  15.6 us
    pallas_call x1, Pallas kernels, weigh(): pl.pallas_call(functools.partial(weigh_kernel, tokens), grid=(groups // s...  14.8 us
    ppermute x7, starting transfers between devices, swap_ctx(): return lax.ppermute(x, 'ctx', [(i, i ^ d) for i in range(ranks)])  12.4 us
    pallas_call x3, Pallas kernels, pick(): pl.pallas_call(functools.partial(pick_kernel, count), in_specs=[pl.BlockS...  12.1 us
    dot_general x5, matrix products, add(): jnp.dot(left, weight[row:row + left.shape[1]], preferred_element_type=F32)  11.1 us
  transfers between devices with their start and end apart: 20, of which 11 were waited for; matrix products, arithmetic and copies ran while one was open for 7% of the time, Pallas kernels for 24%

profile of v9, /device:TPU:0, one launch (start us, length us, event | category | flops | bytes accessed | tf_op | source)
XLA Modules:
  0.0 254.4 jit_solution(13535952343324047377)
XLA Ops:
  2.8 4.3 %shard_map.95 = bf16[8,2064,128]{2,1,0:T(8,128)(2,1)} custom-call(bf16[1024,1024]{1,0:T(8,128)(2,1)} %refs_0_.1, bf16[1024,1024]{1,0:T(8,128)(2,1)} %refs_1_.1, bf16[8,16,128]{2,1,0:T(8,128)(2,1)} %pad_maximum_fusion.4.refs_2_), custom_call_target="tpu_custom_call" | custom-call | bytes 8454144 | tf_op jit(solution)/shard_map/pallas_call | solution.py:198
  7.1 7.3 %all-to-all-start = ((bf16[8,2064,128]{2,1,0:T(8,128)(2,1)}), bf16[8,2064,128]{2,1,0:T(8,128)(2,1)}, u32[]{:S(2)}, u32[]{:S(2)}) async-start(bf16[8,2064,128]{2,1,0:T(8,128)(2,1)} %shard_map.95), calls=%async_computation | async-start | bytes 8454144 | tf_op jit(solution)/shard_map/all_to_all | solution.py:497
  15.1 4.9 %shard_map.99 = bf16[2048,1024]{1,0:T(8,128)(2,1)} custom-call(s32[10]{0:T(128)} %pad_add_fusion.2.where_ref, bf16[1024,4096]{1,0:T(8,128)(2,1)} %weight_ref.5), custom_call_target="tpu_custom_call" | custom-call | flops 1 | bytes 1 | tf_op jit(solution)/shard_map/pallas_call | solution.py:236
  22.2 3.6 %shard_map.96 = bf16[1024,1024]{1,0:T(8,128)(2,1)} custom-call(s32[9]{0:T(128)} %get-tuple-element.52.where_ref, bf16[1024,4096]{1,0:T(8,128)(2,1)} %weight_ref.5), custom_call_target="tpu_custom_call" | custom-call | flops 1 | bytes 1 | tf_op jit(solution)/shard_map/pallas_call | solution.py:236
  25.8 3.6 %shard_map.97.refs_0_ = bf16[1024,1024]{1,0:T(8,128)(2,1)} custom-call(s32[9]{0:T(128)} %get-tuple-element.51.where_ref, bf16[1024,4096]{1,0:T(8,128)(2,1)} %weight_ref.5), custom_call_target="tpu_custom_call" | custom-call | flops 1 | bytes 1 | tf_op jit(solution)/shard_map/pallas_call | solution.py:236
  30.3 2.7 %shard_map.98 = bf16[8,1024,128]{2,1,0:T(8,128)(2,1)} custom-call(bf16[1024,1024]{1,0:T(8,128)(2,1)} %refs_0_.2), custom_call_target="tpu_custom_call" | custom-call | bytes 4194304 | tf_op jit(solution)/shard_map/pallas_call | solution.py:198
  33.0 75.4 %all-to-all-done.q_ref.k_ref = bf16[8,2064,128]{2,1,0:T(8,128)(2,1)} async-done(((bf16[8,2064,128]{2,1,0:T(8,128)(2,1)}), bf16[8,2064,128]{2,1,0:T(8,128)(2,1)}, u32[]{:S(2)}, u32[]{:S(2)}) %all-to-all-start) | async-done | bytes 4227104 | tf_op jit(solution)/shard_map/all_to_all | solution.py:497
  108.4 3.6 %all-to-all-start.1 = ((bf16[8,1024,128]{2,1,0:T(8,128)(2,1)}), bf16[8,1024,128]{2,1,0:T(8,128)(2,1)S(1)}, u32[]{:S(2)}, u32[]{:S(2)}) async-start(bf16[8,1024,128]{2,1,0:T(8,128)(2,1)} %shard_map.98), calls=%async_computation.1 | async-start | bytes 4194304 | tf_op jit(solution)/shard_map/all_to_all | solution.py:497
  112.4 3.1 %slice.120 = bf16[1024,1024]{1,0:T(8,128)(2,1)} slice(bf16[2048,1024]{1,0:T(8,128)(2,1)} %collective-permute-done.1.refs_1_), slice={[0:1024], [0:1024]} | slice | bytes 4194304 | tf_op jit(solution)/shard_map/slice | solution.py:512
  115.5 4.5 %collective-permute-done.2.refs_3_ = bf16[1024,1024]{1,0:T(8,128)(2,1)} collective-permute-done((bf16[1024,1024]{1,0:T(8,128)(2,1)}, bf16[1024,1024]{1,0:T(8,128)(2,1)}, u32[]{:S(2)}, u32[]{:S(2)}) %collective-permute-start.2) | collective-permute-done | bytes 2097184 | tf_op jit(solution)/shard_map/ppermute | solution.py:488
  120.0 6.7 %shard_map.100 = bf16[4096,1024]{1,0:T(8,128)(2,1)} custom-call(bf16[1024,1024]{1,0:T(8,128)(2,1)} %shard_map.97.refs_0_, bf16[2048,1024]{1,0:T(8,128)(2,1)} %collective-permute-done.1.refs_1_, bf16[1024,1024]{1,0:T(8,128)(2,1)} %collective-permute-done.refs_2_, bf16[1024,1024]{1,0:T(8,128)(2,1)} %collective-permute-done.2.refs_3_), custom_call_target="tpu_custom_call" | custom-call | flops 1 | bytes 1 | tf_op jit(solution)/shard_map/pallas_call | solution.py:268
  127.5 19.3 %shard_map.101 = (bf16[256,64,128]{2,1,0:T(8,128)(2,1)S(1)}, bf16[256,64,128]{2,1,0:T(8,128)(2,1)S(1)}, f32[256,64,128]{2,1,0:T(8,128)S(1)}) custom-call(s32[8,1,1024]{2,1,0:T(1,128)S(1)} %bitcast.82, bf16[8,2064,128]{2,1,0:T(8,128)(2,1)} %all-to-all-done.q_ref.k_ref, bf16[8,2064,128]{2,1,0:T(8,128)(2,1)} %all-to-all-done.q_ref.k_ref), custom_call_target="tpu_custom_call" | custom-call | flops 1 | bytes 1 | tf_op jit(solution)/shard_map/pallas_call | solution.py:315
  146.8 14.8 %shard_map.102 = (bf16[128,128,128]{2,1,0:T(8,128)(2,1)}, f32[256,128]{1,0:T(8,128)S(1)}, bf16[128,128,128]{2,1,0:T(8,128)(2,1)}) custom-call(bf16[128,128,128]{2,1,0:T(8,128)(2,1)S(1)} %bitcast.80, bf16[128,128,128]{2,1,0:T(8,128)(2,1)S(1)} %bitcast.81, f32[128,128,128]{2,1,0:T(8,128)S(1)} %bitcast.79), custom_call_target="tpu_custom_call" | custom-call | flops 1 | bytes 1 | tf_op jit(solution)/shard_map/pallas_call | solution.py:361
  161.6 15.6 %shard_map.103 = bf16[128,128,128]{2,1,0:T(8,128)(2,1)S(1)} custom-call(s32[8,1,1024]{2,1,0:T(1,128)S(1)} %bitcast.83, bf16[8,1024,128]{2,1,0:T(8,128)(2,1)S(1)} %all-to-all-done.1.v_ref, bf16[256,64,128]{2,1,0:T(8,128)(2,1)} %bitcast.102, bf16[128,128,128]{2,1,0:T(8,128)(2,1)} %get-tuple-element.26.w_ref), custom_call_target="tpu_custom_call" | custom-call | flops 1 | bytes 1 | tf_op jit(solution)/shard_map/pallas_call | solution.py:419
  178.0 2.7 %collective-permute-start.9 = (bf16[1088,128]{1,0:T(8,128)(2,1)S(1)}, bf16[1088,128]{1,0:T(8,128)(2,1)S(1)}, u32[]{:S(2)}, u32[]{:S(2)}) collective-permute-start(bf16[1088,128]{1,0:T(8,128)(2,1)S(1)} %bitcast.97), channel_id=1, source_target_pairs={{0,16},{4,20},{8,24},{12,28},{16,0},{20,4},{24,8},{28,12},{1,17},{... | collective-permute-start | bytes 835592 | tf_op jit(solution)/shard_map/ppermute | solution.py:494
  189.5 2.7 %collective-permute-done.6 = bf16[1088,128]{1,0:T(8,128)(2,1)S(1)} collective-permute-done((bf16[1088,128]{1,0:T(8,128)(2,1)S(1)}, bf16[1088,128]{1,0:T(8,128)(2,1)S(1)}, u32[]{:S(2)}, u32[]{:S(2)}) %collective-permute-start.6) | collective-permute-done | bytes 278560 | tf_op jit(solution)/shard_map/ppermute | solution.py:485
  195.3 2.9 %collective-permute-start.13 = (bf16[1088,128]{1,0:T(8,128)(2,1)S(1)}, bf16[1088,128]{1,0:T(8,128)(2,1)S(1)}, u32[]{:S(2)}, u32[]{:S(2)}) collective-permute-start(bf16[1088,128]{1,0:T(8,128)(2,1)S(1)} %bitcast.93), channel_id=1, source_target_pairs={{0,24},{4,28},{8,16},{12,20},{16,8},{20,12},{24,0},{28,4},{1,25},{... | collective-permute-start | bytes 835592 | tf_op jit(solution)/shard_map/ppermute | solution.py:494
  198.5 8.2 %collective-permute-done.4 = bf16[1088,128]{1,0:T(8,128)(2,1)S(1)} collective-permute-done((bf16[1088,128]{1,0:T(8,128)(2,1)S(1)}, bf16[1088,128]{1,0:T(8,128)(2,1)S(1)}, u32[]{:S(2)}, u32[]{:S(2)}) %collective-permute-start.4) | collective-permute-done | bytes 278560 | tf_op jit(solution)/shard_map/ppermute | solution.py:494
  208.9 10.4 %collective-permute-done.10 = bf16[1088,128]{1,0:T(8,128)(2,1)S(1)} collective-permute-done((bf16[1088,128]{1,0:T(8,128)(2,1)S(1)}, bf16[1088,128]{1,0:T(8,128)(2,1)S(1)}, u32[]{:S(2)}, u32[]{:S(2)}) %collective-permute-start.10) | collective-permute-done | bytes 278560 | tf_op jit(solution)/shard_map/ppermute | solution.py:494
  223.5 6.1 %collective-permute-done.14 = bf16[1088,128]{1,0:T(8,128)(2,1)S(1)} collective-permute-done((bf16[1088,128]{1,0:T(8,128)(2,1)S(1)}, bf16[1088,128]{1,0:T(8,128)(2,1)S(1)}, u32[]{:S(2)}, u32[]{:S(2)}) %collective-permute-start.14) | collective-permute-done | bytes 278560 | tf_op jit(solution)/shard_map/ppermute | solution.py:494
  232.3 7.0 %collective-permute-done.11 = bf16[1024,256]{1,0:T(8,128)(2,1)S(1)} collective-permute-done((bf16[1024,256]{1,0:T(8,128)(2,1)S(1)}, bf16[1024,256]{1,0:T(8,128)(2,1)S(1)}, u32[]{:S(2)}, u32[]{:S(2)}) %collective-permute-start.11) | collective-permute-done | bytes 524320 | tf_op jit(solution)/shard_map/ppermute | solution.py:485
  239.6 2.5 collective-permute-done.12
  242.1 2.3 fusion.2
  244.7 4.7 %fusion = f32[1024,1024]{1,0:T(8,128)S(1)} fusion(bf16[1024,2048]{1,0:T(8,128)(2,1)S(1)} %constant_dynamic-update-slice_fusion.4, bf16[4096,1024]{1,0:T(8,128)(2,1)S(1)} %bitcast.101), kind=kOutput, calls=%fused_computation | convolution fusion | flops 4294967296 | bytes 12582912 | tf_op jit(solution)/shard_map/dot_general | solution.py:569
  (91 shorter events, 34.4 us)
Async XLA Ops:
  7.1 7.3 %copy-start.1 = (s32[8]{0:T(128)S(1)}, s32[8]{0:T(128)}, u32[]{:S(2)}) copy-start(s32[8]{0:T(128)} %constant.52.clone) | copy-start | bytes 100
  7.1 101.3 %all-to-all-start = ((bf16[8,2064,128]{2,1,0:T(8,128)(2,1)}), bf16[8,2064,128]{2,1,0:T(8,128)(2,1)}, u32[]{:S(2)}, u32[]{:S(2)}) async-start(bf16[8,2064,128]{2,1,0:T(8,128)(2,1)} %shard_map.95), calls=%async_computation | async-start | bytes 8454144 | tf_op jit(solution)/shard_map/all_to_all | solution.py:497
  20.0 92.4 %collective-permute-start.1 = (bf16[2048,1024]{1,0:T(8,128)(2,1)}, bf16[2048,1024]{1,0:T(8,128)(2,1)}, u32[]{:S(2)}, u32[]{:S(2)}) collective-permute-start(bf16[2048,1024]{1,0:T(8,128)(2,1)} %shard_map.99), channel_id=1, source_target_pairs={{0,2},{1,3},{2,0},{3,1},{4,6},{5,7},{6,4},{7,5},{8,10},{9,11},{10,... | collective-permute-start | bytes 12582920 | tf_op jit(solution)/shard_map/ppermute | solution.py:485
  25.7 4.6 %collective-permute-start = (bf16[1024,1024]{1,0:T(8,128)(2,1)}, bf16[1024,1024]{1,0:T(8,128)(2,1)}, u32[]{:S(2)}, u32[]{:S(2)}) collective-permute-start(bf16[1024,1024]{1,0:T(8,128)(2,1)} %shard_map.96), channel_id=1, source_target_pairs={{0,1},{1,0},{2,3},{3,2},{4,5},{5,4},{6,7},{7,6},{8,9},{9,8},{10,11... | collective-permute-start | bytes 6291464 | tf_op jit(solution)/shard_map/ppermute | solution.py:488
  108.4 53.2 %all-to-all-start.1 = ((bf16[8,1024,128]{2,1,0:T(8,128)(2,1)}), bf16[8,1024,128]{2,1,0:T(8,128)(2,1)S(1)}, u32[]{:S(2)}, u32[]{:S(2)}) async-start(bf16[8,1024,128]{2,1,0:T(8,128)(2,1)} %shard_map.98), calls=%async_computation.1 | async-start | bytes 4194304 | tf_op jit(solution)/shard_map/all_to_all | solution.py:497
  115.5 4.5 %collective-permute-start.2 = (bf16[1024,1024]{1,0:T(8,128)(2,1)}, bf16[1024,1024]{1,0:T(8,128)(2,1)}, u32[]{:S(2)}, u32[]{:S(2)}) collective-permute-start(bf16[1024,1024]{1,0:T(8,128)(2,1)} %slice.120), channel_id=1, source_target_pairs={{0,1},{1,0},{2,3},{3,2},{4,5},{5,4},{6,7},{7,6},{8,9},{9,8},{10,11... | collective-permute-start | bytes 6291464 | tf_op jit(solution)/shard_map/ppermute | solution.py:488
  178.0 16.5 %collective-permute-start.9 = (bf16[1088,128]{1,0:T(8,128)(2,1)S(1)}, bf16[1088,128]{1,0:T(8,128)(2,1)S(1)}, u32[]{:S(2)}, u32[]{:S(2)}) collective-permute-start(bf16[1088,128]{1,0:T(8,128)(2,1)S(1)} %bitcast.97), channel_id=1, source_target_pairs={{0,16},{4,20},{8,24},{12,28},{16,0},{20,4},{24,8},{28,12},{1,17},{... | collective-permute-start | bytes 835592 | tf_op jit(solution)/shard_map/ppermute | solution.py:494
  181.6 16.7 %collective-permute-start.3 = (bf16[1088,128]{1,0:T(8,128)(2,1)S(1)}, bf16[1088,128]{1,0:T(8,128)(2,1)S(1)}, u32[]{:S(2)}, u32[]{:S(2)}) collective-permute-start(bf16[1088,128]{1,0:T(8,128)(2,1)S(1)} %bitcast.95), channel_id=1, source_target_pairs={{0,8},{4,12},{8,0},{12,4},{16,24},{20,28},{24,16},{28,20},{1,9},{5... | collective-permute-start | bytes 835592 | tf_op jit(solution)/shard_map/ppermute | solution.py:494
  183.9 8.2 %collective-permute-start.6 = (bf16[1088,128]{1,0:T(8,128)(2,1)S(1)}, bf16[1088,128]{1,0:T(8,128)(2,1)S(1)}, u32[]{:S(2)}, u32[]{:S(2)}) collective-permute-start(bf16[1088,128]{1,0:T(8,128)(2,1)S(1)} %bitcast.92), channel_id=1, source_target_pairs={{0,2},{1,3},{2,0},{3,1},{4,6},{5,7},{6,4},{7,5},{8,10},{9,11},{10,... | collective-permute-start | bytes 835592 | tf_op jit(solution)/shard_map/ppermute | solution.py:485
  186.5 20.2 %collective-permute-start.4 = (bf16[1088,128]{1,0:T(8,128)(2,1)S(1)}, bf16[1088,128]{1,0:T(8,128)(2,1)S(1)}, u32[]{:S(2)}, u32[]{:S(2)}) collective-permute-start(bf16[1088,128]{1,0:T(8,128)(2,1)S(1)} %bitcast.98), channel_id=1, source_target_pairs={{0,12},{4,8},{8,4},{12,0},{16,28},{20,24},{24,20},{28,16},{1,13},{... | collective-permute-start | bytes 835592 | tf_op jit(solution)/shard_map/ppermute | solution.py:494
  188.8 18.3 %collective-permute-start.5 = (bf16[1088,128]{1,0:T(8,128)(2,1)S(1)}, bf16[1088,128]{1,0:T(8,128)(2,1)S(1)}, u32[]{:S(2)}, u32[]{:S(2)}) collective-permute-start(bf16[1088,128]{1,0:T(8,128)(2,1)S(1)} %bitcast.96), channel_id=1, source_target_pairs={{0,4},{4,0},{8,12},{12,8},{16,20},{20,16},{24,28},{28,24},{1,5},{5... | collective-permute-start | bytes 835592 | tf_op jit(solution)/shard_map/ppermute | solution.py:494
  193.0 26.4 %collective-permute-start.10 = (bf16[1088,128]{1,0:T(8,128)(2,1)S(1)}, bf16[1088,128]{1,0:T(8,128)(2,1)S(1)}, u32[]{:S(2)}, u32[]{:S(2)}) collective-permute-start(bf16[1088,128]{1,0:T(8,128)(2,1)S(1)} %bitcast.94), channel_id=1, source_target_pairs={{0,20},{4,16},{8,28},{12,24},{16,4},{20,0},{24,12},{28,8},{1,21},{... | collective-permute-start | bytes 835592 | tf_op jit(solution)/shard_map/ppermute | solution.py:494
  195.3 28.1 %collective-permute-start.13 = (bf16[1088,128]{1,0:T(8,128)(2,1)S(1)}, bf16[1088,128]{1,0:T(8,128)(2,1)S(1)}, u32[]{:S(2)}, u32[]{:S(2)}) collective-permute-start(bf16[1088,128]{1,0:T(8,128)(2,1)S(1)} %bitcast.93), channel_id=1, source_target_pairs={{0,24},{4,28},{8,16},{12,20},{16,8},{20,12},{24,0},{28,4},{1,25},{... | collective-permute-start | bytes 835592 | tf_op jit(solution)/shard_map/ppermute | solution.py:494
  207.5 22.1 %collective-permute-start.7 = (bf16[1024,384]{1,0:T(8,128)(2,1)S(1)}, bf16[1024,384]{1,0:T(8,128)(2,1)S(1)}, u32[]{:S(2)}, u32[]{:S(2)}) collective-permute-start(bf16[1024,384]{1,0:T(8,128)(2,1)S(1)} %pad_maximum_fusion.1), channel_id=1, source_target_pairs={{0,2},{1,3},{2,0},{3,1},{4,6},{5,7},{6,4},{7,5},{8,10},{9,11},{10,... | collective-permute-start | bytes 2359304 | tf_op jit(solution)/shard_map/ppermute | solution.py:485
  208.7 33.4 %slice-start = ((s8[8388608]{0:T(1024)(128)(4,1)}), s8[4194304]{0:T(1024)(128)(4,1)S(1)}, s32[]{:S(2)}) async-start(s8[8388608]{0:T(1024)(128)(4,1)} %bitcast.100), calls=%async_computation.2 | async-start | bytes 8388608
  220.2 9.4 %collective-permute-start.14 = (bf16[1088,128]{1,0:T(8,128)(2,1)S(1)}, bf16[1088,128]{1,0:T(8,128)(2,1)S(1)}, u32[]{:S(2)}, u32[]{:S(2)}) collective-permute-start(bf16[1088,128]{1,0:T(8,128)(2,1)S(1)} %bitcast.99), channel_id=1, source_target_pairs={{0,28},{4,24},{8,20},{12,16},{16,12},{20,8},{24,4},{28,0},{1,29},{... | collective-permute-start | bytes 835592 | tf_op jit(solution)/shard_map/ppermute | solution.py:494
  221.8 17.4 %collective-permute-start.11 = (bf16[1024,256]{1,0:T(8,128)(2,1)S(1)}, bf16[1024,256]{1,0:T(8,128)(2,1)S(1)}, u32[]{:S(2)}, u32[]{:S(2)}) collective-permute-start(bf16[1024,256]{1,0:T(8,128)(2,1)S(1)} %pad_maximum_fusion.2), channel_id=1, source_target_pairs={{0,2},{1,3},{2,0},{3,1},{4,6},{5,7},{6,4},{7,5},{8,10},{9,11},{10,... | collective-permute-start | bytes 1572872 | tf_op jit(solution)/shard_map/ppermute | solution.py:485
  223.4 18.7 %slice-start.1 = ((s8[8388608]{0:T(1024)(128)(4,1)}), s8[4194304]{0:T(1024)(128)(4,1)S(1)}, s32[]{:S(2)}) async-start(s8[8388608]{0:T(1024)(128)(4,1)} %bitcast.100), calls=%async_computation.3 | async-start | bytes 8388608
  230.1 14.4 %collective-permute-start.8 = (bf16[1024,1024]{1,0:T(8,128)(2,1)S(1)}, bf16[1024,1024]{1,0:T(8,128)(2,1)S(1)}, u32[]{:S(2)}, u32[]{:S(2)}) collective-permute-start(bf16[1024,1024]{1,0:T(8,128)(2,1)S(1)} %get-tuple-element.36), channel_id=1, source_target_pairs={{0,1},{1,0},{2,3},{3,2},{4,5},{5,4},{6,7},{7,6},{8,9},{9,8},{10,11... | collective-permute-start | bytes 6291464 | tf_op jit(solution)/shard_map/ppermute | solution.py:488
  230.2 19.3 %collective-permute-start.15 = (bf16[1024,256]{1,0:T(8,128)(2,1)S(1)}, bf16[1024,256]{1,0:T(8,128)(2,1)S(1)}, u32[]{:S(2)}, u32[]{:S(2)}) collective-permute-start(bf16[1024,256]{1,0:T(8,128)(2,1)S(1)} %pad_maximum_fusion.3), channel_id=1, source_target_pairs={{0,1},{1,0},{2,3},{3,2},{4,5},{5,4},{6,7},{7,6},{8,9},{9,8},{10,11... | collective-permute-start | bytes 1572872 | tf_op jit(solution)/shard_map/ppermute | solution.py:488
  230.8 19.4 %collective-permute-start.16 = (bf16[1024,256]{1,0:T(8,128)(2,1)S(1)}, bf16[1024,256]{1,0:T(8,128)(2,1)S(1)}, u32[]{:S(2)}, u32[]{:S(2)}) collective-permute-start(bf16[1024,256]{1,0:T(8,128)(2,1)S(1)} %pad_maximum_fusion.3), channel_id=1, source_target_pairs={{0,2},{1,3},{2,0},{3,1},{4,6},{5,7},{6,4},{7,5},{8,10},{9,11},{10,... | collective-permute-start | bytes 1572872 | tf_op jit(solution)/shard_map/ppermute | solution.py:485
  239.4 2.7 %collective-permute-start.12 = (bf16[1024,512]{1,0:T(8,128)(2,1)S(1)}, bf16[1024,512]{1,0:T(8,128)(2,1)S(1)}, u32[]{:S(2)}, u32[]{:S(2)}) collective-permute-start(bf16[1024,512]{1,0:T(8,128)(2,1)S(1)} %pad_maximum_fusion), channel_id=1, source_target_pairs={{0,1},{1,0},{2,3},{3,2},{4,5},{5,4},{6,7},{7,6},{8,9},{9,8},{10,11... | collective-permute-start | bytes 3145736 | tf_op jit(solution)/shard_map/ppermute | solution.py:488
  249.4 1.0 copy-start
  250.2 2.1 collective-permute-start.17

commit v10 on v9

--- a/solution.py
+++ b/solution.py
@@ -354,9 +354,8 @@
     mean_out[...] = jnp.sum(both, axis=1) / (2.0 * jnp.maximum(jnp.sum(held, axis=1), 1.0))
 
 
-def weigh(q_rows, k_rows, at, tokens):
+def weigh(q_rows, k_rows, at, tokens, step=16):
     groups, rows = q_rows.shape[0], q_rows.shape[1]
-    step = 8
     spec = pl.BlockSpec((step, rows, 128), lambda i: (i, 0, 0))
     return pl.pallas_call(
         functools.partial(weigh_kernel, tokens),
@@ -372,63 +371,64 @@
             jax.ShapeDtypeStruct((groups * PAIR, 128), F32),
             pltpu.HBM((groups, rows, 128), BF16),
         ],
-        compiler_params=params(12),
+        compiler_params=params(16),
         cost_estimate=cost(1, 1),
     )(q_rows, k_rows, at)
 
 
-def mix_kernel(ranks, target_ref, v_ref, early_ref, w_ref, o_out, v_rows):
+def mix_kernel(steps, target_ref, v_ref, early_ref, w_ref, o_out, v_rows):
     i = pl.program_id(0)
     slots = v_rows.shape[0] * SLOTS
+    senders, tokens = v_ref.shape[0], v_ref.shape[1]
     count, rows = w_ref.shape[0], w_ref.shape[1]
-    tokens = v_ref.shape[1]
     half = tokens // 2
 
-    @pl.when(i < ranks)
+    @pl.when(i < steps)
     def _():
-        target = target_ref[0]
-        picked = match(0, slots, target[:, :half]) | match(0, slots, target[:, half:])
-        both = jnp.concatenate([v_ref[0, :half], v_ref[0, half:]], axis=1)
-        out = jnp.dot(picked.astype(BF16), both, preferred_element_type=F32)
-        early = early_ref[...].astype(F32) > 0.0
-        where = pl.ds(pl.multiple_of(i * SLOTS, SLOTS), SLOTS)
-        v_rows[:, where, :] = jnp.where(early, by_slot(out[:, :128]), by_slot(out[:, 128:]))
-
-    @pl.when(i >= ranks)
+        for n in range(senders):
+            target = target_ref[n]
+            picked = match(0, slots, target[:, :half]) | match(0, slots, target[:, half:])
+            both = jnp.concatenate([v_ref[n, :half], v_ref[n, half:]], axis=1)
+            out = jnp.dot(picked.astype(BF16), both, preferred_element_type=F32)
+            early = early_ref[:, n * SLOTS : (n + 1) * SLOTS].astype(F32) > 0.0
+            where = pl.ds(pl.multiple_of((i * senders + n) * SLOTS, SLOTS), SLOTS)
+            v_rows[:, where, :] = jnp.where(early, by_slot(out[:, :128]), by_slot(out[:, 128:]))
+
+    @pl.when(i >= steps)
     def _():
         ones = jnp.ones((rows, 128), BF16)
         for n in range(count):
-            own = v_rows[pl.ds(((i - ranks) * count + n) * PAIR, PAIR)]
+            own = v_rows[pl.ds(((i - steps) * count + n) * PAIR, PAIR)]
             right = jnp.concatenate([own.reshape(rows, 128).astype(BF16), ones], axis=1)
             out = jnp.dot(w_ref[n], right, preferred_element_type=F32)
             total = out[:, 128:]
             o_out[n] = (out[:, :128] / jnp.where(total > 0.0, total, 1.0)).astype(BF16)
 
 
-def mix(target, rows_v, early, weights):
+def mix(target, rows_v, early, weights, senders=4, count=32):
     ranks, tokens = rows_v.shape[0], rows_v.shape[1]
     groups, rows = weights.shape[0], weights.shape[1]
-    count = groups // ranks
+    steps = ranks // senders
 
     def sender(i):
-        return jnp.minimum(i, ranks - 1)
+        return jnp.minimum(i, steps - 1)
 
     def group(i):
-        return jnp.maximum(i - ranks, 0)
+        return jnp.maximum(i - steps, 0)
 
     return pl.pallas_call(
-        functools.partial(mix_kernel, ranks),
-        grid=(2 * ranks,),
+        functools.partial(mix_kernel, steps),
+        grid=(steps + groups // count,),
         in_specs=[
-            pl.BlockSpec((1, 1, tokens), lambda i: (sender(i), 0, 0)),
-            pl.BlockSpec((1, tokens, 128), lambda i: (sender(i), 0, 0)),
-            pl.BlockSpec((CLUSTERS, SLOTS, 128), lambda i: (0, sender(i), 0)),
+            pl.BlockSpec((senders, 1, tokens), lambda i: (sender(i), 0, 0)),
+            pl.BlockSpec((senders, tokens, 128), lambda i: (sender(i), 0, 0)),
+            pl.BlockSpec((CLUSTERS, senders * SLOTS, 128), lambda i: (0, sender(i), 0)),
             pl.BlockSpec((count, rows, rows), lambda i: (group(i), 0, 0)),
         ],
         out_specs=pl.BlockSpec((count, rows, 128), lambda i: (group(i), 0, 0)),
         out_shape=jax.ShapeDtypeStruct((groups, rows, 128), BF16),
         scratch_shapes=[pltpu.VMEM((CLUSTERS, ranks * SLOTS, 128), F32)],
-        compiler_params=params(20),
+        compiler_params=params(22),
         cost_estimate=cost(1, 1),
     )(target, rows_v, early, weights)
 

time: 255 us -> 252 us (0.988)
  Pallas kernels: 82.1 us -> 78.7 us
where the time goes in v10:
time: 252 us; the launch traced here: 251 us
  waiting for transfers between devices  118 us (47%)
  Pallas kernels  78.7 us (31%)
  starting transfers between devices  31.7 us (13%)
  matrix products  11.1 us (4%)
  other arithmetic  5.22 us (2%)
  local copies, waits for them, and re-layouts  4.82 us (2%)
    all_to_all x2, waiting for transfers between devices, exchange(): return lax.all_to_all(x, 'ctx', split_axis=0, concat_axis=0, tiled=True)  75.4 us
    ppermute x7, waiting for transfers between devices, swap_ctx(): return lax.ppermute(x, 'ctx', [(i, i ^ d) for i in range(ranks)])  25.1 us
    pallas_call x1, Pallas kernels, place_pair(): pl.pallas_call(place_pair_kernel, grid=(ranks,), in_specs=[pl.BlockSpec((...  19.3 us
    pallas_call x1, Pallas kernels, weigh(): pl.pallas_call(functools.partial(weigh_kernel, tokens), grid=(groups // s...  14 us
    pallas_call x1, Pallas kernels, mix(): pl.pallas_call(functools.partial(mix_kernel, steps), grid=(steps + groups...  13 us
    ppermute x7, starting transfers between devices, swap_ctx(): return lax.ppermute(x, 'ctx', [(i, i ^ d) for i in range(ranks)])  12.4 us
    pallas_call x3, Pallas kernels, pick(): pl.pallas_call(functools.partial(pick_kernel, count), in_specs=[pl.BlockS...  12.1 us
    dot_general x5, matrix products, add(): jnp.dot(left, weight[row:row + left.shape[1]], preferred_element_type=F32)  11.1 us
  transfers between devices with their start and end apart: 20, of which 11 were waited for; matrix products, arithmetic and copies ran while one was open for 7% of the time, Pallas kernels for 24%

profile of v10, /device:TPU:0, one launch (start us, length us, event | category | flops | bytes accessed | tf_op | source)
XLA Modules:
  0.0 251.0 jit_solution(7636195328636361001)
XLA Ops:
  2.8 4.3 %shard_map.95 = bf16[8,2064,128]{2,1,0:T(8,128)(2,1)} custom-call(bf16[1024,1024]{1,0:T(8,128)(2,1)} %refs_0_.1, bf16[1024,1024]{1,0:T(8,128)(2,1)} %refs_1_.1, bf16[8,16,128]{2,1,0:T(8,128)(2,1)} %pad_maximum_fusion.4.refs_2_), custom_call_target="tpu_custom_call" | custom-call | bytes 8454144 | tf_op jit(solution)/shard_map/pallas_call | solution.py:198
  7.1 7.3 %all-to-all-start = ((bf16[8,2064,128]{2,1,0:T(8,128)(2,1)}), bf16[8,2064,128]{2,1,0:T(8,128)(2,1)}, u32[]{:S(2)}, u32[]{:S(2)}) async-start(bf16[8,2064,128]{2,1,0:T(8,128)(2,1)} %shard_map.95), calls=%async_computation | async-start | bytes 8454144 | tf_op jit(solution)/shard_map/all_to_all | solution.py:497
  15.1 4.9 %shard_map.99 = bf16[2048,1024]{1,0:T(8,128)(2,1)} custom-call(s32[10]{0:T(128)} %pad_add_fusion.2.where_ref, bf16[1024,4096]{1,0:T(8,128)(2,1)} %weight_ref.5), custom_call_target="tpu_custom_call" | custom-call | flops 1 | bytes 1 | tf_op jit(solution)/shard_map/pallas_call | solution.py:236
  22.2 3.6 %shard_map.96 = bf16[1024,1024]{1,0:T(8,128)(2,1)} custom-call(s32[9]{0:T(128)} %get-tuple-element.52.where_ref, bf16[1024,4096]{1,0:T(8,128)(2,1)} %weight_ref.5), custom_call_target="tpu_custom_call" | custom-call | flops 1 | bytes 1 | tf_op jit(solution)/shard_map/pallas_call | solution.py:236
  25.8 3.6 %shard_map.97.refs_0_ = bf16[1024,1024]{1,0:T(8,128)(2,1)} custom-call(s32[9]{0:T(128)} %get-tuple-element.51.where_ref, bf16[1024,4096]{1,0:T(8,128)(2,1)} %weight_ref.5), custom_call_target="tpu_custom_call" | custom-call | flops 1 | bytes 1 | tf_op jit(solution)/shard_map/pallas_call | solution.py:236
  30.3 2.7 %shard_map.98 = bf16[8,1024,128]{2,1,0:T(8,128)(2,1)} custom-call(bf16[1024,1024]{1,0:T(8,128)(2,1)} %refs_0_.2), custom_call_target="tpu_custom_call" | custom-call | bytes 4194304 | tf_op jit(solution)/shard_map/pallas_call | solution.py:198
  33.0 75.4 %all-to-all-done.q_ref.k_ref = bf16[8,2064,128]{2,1,0:T(8,128)(2,1)} async-done(((bf16[8,2064,128]{2,1,0:T(8,128)(2,1)}), bf16[8,2064,128]{2,1,0:T(8,128)(2,1)}, u32[]{:S(2)}, u32[]{:S(2)}) %all-to-all-start) | async-done | bytes 4227104 | tf_op jit(solution)/shard_map/all_to_all | solution.py:497
  108.4 3.6 %all-to-all-start.1 = ((bf16[8,1024,128]{2,1,0:T(8,128)(2,1)}), bf16[8,1024,128]{2,1,0:T(8,128)(2,1)S(1)}, u32[]{:S(2)}, u32[]{:S(2)}) async-start(bf16[8,1024,128]{2,1,0:T(8,128)(2,1)} %shard_map.98), calls=%async_computation.1 | async-start | bytes 4194304 | tf_op jit(solution)/shard_map/all_to_all | solution.py:497
  112.4 3.1 %slice.120 = bf16[1024,1024]{1,0:T(8,128)(2,1)} slice(bf16[2048,1024]{1,0:T(8,128)(2,1)} %collective-permute-done.1.refs_1_), slice={[0:1024], [0:1024]} | slice | bytes 4194304 | tf_op jit(solution)/shard_map/slice | solution.py:512
  115.5 4.5 %collective-permute-done.2.refs_3_ = bf16[1024,1024]{1,0:T(8,128)(2,1)} collective-permute-done((bf16[1024,1024]{1,0:T(8,128)(2,1)}, bf16[1024,1024]{1,0:T(8,128)(2,1)}, u32[]{:S(2)}, u32[]{:S(2)}) %collective-permute-start.2) | collective-permute-done | bytes 2097184 | tf_op jit(solution)/shard_map/ppermute | solution.py:488
  120.0 6.7 %shard_map.100 = bf16[4096,1024]{1,0:T(8,128)(2,1)} custom-call(bf16[1024,1024]{1,0:T(8,128)(2,1)} %shard_map.97.refs_0_, bf16[2048,1024]{1,0:T(8,128)(2,1)} %collective-permute-done.1.refs_1_, bf16[1024,1024]{1,0:T(8,128)(2,1)} %collective-permute-done.refs_2_, bf16[1024,1024]{1,0:T(8,128)(2,1)} %collective-permute-done.2.refs_3_), custom_call_target="tpu_custom_call" | custom-call | flops 1 | bytes 1 | tf_op jit(solution)/shard_map/pallas_call | solution.py:268
  127.5 19.3 %shard_map.101 = (bf16[256,64,128]{2,1,0:T(8,128)(2,1)S(1)}, bf16[256,64,128]{2,1,0:T(8,128)(2,1)S(1)}, f32[256,64,128]{2,1,0:T(8,128)S(1)}) custom-call(s32[8,1,1024]{2,1,0:T(1,128)S(1)} %bitcast.82, bf16[8,2064,128]{2,1,0:T(8,128)(2,1)} %all-to-all-done.q_ref.k_ref, bf16[8,2064,128]{2,1,0:T(8,128)(2,1)} %all-to-all-done.q_ref.k_ref), custom_call_target="tpu_custom_call" | custom-call | flops 1 | bytes 1 | tf_op jit(solution)/shard_map/pallas_call | solution.py:315
  146.8 14.0 %shard_map.102 = (bf16[128,128,128]{2,1,0:T(8,128)(2,1)}, f32[256,128]{1,0:T(8,128)S(1)}, bf16[128,128,128]{2,1,0:T(8,128)(2,1)}) custom-call(bf16[128,128,128]{2,1,0:T(8,128)(2,1)S(1)} %bitcast.80, bf16[128,128,128]{2,1,0:T(8,128)(2,1)S(1)} %bitcast.81, f32[128,128,128]{2,1,0:T(8,128)S(1)} %bitcast.79), custom_call_target="tpu_custom_call" | custom-call | flops 1 | bytes 1 | tf_op jit(solution)/shard_map/pallas_call | solution.py:360
  160.8 13.0 %shard_map.103 = bf16[128,128,128]{2,1,0:T(8,128)(2,1)S(1)} custom-call(s32[8,1,1024]{2,1,0:T(1,128)S(1)} %bitcast.83, bf16[8,1024,128]{2,1,0:T(8,128)(2,1)S(1)} %all-to-all-done.1.v_ref, bf16[256,64,128]{2,1,0:T(8,128)(2,1)} %bitcast.102, bf16[128,128,128]{2,1,0:T(8,128)(2,1)} %get-tuple-element.26.w_ref), custom_call_target="tpu_custom_call" | custom-call | flops 1 | bytes 1 | tf_op jit(solution)/shard_map/pallas_call | solution.py:419
  174.7 2.7 %collective-permute-start.9 = (bf16[1088,128]{1,0:T(8,128)(2,1)S(1)}, bf16[1088,128]{1,0:T(8,128)(2,1)S(1)}, u32[]{:S(2)}, u32[]{:S(2)}) collective-permute-start(bf16[1088,128]{1,0:T(8,128)(2,1)S(1)} %bitcast.97), channel_id=1, source_target_pairs={{0,16},{4,20},{8,24},{12,28},{16,0},{20,4},{24,8},{28,12},{1,17},{... | collective-permute-start | bytes 835592 | tf_op jit(solution)/shard_map/ppermute | solution.py:494
  186.1 2.7 %collective-permute-done.6 = bf16[1088,128]{1,0:T(8,128)(2,1)S(1)} collective-permute-done((bf16[1088,128]{1,0:T(8,128)(2,1)S(1)}, bf16[1088,128]{1,0:T(8,128)(2,1)S(1)}, u32[]{:S(2)}, u32[]{:S(2)}) %collective-permute-start.6) | collective-permute-done | bytes 278560 | tf_op jit(solution)/shard_map/ppermute | solution.py:485
  192.0 2.9 %collective-permute-start.13 = (bf16[1088,128]{1,0:T(8,128)(2,1)S(1)}, bf16[1088,128]{1,0:T(8,128)(2,1)S(1)}, u32[]{:S(2)}, u32[]{:S(2)}) collective-permute-start(bf16[1088,128]{1,0:T(8,128)(2,1)S(1)} %bitcast.93), channel_id=1, source_target_pairs={{0,24},{4,28},{8,16},{12,20},{16,8},{20,12},{24,0},{28,4},{1,25},{... | collective-permute-start | bytes 835592 | tf_op jit(solution)/shard_map/ppermute | solution.py:494
  195.1 8.2 %collective-permute-done.4 = bf16[1088,128]{1,0:T(8,128)(2,1)S(1)} collective-permute-done((bf16[1088,128]{1,0:T(8,128)(2,1)S(1)}, bf16[1088,128]{1,0:T(8,128)(2,1)S(1)}, u32[]{:S(2)}, u32[]{:S(2)}) %collective-permute-start.4) | collective-permute-done | bytes 278560 | tf_op jit(solution)/shard_map/ppermute | solution.py:494
  205.6 10.4 %collective-permute-done.10 = bf16[1088,128]{1,0:T(8,128)(2,1)S(1)} collective-permute-done((bf16[1088,128]{1,0:T(8,128)(2,1)S(1)}, bf16[1088,128]{1,0:T(8,128)(2,1)S(1)}, u32[]{:S(2)}, u32[]{:S(2)}) %collective-permute-start.10) | collective-permute-done | bytes 278560 | tf_op jit(solution)/shard_map/ppermute | solution.py:494
  220.1 6.1 %collective-permute-done.14 = bf16[1088,128]{1,0:T(8,128)(2,1)S(1)} collective-permute-done((bf16[1088,128]{1,0:T(8,128)(2,1)S(1)}, bf16[1088,128]{1,0:T(8,128)(2,1)S(1)}, u32[]{:S(2)}, u32[]{:S(2)}) %collective-permute-start.14) | collective-permute-done | bytes 278560 | tf_op jit(solution)/shard_map/ppermute | solution.py:494
  229.0 7.0 %collective-permute-done.11 = bf16[1024,256]{1,0:T(8,128)(2,1)S(1)} collective-permute-done((bf16[1024,256]{1,0:T(8,128)(2,1)S(1)}, bf16[1024,256]{1,0:T(8,128)(2,1)S(1)}, u32[]{:S(2)}, u32[]{:S(2)}) %collective-permute-start.11) | collective-permute-done | bytes 524320 | tf_op jit(solution)/shard_map/ppermute | solution.py:485
  236.3 2.5 collective-permute-done.12
  238.7 2.3 fusion.2
  241.3 4.7 %fusion = f32[1024,1024]{1,0:T(8,128)S(1)} fusion(bf16[1024,2048]{1,0:T(8,128)(2,1)S(1)} %constant_dynamic-update-slice_fusion.4, bf16[4096,1024]{1,0:T(8,128)(2,1)S(1)} %bitcast.101), kind=kOutput, calls=%fused_computation | convolution fusion | flops 4294967296 | bytes 12582912 | tf_op jit(solution)/shard_map/dot_general | solution.py:569
  (91 shorter events, 34.4 us)
Async XLA Ops:
  7.1 7.3 %copy-start.1 = (s32[8]{0:T(128)S(1)}, s32[8]{0:T(128)}, u32[]{:S(2)}) copy-start(s32[8]{0:T(128)} %constant.52.clone) | copy-start | bytes 100
  7.1 101.3 %all-to-all-start = ((bf16[8,2064,128]{2,1,0:T(8,128)(2,1)}), bf16[8,2064,128]{2,1,0:T(8,128)(2,1)}, u32[]{:S(2)}, u32[]{:S(2)}) async-start(bf16[8,2064,128]{2,1,0:T(8,128)(2,1)} %shard_map.95), calls=%async_computation | async-start | bytes 8454144 | tf_op jit(solution)/shard_map/all_to_all | solution.py:497
  20.0 92.4 %collective-permute-start.1 = (bf16[2048,1024]{1,0:T(8,128)(2,1)}, bf16[2048,1024]{1,0:T(8,128)(2,1)}, u32[]{:S(2)}, u32[]{:S(2)}) collective-permute-start(bf16[2048,1024]{1,0:T(8,128)(2,1)} %shard_map.99), channel_id=1, source_target_pairs={{0,2},{1,3},{2,0},{3,1},{4,6},{5,7},{6,4},{7,5},{8,10},{9,11},{10,... | collective-permute-start | bytes 12582920 | tf_op jit(solution)/shard_map/ppermute | solution.py:485
  25.7 4.6 %collective-permute-start = (bf16[1024,1024]{1,0:T(8,128)(2,1)}, bf16[1024,1024]{1,0:T(8,128)(2,1)}, u32[]{:S(2)}, u32[]{:S(2)}) collective-permute-start(bf16[1024,1024]{1,0:T(8,128)(2,1)} %shard_map.96), channel_id=1, source_target_pairs={{0,1},{1,0},{2,3},{3,2},{4,5},{5,4},{6,7},{7,6},{8,9},{9,8},{10,11... | collective-permute-start | bytes 6291464 | tf_op jit(solution)/shard_map/ppermute | solution.py:488
  108.4 52.4 %all-to-all-start.1 = ((bf16[8,1024,128]{2,1,0:T(8,128)(2,1)}), bf16[8,1024,128]{2,1,0:T(8,128)(2,1)S(1)}, u32[]{:S(2)}, u32[]{:S(2)}) async-start(bf16[8,1024,128]{2,1,0:T(8,128)(2,1)} %shard_map.98), calls=%async_computation.1 | async-start | bytes 4194304 | tf_op jit(solution)/shard_map/all_to_all | solution.py:497
  115.5 4.5 %collective-permute-start.2 = (bf16[1024,1024]{1,0:T(8,128)(2,1)}, bf16[1024,1024]{1,0:T(8,128)(2,1)}, u32[]{:S(2)}, u32[]{:S(2)}) collective-permute-start(bf16[1024,1024]{1,0:T(8,128)(2,1)} %slice.120), channel_id=1, source_target_pairs={{0,1},{1,0},{2,3},{3,2},{4,5},{5,4},{6,7},{7,6},{8,9},{9,8},{10,11... | collective-permute-start | bytes 6291464 | tf_op jit(solution)/shard_map/ppermute | solution.py:488
  174.7 16.5 %collective-permute-start.9 = (bf16[1088,128]{1,0:T(8,128)(2,1)S(1)}, bf16[1088,128]{1,0:T(8,128)(2,1)S(1)}, u32[]{:S(2)}, u32[]{:S(2)}) collective-permute-start(bf16[1088,128]{1,0:T(8,128)(2,1)S(1)} %bitcast.97), channel_id=1, source_target_pairs={{0,16},{4,20},{8,24},{12,28},{16,0},{20,4},{24,8},{28,12},{1,17},{... | collective-permute-start | bytes 835592 | tf_op jit(solution)/shard_map/ppermute | solution.py:494
  178.2 16.7 %collective-permute-start.3 = (bf16[1088,128]{1,0:T(8,128)(2,1)S(1)}, bf16[1088,128]{1,0:T(8,128)(2,1)S(1)}, u32[]{:S(2)}, u32[]{:S(2)}) collective-permute-start(bf16[1088,128]{1,0:T(8,128)(2,1)S(1)} %bitcast.95), channel_id=1, source_target_pairs={{0,8},{4,12},{8,0},{12,4},{16,24},{20,28},{24,16},{28,20},{1,9},{5... | collective-permute-start | bytes 835592 | tf_op jit(solution)/shard_map/ppermute | solution.py:494
  180.6 8.2 %collective-permute-start.6 = (bf16[1088,128]{1,0:T(8,128)(2,1)S(1)}, bf16[1088,128]{1,0:T(8,128)(2,1)S(1)}, u32[]{:S(2)}, u32[]{:S(2)}) collective-permute-start(bf16[1088,128]{1,0:T(8,128)(2,1)S(1)} %bitcast.92), channel_id=1, source_target_pairs={{0,2},{1,3},{2,0},{3,1},{4,6},{5,7},{6,4},{7,5},{8,10},{9,11},{10,... | collective-permute-start | bytes 835592 | tf_op jit(solution)/shard_map/ppermute | solution.py:485
  183.1 20.2 %collective-permute-start.4 = (bf16[1088,128]{1,0:T(8,128)(2,1)S(1)}, bf16[1088,128]{1,0:T(8,128)(2,1)S(1)}, u32[]{:S(2)}, u32[]{:S(2)}) collective-permute-start(bf16[1088,128]{1,0:T(8,128)(2,1)S(1)} %bitcast.98), channel_id=1, source_target_pairs={{0,12},{4,8},{8,4},{12,0},{16,28},{20,24},{24,20},{28,16},{1,13},{... | collective-permute-start | bytes 835592 | tf_op jit(solution)/shard_map/ppermute | solution.py:494
  185.5 18.3 %collective-permute-start.5 = (bf16[1088,128]{1,0:T(8,128)(2,1)S(1)}, bf16[1088,128]{1,0:T(8,128)(2,1)S(1)}, u32[]{:S(2)}, u32[]{:S(2)}) collective-permute-start(bf16[1088,128]{1,0:T(8,128)(2,1)S(1)} %bitcast.96), channel_id=1, source_target_pairs={{0,4},{4,0},{8,12},{12,8},{16,20},{20,16},{24,28},{28,24},{1,5},{5... | collective-permute-start | bytes 835592 | tf_op jit(solution)/shard_map/ppermute | solution.py:494
  189.6 26.4 %collective-permute-start.10 = (bf16[1088,128]{1,0:T(8,128)(2,1)S(1)}, bf16[1088,128]{1,0:T(8,128)(2,1)S(1)}, u32[]{:S(2)}, u32[]{:S(2)}) collective-permute-start(bf16[1088,128]{1,0:T(8,128)(2,1)S(1)} %bitcast.94), channel_id=1, source_target_pairs={{0,20},{4,16},{8,28},{12,24},{16,4},{20,0},{24,12},{28,8},{1,21},{... | collective-permute-start | bytes 835592 | tf_op jit(solution)/shard_map/ppermute | solution.py:494
  192.0 28.1 %collective-permute-start.13 = (bf16[1088,128]{1,0:T(8,128)(2,1)S(1)}, bf16[1088,128]{1,0:T(8,128)(2,1)S(1)}, u32[]{:S(2)}, u32[]{:S(2)}) collective-permute-start(bf16[1088,128]{1,0:T(8,128)(2,1)S(1)} %bitcast.93), channel_id=1, source_target_pairs={{0,24},{4,28},{8,16},{12,20},{16,8},{20,12},{24,0},{28,4},{1,25},{... | collective-permute-start | bytes 835592 | tf_op jit(solution)/shard_map/ppermute | solution.py:494
  204.1 22.1 %collective-permute-start.7 = (bf16[1024,384]{1,0:T(8,128)(2,1)S(1)}, bf16[1024,384]{1,0:T(8,128)(2,1)S(1)}, u32[]{:S(2)}, u32[]{:S(2)}) collective-permute-start(bf16[1024,384]{1,0:T(8,128)(2,1)S(1)} %pad_maximum_fusion.1), channel_id=1, source_target_pairs={{0,2},{1,3},{2,0},{3,1},{4,6},{5,7},{6,4},{7,5},{8,10},{9,11},{10,... | collective-permute-start | bytes 2359304 | tf_op jit(solution)/shard_map/ppermute | solution.py:485
  205.3 33.4 %slice-start = ((s8[8388608]{0:T(1024)(128)(4,1)}), s8[4194304]{0:T(1024)(128)(4,1)S(1)}, s32[]{:S(2)}) async-start(s8[8388608]{0:T(1024)(128)(4,1)} %bitcast.100), calls=%async_computation.2 | async-start | bytes 8388608
  216.8 9.4 %collective-permute-start.14 = (bf16[1088,128]{1,0:T(8,128)(2,1)S(1)}, bf16[1088,128]{1,0:T(8,128)(2,1)S(1)}, u32[]{:S(2)}, u32[]{:S(2)}) collective-permute-start(bf16[1088,128]{1,0:T(8,128)(2,1)S(1)} %bitcast.99), channel_id=1, source_target_pairs={{0,28},{4,24},{8,20},{12,16},{16,12},{20,8},{24,4},{28,0},{1,29},{... | collective-permute-start | bytes 835592 | tf_op jit(solution)/shard_map/ppermute | solution.py:494
  218.5 17.5 %collective-permute-start.11 = (bf16[1024,256]{1,0:T(8,128)(2,1)S(1)}, bf16[1024,256]{1,0:T(8,128)(2,1)S(1)}, u32[]{:S(2)}, u32[]{:S(2)}) collective-permute-start(bf16[1024,256]{1,0:T(8,128)(2,1)S(1)} %pad_maximum_fusion.2), channel_id=1, source_target_pairs={{0,2},{1,3},{2,0},{3,1},{4,6},{5,7},{6,4},{7,5},{8,10},{9,11},{10,... | collective-permute-start | bytes 1572872 | tf_op jit(solution)/shard_map/ppermute | solution.py:485
  220.0 18.7 %slice-start.1 = ((s8[8388608]{0:T(1024)(128)(4,1)}), s8[4194304]{0:T(1024)(128)(4,1)S(1)}, s32[]{:S(2)}) async-start(s8[8388608]{0:T(1024)(128)(4,1)} %bitcast.100), calls=%async_computation.3 | async-start | bytes 8388608
  226.7 14.4 %collective-permute-start.8 = (bf16[1024,1024]{1,0:T(8,128)(2,1)S(1)}, bf16[1024,1024]{1,0:T(8,128)(2,1)S(1)}, u32[]{:S(2)}, u32[]{:S(2)}) collective-permute-start(bf16[1024,1024]{1,0:T(8,128)(2,1)S(1)} %get-tuple-element.36), channel_id=1, source_target_pairs={{0,1},{1,0},{2,3},{3,2},{4,5},{5,4},{6,7},{7,6},{8,9},{9,8},{10,11... | collective-permute-start | bytes 6291464 | tf_op jit(solution)/shard_map/ppermute | solution.py:488
  226.8 19.2 %collective-permute-start.15 = (bf16[1024,256]{1,0:T(8,128)(2,1)S(1)}, bf16[1024,256]{1,0:T(8,128)(2,1)S(1)}, u32[]{:S(2)}, u32[]{:S(2)}) collective-permute-start(bf16[1024,256]{1,0:T(8,128)(2,1)S(1)} %pad_maximum_fusion.3), channel_id=1, source_target_pairs={{0,1},{1,0},{2,3},{3,2},{4,5},{5,4},{6,7},{7,6},{8,9},{9,8},{10,11... | collective-permute-start | bytes 1572872 | tf_op jit(solution)/shard_map/ppermute | solution.py:488
  227.4 19.4 %collective-permute-start.16 = (bf16[1024,256]{1,0:T(8,128)(2,1)S(1)}, bf16[1024,256]{1,0:T(8,128)(2,1)S(1)}, u32[]{:S(2)}, u32[]{:S(2)}) collective-permute-start(bf16[1024,256]{1,0:T(8,128)(2,1)S(1)} %pad_maximum_fusion.3), channel_id=1, source_target_pairs={{0,2},{1,3},{2,0},{3,1},{4,6},{5,7},{6,4},{7,5},{8,10},{9,11},{10,... | collective-permute-start | bytes 1572872 | tf_op jit(solution)/shard_map/ppermute | solution.py:485
  236.0 2.7 %collective-permute-start.12 = (bf16[1024,512]{1,0:T(8,128)(2,1)S(1)}, bf16[1024,512]{1,0:T(8,128)(2,1)S(1)}, u32[]{:S(2)}, u32[]{:S(2)}) collective-permute-start(bf16[1024,512]{1,0:T(8,128)(2,1)S(1)} %pad_maximum_fusion), channel_id=1, source_target_pairs={{0,1},{1,0},{2,3},{3,2},{4,5},{5,4},{6,7},{7,6},{8,9},{9,8},{10,11... | collective-permute-start | bytes 3145736 | tf_op jit(solution)/shard_map/ppermute | solution.py:488
  246.0 1.0 copy-start
  246.8 2.1 collective-permute-start.17

commit v11 on v10

--- a/solution.py
+++ b/solution.py
@@ -147,7 +147,7 @@
 
 def pack_kernel(count, marked, *refs):
     sources = refs[:count]
-    out_ref, held, sems_in, sems_out = refs[count + marked :]
+    out_ref, held, wide, marks, sems_in, sems_out = refs[count + 2 * marked :]
     heads = out_ref.shape[0]
     tokens = sources[0].shape[0]
     parts = 2
@@ -165,9 +165,14 @@
         copy.start()
     writes = []
     if marked:
-        marks_ref = refs[count]
-        there = out_ref.at[:, pl.ds(count * tokens, marks_ref.shape[1])]
-        writes.append(pltpu.make_async_copy(marks_ref, there, sems_out.at[0]))
+        lines = marks.shape[1] // 2
+        for n in range(2):
+            mark = refs[count + n][...].astype(F32)
+            for line in range(lines):
+                wide[:, n * lines + line, :] = mark[:, line * 128 : (line + 1) * 128]
+        marks[...] = wide[...].astype(BF16)
+        there = out_ref.at[:, pl.ds(count * tokens, 2 * lines)]
+        writes.append(pltpu.make_async_copy(marks, there, sems_out.at[0]))
         writes[0].start()
     for n in range(count):
         for p in range(parts):
@@ -184,16 +189,17 @@
         copy.wait()
 
 
-def pack(sources, marks=None):
+def pack(sources, marks=()):
     tokens, width = sources[0].shape
     heads, count = width // 128, len(sources)
-    marked = marks is not None
-    rows = count * tokens + (marks.shape[1] if marked else 0)
+    marked = len(marks) > 0
+    lines = len(marks) * (tokens // 128)
+    rows = count * tokens + lines
     anywhere = pl.BlockSpec(memory_space=pl.ANY)
     args = list(sources)
     in_specs = [anywhere] * count
-    if marked:
-        args.append(marks)
+    for mark in marks:
+        args.append(mark)
         in_specs.append(pl.BlockSpec(memory_space=pltpu.VMEM))
     return pl.pallas_call(
         functools.partial(pack_kernel, count, marked),
@@ -202,6 +208,8 @@
         out_shape=pltpu.HBM((heads, rows, 128), BF16),
         scratch_shapes=[
             pltpu.VMEM((count, tokens, width), BF16),
+            pltpu.VMEM((heads, max(lines, 16), 128), F32),
+            pltpu.VMEM((heads, max(lines, 16), 128), BF16),
             pltpu.SemaphoreType.DMA((2 * count,)),
             pltpu.SemaphoreType.DMA((2 * count * heads + 1,)),
         ],
@@ -496,8 +504,7 @@
     def exchange(x):
         return lax.all_to_all(x, "ctx", split_axis=0, concat_axis=0, tiled=True)
 
-    marks = [x.astype(BF16).reshape(ranks, tokens // 128, 128) for x in (cluster_of, slot_of)]
-    first = exchange(pack((queries, keys), jnp.concatenate(marks, axis=1)))
+    first = exchange(pack((queries, keys), (cluster_of, slot_of)))
     marks = first[:, 2 * tokens :, :].astype(jnp.int32)
     target = marks[:, : tokens // 128, :] * SLOTS + marks[:, tokens // 128 :, :]
     target = target.reshape(ranks, 1, tokens)

time: 252 us -> 249 us (0.988)
  no operation moved by 1% of the time
where the time goes in v11:
time: 249 us
  waiting for transfers between devices  118 us (47%)
  Pallas kernels  78.8 us (32%)
  starting transfers between devices  31.7 us (13%)
  matrix products  11 us (4%)
  local copies, waits for them, and re-layouts  4.82 us (2%)
  other arithmetic  3.09 us (1%)
    all_to_all x2, waiting for transfers between devices, exchange(): return lax.all_to_all(x, 'ctx', split_axis=0, concat_axis=0, tiled=True)  75.4 us
    ppermute x7, waiting for transfers between devices, swap_ctx(): return lax.ppermute(x, 'ctx', [(i, i ^ d) for i in range(ranks)])  25.1 us
    pallas_call x1, Pallas kernels, place_pair(): pl.pallas_call(place_pair_kernel, grid=(ranks,), in_specs=[pl.BlockSpec((...  19.3 us
    pallas_call x1, Pallas kernels, weigh(): pl.pallas_call(functools.partial(weigh_kernel, tokens), grid=(groups // s...  14 us
    pallas_call x1, Pallas kernels, mix(): pl.pallas_call(functools.partial(mix_kernel, steps), grid=(steps + groups...  13 us
    ppermute x7, starting transfers between devices, swap_ctx(): return lax.ppermute(x, 'ctx', [(i, i ^ d) for i in range(ranks)])  12.4 us
    pallas_call x3, Pallas kernels, pick(): pl.pallas_call(functools.partial(pick_kernel, count), in_specs=[pl.BlockS...  12.1 us
    dot_general x5, matrix products, add(): jnp.dot(left, weight[row:row + left.shape[1]], preferred_element_type=F32)  11 us
  transfers between devices with their start and end apart: 20, of which 11 were waited for; matrix products, arithmetic and copies ran while one was open for 7% of the time, Pallas kernels for 24%

profile of v11, /device:TPU:0, one launch (start us, length us, event | category | flops | bytes accessed | tf_op | source)
XLA Modules:
  0.0 248.8 jit_solution(13815696274288302619)
XLA Ops:
  0.6 4.3 %shard_map.95 = bf16[8,2064,128]{2,1,0:T(8,128)(2,1)} custom-call(bf16[1024,1024]{1,0:T(8,128)(2,1)} %refs_0_.1, bf16[1024,1024]{1,0:T(8,128)(2,1)} %refs_1_.1, s32[8,1024]{1,0:T(8,128)} %refs_2_.1, s32[8,1024]{1,0:T(8,128)} %refs_3_.1), custom_call_target="tpu_custom_call" | custom-call | bytes 8454144 | tf_op jit(solution)/shard_map/pallas_call | solution.py:204
  5.0 7.3 %all-to-all-start = ((bf16[8,2064,128]{2,1,0:T(8,128)(2,1)}), bf16[8,2064,128]{2,1,0:T(8,128)(2,1)}, u32[]{:S(2)}, u32[]{:S(2)}) async-start(bf16[8,2064,128]{2,1,0:T(8,128)(2,1)} %shard_map.95), calls=%async_computation | async-start | bytes 8454144 | tf_op jit(solution)/shard_map/all_to_all | solution.py:505
  12.9 4.9 %shard_map.99 = bf16[2048,1024]{1,0:T(8,128)(2,1)} custom-call(s32[10]{0:T(128)} %pad_add_fusion.2.where_ref, bf16[1024,4096]{1,0:T(8,128)(2,1)} %weight_ref.5), custom_call_target="tpu_custom_call" | custom-call | flops 1 | bytes 1 | tf_op jit(solution)/shard_map/pallas_call | solution.py:244
  20.0 3.6 %shard_map.96 = bf16[1024,1024]{1,0:T(8,128)(2,1)} custom-call(s32[9]{0:T(128)} %get-tuple-element.52.where_ref, bf16[1024,4096]{1,0:T(8,128)(2,1)} %weight_ref.5), custom_call_target="tpu_custom_call" | custom-call | flops 1 | bytes 1 | tf_op jit(solution)/shard_map/pallas_call | solution.py:244
  23.7 3.6 %shard_map.97.refs_0_ = bf16[1024,1024]{1,0:T(8,128)(2,1)} custom-call(s32[9]{0:T(128)} %get-tuple-element.51.where_ref, bf16[1024,4096]{1,0:T(8,128)(2,1)} %weight_ref.5), custom_call_target="tpu_custom_call" | custom-call | flops 1 | bytes 1 | tf_op jit(solution)/shard_map/pallas_call | solution.py:244
  28.2 2.7 %shard_map.98 = bf16[8,1024,128]{2,1,0:T(8,128)(2,1)} custom-call(bf16[1024,1024]{1,0:T(8,128)(2,1)} %refs_0_.2), custom_call_target="tpu_custom_call" | custom-call | bytes 4194304 | tf_op jit(solution)/shard_map/pallas_call | solution.py:204
  30.9 75.4 %all-to-all-done.q_ref.k_ref = bf16[8,2064,128]{2,1,0:T(8,128)(2,1)} async-done(((bf16[8,2064,128]{2,1,0:T(8,128)(2,1)}), bf16[8,2064,128]{2,1,0:T(8,128)(2,1)}, u32[]{:S(2)}, u32[]{:S(2)}) %all-to-all-start) | async-done | bytes 4227104 | tf_op jit(solution)/shard_map/all_to_all | solution.py:505
  106.2 3.6 %all-to-all-start.1 = ((bf16[8,1024,128]{2,1,0:T(8,128)(2,1)}), bf16[8,1024,128]{2,1,0:T(8,128)(2,1)S(1)}, u32[]{:S(2)}, u32[]{:S(2)}) async-start(bf16[8,1024,128]{2,1,0:T(8,128)(2,1)} %shard_map.98), calls=%async_computation.1 | async-start | bytes 4194304 | tf_op jit(solution)/shard_map/all_to_all | solution.py:505
  110.3 3.1 %slice.120 = bf16[1024,1024]{1,0:T(8,128)(2,1)} slice(bf16[2048,1024]{1,0:T(8,128)(2,1)} %collective-permute-done.1.refs_1_), slice={[0:1024], [0:1024]} | slice | bytes 4194304 | tf_op jit(solution)/shard_map/slice | solution.py:519
  113.4 4.5 %collective-permute-done.2.refs_3_ = bf16[1024,1024]{1,0:T(8,128)(2,1)} collective-permute-done((bf16[1024,1024]{1,0:T(8,128)(2,1)}, bf16[1024,1024]{1,0:T(8,128)(2,1)}, u32[]{:S(2)}, u32[]{:S(2)}) %collective-permute-start.2) | collective-permute-done | bytes 2097184 | tf_op jit(solution)/shard_map/ppermute | solution.py:496
  117.9 6.7 %shard_map.100 = bf16[4096,1024]{1,0:T(8,128)(2,1)} custom-call(bf16[1024,1024]{1,0:T(8,128)(2,1)} %shard_map.97.refs_0_, bf16[2048,1024]{1,0:T(8,128)(2,1)} %collective-permute-done.1.refs_1_, bf16[1024,1024]{1,0:T(8,128)(2,1)} %collective-permute-done.refs_2_, bf16[1024,1024]{1,0:T(8,128)(2,1)} %collective-permute-done.2.refs_3_), custom_call_target="tpu_custom_call" | custom-call | flops 1 | bytes 1 | tf_op jit(solution)/shard_map/pallas_call | solution.py:276
  125.4 19.3 %shard_map.101 = (bf16[256,64,128]{2,1,0:T(8,128)(2,1)S(1)}, bf16[256,64,128]{2,1,0:T(8,128)(2,1)S(1)}, f32[256,64,128]{2,1,0:T(8,128)S(1)}) custom-call(s32[8,1,1024]{2,1,0:T(1,128)S(1)} %bitcast.74, bf16[8,2064,128]{2,1,0:T(8,128)(2,1)} %all-to-all-done.q_ref.k_ref, bf16[8,2064,128]{2,1,0:T(8,128)(2,1)} %all-to-all-done.q_ref.k_ref), custom_call_target="tpu_custom_call" | custom-call | flops 1 | bytes 1 | tf_op jit(solution)/shard_map/pallas_call | solution.py:323
  144.7 14.0 %shard_map.102 = (bf16[128,128,128]{2,1,0:T(8,128)(2,1)}, f32[256,128]{1,0:T(8,128)S(1)}, bf16[128,128,128]{2,1,0:T(8,128)(2,1)}) custom-call(bf16[128,128,128]{2,1,0:T(8,128)(2,1)S(1)} %bitcast.72, bf16[128,128,128]{2,1,0:T(8,128)(2,1)S(1)} %bitcast.73, f32[128,128,128]{2,1,0:T(8,128)S(1)} %bitcast.71), custom_call_target="tpu_custom_call" | custom-call | flops 1 | bytes 1 | tf_op jit(solution)/shard_map/pallas_call | solution.py:368
  158.7 13.0 %shard_map.103 = bf16[128,128,128]{2,1,0:T(8,128)(2,1)S(1)} custom-call(s32[8,1,1024]{2,1,0:T(1,128)S(1)} %bitcast.75, bf16[8,1024,128]{2,1,0:T(8,128)(2,1)S(1)} %all-to-all-done.1.v_ref, bf16[256,64,128]{2,1,0:T(8,128)(2,1)} %bitcast.94, bf16[128,128,128]{2,1,0:T(8,128)(2,1)} %get-tuple-element.26.w_ref), custom_call_target="tpu_custom_call" | custom-call | flops 1 | bytes 1 | tf_op jit(solution)/shard_map/pallas_call | solution.py:427
  172.6 2.7 %collective-permute-start.9 = (bf16[1088,128]{1,0:T(8,128)(2,1)S(1)}, bf16[1088,128]{1,0:T(8,128)(2,1)S(1)}, u32[]{:S(2)}, u32[]{:S(2)}) collective-permute-start(bf16[1088,128]{1,0:T(8,128)(2,1)S(1)} %bitcast.89), channel_id=1, source_target_pairs={{0,16},{4,20},{8,24},{12,28},{16,0},{20,4},{24,8},{28,12},{1,17},{... | collective-permute-start | bytes 835592 | tf_op jit(solution)/shard_map/ppermute | solution.py:502
  184.0 2.7 %collective-permute-done.6 = bf16[1088,128]{1,0:T(8,128)(2,1)S(1)} collective-permute-done((bf16[1088,128]{1,0:T(8,128)(2,1)S(1)}, bf16[1088,128]{1,0:T(8,128)(2,1)S(1)}, u32[]{:S(2)}, u32[]{:S(2)}) %collective-permute-start.6) | collective-permute-done | bytes 278560 | tf_op jit(solution)/shard_map/ppermute | solution.py:493
  189.9 2.9 %collective-permute-start.13 = (bf16[1088,128]{1,0:T(8,128)(2,1)S(1)}, bf16[1088,128]{1,0:T(8,128)(2,1)S(1)}, u32[]{:S(2)}, u32[]{:S(2)}) collective-permute-start(bf16[1088,128]{1,0:T(8,128)(2,1)S(1)} %bitcast.85), channel_id=1, source_target_pairs={{0,24},{4,28},{8,16},{12,20},{16,8},{20,12},{24,0},{28,4},{1,25},{... | collective-permute-start | bytes 835592 | tf_op jit(solution)/shard_map/ppermute | solution.py:502
  193.0 8.2 %collective-permute-done.4 = bf16[1088,128]{1,0:T(8,128)(2,1)S(1)} collective-permute-done((bf16[1088,128]{1,0:T(8,128)(2,1)S(1)}, bf16[1088,128]{1,0:T(8,128)(2,1)S(1)}, u32[]{:S(2)}, u32[]{:S(2)}) %collective-permute-start.4) | collective-permute-done | bytes 278560 | tf_op jit(solution)/shard_map/ppermute | solution.py:502
  203.5 10.4 %collective-permute-done.10 = bf16[1088,128]{1,0:T(8,128)(2,1)S(1)} collective-permute-done((bf16[1088,128]{1,0:T(8,128)(2,1)S(1)}, bf16[1088,128]{1,0:T(8,128)(2,1)S(1)}, u32[]{:S(2)}, u32[]{:S(2)}) %collective-permute-start.10) | collective-permute-done | bytes 278560 | tf_op jit(solution)/shard_map/ppermute | solution.py:502
  218.0 6.2 %collective-permute-done.14 = bf16[1088,128]{1,0:T(8,128)(2,1)S(1)} collective-permute-done((bf16[1088,128]{1,0:T(8,128)(2,1)S(1)}, bf16[1088,128]{1,0:T(8,128)(2,1)S(1)}, u32[]{:S(2)}, u32[]{:S(2)}) %collective-permute-start.14) | collective-permute-done | bytes 278560 | tf_op jit(solution)/shard_map/ppermute | solution.py:502
  226.8 6.9 %collective-permute-done.11 = bf16[1024,256]{1,0:T(8,128)(2,1)S(1)} collective-permute-done((bf16[1024,256]{1,0:T(8,128)(2,1)S(1)}, bf16[1024,256]{1,0:T(8,128)(2,1)S(1)}, u32[]{:S(2)}, u32[]{:S(2)}) %collective-permute-start.11) | collective-permute-done | bytes 524320 | tf_op jit(solution)/shard_map/ppermute | solution.py:493
  234.1 2.5 collective-permute-done.12
  236.6 2.3 fusion.2
  239.2 4.7 %fusion = f32[1024,1024]{1,0:T(8,128)S(1)} fusion(bf16[1024,2048]{1,0:T(8,128)(2,1)S(1)} %constant_dynamic-update-slice_fusion.4, bf16[4096,1024]{1,0:T(8,128)(2,1)S(1)} %bitcast.93), kind=kOutput, calls=%fused_computation | convolution fusion | flops 4294967296 | bytes 12582912 | tf_op jit(solution)/shard_map/dot_general | solution.py:576
  (87 shorter events, 32.2 us)
Async XLA Ops:
  5.0 7.3 %copy-start.1 = (s32[8]{0:T(128)S(1)}, s32[8]{0:T(128)}, u32[]{:S(2)}) copy-start(s32[8]{0:T(128)} %constant.52.clone) | copy-start | bytes 100
  5.0 101.3 %all-to-all-start = ((bf16[8,2064,128]{2,1,0:T(8,128)(2,1)}), bf16[8,2064,128]{2,1,0:T(8,128)(2,1)}, u32[]{:S(2)}, u32[]{:S(2)}) async-start(bf16[8,2064,128]{2,1,0:T(8,128)(2,1)} %shard_map.95), calls=%async_computation | async-start | bytes 8454144 | tf_op jit(solution)/shard_map/all_to_all | solution.py:505
  17.8 92.4 %collective-permute-start.1 = (bf16[2048,1024]{1,0:T(8,128)(2,1)}, bf16[2048,1024]{1,0:T(8,128)(2,1)}, u32[]{:S(2)}, u32[]{:S(2)}) collective-permute-start(bf16[2048,1024]{1,0:T(8,128)(2,1)} %shard_map.99), channel_id=1, source_target_pairs={{0,2},{1,3},{2,0},{3,1},{4,6},{5,7},{6,4},{7,5},{8,10},{9,11},{10,... | collective-permute-start | bytes 12582920 | tf_op jit(solution)/shard_map/ppermute | solution.py:493
  23.6 4.6 %collective-permute-start = (bf16[1024,1024]{1,0:T(8,128)(2,1)}, bf16[1024,1024]{1,0:T(8,128)(2,1)}, u32[]{:S(2)}, u32[]{:S(2)}) collective-permute-start(bf16[1024,1024]{1,0:T(8,128)(2,1)} %shard_map.96), channel_id=1, source_target_pairs={{0,1},{1,0},{2,3},{3,2},{4,5},{5,4},{6,7},{7,6},{8,9},{9,8},{10,11... | collective-permute-start | bytes 6291464 | tf_op jit(solution)/shard_map/ppermute | solution.py:496
  106.2 52.4 %all-to-all-start.1 = ((bf16[8,1024,128]{2,1,0:T(8,128)(2,1)}), bf16[8,1024,128]{2,1,0:T(8,128)(2,1)S(1)}, u32[]{:S(2)}, u32[]{:S(2)}) async-start(bf16[8,1024,128]{2,1,0:T(8,128)(2,1)} %shard_map.98), calls=%async_computation.1 | async-start | bytes 4194304 | tf_op jit(solution)/shard_map/all_to_all | solution.py:505
  113.4 4.5 %collective-permute-start.2 = (bf16[1024,1024]{1,0:T(8,128)(2,1)}, bf16[1024,1024]{1,0:T(8,128)(2,1)}, u32[]{:S(2)}, u32[]{:S(2)}) collective-permute-start(bf16[1024,1024]{1,0:T(8,128)(2,1)} %slice.120), channel_id=1, source_target_pairs={{0,1},{1,0},{2,3},{3,2},{4,5},{5,4},{6,7},{7,6},{8,9},{9,8},{10,11... | collective-permute-start | bytes 6291464 | tf_op jit(solution)/shard_map/ppermute | solution.py:496
  172.6 16.5 %collective-permute-start.9 = (bf16[1088,128]{1,0:T(8,128)(2,1)S(1)}, bf16[1088,128]{1,0:T(8,128)(2,1)S(1)}, u32[]{:S(2)}, u32[]{:S(2)}) collective-permute-start(bf16[1088,128]{1,0:T(8,128)(2,1)S(1)} %bitcast.89), channel_id=1, source_target_pairs={{0,16},{4,20},{8,24},{12,28},{16,0},{20,4},{24,8},{28,12},{1,17},{... | collective-permute-start | bytes 835592 | tf_op jit(solution)/shard_map/ppermute | solution.py:502
  176.1 16.7 %collective-permute-start.3 = (bf16[1088,128]{1,0:T(8,128)(2,1)S(1)}, bf16[1088,128]{1,0:T(8,128)(2,1)S(1)}, u32[]{:S(2)}, u32[]{:S(2)}) collective-permute-start(bf16[1088,128]{1,0:T(8,128)(2,1)S(1)} %bitcast.87), channel_id=1, source_target_pairs={{0,8},{4,12},{8,0},{12,4},{16,24},{20,28},{24,16},{28,20},{1,9},{5... | collective-permute-start | bytes 835592 | tf_op jit(solution)/shard_map/ppermute | solution.py:502
  178.5 8.2 %collective-permute-start.6 = (bf16[1088,128]{1,0:T(8,128)(2,1)S(1)}, bf16[1088,128]{1,0:T(8,128)(2,1)S(1)}, u32[]{:S(2)}, u32[]{:S(2)}) collective-permute-start(bf16[1088,128]{1,0:T(8,128)(2,1)S(1)} %bitcast.84), channel_id=1, source_target_pairs={{0,2},{1,3},{2,0},{3,1},{4,6},{5,7},{6,4},{7,5},{8,10},{9,11},{10,... | collective-permute-start | bytes 835592 | tf_op jit(solution)/shard_map/ppermute | solution.py:493
  181.0 20.2 %collective-permute-start.4 = (bf16[1088,128]{1,0:T(8,128)(2,1)S(1)}, bf16[1088,128]{1,0:T(8,128)(2,1)S(1)}, u32[]{:S(2)}, u32[]{:S(2)}) collective-permute-start(bf16[1088,128]{1,0:T(8,128)(2,1)S(1)} %bitcast.90), channel_id=1, source_target_pairs={{0,12},{4,8},{8,4},{12,0},{16,28},{20,24},{24,20},{28,16},{1,13},{... | collective-permute-start | bytes 835592 | tf_op jit(solution)/shard_map/ppermute | solution.py:502
  183.4 18.3 %collective-permute-start.5 = (bf16[1088,128]{1,0:T(8,128)(2,1)S(1)}, bf16[1088,128]{1,0:T(8,128)(2,1)S(1)}, u32[]{:S(2)}, u32[]{:S(2)}) collective-permute-start(bf16[1088,128]{1,0:T(8,128)(2,1)S(1)} %bitcast.88), channel_id=1, source_target_pairs={{0,4},{4,0},{8,12},{12,8},{16,20},{20,16},{24,28},{28,24},{1,5},{5... | collective-permute-start | bytes 835592 | tf_op jit(solution)/shard_map/ppermute | solution.py:502
  187.5 26.4 %collective-permute-start.10 = (bf16[1088,128]{1,0:T(8,128)(2,1)S(1)}, bf16[1088,128]{1,0:T(8,128)(2,1)S(1)}, u32[]{:S(2)}, u32[]{:S(2)}) collective-permute-start(bf16[1088,128]{1,0:T(8,128)(2,1)S(1)} %bitcast.86), channel_id=1, source_target_pairs={{0,20},{4,16},{8,28},{12,24},{16,4},{20,0},{24,12},{28,8},{1,21},{... | collective-permute-start | bytes 835592 | tf_op jit(solution)/shard_map/ppermute | solution.py:502
  189.9 28.1 %collective-permute-start.13 = (bf16[1088,128]{1,0:T(8,128)(2,1)S(1)}, bf16[1088,128]{1,0:T(8,128)(2,1)S(1)}, u32[]{:S(2)}, u32[]{:S(2)}) collective-permute-start(bf16[1088,128]{1,0:T(8,128)(2,1)S(1)} %bitcast.85), channel_id=1, source_target_pairs={{0,24},{4,28},{8,16},{12,20},{16,8},{20,12},{24,0},{28,4},{1,25},{... | collective-permute-start | bytes 835592 | tf_op jit(solution)/shard_map/ppermute | solution.py:502
  202.0 22.1 %collective-permute-start.7 = (bf16[1024,384]{1,0:T(8,128)(2,1)S(1)}, bf16[1024,384]{1,0:T(8,128)(2,1)S(1)}, u32[]{:S(2)}, u32[]{:S(2)}) collective-permute-start(bf16[1024,384]{1,0:T(8,128)(2,1)S(1)} %pad_maximum_fusion.1), channel_id=1, source_target_pairs={{0,2},{1,3},{2,0},{3,1},{4,6},{5,7},{6,4},{7,5},{8,10},{9,11},{10,... | collective-permute-start | bytes 2359304 | tf_op jit(solution)/shard_map/ppermute | solution.py:493
  203.2 33.4 %slice-start = ((s8[8388608]{0:T(1024)(128)(4,1)}), s8[4194304]{0:T(1024)(128)(4,1)S(1)}, s32[]{:S(2)}) async-start(s8[8388608]{0:T(1024)(128)(4,1)} %bitcast.92), calls=%async_computation.2 | async-start | bytes 8388608
  214.7 9.4 %collective-permute-start.14 = (bf16[1088,128]{1,0:T(8,128)(2,1)S(1)}, bf16[1088,128]{1,0:T(8,128)(2,1)S(1)}, u32[]{:S(2)}, u32[]{:S(2)}) collective-permute-start(bf16[1088,128]{1,0:T(8,128)(2,1)S(1)} %bitcast.91), channel_id=1, source_target_pairs={{0,28},{4,24},{8,20},{12,16},{16,12},{20,8},{24,4},{28,0},{1,29},{... | collective-permute-start | bytes 835592 | tf_op jit(solution)/shard_map/ppermute | solution.py:502
  216.3 17.4 %collective-permute-start.11 = (bf16[1024,256]{1,0:T(8,128)(2,1)S(1)}, bf16[1024,256]{1,0:T(8,128)(2,1)S(1)}, u32[]{:S(2)}, u32[]{:S(2)}) collective-permute-start(bf16[1024,256]{1,0:T(8,128)(2,1)S(1)} %pad_maximum_fusion.2), channel_id=1, source_target_pairs={{0,2},{1,3},{2,0},{3,1},{4,6},{5,7},{6,4},{7,5},{8,10},{9,11},{10,... | collective-permute-start | bytes 1572872 | tf_op jit(solution)/shard_map/ppermute | solution.py:493
  217.9 18.7 %slice-start.1 = ((s8[8388608]{0:T(1024)(128)(4,1)}), s8[4194304]{0:T(1024)(128)(4,1)S(1)}, s32[]{:S(2)}) async-start(s8[8388608]{0:T(1024)(128)(4,1)} %bitcast.92), calls=%async_computation.3 | async-start | bytes 8388608
  224.6 14.4 %collective-permute-start.8 = (bf16[1024,1024]{1,0:T(8,128)(2,1)S(1)}, bf16[1024,1024]{1,0:T(8,128)(2,1)S(1)}, u32[]{:S(2)}, u32[]{:S(2)}) collective-permute-start(bf16[1024,1024]{1,0:T(8,128)(2,1)S(1)} %get-tuple-element.36), channel_id=1, source_target_pairs={{0,1},{1,0},{2,3},{3,2},{4,5},{5,4},{6,7},{7,6},{8,9},{9,8},{10,11... | collective-permute-start | bytes 6291464 | tf_op jit(solution)/shard_map/ppermute | solution.py:496
  224.7 19.2 %collective-permute-start.15 = (bf16[1024,256]{1,0:T(8,128)(2,1)S(1)}, bf16[1024,256]{1,0:T(8,128)(2,1)S(1)}, u32[]{:S(2)}, u32[]{:S(2)}) collective-permute-start(bf16[1024,256]{1,0:T(8,128)(2,1)S(1)} %pad_maximum_fusion.3), channel_id=1, source_target_pairs={{0,1},{1,0},{2,3},{3,2},{4,5},{5,4},{6,7},{7,6},{8,9},{9,8},{10,11... | collective-permute-start | bytes 1572872 | tf_op jit(solution)/shard_map/ppermute | solution.py:496
  225.3 19.4 %collective-permute-start.16 = (bf16[1024,256]{1,0:T(8,128)(2,1)S(1)}, bf16[1024,256]{1,0:T(8,128)(2,1)S(1)}, u32[]{:S(2)}, u32[]{:S(2)}) collective-permute-start(bf16[1024,256]{1,0:T(8,128)(2,1)S(1)} %pad_maximum_fusion.3), channel_id=1, source_target_pairs={{0,2},{1,3},{2,0},{3,1},{4,6},{5,7},{6,4},{7,5},{8,10},{9,11},{10,... | collective-permute-start | bytes 1572872 | tf_op jit(solution)/shard_map/ppermute | solution.py:493
  233.9 2.7 %collective-permute-start.12 = (bf16[1024,512]{1,0:T(8,128)(2,1)S(1)}, bf16[1024,512]{1,0:T(8,128)(2,1)S(1)}, u32[]{:S(2)}, u32[]{:S(2)}) collective-permute-start(bf16[1024,512]{1,0:T(8,128)(2,1)S(1)} %pad_maximum_fusion), channel_id=1, source_target_pairs={{0,1},{1,0},{2,3},{3,2},{4,5},{5,4},{6,7},{7,6},{8,9},{9,8},{10,11... | collective-permute-start | bytes 3145736 | tf_op jit(solution)/shard_map/ppermute | solution.py:496
  243.9 1.0 copy-start
  244.7 2.1 collective-permute-start.17

commit v12 on v11

--- a/solution.py
+++ b/solution.py
@@ -518,11 +518,6 @@
     beside = pick(heads, out_weight, (2 * y + 1 - core,), cols)
     beside, corner = swap_core(beside), swap_core(both[: both.shape[0] // 2])
     values = after(values, beside, w_own)
-    weight = join(
-        (w_own, both, beside, corner),
-        (0, both.shape[0] // 2, 0, 0),
-        ((0, 512), (512, 256), (768, 256)),
-    )
     rows_v = exchange(after(pack((values,)), first))
 
     def paired(x):
@@ -532,6 +527,11 @@
     weights, means, early = weigh(paired(q_rows), paired(k_rows), paired(at), tokens)
     early = early.reshape(CLUSTERS, cap, 128)
     early, weights = (pltpu.with_memory_space_constraint(x, pltpu.HBM) for x in (early, weights))
+    weight = join(
+        (after(w_own, means), both, beside, corner),
+        (0, both.shape[0] // 2, 0, 0),
+        ((0, 512), (512, 256), (768, 256)),
+    )
     rows_v = after(rows_v, weight)
     mixed = mix(target, rows_v, early, weights).reshape(CLUSTERS, cap, 128)
 
@@ -548,7 +548,7 @@
         return jnp.concatenate([block[:tokens] for block in blocks], axis=1)
 
     plan = (4, 2, 0, 3, 1, 5, 6, 7)
-    waits = {5: (0,), 6: (4,), 7: (5, 9)}
+    waits = {1: (0,), 6: (4,), 7: (5, 9)}
     ends = {}
     for n, d in enumerate(plan):
         if d == 7:

time: 249 us -> 250 us (level)
  waiting for transfers between devices: 118 us -> 124 us
  starting transfers between devices: 31.7 us -> 26.7 us
    ppermute x6, waiting for transfers between devices: 7.85 us -> 3.33 us  [swap_core(): return lax.ppermute(x, 'head', [(0, 1), (1, 0), (2, 3), (3, 2)])]
    ppermute x7, starting transfers between devices: 12.4 us -> 8.01 us  [swap_ctx(): return lax.ppermute(x, 'ctx', [(i, i ^ d) for i in range(ranks)])]
    all_to_all x2, waiting for transfers between devices: 75.4 us -> 79.6 us  [exchange(): return lax.all_to_all(x, 'ctx', split_axis=0, concat_axis=0, tiled=True)]
    ppermute x7, waiting for transfers between devices: 25.1 us -> 28.2 us  [swap_ctx(): return lax.ppermute(x, 'ctx', [(i, i ^ d) for i in range(ranks)])]
    ppermute x5, waiting for transfers between devices: 9.98 us -> 12.6 us  [swap_y(): return lax.ppermute(x, 'head', [(0, 2), (1, 3), (2, 0), (3, 1)])]
where the time goes in v12:
time: 250 us; the launch traced here: 249 us
  waiting for transfers between devices  124 us (50%)
  Pallas kernels  78.9 us (32%)
  starting transfers between devices  26.7 us (11%)
  matrix products  11.1 us (4%)
  local copies, waits for them, and re-layouts  4.86 us (2%)
  other arithmetic  3.01 us (1%)
    all_to_all x2, waiting for transfers between devices, exchange(): return lax.all_to_all(x, 'ctx', split_axis=0, concat_axis=0, tiled=True)  79.6 us
    ppermute x7, waiting for transfers between devices, swap_ctx(): return lax.ppermute(x, 'ctx', [(i, i ^ d) for i in range(ranks)])  28.2 us
    pallas_call x1, Pallas kernels, place_pair(): pl.pallas_call(place_pair_kernel, grid=(ranks,), in_specs=[pl.BlockSpec((...  19.3 us
    pallas_call x1, Pallas kernels, weigh(): pl.pallas_call(functools.partial(weigh_kernel, tokens), grid=(groups // s...  14 us
    pallas_call x1, Pallas kernels, mix(): pl.pallas_call(functools.partial(mix_kernel, steps), grid=(steps + groups...  13 us
    ppermute x5, waiting for transfers between devices, swap_y(): return lax.ppermute(x, 'head', [(0, 2), (1, 3), (2, 0), (3, 1)])  12.6 us
    pallas_call x3, Pallas kernels, pick(): pl.pallas_call(functools.partial(pick_kernel, count), in_specs=[pl.BlockS...  12.1 us
    dot_general x5, matrix products, add(): jnp.dot(left, weight[row:row + left.shape[1]], preferred_element_type=F32)  11.1 us
  transfers between devices with their start and end apart: 20, of which 11 were waited for; matrix products, arithmetic and copies ran while one was open for 7% of the time, Pallas kernels for 24%

profile of v12, /device:TPU:0, one launch (start us, length us, event | category | flops | bytes accessed | tf_op | source)
XLA Modules:
  0.0 249.3 jit_solution(8281731050102965479)
XLA Ops:
  0.6 4.4 %shard_map.95 = bf16[8,2064,128]{2,1,0:T(8,128)(2,1)} custom-call(bf16[1024,1024]{1,0:T(8,128)(2,1)} %refs_0_.1, bf16[1024,1024]{1,0:T(8,128)(2,1)} %refs_1_.1, s32[8,1024]{1,0:T(8,128)} %refs_2_.1, s32[8,1024]{1,0:T(8,128)} %refs_3_.1), custom_call_target="tpu_custom_call" | custom-call | bytes 8454144 | tf_op jit(solution)/shard_map/pallas_call | solution.py:204
  5.0 7.3 %all-to-all-start = ((bf16[8,2064,128]{2,1,0:T(8,128)(2,1)}), bf16[8,2064,128]{2,1,0:T(8,128)(2,1)}, u32[]{:S(2)}, u32[]{:S(2)}) async-start(bf16[8,2064,128]{2,1,0:T(8,128)(2,1)} %shard_map.95), calls=%async_computation | async-start | bytes 8454144 | tf_op jit(solution)/shard_map/all_to_all | solution.py:505
  12.9 4.9 %shard_map.101 = bf16[2048,1024]{1,0:T(8,128)(2,1)} custom-call(s32[10]{0:T(128)} %pad_add_fusion.2.where_ref, bf16[1024,4096]{1,0:T(8,128)(2,1)} %weight_ref.5), custom_call_target="tpu_custom_call" | custom-call | flops 1 | bytes 1 | tf_op jit(solution)/shard_map/pallas_call | solution.py:244
  20.0 3.6 %shard_map.96 = bf16[1024,1024]{1,0:T(8,128)(2,1)} custom-call(s32[9]{0:T(128)} %get-tuple-element.54.where_ref, bf16[1024,4096]{1,0:T(8,128)(2,1)} %weight_ref.5), custom_call_target="tpu_custom_call" | custom-call | flops 1 | bytes 1 | tf_op jit(solution)/shard_map/pallas_call | solution.py:244
  23.7 3.6 %shard_map.97.refs_0_ = bf16[1024,1024]{1,0:T(8,128)(2,1)} custom-call(s32[9]{0:T(128)} %get-tuple-element.53.where_ref, bf16[1024,4096]{1,0:T(8,128)(2,1)} %weight_ref.5), custom_call_target="tpu_custom_call" | custom-call | flops 1 | bytes 1 | tf_op jit(solution)/shard_map/pallas_call | solution.py:244
  28.1 2.7 %shard_map.98 = bf16[8,1024,128]{2,1,0:T(8,128)(2,1)} custom-call(bf16[1024,1024]{1,0:T(8,128)(2,1)} %refs_0_.2), custom_call_target="tpu_custom_call" | custom-call | bytes 4194304 | tf_op jit(solution)/shard_map/pallas_call | solution.py:204
  30.8 75.4 %all-to-all-done.q_ref.k_ref = bf16[8,2064,128]{2,1,0:T(8,128)(2,1)} async-done(((bf16[8,2064,128]{2,1,0:T(8,128)(2,1)}), bf16[8,2064,128]{2,1,0:T(8,128)(2,1)}, u32[]{:S(2)}, u32[]{:S(2)}) %all-to-all-start) | async-done | bytes 4227104 | tf_op jit(solution)/shard_map/all_to_all | solution.py:505
  106.3 3.6 %all-to-all-start.1 = ((bf16[8,1024,128]{2,1,0:T(8,128)(2,1)}), bf16[8,1024,128]{2,1,0:T(8,128)(2,1)S(1)}, u32[]{:S(2)}, u32[]{:S(2)}) async-start(bf16[8,1024,128]{2,1,0:T(8,128)(2,1)} %shard_map.98), calls=%async_computation.1 | async-start | bytes 4194304 | tf_op jit(solution)/shard_map/all_to_all | solution.py:505
  110.2 3.1 %slice.120 = bf16[1024,1024]{1,0:T(8,128)(2,1)} slice(bf16[2048,1024]{1,0:T(8,128)(2,1)} %collective-permute-done.1.refs_1_), slice={[0:1024], [0:1024]} | slice | bytes 4194304 | tf_op jit(solution)/shard_map/slice | solution.py:519
  114.1 19.3 %shard_map.99 = (bf16[256,64,128]{2,1,0:T(8,128)(2,1)S(1)}, bf16[256,64,128]{2,1,0:T(8,128)(2,1)S(1)}, f32[256,64,128]{2,1,0:T(8,128)S(1)}) custom-call(s32[8,1,1024]{2,1,0:T(1,128)S(1)} %bitcast.74, bf16[8,2064,128]{2,1,0:T(8,128)(2,1)} %all-to-all-done.q_ref.k_ref, bf16[8,2064,128]{2,1,0:T(8,128)(2,1)} %all-to-all-done.q_ref.k_ref), custom_call_target="tpu_custom_call" | custom-call | flops 1 | bytes 1 | tf_op jit(solution)/shard_map/pallas_call | solution.py:323
  133.4 14.0 %shard_map.100 = (bf16[128,128,128]{2,1,0:T(8,128)(2,1)}, f32[256,128]{1,0:T(8,128)S(1)}, bf16[128,128,128]{2,1,0:T(8,128)(2,1)}) custom-call(bf16[128,128,128]{2,1,0:T(8,128)(2,1)S(1)} %bitcast.72, bf16[128,128,128]{2,1,0:T(8,128)(2,1)S(1)} %bitcast.73, f32[128,128,128]{2,1,0:T(8,128)S(1)} %bitcast.71), custom_call_target="tpu_custom_call" | custom-call | flops 1 | bytes 1 | tf_op jit(solution)/shard_map/pallas_call | solution.py:368
  147.4 6.8 %shard_map.102 = bf16[4096,1024]{1,0:T(8,128)(2,1)} custom-call(bf16[1024,1024]{1,0:T(8,128)(2,1)} %shard_map.97.refs_0_, bf16[2048,1024]{1,0:T(8,128)(2,1)} %collective-permute-done.1.refs_1_, bf16[1024,1024]{1,0:T(8,128)(2,1)} %collective-permute-done.refs_2_, bf16[1024,1024]{1,0:T(8,128)(2,1)} %collective-permute-done.2.refs_3_), custom_call_target="tpu_custom_call" | custom-call | flops 1 | bytes 1 | tf_op jit(solution)/shard_map/pallas_call | solution.py:276
  154.2 4.1 %all-to-all-done.1.v_ref = bf16[8,1024,128]{2,1,0:T(8,128)(2,1)S(1)} async-done(((bf16[8,1024,128]{2,1,0:T(8,128)(2,1)}), bf16[8,1024,128]{2,1,0:T(8,128)(2,1)S(1)}, u32[]{:S(2)}, u32[]{:S(2)}) %all-to-all-start.1) | async-done | bytes 2097184 | tf_op jit(solution)/shard_map/all_to_all | solution.py:505
  158.3 13.0 %shard_map.103 = bf16[128,128,128]{2,1,0:T(8,128)(2,1)S(1)} custom-call(s32[8,1,1024]{2,1,0:T(1,128)S(1)} %bitcast.75, bf16[8,1024,128]{2,1,0:T(8,128)(2,1)S(1)} %all-to-all-done.1.v_ref, bf16[256,64,128]{2,1,0:T(8,128)(2,1)} %bitcast.94, bf16[128,128,128]{2,1,0:T(8,128)(2,1)} %get-tuple-element.29.w_ref), custom_call_target="tpu_custom_call" | custom-call | flops 1 | bytes 1 | tf_op jit(solution)/shard_map/pallas_call | solution.py:427
  173.1 2.9 %collective-permute-start.3 = (bf16[1088,128]{1,0:T(8,128)(2,1)S(1)}, bf16[1088,128]{1,0:T(8,128)(2,1)S(1)}, u32[]{:S(2)}, u32[]{:S(2)}) collective-permute-start(bf16[1088,128]{1,0:T(8,128)(2,1)S(1)} %bitcast.87), channel_id=1, source_target_pairs={{0,8},{4,12},{8,0},{12,4},{16,24},{20,28},{24,16},{28,20},{1,9},{5... | collective-permute-start | bytes 835592 | tf_op jit(solution)/shard_map/ppermute | solution.py:502
  179.6 5.3 %collective-permute-done.5 = bf16[1088,128]{1,0:T(8,128)(2,1)S(1)} collective-permute-done((bf16[1088,128]{1,0:T(8,128)(2,1)S(1)}, bf16[1088,128]{1,0:T(8,128)(2,1)S(1)}, u32[]{:S(2)}, u32[]{:S(2)}) %collective-permute-start.5) | collective-permute-done | bytes 278560 | tf_op jit(solution)/shard_map/ppermute | solution.py:493
  189.3 2.4 collective-permute-start.13
  192.0 6.1 %collective-permute-done.4 = bf16[1088,128]{1,0:T(8,128)(2,1)S(1)} collective-permute-done((bf16[1088,128]{1,0:T(8,128)(2,1)S(1)}, bf16[1088,128]{1,0:T(8,128)(2,1)S(1)}, u32[]{:S(2)}, u32[]{:S(2)}) %collective-permute-start.4) | collective-permute-done | bytes 278560 | tf_op jit(solution)/shard_map/ppermute | solution.py:502
  198.2 4.1 %collective-permute-done.6 = bf16[1088,128]{1,0:T(8,128)(2,1)S(1)} collective-permute-done((bf16[1088,128]{1,0:T(8,128)(2,1)S(1)}, bf16[1088,128]{1,0:T(8,128)(2,1)S(1)}, u32[]{:S(2)}, u32[]{:S(2)}) %collective-permute-start.6) | collective-permute-done | bytes 278560 | tf_op jit(solution)/shard_map/ppermute | solution.py:502
  204.2 9.5 %collective-permute-done.10 = bf16[1088,128]{1,0:T(8,128)(2,1)S(1)} collective-permute-done((bf16[1088,128]{1,0:T(8,128)(2,1)S(1)}, bf16[1088,128]{1,0:T(8,128)(2,1)S(1)}, u32[]{:S(2)}, u32[]{:S(2)}) %collective-permute-start.10) | collective-permute-done | bytes 278560 | tf_op jit(solution)/shard_map/ppermute | solution.py:502
  217.1 8.6 %collective-permute-done.14 = bf16[1088,128]{1,0:T(8,128)(2,1)S(1)} collective-permute-done((bf16[1088,128]{1,0:T(8,128)(2,1)S(1)}, bf16[1088,128]{1,0:T(8,128)(2,1)S(1)}, u32[]{:S(2)}, u32[]{:S(2)}) %collective-permute-start.14) | collective-permute-done | bytes 278560 | tf_op jit(solution)/shard_map/ppermute | solution.py:502
  227.3 6.9 %collective-permute-done.11 = bf16[1024,256]{1,0:T(8,128)(2,1)S(1)} collective-permute-done((bf16[1024,256]{1,0:T(8,128)(2,1)S(1)}, bf16[1024,256]{1,0:T(8,128)(2,1)S(1)}, u32[]{:S(2)}, u32[]{:S(2)}) %collective-permute-start.11) | collective-permute-done | bytes 524320 | tf_op jit(solution)/shard_map/ppermute | solution.py:493
  234.6 2.5 collective-permute-done.12
  239.7 4.7 %fusion = f32[1024,1024]{1,0:T(8,128)S(1)} fusion(bf16[1024,2048]{1,0:T(8,128)(2,1)S(1)} %constant_dynamic-update-slice_fusion.4, bf16[4096,1024]{1,0:T(8,128)(2,1)S(1)} %bitcast.93), kind=kOutput, calls=%fused_computation | convolution fusion | flops 4294967296 | bytes 12582912 | tf_op jit(solution)/shard_map/dot_general | solution.py:576
  (87 shorter events, 29.4 us)
Async XLA Ops:
  5.0 7.3 %copy-start.1 = (s32[8]{0:T(128)S(1)}, s32[8]{0:T(128)}, u32[]{:S(2)}) copy-start(s32[8]{0:T(128)} %constant.52.clone) | copy-start | bytes 100
  5.0 101.3 %all-to-all-start = ((bf16[8,2064,128]{2,1,0:T(8,128)(2,1)}), bf16[8,2064,128]{2,1,0:T(8,128)(2,1)}, u32[]{:S(2)}, u32[]{:S(2)}) async-start(bf16[8,2064,128]{2,1,0:T(8,128)(2,1)} %shard_map.95), calls=%async_computation | async-start | bytes 8454144 | tf_op jit(solution)/shard_map/all_to_all | solution.py:505
  17.8 92.4 %collective-permute-start.1 = (bf16[2048,1024]{1,0:T(8,128)(2,1)}, bf16[2048,1024]{1,0:T(8,128)(2,1)}, u32[]{:S(2)}, u32[]{:S(2)}) collective-permute-start(bf16[2048,1024]{1,0:T(8,128)(2,1)} %shard_map.101), channel_id=1, source_target_pairs={{0,2},{1,3},{2,0},{3,1},{4,6},{5,7},{6,4},{7,5},{8,10},{9,11},{10,... | collective-permute-start | bytes 12582920 | tf_op jit(solution)/shard_map/ppermute | solution.py:493
  23.6 4.6 %collective-permute-start = (bf16[1024,1024]{1,0:T(8,128)(2,1)}, bf16[1024,1024]{1,0:T(8,128)(2,1)}, u32[]{:S(2)}, u32[]{:S(2)}) collective-permute-start(bf16[1024,1024]{1,0:T(8,128)(2,1)} %shard_map.96), channel_id=1, source_target_pairs={{0,1},{1,0},{2,3},{3,2},{4,5},{5,4},{6,7},{7,6},{8,9},{9,8},{10,11... | collective-permute-start | bytes 6291464 | tf_op jit(solution)/shard_map/ppermute | solution.py:496
  106.3 52.1 %all-to-all-start.1 = ((bf16[8,1024,128]{2,1,0:T(8,128)(2,1)}), bf16[8,1024,128]{2,1,0:T(8,128)(2,1)S(1)}, u32[]{:S(2)}, u32[]{:S(2)}) async-start(bf16[8,1024,128]{2,1,0:T(8,128)(2,1)} %shard_map.98), calls=%async_computation.1 | async-start | bytes 4194304 | tf_op jit(solution)/shard_map/all_to_all | solution.py:505
  113.3 34.1 %collective-permute-start.2 = (bf16[1024,1024]{1,0:T(8,128)(2,1)}, bf16[1024,1024]{1,0:T(8,128)(2,1)}, u32[]{:S(2)}, u32[]{:S(2)}) collective-permute-start(bf16[1024,1024]{1,0:T(8,128)(2,1)} %slice.120), channel_id=1, source_target_pairs={{0,1},{1,0},{2,3},{3,2},{4,5},{5,4},{6,7},{7,6},{8,9},{9,8},{10,11... | collective-permute-start | bytes 6291464 | tf_op jit(solution)/shard_map/ppermute | solution.py:496
  172.2 16.3 %collective-permute-start.9 = (bf16[1088,128]{1,0:T(8,128)(2,1)S(1)}, bf16[1088,128]{1,0:T(8,128)(2,1)S(1)}, u32[]{:S(2)}, u32[]{:S(2)}) collective-permute-start(bf16[1088,128]{1,0:T(8,128)(2,1)S(1)} %bitcast.89), channel_id=1, source_target_pairs={{0,16},{4,20},{8,24},{12,28},{16,0},{20,4},{24,8},{28,12},{1,17},{... | collective-permute-start | bytes 835592 | tf_op jit(solution)/shard_map/ppermute | solution.py:502
  173.1 18.6 %collective-permute-start.3 = (bf16[1088,128]{1,0:T(8,128)(2,1)S(1)}, bf16[1088,128]{1,0:T(8,128)(2,1)S(1)}, u32[]{:S(2)}, u32[]{:S(2)}) collective-permute-start(bf16[1088,128]{1,0:T(8,128)(2,1)S(1)} %bitcast.87), channel_id=1, source_target_pairs={{0,8},{4,12},{8,0},{12,4},{16,24},{20,28},{24,16},{28,20},{1,9},{5... | collective-permute-start | bytes 835592 | tf_op jit(solution)/shard_map/ppermute | solution.py:502
  176.8 8.1 %collective-permute-start.5 = (bf16[1088,128]{1,0:T(8,128)(2,1)S(1)}, bf16[1088,128]{1,0:T(8,128)(2,1)S(1)}, u32[]{:S(2)}, u32[]{:S(2)}) collective-permute-start(bf16[1088,128]{1,0:T(8,128)(2,1)S(1)} %bitcast.84), channel_id=1, source_target_pairs={{0,2},{1,3},{2,0},{3,1},{4,6},{5,7},{6,4},{7,5},{8,10},{9,11},{10,... | collective-permute-start | bytes 835592 | tf_op jit(solution)/shard_map/ppermute | solution.py:493
  179.4 18.6 %collective-permute-start.4 = (bf16[1088,128]{1,0:T(8,128)(2,1)S(1)}, bf16[1088,128]{1,0:T(8,128)(2,1)S(1)}, u32[]{:S(2)}, u32[]{:S(2)}) collective-permute-start(bf16[1088,128]{1,0:T(8,128)(2,1)S(1)} %bitcast.88), channel_id=1, source_target_pairs={{0,12},{4,8},{8,4},{12,0},{16,28},{20,24},{24,20},{28,16},{1,13},{... | collective-permute-start | bytes 835592 | tf_op jit(solution)/shard_map/ppermute | solution.py:502
  185.8 16.5 %collective-permute-start.6 = (bf16[1088,128]{1,0:T(8,128)(2,1)S(1)}, bf16[1088,128]{1,0:T(8,128)(2,1)S(1)}, u32[]{:S(2)}, u32[]{:S(2)}) collective-permute-start(bf16[1088,128]{1,0:T(8,128)(2,1)S(1)} %bitcast.90), channel_id=1, source_target_pairs={{0,4},{4,0},{8,12},{12,8},{16,20},{20,16},{24,28},{28,24},{1,5},{5... | collective-permute-start | bytes 835592 | tf_op jit(solution)/shard_map/ppermute | solution.py:502
  187.3 26.4 %collective-permute-start.10 = (bf16[1088,128]{1,0:T(8,128)(2,1)S(1)}, bf16[1088,128]{1,0:T(8,128)(2,1)S(1)}, u32[]{:S(2)}, u32[]{:S(2)}) collective-permute-start(bf16[1088,128]{1,0:T(8,128)(2,1)S(1)} %bitcast.86), channel_id=1, source_target_pairs={{0,20},{4,16},{8,28},{12,24},{16,4},{20,0},{24,12},{28,8},{1,21},{... | collective-permute-start | bytes 835592 | tf_op jit(solution)/shard_map/ppermute | solution.py:502
  189.3 27.7 %collective-permute-start.13 = (bf16[1088,128]{1,0:T(8,128)(2,1)S(1)}, bf16[1088,128]{1,0:T(8,128)(2,1)S(1)}, u32[]{:S(2)}, u32[]{:S(2)}) collective-permute-start(bf16[1088,128]{1,0:T(8,128)(2,1)S(1)} %bitcast.85), channel_id=1, source_target_pairs={{0,24},{4,28},{8,16},{12,20},{16,8},{20,12},{24,0},{28,4},{1,25},{... | collective-permute-start | bytes 835592 | tf_op jit(solution)/shard_map/ppermute | solution.py:502
  202.5 34.6 %slice-start = ((s8[8388608]{0:T(1024)(128)(4,1)}), s8[4194304]{0:T(1024)(128)(4,1)S(1)}, s32[]{:S(2)}) async-start(s8[8388608]{0:T(1024)(128)(4,1)} %bitcast.92), calls=%async_computation.2 | async-start | bytes 8388608
  202.6 23.0 %collective-permute-start.7 = (bf16[1024,384]{1,0:T(8,128)(2,1)S(1)}, bf16[1024,384]{1,0:T(8,128)(2,1)S(1)}, u32[]{:S(2)}, u32[]{:S(2)}) collective-permute-start(bf16[1024,384]{1,0:T(8,128)(2,1)S(1)} %pad_maximum_fusion.1), channel_id=1, source_target_pairs={{0,2},{1,3},{2,0},{3,1},{4,6},{5,7},{6,4},{7,5},{8,10},{9,11},{10,... | collective-permute-start | bytes 2359304 | tf_op jit(solution)/shard_map/ppermute | solution.py:493
  213.8 20.5 %collective-permute-start.11 = (bf16[1024,256]{1,0:T(8,128)(2,1)S(1)}, bf16[1024,256]{1,0:T(8,128)(2,1)S(1)}, u32[]{:S(2)}, u32[]{:S(2)}) collective-permute-start(bf16[1024,256]{1,0:T(8,128)(2,1)S(1)} %pad_maximum_fusion.2), channel_id=1, source_target_pairs={{0,2},{1,3},{2,0},{3,1},{4,6},{5,7},{6,4},{7,5},{8,10},{9,11},{10,... | collective-permute-start | bytes 1572872 | tf_op jit(solution)/shard_map/ppermute | solution.py:493
  216.2 9.4 %collective-permute-start.14 = (bf16[1088,128]{1,0:T(8,128)(2,1)S(1)}, bf16[1088,128]{1,0:T(8,128)(2,1)S(1)}, u32[]{:S(2)}, u32[]{:S(2)}) collective-permute-start(bf16[1088,128]{1,0:T(8,128)(2,1)S(1)} %bitcast.91), channel_id=1, source_target_pairs={{0,28},{4,24},{8,20},{12,16},{16,12},{20,8},{24,4},{28,0},{1,29},{... | collective-permute-start | bytes 835592 | tf_op jit(solution)/shard_map/ppermute | solution.py:502
  216.8 20.3 %slice-start.1 = ((s8[8388608]{0:T(1024)(128)(4,1)}), s8[4194304]{0:T(1024)(128)(4,1)S(1)}, s32[]{:S(2)}) async-start(s8[8388608]{0:T(1024)(128)(4,1)} %bitcast.92), calls=%async_computation.3 | async-start | bytes 8388608
  226.1 13.4 %collective-permute-start.8 = (bf16[1024,1024]{1,0:T(8,128)(2,1)S(1)}, bf16[1024,1024]{1,0:T(8,128)(2,1)S(1)}, u32[]{:S(2)}, u32[]{:S(2)}) collective-permute-start(bf16[1024,1024]{1,0:T(8,128)(2,1)S(1)} %get-tuple-element.38), channel_id=1, source_target_pairs={{0,1},{1,0},{2,3},{3,2},{4,5},{5,4},{6,7},{7,6},{8,9},{9,8},{10,11... | collective-permute-start | bytes 6291464 | tf_op jit(solution)/shard_map/ppermute | solution.py:496
  226.2 18.2 %collective-permute-start.15 = (bf16[1024,256]{1,0:T(8,128)(2,1)S(1)}, bf16[1024,256]{1,0:T(8,128)(2,1)S(1)}, u32[]{:S(2)}, u32[]{:S(2)}) collective-permute-start(bf16[1024,256]{1,0:T(8,128)(2,1)S(1)} %pad_maximum_fusion.3), channel_id=1, source_target_pairs={{0,1},{1,0},{2,3},{3,2},{4,5},{5,4},{6,7},{7,6},{8,9},{9,8},{10,11... | collective-permute-start | bytes 1572872 | tf_op jit(solution)/shard_map/ppermute | solution.py:496
  226.8 18.4 %collective-permute-start.16 = (bf16[1024,256]{1,0:T(8,128)(2,1)S(1)}, bf16[1024,256]{1,0:T(8,128)(2,1)S(1)}, u32[]{:S(2)}, u32[]{:S(2)}) collective-permute-start(bf16[1024,256]{1,0:T(8,128)(2,1)S(1)} %pad_maximum_fusion.3), channel_id=1, source_target_pairs={{0,2},{1,3},{2,0},{3,1},{4,6},{5,7},{6,4},{7,5},{8,10},{9,11},{10,... | collective-permute-start | bytes 1572872 | tf_op jit(solution)/shard_map/ppermute | solution.py:493
  234.4 2.7 %collective-permute-start.12 = (bf16[1024,512]{1,0:T(8,128)(2,1)S(1)}, bf16[1024,512]{1,0:T(8,128)(2,1)S(1)}, u32[]{:S(2)}, u32[]{:S(2)}) collective-permute-start(bf16[1024,512]{1,0:T(8,128)(2,1)S(1)} %pad_maximum_fusion), channel_id=1, source_target_pairs={{0,1},{1,0},{2,3},{3,2},{4,5},{5,4},{6,7},{7,6},{8,9},{9,8},{10,11... | collective-permute-start | bytes 3145736 | tf_op jit(solution)/shard_map/ppermute | solution.py:496
  244.4 1.0 copy-start
  245.1 2.1 collective-permute-start.17

commit v13 on v11

--- a/solution.py
+++ b/solution.py
@@ -413,7 +413,7 @@
             o_out[n] = (out[:, :128] / jnp.where(total > 0.0, total, 1.0)).astype(BF16)
 
 
-def mix(target, rows_v, early, weights, senders=4, count=32):
+def mix(target, rows_v, early, weights, senders=4, count=64):
     ranks, tokens = rows_v.shape[0], rows_v.shape[1]
     groups, rows = weights.shape[0], weights.shape[1]
     steps = ranks // senders

time: 249 us -> 249 us (level)
  no operation moved by 1% of the time
where the time goes in v13:
time: 249 us; the launch traced here: 248 us
  waiting for transfers between devices  118 us (47%)
  Pallas kernels  78.1 us (31%)
  starting transfers between devices  31.7 us (13%)
  matrix products  11.1 us (4%)
  local copies, waits for them, and re-layouts  4.82 us (2%)
  other arithmetic  3.09 us (1%)
    all_to_all x2, waiting for transfers between devices, exchange(): return lax.all_to_all(x, 'ctx', split_axis=0, concat_axis=0, tiled=True)  75.4 us
    ppermute x7, waiting for transfers between devices, swap_ctx(): return lax.ppermute(x, 'ctx', [(i, i ^ d) for i in range(ranks)])  25.1 us
    pallas_call x1, Pallas kernels, place_pair(): pl.pallas_call(place_pair_kernel, grid=(ranks,), in_specs=[pl.BlockSpec((...  19.3 us
    pallas_call x1, Pallas kernels, weigh(): pl.pallas_call(functools.partial(weigh_kernel, tokens), grid=(groups // s...  14 us
    ppermute x7, starting transfers between devices, swap_ctx(): return lax.ppermute(x, 'ctx', [(i, i ^ d) for i in range(ranks)])  12.4 us
    pallas_call x1, Pallas kernels, mix(): pl.pallas_call(functools.partial(mix_kernel, steps), grid=(steps + groups...  12.3 us
    pallas_call x3, Pallas kernels, pick(): pl.pallas_call(functools.partial(pick_kernel, count), in_specs=[pl.BlockS...  12.1 us
    dot_general x5, matrix products, add(): jnp.dot(left, weight[row:row + left.shape[1]], preferred_element_type=F32)  11.1 us
  transfers between devices with their start and end apart: 20, of which 11 were waited for; matrix products, arithmetic and copies ran while one was open for 7% of the time, Pallas kernels for 24%

profile of v13, /device:TPU:0, one launch (start us, length us, event | category | flops | bytes accessed | tf_op | source)
XLA Modules:
  0.0 248.1 jit_solution(3644430302146574671)
XLA Ops:
  0.6 4.3 %shard_map.95 = bf16[8,2064,128]{2,1,0:T(8,128)(2,1)} custom-call(bf16[1024,1024]{1,0:T(8,128)(2,1)} %refs_0_.1, bf16[1024,1024]{1,0:T(8,128)(2,1)} %refs_1_.1, s32[8,1024]{1,0:T(8,128)} %refs_2_.1, s32[8,1024]{1,0:T(8,128)} %refs_3_.1), custom_call_target="tpu_custom_call" | custom-call | bytes 8454144 | tf_op jit(solution)/shard_map/pallas_call | solution.py:204
  5.0 7.3 %all-to-all-start = ((bf16[8,2064,128]{2,1,0:T(8,128)(2,1)}), bf16[8,2064,128]{2,1,0:T(8,128)(2,1)}, u32[]{:S(2)}, u32[]{:S(2)}) async-start(bf16[8,2064,128]{2,1,0:T(8,128)(2,1)} %shard_map.95), calls=%async_computation | async-start | bytes 8454144 | tf_op jit(solution)/shard_map/all_to_all | solution.py:505
  12.9 4.9 %shard_map.99 = bf16[2048,1024]{1,0:T(8,128)(2,1)} custom-call(s32[10]{0:T(128)} %pad_add_fusion.2.where_ref, bf16[1024,4096]{1,0:T(8,128)(2,1)} %weight_ref.5), custom_call_target="tpu_custom_call" | custom-call | flops 1 | bytes 1 | tf_op jit(solution)/shard_map/pallas_call | solution.py:244
  20.0 3.6 %shard_map.96 = bf16[1024,1024]{1,0:T(8,128)(2,1)} custom-call(s32[9]{0:T(128)} %get-tuple-element.52.where_ref, bf16[1024,4096]{1,0:T(8,128)(2,1)} %weight_ref.5), custom_call_target="tpu_custom_call" | custom-call | flops 1 | bytes 1 | tf_op jit(solution)/shard_map/pallas_call | solution.py:244
  23.7 3.6 %shard_map.97.refs_0_ = bf16[1024,1024]{1,0:T(8,128)(2,1)} custom-call(s32[9]{0:T(128)} %get-tuple-element.51.where_ref, bf16[1024,4096]{1,0:T(8,128)(2,1)} %weight_ref.5), custom_call_target="tpu_custom_call" | custom-call | flops 1 | bytes 1 | tf_op jit(solution)/shard_map/pallas_call | solution.py:244
  28.2 2.7 %shard_map.98 = bf16[8,1024,128]{2,1,0:T(8,128)(2,1)} custom-call(bf16[1024,1024]{1,0:T(8,128)(2,1)} %refs_0_.2), custom_call_target="tpu_custom_call" | custom-call | bytes 4194304 | tf_op jit(solution)/shard_map/pallas_call | solution.py:204
  30.9 75.4 %all-to-all-done.q_ref.k_ref = bf16[8,2064,128]{2,1,0:T(8,128)(2,1)} async-done(((bf16[8,2064,128]{2,1,0:T(8,128)(2,1)}), bf16[8,2064,128]{2,1,0:T(8,128)(2,1)}, u32[]{:S(2)}, u32[]{:S(2)}) %all-to-all-start) | async-done | bytes 4227104 | tf_op jit(solution)/shard_map/all_to_all | solution.py:505
  106.2 3.6 %all-to-all-start.1 = ((bf16[8,1024,128]{2,1,0:T(8,128)(2,1)}), bf16[8,1024,128]{2,1,0:T(8,128)(2,1)S(1)}, u32[]{:S(2)}, u32[]{:S(2)}) async-start(bf16[8,1024,128]{2,1,0:T(8,128)(2,1)} %shard_map.98), calls=%async_computation.1 | async-start | bytes 4194304 | tf_op jit(solution)/shard_map/all_to_all | solution.py:505
  110.3 3.1 %slice.120 = bf16[1024,1024]{1,0:T(8,128)(2,1)} slice(bf16[2048,1024]{1,0:T(8,128)(2,1)} %collective-permute-done.1.refs_1_), slice={[0:1024], [0:1024]} | slice | bytes 4194304 | tf_op jit(solution)/shard_map/slice | solution.py:519
  113.4 4.5 %collective-permute-done.2.refs_3_ = bf16[1024,1024]{1,0:T(8,128)(2,1)} collective-permute-done((bf16[1024,1024]{1,0:T(8,128)(2,1)}, bf16[1024,1024]{1,0:T(8,128)(2,1)}, u32[]{:S(2)}, u32[]{:S(2)}) %collective-permute-start.2) | collective-permute-done | bytes 2097184 | tf_op jit(solution)/shard_map/ppermute | solution.py:496
  117.9 6.7 %shard_map.100 = bf16[4096,1024]{1,0:T(8,128)(2,1)} custom-call(bf16[1024,1024]{1,0:T(8,128)(2,1)} %shard_map.97.refs_0_, bf16[2048,1024]{1,0:T(8,128)(2,1)} %collective-permute-done.1.refs_1_, bf16[1024,1024]{1,0:T(8,128)(2,1)} %collective-permute-done.refs_2_, bf16[1024,1024]{1,0:T(8,128)(2,1)} %collective-permute-done.2.refs_3_), custom_call_target="tpu_custom_call" | custom-call | flops 1 | bytes 1 | tf_op jit(solution)/shard_map/pallas_call | solution.py:276
  125.4 19.3 %shard_map.101 = (bf16[256,64,128]{2,1,0:T(8,128)(2,1)S(1)}, bf16[256,64,128]{2,1,0:T(8,128)(2,1)S(1)}, f32[256,64,128]{2,1,0:T(8,128)S(1)}) custom-call(s32[8,1,1024]{2,1,0:T(1,128)S(1)} %bitcast.74, bf16[8,2064,128]{2,1,0:T(8,128)(2,1)} %all-to-all-done.q_ref.k_ref, bf16[8,2064,128]{2,1,0:T(8,128)(2,1)} %all-to-all-done.q_ref.k_ref), custom_call_target="tpu_custom_call" | custom-call | flops 1 | bytes 1 | tf_op jit(solution)/shard_map/pallas_call | solution.py:323
  144.7 14.0 %shard_map.102 = (bf16[128,128,128]{2,1,0:T(8,128)(2,1)}, f32[256,128]{1,0:T(8,128)S(1)}, bf16[128,128,128]{2,1,0:T(8,128)(2,1)}) custom-call(bf16[128,128,128]{2,1,0:T(8,128)(2,1)S(1)} %bitcast.72, bf16[128,128,128]{2,1,0:T(8,128)(2,1)S(1)} %bitcast.73, f32[128,128,128]{2,1,0:T(8,128)S(1)} %bitcast.71), custom_call_target="tpu_custom_call" | custom-call | flops 1 | bytes 1 | tf_op jit(solution)/shard_map/pallas_call | solution.py:368
  158.7 12.3 %shard_map.103 = bf16[128,128,128]{2,1,0:T(8,128)(2,1)S(1)} custom-call(s32[8,1,1024]{2,1,0:T(1,128)S(1)} %bitcast.75, bf16[8,1024,128]{2,1,0:T(8,128)(2,1)S(1)} %all-to-all-done.1.v_ref, bf16[256,64,128]{2,1,0:T(8,128)(2,1)} %bitcast.94, bf16[128,128,128]{2,1,0:T(8,128)(2,1)} %get-tuple-element.26.w_ref), custom_call_target="tpu_custom_call" | custom-call | flops 1 | bytes 1 | tf_op jit(solution)/shard_map/pallas_call | solution.py:427
  171.9 2.7 %collective-permute-start.9 = (bf16[1088,128]{1,0:T(8,128)(2,1)S(1)}, bf16[1088,128]{1,0:T(8,128)(2,1)S(1)}, u32[]{:S(2)}, u32[]{:S(2)}) collective-permute-start(bf16[1088,128]{1,0:T(8,128)(2,1)S(1)} %bitcast.89), channel_id=1, source_target_pairs={{0,16},{4,20},{8,24},{12,28},{16,0},{20,4},{24,8},{28,12},{1,17},{... | collective-permute-start | bytes 835592 | tf_op jit(solution)/shard_map/ppermute | solution.py:502
  183.3 2.7 %collective-permute-done.6 = bf16[1088,128]{1,0:T(8,128)(2,1)S(1)} collective-permute-done((bf16[1088,128]{1,0:T(8,128)(2,1)S(1)}, bf16[1088,128]{1,0:T(8,128)(2,1)S(1)}, u32[]{:S(2)}, u32[]{:S(2)}) %collective-permute-start.6) | collective-permute-done | bytes 278560 | tf_op jit(solution)/shard_map/ppermute | solution.py:493
  189.2 2.9 %collective-permute-start.13 = (bf16[1088,128]{1,0:T(8,128)(2,1)S(1)}, bf16[1088,128]{1,0:T(8,128)(2,1)S(1)}, u32[]{:S(2)}, u32[]{:S(2)}) collective-permute-start(bf16[1088,128]{1,0:T(8,128)(2,1)S(1)} %bitcast.85), channel_id=1, source_target_pairs={{0,24},{4,28},{8,16},{12,20},{16,8},{20,12},{24,0},{28,4},{1,25},{... | collective-permute-start | bytes 835592 | tf_op jit(solution)/shard_map/ppermute | solution.py:502
  192.3 8.2 %collective-permute-done.4 = bf16[1088,128]{1,0:T(8,128)(2,1)S(1)} collective-permute-done((bf16[1088,128]{1,0:T(8,128)(2,1)S(1)}, bf16[1088,128]{1,0:T(8,128)(2,1)S(1)}, u32[]{:S(2)}, u32[]{:S(2)}) %collective-permute-start.4) | collective-permute-done | bytes 278560 | tf_op jit(solution)/shard_map/ppermute | solution.py:502
  202.7 10.4 %collective-permute-done.10 = bf16[1088,128]{1,0:T(8,128)(2,1)S(1)} collective-permute-done((bf16[1088,128]{1,0:T(8,128)(2,1)S(1)}, bf16[1088,128]{1,0:T(8,128)(2,1)S(1)}, u32[]{:S(2)}, u32[]{:S(2)}) %collective-permute-start.10) | collective-permute-done | bytes 278560 | tf_op jit(solution)/shard_map/ppermute | solution.py:502
  217.3 6.2 %collective-permute-done.14 = bf16[1088,128]{1,0:T(8,128)(2,1)S(1)} collective-permute-done((bf16[1088,128]{1,0:T(8,128)(2,1)S(1)}, bf16[1088,128]{1,0:T(8,128)(2,1)S(1)}, u32[]{:S(2)}, u32[]{:S(2)}) %collective-permute-start.14) | collective-permute-done | bytes 278560 | tf_op jit(solution)/shard_map/ppermute | solution.py:502
  226.1 6.9 %collective-permute-done.11 = bf16[1024,256]{1,0:T(8,128)(2,1)S(1)} collective-permute-done((bf16[1024,256]{1,0:T(8,128)(2,1)S(1)}, bf16[1024,256]{1,0:T(8,128)(2,1)S(1)}, u32[]{:S(2)}, u32[]{:S(2)}) %collective-permute-start.11) | collective-permute-done | bytes 524320 | tf_op jit(solution)/shard_map/ppermute | solution.py:493
  233.4 2.5 collective-permute-done.12
  235.9 2.3 fusion.2
  238.5 4.7 %fusion = f32[1024,1024]{1,0:T(8,128)S(1)} fusion(bf16[1024,2048]{1,0:T(8,128)(2,1)S(1)} %constant_dynamic-update-slice_fusion.4, bf16[4096,1024]{1,0:T(8,128)(2,1)S(1)} %bitcast.93), kind=kOutput, calls=%fused_computation | convolution fusion | flops 4294967296 | bytes 12582912 | tf_op jit(solution)/shard_map/dot_general | solution.py:576
  (87 shorter events, 32.2 us)
Async XLA Ops:
  5.0 7.3 %copy-start.1 = (s32[8]{0:T(128)S(1)}, s32[8]{0:T(128)}, u32[]{:S(2)}) copy-start(s32[8]{0:T(128)} %constant.52.clone) | copy-start | bytes 100
  5.0 101.3 %all-to-all-start = ((bf16[8,2064,128]{2,1,0:T(8,128)(2,1)}), bf16[8,2064,128]{2,1,0:T(8,128)(2,1)}, u32[]{:S(2)}, u32[]{:S(2)}) async-start(bf16[8,2064,128]{2,1,0:T(8,128)(2,1)} %shard_map.95), calls=%async_computation | async-start | bytes 8454144 | tf_op jit(solution)/shard_map/all_to_all | solution.py:505
  17.8 92.4 %collective-permute-start.1 = (bf16[2048,1024]{1,0:T(8,128)(2,1)}, bf16[2048,1024]{1,0:T(8,128)(2,1)}, u32[]{:S(2)}, u32[]{:S(2)}) collective-permute-start(bf16[2048,1024]{1,0:T(8,128)(2,1)} %shard_map.99), channel_id=1, source_target_pairs={{0,2},{1,3},{2,0},{3,1},{4,6},{5,7},{6,4},{7,5},{8,10},{9,11},{10,... | collective-permute-start | bytes 12582920 | tf_op jit(solution)/shard_map/ppermute | solution.py:493
  23.6 4.6 %collective-permute-start = (bf16[1024,1024]{1,0:T(8,128)(2,1)}, bf16[1024,1024]{1,0:T(8,128)(2,1)}, u32[]{:S(2)}, u32[]{:S(2)}) collective-permute-start(bf16[1024,1024]{1,0:T(8,128)(2,1)} %shard_map.96), channel_id=1, source_target_pairs={{0,1},{1,0},{2,3},{3,2},{4,5},{5,4},{6,7},{7,6},{8,9},{9,8},{10,11... | collective-permute-start | bytes 6291464 | tf_op jit(solution)/shard_map/ppermute | solution.py:496
  106.2 52.4 %all-to-all-start.1 = ((bf16[8,1024,128]{2,1,0:T(8,128)(2,1)}), bf16[8,1024,128]{2,1,0:T(8,128)(2,1)S(1)}, u32[]{:S(2)}, u32[]{:S(2)}) async-start(bf16[8,1024,128]{2,1,0:T(8,128)(2,1)} %shard_map.98), calls=%async_computation.1 | async-start | bytes 4194304 | tf_op jit(solution)/shard_map/all_to_all | solution.py:505
  113.4 4.5 %collective-permute-start.2 = (bf16[1024,1024]{1,0:T(8,128)(2,1)}, bf16[1024,1024]{1,0:T(8,128)(2,1)}, u32[]{:S(2)}, u32[]{:S(2)}) collective-permute-start(bf16[1024,1024]{1,0:T(8,128)(2,1)} %slice.120), channel_id=1, source_target_pairs={{0,1},{1,0},{2,3},{3,2},{4,5},{5,4},{6,7},{7,6},{8,9},{9,8},{10,11... | collective-permute-start | bytes 6291464 | tf_op jit(solution)/shard_map/ppermute | solution.py:496
  171.9 16.5 %collective-permute-start.9 = (bf16[1088,128]{1,0:T(8,128)(2,1)S(1)}, bf16[1088,128]{1,0:T(8,128)(2,1)S(1)}, u32[]{:S(2)}, u32[]{:S(2)}) collective-permute-start(bf16[1088,128]{1,0:T(8,128)(2,1)S(1)} %bitcast.89), channel_id=1, source_target_pairs={{0,16},{4,20},{8,24},{12,28},{16,0},{20,4},{24,8},{28,12},{1,17},{... | collective-permute-start | bytes 835592 | tf_op jit(solution)/shard_map/ppermute | solution.py:502
  175.4 16.7 %collective-permute-start.3 = (bf16[1088,128]{1,0:T(8,128)(2,1)S(1)}, bf16[1088,128]{1,0:T(8,128)(2,1)S(1)}, u32[]{:S(2)}, u32[]{:S(2)}) collective-permute-start(bf16[1088,128]{1,0:T(8,128)(2,1)S(1)} %bitcast.87), channel_id=1, source_target_pairs={{0,8},{4,12},{8,0},{12,4},{16,24},{20,28},{24,16},{28,20},{1,9},{5... | collective-permute-start | bytes 835592 | tf_op jit(solution)/shard_map/ppermute | solution.py:502
  177.7 8.2 %collective-permute-start.6 = (bf16[1088,128]{1,0:T(8,128)(2,1)S(1)}, bf16[1088,128]{1,0:T(8,128)(2,1)S(1)}, u32[]{:S(2)}, u32[]{:S(2)}) collective-permute-start(bf16[1088,128]{1,0:T(8,128)(2,1)S(1)} %bitcast.84), channel_id=1, source_target_pairs={{0,2},{1,3},{2,0},{3,1},{4,6},{5,7},{6,4},{7,5},{8,10},{9,11},{10,... | collective-permute-start | bytes 835592 | tf_op jit(solution)/shard_map/ppermute | solution.py:493
  180.3 20.2 %collective-permute-start.4 = (bf16[1088,128]{1,0:T(8,128)(2,1)S(1)}, bf16[1088,128]{1,0:T(8,128)(2,1)S(1)}, u32[]{:S(2)}, u32[]{:S(2)}) collective-permute-start(bf16[1088,128]{1,0:T(8,128)(2,1)S(1)} %bitcast.90), channel_id=1, source_target_pairs={{0,12},{4,8},{8,4},{12,0},{16,28},{20,24},{24,20},{28,16},{1,13},{... | collective-permute-start | bytes 835592 | tf_op jit(solution)/shard_map/ppermute | solution.py:502
  182.7 18.3 %collective-permute-start.5 = (bf16[1088,128]{1,0:T(8,128)(2,1)S(1)}, bf16[1088,128]{1,0:T(8,128)(2,1)S(1)}, u32[]{:S(2)}, u32[]{:S(2)}) collective-permute-start(bf16[1088,128]{1,0:T(8,128)(2,1)S(1)} %bitcast.88), channel_id=1, source_target_pairs={{0,4},{4,0},{8,12},{12,8},{16,20},{20,16},{24,28},{28,24},{1,5},{5... | collective-permute-start | bytes 835592 | tf_op jit(solution)/shard_map/ppermute | solution.py:502
  186.8 26.4 %collective-permute-start.10 = (bf16[1088,128]{1,0:T(8,128)(2,1)S(1)}, bf16[1088,128]{1,0:T(8,128)(2,1)S(1)}, u32[]{:S(2)}, u32[]{:S(2)}) collective-permute-start(bf16[1088,128]{1,0:T(8,128)(2,1)S(1)} %bitcast.86), channel_id=1, source_target_pairs={{0,20},{4,16},{8,28},{12,24},{16,4},{20,0},{24,12},{28,8},{1,21},{... | collective-permute-start | bytes 835592 | tf_op jit(solution)/shard_map/ppermute | solution.py:502
  189.2 28.1 %collective-permute-start.13 = (bf16[1088,128]{1,0:T(8,128)(2,1)S(1)}, bf16[1088,128]{1,0:T(8,128)(2,1)S(1)}, u32[]{:S(2)}, u32[]{:S(2)}) collective-permute-start(bf16[1088,128]{1,0:T(8,128)(2,1)S(1)} %bitcast.85), channel_id=1, source_target_pairs={{0,24},{4,28},{8,16},{12,20},{16,8},{20,12},{24,0},{28,4},{1,25},{... | collective-permute-start | bytes 835592 | tf_op jit(solution)/shard_map/ppermute | solution.py:502
  201.3 22.1 %collective-permute-start.7 = (bf16[1024,384]{1,0:T(8,128)(2,1)S(1)}, bf16[1024,384]{1,0:T(8,128)(2,1)S(1)}, u32[]{:S(2)}, u32[]{:S(2)}) collective-permute-start(bf16[1024,384]{1,0:T(8,128)(2,1)S(1)} %pad_maximum_fusion.1), channel_id=1, source_target_pairs={{0,2},{1,3},{2,0},{3,1},{4,6},{5,7},{6,4},{7,5},{8,10},{9,11},{10,... | collective-permute-start | bytes 2359304 | tf_op jit(solution)/shard_map/ppermute | solution.py:493
  202.5 33.4 %slice-start = ((s8[8388608]{0:T(1024)(128)(4,1)}), s8[4194304]{0:T(1024)(128)(4,1)S(1)}, s32[]{:S(2)}) async-start(s8[8388608]{0:T(1024)(128)(4,1)} %bitcast.92), calls=%async_computation.2 | async-start | bytes 8388608
  214.0 9.4 %collective-permute-start.14 = (bf16[1088,128]{1,0:T(8,128)(2,1)S(1)}, bf16[1088,128]{1,0:T(8,128)(2,1)S(1)}, u32[]{:S(2)}, u32[]{:S(2)}) collective-permute-start(bf16[1088,128]{1,0:T(8,128)(2,1)S(1)} %bitcast.91), channel_id=1, source_target_pairs={{0,28},{4,24},{8,20},{12,16},{16,12},{20,8},{24,4},{28,0},{1,29},{... | collective-permute-start | bytes 835592 | tf_op jit(solution)/shard_map/ppermute | solution.py:502
  215.6 17.4 %collective-permute-start.11 = (bf16[1024,256]{1,0:T(8,128)(2,1)S(1)}, bf16[1024,256]{1,0:T(8,128)(2,1)S(1)}, u32[]{:S(2)}, u32[]{:S(2)}) collective-permute-start(bf16[1024,256]{1,0:T(8,128)(2,1)S(1)} %pad_maximum_fusion.2), channel_id=1, source_target_pairs={{0,2},{1,3},{2,0},{3,1},{4,6},{5,7},{6,4},{7,5},{8,10},{9,11},{10,... | collective-permute-start | bytes 1572872 | tf_op jit(solution)/shard_map/ppermute | solution.py:493
  217.2 18.7 %slice-start.1 = ((s8[8388608]{0:T(1024)(128)(4,1)}), s8[4194304]{0:T(1024)(128)(4,1)S(1)}, s32[]{:S(2)}) async-start(s8[8388608]{0:T(1024)(128)(4,1)} %bitcast.92), calls=%async_computation.3 | async-start | bytes 8388608
  223.9 14.4 %collective-permute-start.8 = (bf16[1024,1024]{1,0:T(8,128)(2,1)S(1)}, bf16[1024,1024]{1,0:T(8,128)(2,1)S(1)}, u32[]{:S(2)}, u32[]{:S(2)}) collective-permute-start(bf16[1024,1024]{1,0:T(8,128)(2,1)S(1)} %get-tuple-element.36), channel_id=1, source_target_pairs={{0,1},{1,0},{2,3},{3,2},{4,5},{5,4},{6,7},{7,6},{8,9},{9,8},{10,11... | collective-permute-start | bytes 6291464 | tf_op jit(solution)/shard_map/ppermute | solution.py:496
  224.0 19.2 %collective-permute-start.15 = (bf16[1024,256]{1,0:T(8,128)(2,1)S(1)}, bf16[1024,256]{1,0:T(8,128)(2,1)S(1)}, u32[]{:S(2)}, u32[]{:S(2)}) collective-permute-start(bf16[1024,256]{1,0:T(8,128)(2,1)S(1)} %pad_maximum_fusion.3), channel_id=1, source_target_pairs={{0,1},{1,0},{2,3},{3,2},{4,5},{5,4},{6,7},{7,6},{8,9},{9,8},{10,11... | collective-permute-start | bytes 1572872 | tf_op jit(solution)/shard_map/ppermute | solution.py:496
  224.6 19.4 %collective-permute-start.16 = (bf16[1024,256]{1,0:T(8,128)(2,1)S(1)}, bf16[1024,256]{1,0:T(8,128)(2,1)S(1)}, u32[]{:S(2)}, u32[]{:S(2)}) collective-permute-start(bf16[1024,256]{1,0:T(8,128)(2,1)S(1)} %pad_maximum_fusion.3), channel_id=1, source_target_pairs={{0,2},{1,3},{2,0},{3,1},{4,6},{5,7},{6,4},{7,5},{8,10},{9,11},{10,... | collective-permute-start | bytes 1572872 | tf_op jit(solution)/shard_map/ppermute | solution.py:493
  233.2 2.7 %collective-permute-start.12 = (bf16[1024,512]{1,0:T(8,128)(2,1)S(1)}, bf16[1024,512]{1,0:T(8,128)(2,1)S(1)}, u32[]{:S(2)}, u32[]{:S(2)}) collective-permute-start(bf16[1024,512]{1,0:T(8,128)(2,1)S(1)} %pad_maximum_fusion), channel_id=1, source_target_pairs={{0,1},{1,0},{2,3},{3,2},{4,5},{5,4},{6,7},{7,6},{8,9},{9,8},{10,11... | collective-permute-start | bytes 3145736 | tf_op jit(solution)/shard_map/ppermute | solution.py:496
  243.2 1.0 copy-start
  243.9 2.1 collective-permute-start.17
